TPU v7x, 32 devices: a whole 2x2x4 slice. The times are simulated.
32 devices in a mesh: dp: 8 (over z, x), expert: 4 (over y, core).
Axes of the slice: x: 2, y: 2, z: 4, core: 2. Of those that a mesh axis runs over, the one named last changes fastest.
Arguments:
- block_input: bfloat16 [8192, 2048], P(('dp', 'expert')), may hold values from -6 to 6
- segment_ids: int32 [8192], P(('dp', 'expert')), may hold values from 0 to 12, as said below
- expert_ids: int32 [8192, 4], P(('dp', 'expert')), may hold values from 0 to 7, all different within a row
- priority: int32 [32, 256], P(('dp', 'expert')), may hold values from 0 to 255, each once within a row
- cotangent: bfloat16 [8192, 2048], P(('dp', 'expert')), may hold values from -6 to 6
- norm1_gain: bfloat16 [2048], replicated, may hold values from 0.5 to 1.5
- qkv_weight: bfloat16 [3, 2048, 2048], P(None, None, 'expert'), may hold values from -0.125 to 0.125
- qkv_bias: bfloat16 [3, 2048], P(None, 'expert'), may hold values from -1.796875 to 1.796875
- out_weight: bfloat16 [2048, 2048], P('expert'), may hold values from -0.375 to 0.375
- norm2_gain: bfloat16 [2048], replicated, may hold values from 0.5 to 1.5
- router_weight: bfloat16 [2048, 8], replicated, may hold values from -0.0625 to 0.0625
- shared_gate_vector: bfloat16 [2048], replicated, may hold values from -0.125 to 0.125
- shared_gate_up: bfloat16 [2, 2048, 5632], P(None, None, 'expert'), may hold values from -0.125 to 0.125
- shared_down: bfloat16 [5632, 2048], P('expert'), may hold values from -0.21875 to 0.21875
- expert_gate_up: bfloat16 [8, 2, 2048, 1408], P('expert'), may hold values from -0.125 to 0.125
- expert_down: bfloat16 [8, 1408, 2048], P('expert'), may hold values from -0.4375 to 0.4375
Outputs:
- mixed: bfloat16 [8192, 2048], P(('dp', 'expert'))
- input_grad: bfloat16 [8192, 2048], P(('dp', 'expert'))
- norm1_gain_grad: float32 [2048], replicated
- qkv_weight_grad: float32 [3, 2048, 2048], P(None, 'dp', 'expert')
- qkv_bias_grad: float32 [3, 2048], replicated
- out_weight_grad: float32 [2048, 2048], P('expert', 'dp')
- norm2_gain_grad: float32 [2048], replicated
- router_weight_grad: float32 [2048, 8], replicated
- shared_gate_vector_grad: float32 [2048], replicated
- shared_gate_up_grad: float32 [2, 2048, 5632], P(None, 'dp', 'expert')
- shared_down_grad: float32 [5632, 2048], P('expert', 'dp')
- expert_gate_up_grad: float32 [8, 2, 2048, 1408], P('expert', None, 'dp')
- expert_down_grad: float32 [8, 1408, 2048], P('expert', None, 'dp')
Inputs may be any that keep to these rules, and one draw needn't show every extreme that they name: `segment_ids`: each block of 1024 consecutive tokens is one tree. Its first 512 tokens are the trunk, segment 0. The rest holds the segments 1 to 4 * (3) in rising order, each non-empty: branch b (from 0) is segment 1 + b * 3, followed by its 2 leaves. `expert_ids`: each token names 4 different experts; every expert is named by some token. `priority`: each row is a permutation of 0 to 255; row r orders the r-th block of 256 tokens.
All inputs are finite; a program needn't handle non-finite values.
Results may differ from a plain program's by a relative error of at most 0.02.
Values may be sent and summed in bfloat16 or wider, within the bound.
No kernel may reach another device: no remote copies, remote signals or barrier semaphores. Data moves between devices by JAX's collectives and lax.ppermute only.
A program may use at most 384 MiB of HBM per device.

v0:
```python
import math

import jax
import jax.numpy as jnp
from jax import lax
from jax.sharding import PartitionSpec as P

HEAD_DIM = 128
TOP = 4
BRANCHES = 4
LEAVES = 2


EPSILON = 1e-06
THETA = 1000000.0
HIGHEST = lax.Precision.HIGHEST
NEGATIVE = -1e30


def rms_scale(values):
    return lax.rsqrt(jnp.mean(values * values, axis=-1, keepdims=True) + EPSILON)


def tree_positions(segments):
    count_seg = 1 + BRANCHES * (1 + LEAVES)
    seg_range = jnp.arange(count_seg, dtype=jnp.int32)
    onehot = (segments[:, None] == seg_range[None, :]).astype(jnp.float32)
    seg_length = jnp.sum(onehot, axis=0)
    seg_start = jnp.cumsum(seg_length) - seg_length
    offset = jnp.maximum(segments - 1, 0) % (LEAVES + 1)
    is_leaf = (segments > 0) & (offset > 0)
    parent = segments - offset
    parent_hot = (parent[:, None] == seg_range[None, :]).astype(jnp.float32)
    own_start = jnp.sum(onehot * seg_start[None, :], axis=1)
    parent_length = jnp.sum(parent_hot * seg_length[None, :], axis=1)
    places = jnp.arange(segments.shape[0], dtype=jnp.int32).astype(jnp.float32)
    trunk_part = jnp.where(segments > 0, seg_length[0], jnp.float32(0.0))
    leaf_part = jnp.where(is_leaf, parent_length, jnp.float32(0.0))
    return places - own_start + trunk_part + leaf_part


def visible(seg_rows, place_rows, seg_cols, place_cols):
    query_seg = seg_rows[:, None]
    key_seg = seg_cols[None, :]
    branch_key = (key_seg > 0) & ((key_seg - 1) % (LEAVES + 1) == 0)
    related = (
        (key_seg == query_seg)
        | (key_seg == 0)
        | branch_key & (query_seg > key_seg) & (query_seg <= key_seg + LEAVES)
    )
    return related & (place_cols[None, :] <= place_rows[:, None])


def rope_tables(positions):
    half_dim = HEAD_DIM // 2
    frequency = jnp.exp(
        jnp.arange(half_dim, dtype=jnp.float32) * jnp.float32(-2.0 * math.log(THETA) / HEAD_DIM)
    )
    angles = positions[:, None] * frequency[None, :]
    cosine = jnp.cos(angles)
    sine_table = jnp.sin(angles)
    return (
        jnp.concatenate([cosine, cosine], axis=-1)[:, None, :],
        jnp.concatenate([sine_table, sine_table], axis=-1)[:, None, :],
    )


def rotate(values, cosine, sine_table):
    half_dim = values.shape[-1] // 2
    turned = jnp.concatenate([-values[..., half_dim:], values[..., :half_dim]], axis=-1)
    return values * cosine + turned * sine_table


def unrotate(gradient, cosine, sine_table):
    half_dim = gradient.shape[-1] // 2
    scaled = gradient * sine_table
    return gradient * cosine + jnp.concatenate(
        [scaled[..., half_dim:], -scaled[..., :half_dim]], axis=-1
    )


def route_slots(choice_ids, order, expert_count, capacity):
    chosen = (choice_ids[..., None] == jnp.arange(expert_count, dtype=jnp.int32)).astype(
        jnp.float32
    )
    assigned = jnp.sum(chosen, axis=2)
    earlier = (order[:, None, :] < order[:, :, None]).astype(jnp.float32)
    slot_table = jnp.einsum("nts,nse->nte", earlier, assigned, precision=HIGHEST)
    slot_pair = jnp.sum(chosen * slot_table[:, :, None, :], axis=-1)
    return (chosen, slot_pair < capacity, slot_pair.astype(jnp.int32))


def swiglu_grads(act_grad, gate_pre, up_pre):
    gate_sig = jax.nn.sigmoid(gate_pre)
    gate_silu = gate_pre * gate_sig
    gate_grad = (act_grad * up_pre * gate_sig * (1.0 + gate_pre * (1.0 - gate_sig))).astype(
        jnp.bfloat16
    )
    up_grad = (act_grad * gate_silu).astype(jnp.bfloat16)
    return (gate_grad, up_grad)


def per_device(
    block_input,
    segment_ids,
    expert_ids,
    priority,
    cotangent,
    norm1_gain,
    qkv_weight,
    qkv_bias,
    out_weight,
    norm2_gain,
    router_weight,
    shared_gate_vector,
    shared_gate_up,
    shared_down,
    expert_gate_up,
    expert_down,
):
    group_width = lax.axis_size("expert")
    member = lax.axis_index("expert")
    rows_each = block_input.shape[0]
    width_model = block_input.shape[1]
    group_rows = rows_each * group_width
    head_cols = qkv_weight.shape[2]
    local_heads = head_cols // HEAD_DIM
    experts_local = expert_gate_up.shape[0]
    expert_count = experts_local * group_width
    capacity = (9 * rows_each * TOP + 8 * expert_count - 1) // (8 * expert_count)
    dummy_slot = expert_count * capacity
    row_start = member * rows_each
    score_scale = 1.0 / math.sqrt(HEAD_DIM)
    gain_one = norm1_gain.astype(jnp.float32)
    gain_two = norm2_gain.astype(jnp.float32)
    zero_row = jnp.zeros((1, width_model), jnp.bfloat16)
    input_float = block_input.astype(jnp.float32)
    inv_one = rms_scale(input_float)
    normed_one = (input_float * inv_one * gain_one).astype(jnp.bfloat16)
    gathered, seg_sent, cot_all = (
        lax.all_gather(normed_one, "expert", axis=0, tiled=True),
        lax.all_gather(segment_ids.astype(jnp.bfloat16), "expert", axis=0, tiled=True),
        lax.all_gather(cotangent, "expert", axis=0, tiled=True),
    )
    segments = seg_sent.astype(jnp.int32)
    positions = tree_positions(segments)
    cosine, sine_table = rope_tables(positions)
    projected = jnp.einsum("td,jdh->jth", gathered, qkv_weight, preferred_element_type=jnp.float32)
    projected = projected + qkv_bias.astype(jnp.float32)[:, None, :]
    head_shape = (group_rows, local_heads, HEAD_DIM)
    query_rot = rotate(projected[0].reshape(head_shape), cosine, sine_table).astype(jnp.bfloat16)
    key_rot = rotate(projected[1].reshape(head_shape), cosine, sine_table).astype(jnp.bfloat16)
    value_rows = projected[2].reshape(head_shape).astype(jnp.bfloat16)
    block_rows = min(512, group_rows)
    blocks = group_rows // block_rows
    places = jnp.arange(group_rows, dtype=jnp.int32)
    query_blocks = query_rot.reshape(blocks, block_rows, local_heads, HEAD_DIM)
    seg_blocks = segments.reshape(blocks, block_rows)
    place_blocks = places.reshape(blocks, block_rows)

    def block_scores(query_block, seg_block, place_block):
        raw = (
            jnp.einsum("bhd,khd->hbk", query_block, key_rot, preferred_element_type=jnp.float32)
            * score_scale
        )
        return jnp.where(visible(seg_block, place_block, segments, places)[None], raw, NEGATIVE)

    def attend_block(inputs):
        query_block, seg_block, place_block = inputs
        scores = block_scores(query_block, seg_block, place_block)
        peak = jnp.max(scores, axis=-1, keepdims=True)
        weights_raw = jnp.exp(scores - peak)
        total = jnp.sum(weights_raw, axis=-1, keepdims=True)
        weights_low = (weights_raw / total).astype(jnp.bfloat16)
        mixed_heads = jnp.einsum(
            "hbk,khd->bhd", weights_low, value_rows, preferred_element_type=jnp.float32
        )
        return (mixed_heads.astype(jnp.bfloat16), (peak + jnp.log(total))[..., 0])

    attended_blocks, log_totals = lax.map(attend_block, (query_blocks, seg_blocks, place_blocks))
    attended = attended_blocks.reshape(group_rows, head_cols)
    attn_term = jnp.dot(attended, out_weight, preferred_element_type=jnp.float32)
    own_input = lax.dynamic_update_slice_in_dim(
        jnp.zeros((group_rows, width_model), jnp.float32), input_float, row_start, 0
    )
    hidden_all = lax.psum(attn_term + own_input, "expert")
    inv_two = rms_scale(hidden_all)
    normed_all = (hidden_all * inv_two * gain_two).astype(jnp.bfloat16)
    hidden_own = lax.dynamic_slice_in_dim(hidden_all, row_start, rows_each, 0)
    shared_gate = jax.nn.sigmoid(
        jnp.dot(normed_all, shared_gate_vector, preferred_element_type=jnp.float32)
    )
    shared_pre = jnp.einsum(
        "td,jdf->jtf", normed_all, shared_gate_up, preferred_element_type=jnp.float32
    )
    shared_act = (jax.nn.silu(shared_pre[0]) * shared_pre[1]).astype(jnp.bfloat16)
    shared_part = jnp.dot(shared_act, shared_down, preferred_element_type=jnp.float32)
    shared_term = shared_gate[:, None] * shared_part
    view_normed = lax.dynamic_slice_in_dim(normed_all, row_start, rows_each, 0)
    chosen, kept_pairs, slot_pair = route_slots(expert_ids[None], priority, expert_count, capacity)
    chosen = chosen[0]
    taken = kept_pairs[0]
    flat_slot = jnp.where(taken, expert_ids * capacity + slot_pair[0], dummy_slot)
    pair_ids = jnp.arange(rows_each * TOP, dtype=jnp.int32)
    slot_owner = (
        jnp.full((dummy_slot + 1,), rows_each * TOP, jnp.int32)
        .at[flat_slot.reshape(-1)]
        .set(pair_ids)[:dummy_slot]
    )
    outbound = jnp.concatenate([view_normed, zero_row], axis=0)[slot_owner // TOP].reshape(
        expert_count, capacity, width_model
    )
    received_rows = lax.all_to_all(outbound, "expert", split_axis=0, concat_axis=0, tiled=True)
    slot_count = received_rows.shape[1]
    split_rows = received_rows.reshape(group_width, experts_local, slot_count, width_model)
    pre_values = jnp.einsum(
        "jlcd,lkdf->jlckf", split_rows, expert_gate_up, preferred_element_type=jnp.float32
    )
    activation = (jax.nn.silu(pre_values[:, :, :, 0]) * pre_values[:, :, :, 1]).astype(jnp.bfloat16)
    output = jnp.einsum(
        "jlcf,lfd->jlcd", activation, expert_down, preferred_element_type=jnp.float32
    )
    pre_values, output = (
        pre_values.reshape(expert_count, slot_count, 2, -1),
        output.astype(jnp.bfloat16).reshape(expert_count, slot_count, width_model),
    )
    returned = lax.all_to_all(output, "expert", split_axis=0, concat_axis=0, tiled=True)
    expert_pre = pre_values
    router_probs = jax.nn.softmax(
        jnp.dot(view_normed, router_weight, preferred_element_type=jnp.float32), axis=-1
    )
    gate_values = jnp.sum(chosen * router_probs[:, None, :], axis=-1)
    taken_float = taken.astype(jnp.float32)
    pair_weight = gate_values * taken_float
    pair_out = jnp.concatenate([returned.reshape(dummy_slot, width_model), zero_row], axis=0)[
        flat_slot
    ]
    mixture = jnp.sum(pair_weight[..., None] * pair_out.astype(jnp.float32), axis=1)
    scattered = lax.psum_scatter(
        shared_term.astype(jnp.bfloat16), "expert", scatter_dimension=0, tiled=True
    ).astype(jnp.float32)
    mixed_out = (hidden_own + scattered + mixture).astype(jnp.bfloat16)
    cot_all_float = cot_all.astype(jnp.float32)
    view_cot_float = cotangent.astype(jnp.float32)
    gate_grad = taken_float * jnp.sum(
        view_cot_float[:, None, :] * pair_out.astype(jnp.float32), axis=-1
    )
    weight_flat = jnp.concatenate([pair_weight.reshape(-1), jnp.zeros((1,), jnp.float32)])
    cot_padded = jnp.concatenate([cotangent, zero_row], axis=0)
    slot_grad = (
        weight_flat[slot_owner][:, None] * cot_padded[slot_owner // TOP].astype(jnp.float32)
    ).astype(jnp.bfloat16)
    slot_grad = slot_grad.reshape(expert_count, capacity, width_model)
    grad_arrived = lax.all_to_all(slot_grad, "expert", split_axis=0, concat_axis=0, tiled=True)
    split_grad = grad_arrived.reshape(group_width, experts_local, capacity, width_model)
    split_rows = received_rows.reshape(group_width, experts_local, capacity, width_model)
    pre_values = expert_pre.reshape(group_width, experts_local, capacity, 2, -1)
    gate_pre = pre_values[:, :, :, 0]
    up_pre = pre_values[:, :, :, 1]
    activation = (jax.nn.silu(gate_pre) * up_pre).astype(jnp.bfloat16)
    act_grad = jnp.einsum(
        "jlcd,lfd->jlcf", split_grad, expert_down, preferred_element_type=jnp.float32
    )
    expert_gate_grad, expert_up_grad = swiglu_grads(act_grad, gate_pre, up_pre)
    both_grad = jnp.stack([expert_gate_grad, expert_up_grad], axis=3)
    down_weight_grad = jnp.einsum(
        "jlcf,jlcd->lfd", activation, split_grad, preferred_element_type=jnp.float32
    )
    gate_up_weight_grad = jnp.einsum(
        "jlcd,jlckf->lkdf", split_rows, both_grad, preferred_element_type=jnp.float32
    )
    row_grad = jnp.einsum(
        "jlckf,lkdf->jlcd", both_grad, expert_gate_up, preferred_element_type=jnp.float32
    )
    row_grad = row_grad.astype(jnp.bfloat16).reshape(expert_count, capacity, width_model)
    row_back = lax.all_to_all(row_grad, "expert", split_axis=0, concat_axis=0, tiled=True)
    pair_back = jnp.concatenate([row_back.reshape(dummy_slot, width_model), zero_row], axis=0)[
        flat_slot
    ]
    mixture_grad = jnp.sum(pair_back.astype(jnp.float32), axis=1)
    prob_grad = jnp.sum(chosen * gate_grad[..., None], axis=1)
    logit_grad = router_probs * (
        prob_grad - jnp.sum(router_probs * prob_grad, axis=-1, keepdims=True)
    )
    router_grad = jnp.einsum(
        "td,te->de", view_normed.astype(jnp.float32), logit_grad, precision=HIGHEST
    )
    view_grad = mixture_grad + jnp.dot(
        logit_grad, router_weight.astype(jnp.float32).T, precision=HIGHEST
    )
    gate_logit_grad = (
        jnp.sum(cot_all_float * shared_part, axis=-1) * shared_gate * (1.0 - shared_gate)
    )
    gate_vector_grad = jnp.einsum(
        "t,td->d", gate_logit_grad, normed_all.astype(jnp.float32), precision=HIGHEST
    )
    shared_out_grad = (cot_all_float * shared_gate[:, None]).astype(jnp.bfloat16)
    shared_act_grad = jnp.einsum(
        "td,fd->tf", shared_out_grad, shared_down, preferred_element_type=jnp.float32
    )
    shared_gate_grad, shared_up_grad = swiglu_grads(shared_act_grad, shared_pre[0], shared_pre[1])
    shared_both = jnp.stack([shared_gate_grad, shared_up_grad])
    shared_down_grad = jnp.einsum(
        "tf,td->fd", shared_act, shared_out_grad, preferred_element_type=jnp.float32
    )
    shared_gate_up_grad = jnp.einsum(
        "td,jtf->jdf", normed_all, shared_both, preferred_element_type=jnp.float32
    )
    normed_term = jnp.einsum(
        "jtf,jdf->td", shared_both, shared_gate_up, preferred_element_type=jnp.float32
    )
    normed_term = (
        normed_term + gate_logit_grad[:, None] * shared_gate_vector.astype(jnp.float32)[None, :]
    )
    view_placed = lax.dynamic_update_slice_in_dim(
        jnp.zeros((group_rows, width_model), jnp.float32), view_grad, row_start, 0
    )
    normed_grad = lax.psum((normed_term + view_placed).astype(jnp.bfloat16), "expert").astype(
        jnp.float32
    )
    hat_two = hidden_all * inv_two
    scaled_two = normed_grad * gain_two
    hidden_grad = cot_all_float + inv_two * (
        scaled_two - hat_two * jnp.mean(scaled_two * hat_two, axis=-1, keepdims=True)
    )
    gain_two_grad = jnp.sum(
        lax.dynamic_slice_in_dim(normed_grad * hat_two, row_start, rows_each, 0), axis=0
    )
    hidden_low = hidden_grad.astype(jnp.bfloat16)
    hidden_own_grad = lax.dynamic_slice_in_dim(hidden_grad, row_start, rows_each, 0)
    out_weight_grad = jnp.einsum(
        "th,td->hd", attended, hidden_low, preferred_element_type=jnp.float32
    )
    attended_grad = jnp.einsum(
        "td,hd->th", hidden_low, out_weight, preferred_element_type=jnp.float32
    )
    attended_grad = attended_grad.astype(jnp.bfloat16).reshape(
        blocks, block_rows, local_heads, HEAD_DIM
    )

    def backward_block(carry, inputs):
        key_grad, value_grad = carry
        query_block, seg_block, place_block, out_grad_block, log_block = inputs
        scores = block_scores(query_block, seg_block, place_block)
        weights_raw = jnp.exp(scores - log_block[..., None])
        weight_grad = jnp.einsum(
            "bhd,khd->hbk", out_grad_block, value_rows, preferred_element_type=jnp.float32
        )
        delta = jnp.sum(weights_raw * weight_grad, axis=-1, keepdims=True)
        score_grad = (weights_raw * (weight_grad - delta)).astype(jnp.bfloat16)
        query_grad = (
            jnp.einsum("hbk,khd->bhd", score_grad, key_rot, preferred_element_type=jnp.float32)
            * score_scale
        )
        key_grad = (
            key_grad
            + jnp.einsum(
                "hbk,bhd->khd", score_grad, query_block, preferred_element_type=jnp.float32
            )
            * score_scale
        )
        value_grad = value_grad + jnp.einsum(
            "hbk,bhd->khd",
            weights_raw.astype(jnp.bfloat16),
            out_grad_block,
            preferred_element_type=jnp.float32,
        )
        return ((key_grad, value_grad), query_grad)

    zero_heads = jnp.zeros(head_shape, jnp.float32)
    (key_grad, value_grad), query_grad = lax.scan(
        backward_block,
        (zero_heads, zero_heads),
        (query_blocks, seg_blocks, place_blocks, attended_grad, log_totals),
    )
    query_grad = query_grad.reshape(head_shape)
    projected_grad = jnp.stack(
        [
            unrotate(query_grad, cosine, sine_table).astype(jnp.bfloat16),
            unrotate(key_grad, cosine, sine_table).astype(jnp.bfloat16),
            value_grad.astype(jnp.bfloat16),
        ]
    ).reshape(3, group_rows, head_cols)
    qkv_weight_grad = jnp.einsum(
        "td,jth->jdh", gathered, projected_grad, preferred_element_type=jnp.float32
    )
    bias_grad = jnp.sum(projected_grad.astype(jnp.float32), axis=1)
    normed_one_grad = lax.psum_scatter(
        jnp.einsum(
            "jth,jdh->td", projected_grad, qkv_weight, preferred_element_type=jnp.float32
        ).astype(jnp.bfloat16),
        "expert",
        scatter_dimension=0,
        tiled=True,
    ).astype(jnp.float32)
    hat_one = input_float * inv_one
    scaled_one = normed_one_grad * gain_one
    input_grad = (
        hidden_own_grad
        + inv_one * (scaled_one - hat_one * jnp.mean(scaled_one * hat_one, axis=-1, keepdims=True))
    ).astype(jnp.bfloat16)
    gain_one_grad = jnp.sum(normed_one_grad * hat_one, axis=0)
    bias_full = lax.dynamic_update_slice_in_dim(
        jnp.zeros((3, head_cols * group_width), jnp.float32), bias_grad, member * head_cols, 1
    )
    gain_one_sum, gain_two_sum, router_sum, vector_sum, bias_sum = lax.psum(
        (gain_one_grad, gain_two_grad, router_grad, gate_vector_grad, bias_full), ("dp", "expert")
    )
    qkv_sum, out_sum, shared_up_sum, shared_down_sum, expert_up_sum, expert_down_sum = (
        lax.psum_scatter(
            qkv_weight_grad.astype(jnp.bfloat16), "dp", scatter_dimension=1, tiled=True
        ).astype(jnp.float32),
        lax.psum_scatter(
            out_weight_grad.astype(jnp.bfloat16), "dp", scatter_dimension=1, tiled=True
        ).astype(jnp.float32),
        lax.psum_scatter(
            shared_gate_up_grad.astype(jnp.bfloat16), "dp", scatter_dimension=1, tiled=True
        ).astype(jnp.float32),
        lax.psum_scatter(
            shared_down_grad.astype(jnp.bfloat16), "dp", scatter_dimension=1, tiled=True
        ).astype(jnp.float32),
        lax.psum_scatter(
            gate_up_weight_grad.astype(jnp.bfloat16), "dp", scatter_dimension=2, tiled=True
        ).astype(jnp.float32),
        lax.psum_scatter(
            down_weight_grad.astype(jnp.bfloat16), "dp", scatter_dimension=2, tiled=True
        ).astype(jnp.float32),
    )
    return (
        mixed_out,
        input_grad,
        gain_one_sum,
        qkv_sum,
        bias_sum,
        out_sum,
        gain_two_sum,
        router_sum,
        vector_sum,
        shared_up_sum,
        shared_down_sum,
        expert_up_sum,
        expert_down_sum,
    )


def solution(mesh):
    return jax.shard_map(
        per_device,
        mesh=mesh,
        in_specs=(
            P(("dp", "expert"), None),
            P(("dp", "expert")),
            P(("dp", "expert"), None),
            P(("dp", "expert"), None),
            P(("dp", "expert"), None),
            P(),
            P(None, None, "expert"),
            P(None, "expert"),
            P("expert", None),
            P(),
            P(),
            P(),
            P(None, None, "expert"),
            P("expert", None),
            P("expert", None, None, None),
            P("expert", None, None),
        ),
        out_specs=(
            P(("dp", "expert"), None),
            P(("dp", "expert"), None),
            P(),
            P(None, "dp", "expert"),
            P(),
            P("expert", "dp"),
            P(),
            P(),
            P(),
            P(None, "dp", "expert"),
            P("expert", "dp"),
            P("expert", None, "dp", None),
            P("expert", None, "dp"),
        ),
        check_vma=False,
    )
```

profile of v0, /device:TPU:8, one launch (start us, length us, event | category | flops | bytes accessed | tf_op | source)
XLA Modules:
  0.0 2052.2 jit_solution(1508612826863332845)
XLA Ops:
  12.8 5.1 all-gather
  18.5 4.0 multiply_cosine_fusion.1
  28.4 20.2 all-gather.4.cloned.1.call-done
  48.5 10.4 add_bitcast_fusion
  82.0 4.0 copy.147
  89.8 22.3 %while.32 = (s32[]{:T(128)}, bf16[2,512,4,128]{3,2,1,0:T(4,128)(2,1)}, f32[2,4,512]{2,1,0:T(4,128)S(1)}, s32[1024]{0:T(1024)S(1)}, s32[2,512]{1,0:T(2,128)S(1)},...) while((s32[]{:T(128)}, ...), condition=%wide.region_8.9_spmd.clone, body=%wide.region_5.8_spmd.clone.sunk | while | flops 1103898624 | bytes 44142800 | solution.py:180
  112.1 7.2 fusion.116
  124.1 4.3 scatter_custom_fusion
  128.5 147.3 %all-reduce.9.cloned.1.call-done = f32[1024,2048]{1,0:T(8,128)} async-done(((f32[1024,2048]{1,0:T(8,128)}), f32[1024,2048]{1,0:T(8,128)}) %all-reduce.9.cloned.1.call-update) | async-done | bytes 8388624 | tf_op jit(solution)/shard_map/psum | solution.py:186
  275.8 4.0 multiply_reduce_fusion.4
  279.8 7.6 multiply_convert_fusion.2
  290.6 5.9 gather_fusion
  296.5 5.1 all-to-all-start
  307.4 6.0 gather_fusion.3
  318.1 6.5 gather_fusion.2
  324.7 5.4 fusion.51
  330.1 47.8 %all-to-all-done = bf16[8,144,2048]{2,1,0:T(8,128)(2,1)} async-done(((bf16[8,144,2048]{2,1,0:T(8,128)(2,1)}), bf16[8,144,2048]{2,1,0:T(8,128)(2,1)}, u32[]{:S(2)}, u32[]{:S(2)}) %all-to-all-start) | async-done | bytes 4718624 | tf_op jit(solution)/shard_map/all_to_all | solution.py:213
  377.9 5.2 all-to-all-start.2
  383.1 18.9 convolution_bitcast_fusion
  403.1 23.4 %fusion.54 = f32[4,2,144,2,1408]{4,2,3,0,1:T(8,128)} fusion(bf16[2,2,2048,1408]{3,2,1,0:T(8,128)(2,1)} %param.34, bf16[4,2,144,2048,1]{3,2,1,0,4:T(8,128)(2,1)} %bitcast.18), kind=kOutput, calls=%fused_computation.100 | convolution fusion | flops 13287555072 | bytes 40763392 | tf_op jit(solution)/shard_map/jlcd,lkdf->jlckf/dot_general | solution.py:216
  426.5 10.4 all-to-all-done.2
  436.9 17.2 fusion.78
  454.2 22.4 %fusion.44 = bf16[2,4,144,2048,1]{3,2,0,1,4:T(8,128)(2,1)} fusion(bf16[2,2,2048,1408]{3,2,1,0:T(8,128)(2,1)} %param.34, bf16[4,2,144,1,1408]{4,2,0,1,3:T(8,128)(2,1)} %get-tuple-element.575, bf16[4,2,144,1,1408]{4,2,0,1,3:T(8,128)(2,1)} %get-tuple-element.574), kind=kOutput, calls=%fused_computation.75 | convolution fusion | flops 13290799104 | bytes 34275328 | tf_op jit(solution)/shard_map/jlckf,lkdf->jlcd/dot_general | solution.py:272
  481.8 4.9 all-to-all-start.3
  486.8 18.4 fusion.84
  505.2 10.5 convert_bitcast_fusion.2
  518.6 22.0 %all-to-all-done.3 = bf16[8,144,2048]{2,1,0:T(8,128)(2,1)} async-done(((bf16[8,144,2048]{2,1,0:T(8,128)(2,1)}), bf16[8,144,2048]{2,1,0:T(8,128)(2,1)}, u32[]{:S(2)}, u32[]{:S(2)}) %all-to-all-start.3) | async-done | bytes 4718624 | tf_op jit(solution)/shard_map/all_to_all | solution.py:276
  540.6 5.0 all-to-all-start.1
  545.7 12.4 fusion.53
  558.1 17.0 bitcast_add_fusion.2
  575.2 5.3 concatenate.64
  580.4 11.8 gather_fusion.4
  592.2 8.4 reshape.852
  600.7 10.0 reduce_sum.215
  610.6 5.3 concatenate.61
  615.9 11.8 gather_fusion.1
  627.7 8.3 reshape.851
  636.1 11.3 multiply_reduce_fusion.2
  648.1 4.7 fusion.86
  652.8 6.1 convert_element_type.285
  659.5 10.9 convolution_convert_fusion
  676.2 69.7 %all-reduce.11.cloned.1.call-done = bf16[1024,2048]{1,0:T(8,128)(2,1)} async-done(((bf16[1024,2048]{1,0:T(8,128)(2,1)}), bf16[1024,2048]{1,0:T(8,128)(2,1)}) %all-reduce.11.cloned.1.call-update) | async-done | bytes 4194320 | tf_op jit(solution)/shard_map/psum | solution.py:318
  745.9 5.9 multiply_reduce_fusion.1
  753.0 6.1 convert_add_fusion
  765.8 8.2 convolution_convert_fusion.1
  774.1 39.3 %while.33 = (s32[]{:T(128)}, f32[1024,4,128]{0,2,1:T(8,128)}, f32[1024,4,128]{0,2,1:T(8,128)}, f32[2,512,4,128]{3,1,2,0:T(8,128)}, bf16[2,512,4,128]{3,1,2,0:T(8...) while((s32[]{:T(128)}, f32[1024,4,128]{0,2,1:T(8,128)}, ...), condition=%wide.region_28.29_spmd.clone, body=%wide.region_26.28_spmd.clone.sunk | while | flops 2723424256 | bytes 122777952 | solution.py:371
  798.1 5.1 bitcast_add_fusion.7
  813.4 4.4 copy.164
  830.5 4.0 bitcast_multiply_fusion.2
  844.0 11.5 bitcast_convert_fusion.3
  855.6 11.3 convert_bitcast_fusion.1
  866.9 18.5 convert_bitcast_fusion
  885.5 14.6 bitcast_convert_fusion.1
  900.2 24.8 %fusion.46 = bf16[2,2,2048,1408]{2,3,1,0:T(8,128)(2,1)} fusion(bf16[4,2,144,2048,1]{3,2,1,0,4:T(8,128)(2,1)} %bitcast.18, bf16[4,2,144,1,1408]{4,2,0,1,3:T(8,128)(2,1)} %get-tuple-element.575, bf16[4,2,144,1,1408]{4,2,0,1,3:T(8,128)(2,1)} %get-tuple-element.574), kind=kOutput, calls=%fused_computation.77 | convolution fusion | flops 13302333440 | bytes 34275328 | tf_op jit(solution)/shard_map/jlcd,jlckf->lkdf/dot_general | solution.py:269
  930.9 4.3 add_convert_fusion
  941.6 37.1 %reduce-scatter.15.cloned.1.call-done = bf16[512,256]{1,0:T(8,128)(2,1)} async-done(((bf16[512,2048]{1,0:T(8,128)(2,1)}), bf16[512,256]{1,0:T(8,128)(2,1)}) %reduce-scatter.15.cloned.1.call-update) | async-done | bytes 262160 | tf_op jit(solution)/shard_map/reduce_scatter | solution.py:413
  980.5 44.9 %reduce-scatter.11.cloned.1.call-done = bf16[256,2048]{1,0:T(8,128)(2,1)} async-done(((bf16[1024,2048]{1,0:T(8,128)(2,1)}), bf16[256,2048]{1,0:T(8,128)(2,1)}) %reduce-scatter.11.cloned.1.call-update) | async-done | bytes 1048592 | tf_op jit(solution)/shard_map/reduce_scatter | solution.py:388
  1031.0 44.0 %all-reduce.4 = (f32[2048]{0:T(1024)}, f32[3,2048]{1,0:T(4,128)}, f32[2048]{0:T(1024)}, f32[2048]{0:T(1024)}) all-reduce(f32[2048]{0:T(1024)S(1)} %get-tuple-element.510, f32[3,2048]{1,0:T(4,128)S(1)} %constant_dynamic-update-slice_fusion, f32[2048]{0:T(1024)S(1)} %fusion.99, ...), channel_id=1, replica_groups=mesh['dp'=8,'expert'=4] {'dp','expert'}, use_global_device_ids=true, to_apply=%region_32.33 | all-reduce | flops 12288 | bytes 98304 | tf_op jit(solution)/shard_map/psum | solution.py:406
  1075.0 73.1 %reduce-scatter.13.cloned.1.call-done = bf16[3,256,512]{1,2,0:T(8,128)(2,1)} async-done(((bf16[3,2048,512]{1,2,0:T(8,128)(2,1)}), bf16[3,256,512]{1,2,0:T(8,128)(2,1)}) %reduce-scatter.13.cloned.1.call-update) | async-done | bytes 786448 | tf_op jit(solution)/shard_map/reduce_scatter | solution.py:410
  1150.7 192.5 %reduce-scatter.17.cloned.1.call-done = bf16[2,256,1408]{1,2,0:T(8,128)(2,1)} async-done(((bf16[2,2048,1408]{1,2,0:T(8,128)(2,1)}), bf16[2,256,1408]{1,2,0:T(8,128)(2,1)}) %reduce-scatter.17.cloned.1.call-update) | async-done | bytes 1441808 | tf_op jit(solution)/shard_map/reduce_scatter | solution.py:416
  1346.1 193.2 %reduce-scatter.23.cloned.1.call-done = bf16[2,1408,256]{2,1,0:T(8,128)(2,1)} async-done(((bf16[2,1408,2048]{2,1,0:T(8,128)(2,1)}), bf16[2,1408,256]{2,1,0:T(8,128)(2,1)}) %reduce-scatter.23.cloned.1.call-update) | async-done | bytes 1441808 | tf_op jit(solution)/shard_map/reduce_scatter | solution.py:425
  1542.4 374.6 %reduce-scatter.21.cloned.1.call-done = bf16[2,2,256,1408]{2,3,1,0:T(8,128)(2,1)} async-done(((bf16[2,2,2048,1408]{2,3,1,0:T(8,128)(2,1)}), bf16[2,2,256,1408]{2,3,1,0:T(8,128)(2,1)}) %reduce-scatter.21.cloned.1.call-update) | async-done | bytes 2883600 | tf_op jit(solution)/shard_map/reduce_scatter | solution.py:422
  1917.1 5.1 copy.179
  1922.2 121.6 %all-reduce.13.cloned.1.call-done = f32[2048,8]{0,1:T(8,128)} async-done(((f32[2048,8]{0,1:T(8,128)}), f32[2048,8]{0,1:T(8,128)}) %all-reduce.13.cloned.1.call-update) | async-done | bytes 65552 | tf_op jit(solution)/shard_map/psum | solution.py:406
  (376 shorter events, 189.2 us)
Async XLA Ops:
  7.2 104.9 %copy-start = (bf16[512,2048]{1,0:T(8,128)(2,1)S(1)}, bf16[512,2048]{1,0:T(8,128)(2,1)}, u32[]{:S(2)}) copy-start(bf16[512,2048]{1,0:T(8,128)(2,1)} %param.28) | copy-start | bytes 6291460
  7.2 5.6 copy-start.82
  7.2 11.3 copy-start.80
  7.2 41.3 %all-gather.4.cloned.1.call-start = ((), (), s32[]{:S(2)}) async-start(), calls=%async_computation.12 | async-start | bytes 5242880 | tf_op jit(solution)/shard_map/all_gather | solution.py:141
  12.7 263.1 %all-reduce.9.cloned.1.call-start = ((), (), s32[]{:S(2)}) async-start(), calls=%async_computation.13 | async-start | bytes 16777216 | tf_op jit(solution)/shard_map/psum | solution.py:186
  112.1 7.3 copy-start.3
  112.1 7.3 copy-start.28
  112.1 7.3 copy-start.43
  112.1 7.3 copy-start.45
  112.1 7.3 copy-start.60
  112.1 7.3 copy-start.14
  123.4 156.4 %copy-start.49 = (f32[2048]{0:T(1024)}, f32[2048]{0:T(1024)S(1)}, u32[]{:S(2)}) copy-start(f32[2048]{0:T(1024)S(1)} %convert_element_type.259) | copy-start | bytes 24580
  123.8 192.8 %copy-start.64 = (f32[256,4]{0,1:T(4,128)}, f32[256,4]{0,1:T(4,128)S(1)}, u32[]{:S(2)}) copy-start(f32[256,4]{0,1:T(4,128)S(1)} %select_reduce_fusion.4) | copy-start | bytes 12292
  279.8 7.6 copy-start.66
  296.5 5.8 copy-start.74
  296.5 81.4 %all-to-all-start = ((bf16[8,144,2048]{2,1,0:T(8,128)(2,1)}), bf16[8,144,2048]{2,1,0:T(8,128)(2,1)}, u32[]{:S(2)}, u32[]{:S(2)}) async-start(bf16[8,144,2048]{2,1,0:T(8,128)(2,1)} %bitcast.300), calls=%async_computation.1 | async-start | bytes 9437184 | tf_op jit(solution)/shard_map/all_to_all | solution.py:213
  301.6 185.2 %all-gather.6.cloned.1.call-start = ((), (), s32[]{:S(2)}) async-start(), calls=%async_computation.15 | async-start | bytes 5242880 | tf_op jit(solution)/shard_map/all_gather | solution.py:143
  307.4 6.6 copy-start.51
  316.0 8.6 copy-start.72
  377.9 59.0 %all-to-all-start.2 = ((bf16[8,144,2048]{2,1,0:T(8,128)(2,1)}), bf16[8,144,2048]{2,1,0:T(8,128)(2,1)}, u32[]{:S(2)}, u32[]{:S(2)}) async-start(bf16[8,144,2048]{2,1,0:T(8,128)(2,1)} %fusion.51), calls=%async_computation.3 | async-start | bytes 9437184 | tf_op jit(solution)/shard_map/all_to_all | solution.py:254
  383.1 18.9 copy-start.7
  481.8 58.8 %all-to-all-start.3 = ((bf16[8,144,2048]{2,1,0:T(8,128)(2,1)}), bf16[8,144,2048]{2,1,0:T(8,128)(2,1)}, u32[]{:S(2)}, u32[]{:S(2)}) async-start(bf16[8,144,2048]{2,1,0:T(8,128)(2,1)} %bitcast.298), calls=%async_computation.4 | async-start | bytes 9437184 | tf_op jit(solution)/shard_map/all_to_all | solution.py:276
  486.8 18.4 copy-start.84
  540.6 70.0 %all-to-all-start.1 = ((bf16[8,144,2048]{2,1,0:T(8,128)(2,1)}), bf16[8,144,2048]{2,1,0:T(8,128)(2,1)}, u32[]{:S(2)}, u32[]{:S(2)}) async-start(bf16[8,144,2048]{2,1,0:T(8,128)(2,1)} %bitcast.297), calls=%async_computation.2 | async-start | bytes 9437184 | tf_op jit(solution)/shard_map/all_to_all | solution.py:227
  545.6 200.3 %all-reduce.11.cloned.1.call-start = ((), (), s32[]{:S(2)}) async-start(), calls=%async_computation.16 | async-start | bytes 8388608 | tf_op jit(solution)/shard_map/psum | solution.py:318
  545.7 12.4 copy-start.79
  545.7 12.4 copy-start.85
  545.7 12.4 copy-start.86
  558.1 17.1 copy-start.70
  575.2 5.3 copy-start.17
  627.7 8.3 copy-start.40
  636.0 11.4 copy-start.65
  636.0 11.4 copy-start.63
  636.0 11.4 copy-start.59
  636.0 11.4 copy-start.73
  636.0 11.4 copy-start.76
  636.0 12.0 copy-start.52
  636.0 12.0 copy-start.54
  648.1 10.8 copy-start.77
  658.9 272.0 %reduce-scatter.9.cloned.1.call-start = ((), (), s32[]{:S(2)}) async-start(), calls=%async_computation.14 | async-start | bytes 5242880 | tf_op jit(solution)/shard_map/reduce_scatter | solution.py:239
  659.5 279.8 %reduce-scatter.19.cloned.1.call-start = ((), (), s32[]{:S(2)}) async-start(), calls=%async_computation.22 | async-start | bytes 6488064 | tf_op jit(solution)/shard_map/reduce_scatter | solution.py:419
  670.5 75.4 %copy-start.50 = (f32[2048]{0:T(1024)S(1)}, f32[2048]{0:T(1024)}, u32[]{:S(2)}) copy-start(f32[2048]{0:T(1024)} %copy-done.49) | copy-start | bytes 24580
  670.5 308.2 %reduce-scatter.15.cloned.1.call-start = ((), (), s32[]{:S(2)}) async-start(), calls=%async_computation.19 | async-start | bytes 2359296 | tf_op jit(solution)/shard_map/reduce_scatter | solution.py:413
  745.9 5.9 copy-start.9
  745.9 7.0 copy-start.38
  745.9 7.0 copy-start.67
  765.8 8.3 copy-start.4
  765.8 8.3 copy-start.29
  765.8 8.3 copy-start.44
  765.8 8.3 copy-start.46
  765.8 8.3 copy-start.61
  774.0 251.3 %reduce-scatter.11.cloned.1.call-start = ((), (), s32[]{:S(2)}) async-start(), calls=%async_computation.17 | async-start | bytes 5242880 | tf_op jit(solution)/shard_map/reduce_scatter | solution.py:388
  798.1 5.1 copy-start.12
  822.2 8.3 copy-start.31
  844.0 11.5 copy-start.32
  855.5 292.6 %reduce-scatter.13.cloned.1.call-start = ((), (), s32[]{:S(2)}) async-start(), calls=%async_computation.18 | async-start | bytes 7077888 | tf_op jit(solution)/shard_map/reduce_scatter | solution.py:410
  866.9 476.3 %reduce-scatter.17.cloned.1.call-start = ((), (), s32[]{:S(2)}) async-start(), calls=%async_computation.21 | async-start | bytes 12976128 | tf_op jit(solution)/shard_map/reduce_scatter | solution.py:416
  885.5 653.8 %reduce-scatter.23.cloned.1.call-start = ((), (), s32[]{:S(2)}) async-start(), calls=%async_computation.24 | async-start | bytes 12976128 | tf_op jit(solution)/shard_map/reduce_scatter | solution.py:425
  900.2 1016.9 %reduce-scatter.21.cloned.1.call-start = ((), (), s32[]{:S(2)}) async-start(), calls=%async_computation.23 | async-start | bytes 25952256 | tf_op jit(solution)/shard_map/reduce_scatter | solution.py:422
  925.1 1118.7 %all-reduce.13.cloned.1.call-start = ((), (), s32[]{:S(2)}) async-start(), calls=%async_computation.20 | async-start | bytes 131072 | tf_op jit(solution)/shard_map/psum | solution.py:406
  930.9 5.2 copy-start.10
  937.2 88.2 %copy-start.15 = (bf16[256,2048]{1,0:T(8,128)(2,1)S(1)}, bf16[256,2048]{1,0:T(8,128)(2,1)}, u32[]{:S(2)}) copy-start(bf16[256,2048]{1,0:T(8,128)(2,1)} %param.20) | copy-start | bytes 3145732
  937.2 88.1 %copy-start.48 = (f32[2048]{0:T(1024)S(1)}, f32[2048]{0:T(1024)}, u32[]{:S(2)}) copy-start(f32[2048]{0:T(1024)} %copy-done.47) | copy-start | bytes 24580
  937.2 88.1 %copy-start.69 = (f32[256]{0:T(256)S(1)}, f32[256]{0:T(256)}, u32[]{:S(2)}) copy-start(f32[256]{0:T(256)} %copy-done.68) | copy-start | bytes 3076
  (49 other events, 107.7 us)
Sparse Core Ops, SparseCore 0:
  12.9 35.6 all-gather.3
  122.9 152.8 all-reduce.8
  304.0 58.4 all-gather.5
  659.0 86.8 all-reduce.10
  748.4 44.6 reduce-scatter.8
  797.2 110.3 reduce-scatter.18
  911.1 67.5 reduce-scatter.14
  981.2 44.1 reduce-scatter.10
  1029.4 118.6 reduce-scatter.12
  1152.0 191.1 reduce-scatter.16
  1347.2 192.0 reduce-scatter.22
  1543.5 373.4 reduce-scatter.20
  1924.1 119.5 all-reduce.12
where the time goes:
time: 2070 us; the launch traced here: 2050 us
  waiting for transfers between devices  1360 us (66%)
  matrix products  311 us (15%)
  local copies, waits for them, and re-layouts  162 us (8%)
  other arithmetic  137 us (7%)
  blocking collectives  49.1 us (2%)
  starting transfers between devices  20.7 us (1%)
    reduce_scatter x1, waiting for transfers between devices, per_device(): lax.psum_scatter(gate_up_weight_grad.astype(jnp.bfloat16), 'dp', scatter_...  375 us
    reduce_scatter x1, waiting for transfers between devices, per_device(): lax.psum_scatter(down_weight_grad.astype(jnp.bfloat16), 'dp', scatter_dim...  193 us
    reduce_scatter x1, waiting for transfers between devices, per_device(): lax.psum_scatter(shared_gate_up_grad.astype(jnp.bfloat16), 'dp', scatter_...  193 us
    psum x1, waiting for transfers between devices, per_device(): hidden_all = lax.psum(attn_term + own_input, 'expert')  147 us
    psum x1, waiting for transfers between devices, per_device(): lax.psum((gain_one_grad, gain_two_grad, router_grad, gate_vector_grad, bi...  122 us
    reduce_scatter x1, waiting for transfers between devices, per_device(): lax.psum_scatter(qkv_weight_grad.astype(jnp.bfloat16), 'dp', scatter_dime...  73.1 us
    psum x1, waiting for transfers between devices, per_device(): lax.psum((normed_term + view_placed).astype(jnp.bfloat16), 'expert')  69.7 us
    all_to_all x1, waiting for transfers between devices, per_device(): lax.all_to_all(outbound, 'expert', split_axis=0, concat_axis=0, tiled=True)  47.8 us
  transfers between devices with their start and end apart: 17, of which 13 were waited for; matrix products, arithmetic and copies ran while one was open for 22% of the time, Pallas kernels for 0%

commit v1 on v0

v1 whole, which is shorter than its diff:
```python
import math

import numpy as np

import jax
import jax.numpy as jnp
from jax import lax
from jax.sharding import PartitionSpec as P

HEAD_DIM = 128
TOP = 4
BRANCHES = 4
LEAVES = 2

EPSILON = 1e-06
THETA = 1000000.0
NEGATIVE = -1e30
BF16 = jnp.bfloat16
F32 = jnp.float32


def rms_scale(values):
    return lax.rsqrt(jnp.mean(values * values, axis=-1, keepdims=True) + EPSILON)


def tree_positions(segments, places):
    count_seg = 1 + BRANCHES * (1 + LEAVES)
    seg_range = jnp.arange(count_seg, dtype=jnp.int32)
    onehot = (segments[:, None] == seg_range[None, :]).astype(F32)
    seg_length = jnp.sum(onehot, axis=0)
    seg_start = jnp.cumsum(seg_length) - seg_length
    offset = jnp.maximum(segments - 1, 0) % (LEAVES + 1)
    is_leaf = (segments > 0) & (offset > 0)
    parent = segments - offset
    parent_hot = (parent[:, None] == seg_range[None, :]).astype(F32)
    own_start = jnp.sum(onehot * seg_start[None, :], axis=1)
    parent_length = jnp.sum(parent_hot * seg_length[None, :], axis=1)
    trunk_part = jnp.where(segments > 0, seg_length[0], F32(0.0))
    leaf_part = jnp.where(is_leaf, parent_length, F32(0.0))
    return places.astype(F32) - own_start + trunk_part + leaf_part


def visible(seg_rows, place_rows, seg_cols, place_cols):
    query_seg = seg_rows[:, None]
    key_seg = seg_cols[None, :]
    branch_key = (key_seg > 0) & ((key_seg - 1) % (LEAVES + 1) == 0)
    related = (
        (key_seg == query_seg)
        | (key_seg == 0)
        | branch_key & (query_seg > key_seg) & (query_seg <= key_seg + LEAVES)
    )
    return related & (place_cols[None, :] <= place_rows[:, None])


def rope_tables(positions):
    half_dim = HEAD_DIM // 2
    frequency = jnp.exp(
        jnp.arange(half_dim, dtype=F32) * F32(-2.0 * math.log(THETA) / HEAD_DIM)
    )
    angles = positions[:, None] * frequency[None, :]
    cosine = jnp.cos(angles)
    sine_table = jnp.sin(angles)
    return (
        jnp.concatenate([cosine, cosine], axis=-1)[:, None, :],
        jnp.concatenate([sine_table, sine_table], axis=-1)[:, None, :],
    )


def rotate(values, cosine, sine_table):
    half_dim = values.shape[-1] // 2
    turned = jnp.concatenate([-values[..., half_dim:], values[..., :half_dim]], axis=-1)
    return values * cosine + turned * sine_table


def unrotate(gradient, cosine, sine_table):
    half_dim = gradient.shape[-1] // 2
    scaled = gradient * sine_table
    return gradient * cosine + jnp.concatenate(
        [scaled[..., half_dim:], -scaled[..., :half_dim]], axis=-1
    )


def swiglu_grads(act_grad, gate_pre, up_pre):
    gate_sig = jax.nn.sigmoid(gate_pre)
    gate_silu = gate_pre * gate_sig
    gate_grad = (act_grad * up_pre * gate_sig * (1.0 + gate_pre * (1.0 - gate_sig))).astype(BF16)
    up_grad = (act_grad * gate_silu).astype(BF16)
    return (gate_grad, up_grad)


def dot(left, right):
    return jnp.dot(left, right, preferred_element_type=F32)


def dot_nt(left, right):
    return lax.dot_general(left, right, (((1,), (1,)), ((), ())), preferred_element_type=F32)


def dot_tn(left, right):
    return lax.dot_general(left, right, (((0,), (0,)), ((), ())), preferred_element_type=F32)


def cube_of(count):
    digits, left = [], count
    while left > 1:
        size = 4 if left % 4 == 0 else 2
        digits.append(size)
        left //= size
    table = []
    for index in range(count):
        rest, corner = index, 0
        for size, shift in reversed(
            [(s, int(math.log2(math.prod(digits[i + 1 :])))) for i, s in enumerate(digits)]
        ):
            digit = rest % size
            rest //= size
            corner |= (digit ^ (digit >> 1)) << shift
        table.append(corner)
    return table


def swap(values, axis, table, bit):
    where = {corner: index for index, corner in enumerate(table)}
    pairs = [(index, where[corner ^ bit]) for index, corner in enumerate(table)]
    return lax.ppermute(values, axis, pairs)


def group_gather(own, count):
    table = list(range(count))
    blocks = [own] + [None] * (count - 1)
    for place in sorted(range(1, count), key=lambda p: (p & -p) != p or -p):
        bit = place & -place
        blocks[place] = swap(blocks[place ^ bit], "expert", table, bit)
    return blocks


def group_sum(blocks):
    count = len(blocks)
    table = list(range(count))
    bit = 1
    blocks = list(blocks)
    step = 1
    while bit < count:
        keep = [p for p in range(count) if p % (2 * bit) == 0]
        sent = [blocks[p + bit].astype(BF16) for p in keep]
        came = [swap(value, "expert", table, bit) for value in sent]
        for p, value in zip(keep, came):
            blocks[p] = blocks[p].astype(F32) + value.astype(F32)
        bit *= 2
    return blocks[0]


def per_device(
    block_input,
    segment_ids,
    expert_ids,
    priority,
    cotangent,
    norm1_gain,
    qkv_weight,
    qkv_bias,
    out_weight,
    norm2_gain,
    router_weight,
    shared_gate_vector,
    shared_gate_up,
    shared_down,
    expert_gate_up,
    expert_down,
):
    width = lax.axis_size("expert")
    member = lax.axis_index("expert")
    dp_count = lax.axis_size("dp")
    rows_each, dim = block_input.shape
    rows = rows_each * width
    head_cols = qkv_weight.shape[2]
    local_heads = head_cols // HEAD_DIM
    local_experts = expert_gate_up.shape[0]
    expert_count = local_experts * width
    capacity = (9 * rows_each * TOP + 8 * expert_count - 1) // (8 * expert_count)
    score_scale = 1.0 / math.sqrt(HEAD_DIM)
    gain_one = norm1_gain.astype(F32)
    gain_two = norm2_gain.astype(F32)

    cube = cube_of(dp_count)
    cube_bits = int(math.log2(dp_count))
    colours = []
    for colour in range(cube_bits):
        bits = [1 << ((colour + i) % cube_bits) for i in range(cube_bits)]
        order = [0]
        for bit in reversed(bits):
            order = order + [p | bit for p in order]
        colours.append((bits, order))
    at_corner = {corner: index for index, corner in enumerate(cube)}
    block_table = np.array(
        [
            [[at_corner[cube[index] ^ p] for p in order] for _, order in colours]
            for index in range(dp_count)
        ],
        np.int32,
    )
    my_blocks = jnp.asarray(block_table)[lax.axis_index("dp")]
    block_dim = dim // dp_count

    def reordered(values, colour, first, last):
        return jnp.concatenate(
            [
                lax.dynamic_slice_in_dim(
                    values, my_blocks[colour % cube_bits, q] * block_dim, block_dim, 1
                )
                for q in range(first, last)
            ],
            axis=1,
        )

    def weight_sum(colour, values, other, dim_first):
        bits, _ = colours[colour % cube_bits]
        half = dp_count // 2

        def product(first, last):
            side = reordered(values, colour, first, last)
            return (dot_tn(side, other) if dim_first else dot_tn(other, side)).astype(BF16)

        axis = 0 if dim_first else 1

        def part(array, first, last):
            return lax.slice_in_dim(array, first * block_dim, last * block_dim, axis=axis)

        sent = product(half, dp_count)
        own = product(0, half)
        came = [swap(sent, "dp", cube, bits[0])]
        size = half
        for bit in bits[1:]:
            size //= 2
            total = part(own, size, 2 * size).astype(F32)
            for array in came:
                total = total + part(array, size, 2 * size).astype(F32)
            came.append(swap(total.astype(BF16), "dp", cube, bit))
        total = part(own, 0, 1).astype(F32)
        for array in came:
            total = total + part(array, 0, 1).astype(F32)
        return total

    input_blocks = group_gather(block_input, width)
    small = jnp.concatenate(
        [segment_ids[None, :], priority, expert_ids.T], axis=0
    ).astype(BF16)
    small_blocks = group_gather(small, width)
    out_blocks = group_gather(out_weight, width)
    cot_blocks = group_gather(cotangent, width)
    small_all = jnp.concatenate(small_blocks, axis=1).astype(jnp.int32)
    segments = small_all[0]
    order_all = small_all[1].reshape(width, rows_each)
    ids_all = small_all[2:].T
    block_place = (member ^ jnp.arange(width, dtype=jnp.int32)) * rows_each
    places = (block_place[:, None] + jnp.arange(rows_each, dtype=jnp.int32)[None, :]).reshape(-1)

    input_all = jnp.concatenate(input_blocks, axis=0)
    input_float = input_all.astype(F32)
    inv_one_all = rms_scale(input_float)
    normed_one = (input_float * inv_one_all * gain_one).astype(BF16)
    cosine, sine_table = rope_tables(tree_positions(segments, places))
    head_shape = (rows, local_heads, HEAD_DIM)
    projected = [
        (dot(normed_one, qkv_weight[j]) + qkv_bias[j].astype(F32)[None, :]).reshape(head_shape)
        for j in range(3)
    ]
    query_rot = rotate(projected[0], cosine, sine_table).astype(BF16)
    key_rot = rotate(projected[1], cosine, sine_table).astype(BF16)
    value_rows = projected[2].astype(BF16)
    block_rows = min(512, rows)
    blocks = rows // block_rows
    query_blocks = query_rot.reshape(blocks, block_rows, local_heads, HEAD_DIM)
    seg_blocks = segments.reshape(blocks, block_rows)
    place_blocks = places.reshape(blocks, block_rows)

    def block_scores(query_block, seg_block, place_block):
        raw = (
            jnp.einsum("bhd,khd->hbk", query_block, key_rot, preferred_element_type=F32)
            * score_scale
        )
        return jnp.where(visible(seg_block, place_block, segments, places)[None], raw, NEGATIVE)

    def attend_block(inputs):
        query_block, seg_block, place_block = inputs
        scores = block_scores(query_block, seg_block, place_block)
        peak = jnp.max(scores, axis=-1, keepdims=True)
        weights_raw = jnp.exp(scores - peak)
        total = jnp.sum(weights_raw, axis=-1, keepdims=True)
        weights_low = (weights_raw / total).astype(BF16)
        mixed_heads = jnp.einsum(
            "hbk,khd->bhd", weights_low, value_rows, preferred_element_type=F32
        )
        return (mixed_heads.astype(BF16), (peak + jnp.log(total))[..., 0])

    attended_blocks, log_totals = lax.map(attend_block, (query_blocks, seg_blocks, place_blocks))
    attended = attended_blocks.reshape(rows, head_cols)

    attended_all = jnp.concatenate(
        [
            jnp.concatenate(
                [came[(q ^ p) * rows_each : ((q ^ p) + 1) * rows_each] for q in range(width)], axis=0
            )
            for p, came in enumerate(group_gather(attended, width))
        ],
        axis=1,
    )
    out_all = jnp.concatenate(out_blocks, axis=0)
    hidden = input_float + dot(attended_all, out_all)
    inv_two = rms_scale(hidden)
    normed = (hidden * inv_two * gain_two).astype(BF16)
    hidden_own = hidden[:rows_each]
    inv_two_own = inv_two[:rows_each]

    side_weight = jnp.concatenate([router_weight, shared_gate_vector[:, None]], axis=1)
    side_pre = dot(normed, side_weight)
    router_probs = jax.nn.softmax(side_pre[:, :expert_count], axis=-1)
    shared_gate = jax.nn.sigmoid(side_pre[:, expert_count])
    local_ids = member * local_experts + jnp.arange(local_experts, dtype=jnp.int32)
    named = jnp.any(ids_all[:, :, None] == local_ids[None, None, :], axis=1)
    named_blocks = named.reshape(width, rows_each, local_experts)
    earlier = (order_all[:, None, :] < order_all[:, :, None]).astype(BF16)
    slot = jnp.einsum(
        "pts,psl->ptl", earlier, named_blocks.astype(BF16), preferred_element_type=F32
    )
    slot_range = jnp.arange(capacity, dtype=F32)
    place_hot = (
        (slot.transpose(0, 2, 1)[:, :, None, :] == slot_range[None, None, :, None])
        & named_blocks.transpose(0, 2, 1)[:, :, None, :]
    )
    place_low = place_hot.astype(BF16)
    probs_local = lax.dynamic_slice_in_dim(
        router_probs, member * local_experts, local_experts, 1
    ).reshape(width, rows_each, local_experts)
    gate_slot = jnp.sum(
        jnp.where(place_hot, probs_local.transpose(0, 2, 1)[:, :, None, :], 0.0), axis=-1
    )

    cot_all = jnp.concatenate(cot_blocks, axis=0)
    cot_float = cot_all.astype(F32)
    slots = width * capacity

    def dispatch(values, expert):
        return jnp.einsum(
            "pct,ptd->pcd",
            place_low[:, expert],
            values.reshape(width, rows_each, dim),
            preferred_element_type=F32,
        ).reshape(slots, dim)

    shared_pre = [dot(normed, shared_gate_up[j]) for j in range(2)]
    shared_act = (jax.nn.silu(shared_pre[0]) * shared_pre[1]).astype(BF16)
    shared_out_grad = (cot_float * shared_gate[:, None]).astype(BF16)
    shared_act_grad = dot_nt(shared_out_grad, shared_down)
    shared_gate_grad, shared_up_grad = swiglu_grads(shared_act_grad, shared_pre[0], shared_pre[1])
    shared_up_sums = [
        weight_sum(0, normed, shared_gate_grad, True),
        weight_sum(1, normed, shared_up_grad, True),
    ]
    shared_down_sum = weight_sum(2, shared_out_grad, shared_act, False)

    expert_up_sums, expert_down_sums = [], []
    gated_rows, row_grads, gate_grads = [], [], []
    for expert in range(local_experts):
        rows_in = dispatch(normed, expert).astype(BF16)
        cot_in = dispatch(cot_all, expert)
        gate_in = gate_slot[:, expert].reshape(slots, 1)
        slot_grad = (gate_in * cot_in).astype(BF16)
        gate_pre = dot(rows_in, expert_gate_up[expert, 0])
        up_pre = dot(rows_in, expert_gate_up[expert, 1])
        activation = (jax.nn.silu(gate_pre) * up_pre).astype(BF16)
        act_grad = dot_nt(slot_grad, expert_down[expert])
        gate_pre_grad, up_pre_grad = swiglu_grads(act_grad, gate_pre, up_pre)
        expert_up_sums.append(
            [
                weight_sum(3 * expert, rows_in, gate_pre_grad, True),
                weight_sum(3 * expert + 1, rows_in, up_pre_grad, True),
            ]
        )
        expert_down_sums.append(weight_sum(3 * expert + 2, slot_grad, activation, False))
        output = dot(activation, expert_down[expert]).astype(BF16).astype(F32)
        gate_grads.append(jnp.sum(output * cot_in, axis=-1).reshape(width, capacity))
        gated_rows.append((gate_in * output).astype(BF16).reshape(width, capacity, dim))
        row_grads.append(
            (
                dot_nt(gate_pre_grad, expert_gate_up[expert, 0])
                + dot_nt(up_pre_grad, expert_gate_up[expert, 1])
            )
            .astype(BF16)
            .reshape(width, capacity, dim)
        )

    all_hot = place_low.reshape(width, local_experts * capacity, rows_each)

    def combine(pieces):
        stacked = jnp.stack(pieces, axis=1).reshape(width, local_experts * capacity, dim)
        return jnp.einsum("pct,pcd->ptd", all_hot, stacked, preferred_element_type=F32).reshape(
            rows, dim
        )

    shared_part = dot(shared_act, shared_down)

    prob_grad_local = jnp.sum(
        jnp.where(place_hot, jnp.stack(gate_grads, axis=1)[..., None], 0.0), axis=2
    ).transpose(0, 2, 1).reshape(rows, local_experts)
    prob_grad = lax.dynamic_update_slice_in_dim(
        jnp.zeros((rows, expert_count), F32), prob_grad_local, member * local_experts, 1
    )
    logit_grad = router_probs * (
        prob_grad - jnp.sum(router_probs * prob_grad, axis=-1, keepdims=True)
    )
    gate_logit_grad = (
        jnp.sum(cot_float * shared_part, axis=-1) * shared_gate * (1.0 - shared_gate)
    )
    side_grad = jnp.concatenate([logit_grad, gate_logit_grad[:, None]], axis=1)
    side_high = side_grad.astype(BF16)
    side_low = (side_grad - side_high.astype(F32)).astype(BF16)
    side_both = jnp.concatenate([side_high, side_low], axis=1)
    side_weight_both = jnp.concatenate([side_weight, side_weight], axis=1)
    side_sum = dot_tn(side_both, normed)
    side_sum = side_sum[: expert_count + 1] + side_sum[expert_count + 1 :]
    normed_grad_part = (
        dot_nt(shared_gate_grad, shared_gate_up[0])
        + dot_nt(shared_up_grad, shared_gate_up[1])
        + combine(row_grads)
        + dot_nt(side_both, side_weight_both)
    )
    normed_grad = group_sum(
        [normed_grad_part[p * rows_each : (p + 1) * rows_each] for p in range(width)]
    )
    hat_two = hidden_own * inv_two_own
    scaled_two = normed_grad * gain_two
    hidden_grad = cotangent.astype(F32) + inv_two_own * (
        scaled_two - hat_two * jnp.mean(scaled_two * hat_two, axis=-1, keepdims=True)
    )
    gain_two_grad = jnp.sum(normed_grad * hat_two, axis=0)
    hidden_low = jnp.concatenate(group_gather(hidden_grad.astype(BF16), width), axis=0)

    mixed_part = shared_gate[:, None] * shared_part + combine(gated_rows)
    mixed_sum = group_sum([mixed_part[p * rows_each : (p + 1) * rows_each] for p in range(width)])
    mixed_out = (hidden_own + mixed_sum).astype(BF16)

    attended_grad = (
        dot_nt(hidden_low, out_weight)
        .astype(BF16)
        .reshape(blocks, block_rows, local_heads, HEAD_DIM)
    )
    out_sum = weight_sum(0, hidden_low, attended, False)

    def backward_block(carry, inputs):
        key_grad, value_grad = carry
        query_block, seg_block, place_block, out_grad_block, log_block = inputs
        scores = block_scores(query_block, seg_block, place_block)
        weights_raw = jnp.exp(scores - log_block[..., None])
        weight_grad = jnp.einsum(
            "bhd,khd->hbk", out_grad_block, value_rows, preferred_element_type=F32
        )
        delta = jnp.sum(weights_raw * weight_grad, axis=-1, keepdims=True)
        score_grad = (weights_raw * (weight_grad - delta)).astype(BF16)
        query_grad = (
            jnp.einsum("hbk,khd->bhd", score_grad, key_rot, preferred_element_type=F32)
            * score_scale
        )
        key_grad = (
            key_grad
            + jnp.einsum("hbk,bhd->khd", score_grad, query_block, preferred_element_type=F32)
            * score_scale
        )
        value_grad = value_grad + jnp.einsum(
            "hbk,bhd->khd", weights_raw.astype(BF16), out_grad_block, preferred_element_type=F32
        )
        return ((key_grad, value_grad), query_grad)

    zero_heads = jnp.zeros(head_shape, F32)
    (key_grad, value_grad), query_grad = lax.scan(
        backward_block,
        (zero_heads, zero_heads),
        (query_blocks, seg_blocks, place_blocks, attended_grad, log_totals),
    )
    query_grad = query_grad.reshape(head_shape)
    projected_grad = [
        unrotate(query_grad, cosine, sine_table).astype(BF16).reshape(rows, head_cols),
        unrotate(key_grad, cosine, sine_table).astype(BF16).reshape(rows, head_cols),
        value_grad.astype(BF16).reshape(rows, head_cols),
    ]
    qkv_sum = jnp.stack([weight_sum(j, normed_one, projected_grad[j], True) for j in range(3)])
    bias_grad = jnp.stack([jnp.sum(grad.astype(F32), axis=0) for grad in projected_grad])
    normed_one_part = sum(dot_nt(projected_grad[j], qkv_weight[j]) for j in range(3))
    normed_one_grad = group_sum(
        [normed_one_part[p * rows_each : (p + 1) * rows_each] for p in range(width)]
    )
    inv_one = inv_one_all[:rows_each]
    hat_one = block_input.astype(F32) * inv_one
    scaled_one = normed_one_grad * gain_one
    input_grad = (
        hidden_grad
        + inv_one * (scaled_one - hat_one * jnp.mean(scaled_one * hat_one, axis=-1, keepdims=True))
    ).astype(BF16)
    gain_one_grad = jnp.sum(normed_one_grad * hat_one, axis=0)

    def everywhere(values):
        bit = 1
        while bit < width:
            values = values + swap(values, "expert", list(range(width)), bit)
            bit *= 2
        bit = 1
        while bit < dp_count:
            values = values + swap(values, "dp", cube, bit)
            bit *= 2
        return values

    first_sums = everywhere(jnp.concatenate([gain_two_grad[None, :], side_sum], axis=0))
    bias_full = lax.dynamic_update_slice_in_dim(
        jnp.zeros((3, dim), F32), bias_grad, member * head_cols, 1
    )
    last_sums = everywhere(jnp.concatenate([gain_one_grad[None, :], bias_full], axis=0))
    return (
        mixed_out,
        input_grad,
        last_sums[0],
        qkv_sum,
        last_sums[1:],
        out_sum,
        first_sums[0],
        first_sums[1 : 1 + expert_count].T,
        first_sums[1 + expert_count],
        jnp.stack(shared_up_sums),
        shared_down_sum,
        jnp.stack([jnp.stack(pair) for pair in expert_up_sums]),
        jnp.stack(expert_down_sums),
    )


def solution(mesh):
    return jax.shard_map(
        per_device,
        mesh=mesh,
        in_specs=(
            P(("dp", "expert"), None),
            P(("dp", "expert")),
            P(("dp", "expert"), None),
            P(("dp", "expert"), None),
            P(("dp", "expert"), None),
            P(),
            P(None, None, "expert"),
            P(None, "expert"),
            P("expert", None),
            P(),
            P(),
            P(),
            P(None, None, "expert"),
            P("expert", None),
            P("expert", None, None, None),
            P("expert", None, None),
        ),
        out_specs=(
            P(("dp", "expert"), None),
            P(("dp", "expert"), None),
            P(),
            P(None, "dp", "expert"),
            P(),
            P("expert", "dp"),
            P(),
            P(),
            P(),
            P(None, "dp", "expert"),
            P("expert", "dp"),
            P("expert", None, "dp", None),
            P("expert", None, "dp"),
        ),
        check_vma=False,
    )
```

time: 2070 us -> 1310 us (0.63)
  waiting for transfers between devices: 1360 us -> 465 us
  starting transfers between devices: 20.7 us -> 120 us
  matrix products: 311 us -> 404 us
  local copies, waits for them, and re-layouts: 162 us -> 109 us
  blocking collectives: 49.1 us -> 0 us
  other arithmetic: 137 us -> 182 us
    reduce_scatter x8 -> x0, waiting for transfers between devices: 915 us -> none  [the longest x1 375 us: per_device(): lax.psum_scatter(gate_up_weight_grad.astype(jnp.bfloat16), 'dp', scatter_...]
    ppermute x0 -> x76, waiting for transfers between devices: none -> 465 us  [swap(): return lax.ppermute(values, axis, pairs)]
    psum x3 -> x0, waiting for transfers between devices: 339 us -> none  [the longest x1 147 us: per_device(): hidden_all = lax.psum(attn_term + own_input, 'expert')]
    ppermute x0 -> x76, starting transfers between devices: none -> 120 us  [swap(): return lax.ppermute(values, axis, pairs)]
    dot_general x32 -> x70, matrix products: 295 us -> 383 us  [the longest x14 127 us: dot(): return jnp.dot(left, right, preferred_element_type=F32)]
    all_to_all x4 -> x0, waiting for transfers between devices: 80.2 us -> none  [the longest x1 47.8 us: per_device(): lax.all_to_all(outbound, 'expert', split_axis=0, concat_axis=0, tiled=True)]
    psum x1 -> x0, blocking collectives: 44 us -> none  [per_device(): lax.psum((gain_one_grad, gain_two_grad, router_grad, gate_vector_grad, bi...]
    gather x5 -> x0, local copies, waits for them, and re-layouts: 41.9 us -> none  [the longest x1 11.8 us: per_device(): jnp.concatenate([row_back.reshape(dummy_slot, width_model), zero_row], ax...]
  transfers between devices with their start and end apart: 17 -> 76, of which waited for: 13 -> 25; matrix products, arithmetic and copies ran while one was open for 22% -> 41% of each run, Pallas kernels for 0% -> 0%
where the time goes in v1:
time: 1310 us; the launch traced here: 1300 us
  waiting for transfers between devices  465 us (35%)
  matrix products  404 us (31%)
  other arithmetic  182 us (14%)
  starting transfers between devices  120 us (9%)
  local copies, waits for them, and re-layouts  109 us (8%)
  between operations  19.6 us (1%)
    ppermute x76, waiting for transfers between devices, swap(): return lax.ppermute(values, axis, pairs)  465 us
    dot_general x14, matrix products, dot(): return jnp.dot(left, right, preferred_element_type=F32)  127 us
    ppermute x76, starting transfers between devices, swap(): return lax.ppermute(values, axis, pairs)  120 us
    dot_general x14, matrix products, dot_nt(): lax.dot_general(left, right, (((1,), (1,)), ((), ())), preferred_element_...  118 us
    dot_general x27, matrix products, dot_tn(): lax.dot_general(left, right, (((0,), (0,)), ((), ())), preferred_element_...  103 us
    convert_element_type x26, other arithmetic, weight_sum(): came.append(swap(total.astype(BF16), 'dp', cube, bit))  47.7 us
    unnamed x526, local copies, waits for them, and re-layouts  28.3 us
  transfers between devices with their start and end apart: 76, of which 25 were waited for; matrix products, arithmetic and copies ran while one was open for 41% of the time, Pallas kernels for 0%

profile of v1, /device:TPU:8, one launch (start us, length us, event | category | flops | bytes accessed | tf_op | source)
XLA Modules:
  0.0 1300.5 jit_solution(14043370858709181008)
XLA Ops:
  36.3 4.6 multiply_cosine_fusion.1
  62.8 6.9 fusion.288
  76.0 5.3 fusion.285
  99.1 5.2 add_convert_fusion.12
  108.7 19.9 %while.32 = (s32[]{:T(128)}, bf16[2,512,4,128]{3,2,1,0:T(4,128)(2,1)}, f32[2,4,512]{2,1,0:T(4,128)S(1)}, s32[1,1024]{1,0:T(1,128)S(1)}, s32[2,512]{1,0:T(2,128)S...) while((s32[]{:T(128)}, ...), condition=%wide.region_8.9_spmd.clone, body=%wide.region_5.8_spmd.clone.sunk | while | flops 1103899648 | bytes 31576712 | solution.py:296
  133.0 7.5 constant_dynamic-slice_fusion.108
  144.9 11.5 collective-permute-done.7
  166.0 25.7 %multiply_reduce_fusion.1 = (f32[1024]{0:T(1024)S(1)}, f32[1024,2048]{1,0:T(8,128)}) fusion(bf16[512,2048]{1,0:T(8,128)(2,1)} %copy-done.227, bf16[512,2048]{1,0:T(8,128)(2,1)} %collective-permute-done.10, bf16[512,2048]{1,0:T(8,128)(2,1)} %collective-permute-done.9, bf16[512,2048]{1,0:T(8,128)(2,1)} %param.29, bf16[256,512]{1,0:T(8,128)(2,1)} %get-tuple-element.704, ...), kind=kOutput, calls=%fused_computation.88 | convolution fusion | flops 8692694016 | bytes 25169920 | tf_op jit(solution)/shard_map/dot_general | solution.py:92
  191.7 4.2 multiply_convert_fusion.1
  200.8 8.2 fusion.76
  209.0 8.1 fusion.64
  224.1 10.3 multiply_convert_fusion.14
  234.4 7.4 fusion.138
  244.0 8.6 multiply_convert_fusion.13
  252.6 7.3 fusion.141
  260.6 11.8 fusion.84
  272.4 12.2 multiply_convert_fusion.4
  284.6 9.1 fusion.41
  295.3 5.9 multiply_convert_fusion.6
  326.8 9.2 fusion.466
  338.1 13.9 %multiply_convert_fusion.2 = (bf16[1024,1408]{1,0:T(8,128)(2,1)S(1)}, bf16[1024,1408]{1,0:T(8,128)(2,1)}) fusion(f32[1024,1408]{1,0:T(8,128)} %fusion.84, f32[1024,1408]{1,0:T(8,128)} %get-tuple-element.764, bf16[1024,2048]{1,0:T(8,128)(2,1)S(1)} %get-tuple-element.728, bf16[1408,2048]{1,0:T(8,128)(2,1)} %param.34), kind=kOutput, calls=%fused_computation.126 | convolution fusion | flops 5924323328 | bytes 27262976 | tf_op jit(solution)/shard_map/dot_general | solution.py:96
  353.6 10.8 fusion.78
  364.4 10.9 fusion.82
  375.3 8.3 multiply_convert_fusion.12
  383.6 6.5 fusion.70
  390.2 7.0 multiply_convert_fusion.10
  397.3 7.1 fusion.58
  404.4 6.9 add_convert_fusion.1
  411.3 7.0 add_convert_fusion
  421.9 9.1 fusion.479
  447.4 4.2 convolution_convert_fusion.11
  451.7 4.3 convolution_convert_fusion.9
  460.2 4.8 convolution_convert_fusion.13
  465.2 5.1 convolution_convert_fusion.17
  470.3 5.0 convolution_convert_fusion.16
  475.4 5.1 convolution_convert_fusion.15
  484.8 5.3 convolution_convert_fusion.12
  492.0 7.0 convolution_convert_fusion.14
  499.0 4.2 convolution_convert_fusion.6
  503.2 12.2 collective-permute-done.20
  525.2 21.6 %collective-permute-done.45 = f32[10,2048]{1,0:T(8,128)S(1)} collective-permute-done((f32[10,2048]{1,0:T(8,128)S(1)}, f32[10,2048]{1,0:T(8,128)S(1)}, u32[]{:S(2)}, u32[]{:S(2)}) %collective-permute-start.45) | collective-permute-done | bytes 81952 | tf_op jit(solution)/shard_map/ppermute | solution.py:125
  548.5 4.2 convolution_convert_fusion.4
  563.6 5.1 fusion.464
  571.3 59.8 %collective-permute-start.67 = (bf16[1024,1408]{1,0:T(8,128)(2,1)}, bf16[1024,1408]{1,0:T(8,128)(2,1)S(1)}, u32[]{:S(2)}, u32[]{:S(2)}) collective-permute-start(bf16[1024,1408]{1,0:T(8,128)(2,1)} %convolution_convert_fusion.4), channel_id=1, source_target_pairs={{0,8},{4,12},{8,0},{12,4},{16,24},{20,28},{24,16},{28,20},{1,9},{5... | collective-permute-start | bytes 8650760 | tf_op jit(solution)/shard_map/ppermute | solution.py:125
  645.0 40.7 %collective-permute-done.64 = bf16[1024,1408]{1,0:T(8,128)(2,1)S(1)} collective-permute-done((bf16[1024,1408]{1,0:T(8,128)(2,1)}, bf16[1024,1408]{1,0:T(8,128)(2,1)S(1)}, u32[]{:S(2)}, u32[]{:S(2)}) %collective-permute-start.64) | collective-permute-done | bytes 2883616 | tf_op jit(solution)/shard_map/ppermute | solution.py:125
  688.6 67.5 %collective-permute-done.67 = bf16[1024,1408]{1,0:T(8,128)(2,1)S(1)} collective-permute-done((bf16[1024,1408]{1,0:T(8,128)(2,1)}, bf16[1024,1408]{1,0:T(8,128)(2,1)S(1)}, u32[]{:S(2)}, u32[]{:S(2)}) %collective-permute-start.67) | collective-permute-done | bytes 2883616 | tf_op jit(solution)/shard_map/ppermute | solution.py:125
  763.3 51.9 %collective-permute-done.52 = bf16[1024,1408]{1,0:T(8,128)(2,1)S(1)} collective-permute-done((bf16[1024,1408]{1,0:T(8,128)(2,1)}, bf16[1024,1408]{1,0:T(8,128)(2,1)S(1)}, u32[]{:S(2)}, u32[]{:S(2)}) %collective-permute-start.52) | collective-permute-done | bytes 2883616 | tf_op jit(solution)/shard_map/ppermute | solution.py:125
  820.1 6.1 convolution_convert_fusion.20
  828.3 45.3 %while.33 = (s32[]{:T(128)}, f32[1024,4,128]{0,2,1:T(8,128)S(1)}, f32[1024,4,128]{0,2,1:T(8,128)}, f32[2,512,4,128]{3,1,2,0:T(8,128)}, bf16[2,512,4,128]{3,1,2,0...) while((s32[]{:T(128)}, f32[1024,4,128]{0,2,1:T(8,128)S(1)}, ...), condition=%wide.region_22.23_spmd.clone, body=%wide.region_20.22_spmd.clone.sunk | while | flops 2723425280 | bytes 181516240 | solution.py:475
  868.5 5.0 bitcast_add_fusion.8
  904.5 7.3 fusion.271
  913.4 7.7 fusion.275
  924.6 8.9 fusion.480
  975.4 48.0 %collective-permute-done.68 = bf16[512,1408]{1,0:T(8,128)(2,1)S(1)} collective-permute-done((bf16[512,1408]{1,0:T(8,128)(2,1)S(1)}, bf16[512,1408]{1,0:T(8,128)(2,1)S(1)}, u32[]{:S(2)}, u32[]{:S(2)}) %collective-permute-start.68) | collective-permute-done | bytes 1441824 | tf_op jit(solution)/shard_map/ppermute | solution.py:125
  1032.0 46.1 %collective-permute-done.53 = bf16[512,1408]{1,0:T(8,128)(2,1)S(1)} collective-permute-done((bf16[512,1408]{1,0:T(8,128)(2,1)S(1)}, bf16[512,1408]{1,0:T(8,128)(2,1)S(1)}, u32[]{:S(2)}, u32[]{:S(2)}) %collective-permute-start.53) | collective-permute-done | bytes 1441824 | tf_op jit(solution)/shard_map/ppermute | solution.py:125
  1079.6 13.4 %collective-permute-done.72 = bf16[1408,256]{1,0:T(8,128)(2,1)S(1)} collective-permute-done((bf16[1408,256]{1,0:T(8,128)(2,1)}, bf16[1408,256]{1,0:T(8,128)(2,1)S(1)}, u32[]{:S(2)}, u32[]{:S(2)}) %collective-permute-start.72) | collective-permute-done | bytes 720928 | tf_op jit(solution)/shard_map/ppermute | solution.py:125
  1094.7 13.7 %collective-permute-done.75 = bf16[1408,256]{1,0:T(8,128)(2,1)S(1)} collective-permute-done((bf16[1408,256]{1,0:T(8,128)(2,1)S(1)}, bf16[1408,256]{1,0:T(8,128)(2,1)S(1)}, u32[]{:S(2)}, u32[]{:S(2)}) %collective-permute-start.75) | collective-permute-done | bytes 720928 | tf_op jit(solution)/shard_map/ppermute | solution.py:125
  1110.6 26.6 %collective-permute-done.60 = bf16[256,1408]{1,0:T(8,128)(2,1)S(1)} collective-permute-done((bf16[256,1408]{1,0:T(8,128)(2,1)}, bf16[256,1408]{1,0:T(8,128)(2,1)S(1)}, u32[]{:S(2)}, u32[]{:S(2)}) %collective-permute-start.60) | collective-permute-done | bytes 720928 | tf_op jit(solution)/shard_map/ppermute | solution.py:125
  1141.9 9.0 collective-permute-done.66
  1155.9 14.1 %collective-permute-done.57 = bf16[1408,256]{1,0:T(8,128)(2,1)S(1)} collective-permute-done((bf16[1408,256]{1,0:T(8,128)(2,1)S(1)}, bf16[1408,256]{1,0:T(8,128)(2,1)S(1)}, u32[]{:S(2)}, u32[]{:S(2)}) %collective-permute-start.57) | collective-permute-done | bytes 720928 | tf_op jit(solution)/shard_map/ppermute | solution.py:125
  1173.5 33.7 %collective-permute-done.51 = bf16[256,1408]{1,0:T(8,128)(2,1)S(1)} collective-permute-done((bf16[256,1408]{1,0:T(8,128)(2,1)}, bf16[256,1408]{1,0:T(8,128)(2,1)S(1)}, u32[]{:S(2)}, u32[]{:S(2)}) %collective-permute-start.51) | collective-permute-done | bytes 720928 | tf_op jit(solution)/shard_map/ppermute | solution.py:125
  1228.7 7.2 collective-permute-done.42
  1238.5 8.6 collective-permute-done.33
  1251.5 22.3 %collective-permute-done.43 = bf16[512,256]{1,0:T(8,128)(2,1)S(1)} collective-permute-done((bf16[512,256]{1,0:T(8,128)(2,1)S(1)}, bf16[512,256]{1,0:T(8,128)(2,1)S(1)}, u32[]{:S(2)}, u32[]{:S(2)}) %collective-permute-start.43) | collective-permute-done | bytes 262176 | tf_op jit(solution)/shard_map/ppermute | solution.py:125
  (979 shorter events, 437.2 us)
Async XLA Ops:
  2.7 22.9 %collective-permute-start.4 = (bf16[6,256]{1,0:T(8,128)(2,1)S(1)}, bf16[6,256]{1,0:T(8,128)(2,1)S(1)}, u32[]{:S(2)}, u32[]{:S(2)}) collective-permute-start(bf16[6,256]{1,0:T(8,128)(2,1)S(1)} %pad_maximum_fusion.22), channel_id=1, source_target_pairs={{0,2},{1,3},{2,0},{3,1},{4,6},{5,7},{6,4},{7,5},{8,10},{9,11},{10,... | collective-permute-start | bytes 9224 | tf_op jit(solution)/shard_map/ppermute | solution.py:125
  4.3 26.7 %collective-permute-start.3 = (bf16[6,256]{1,0:T(8,128)(2,1)S(1)}, bf16[6,256]{1,0:T(8,128)(2,1)S(1)}, u32[]{:S(2)}, u32[]{:S(2)}) collective-permute-start(bf16[6,256]{1,0:T(8,128)(2,1)S(1)} %pad_maximum_fusion.22), channel_id=1, source_target_pairs={{0,1},{1,0},{2,3},{3,2},{4,5},{5,4},{6,7},{7,6},{8,9},{9,8},{10,11... | collective-permute-start | bytes 9224 | tf_op jit(solution)/shard_map/ppermute | solution.py:125
  4.3 36.7 %collective-permute-start.1 = (bf16[256,2048]{1,0:T(8,128)(2,1)}, bf16[256,2048]{1,0:T(8,128)(2,1)S(1)}, u32[]{:S(2)}, u32[]{:S(2)}) collective-permute-start(bf16[256,2048]{1,0:T(8,128)(2,1)} %param.21), channel_id=1, source_target_pairs={{0,2},{1,3},{2,0},{3,1},{4,6},{5,7},{6,4},{7,5},{8,10},{9,11},{10,... | collective-permute-start | bytes 3145736 | tf_op jit(solution)/shard_map/ppermute | solution.py:125
  4.8 53.4 %collective-permute-start = (bf16[256,2048]{1,0:T(8,128)(2,1)}, bf16[256,2048]{1,0:T(8,128)(2,1)}, u32[]{:S(2)}, u32[]{:S(2)}) collective-permute-start(bf16[256,2048]{1,0:T(8,128)(2,1)} %param.21), channel_id=1, source_target_pairs={{0,1},{1,0},{2,3},{3,2},{4,5},{5,4},{6,7},{7,6},{8,9},{9,8},{10,11... | collective-permute-start | bytes 3145736 | tf_op jit(solution)/shard_map/ppermute | solution.py:125
  5.0 48.0 %collective-permute-start.16 = (bf16[256,2048]{1,0:T(8,128)(2,1)}, bf16[256,2048]{1,0:T(8,128)(2,1)}, u32[]{:S(2)}, u32[]{:S(2)}) collective-permute-start(bf16[256,2048]{1,0:T(8,128)(2,1)} %param.25), channel_id=1, source_target_pairs={{0,2},{1,3},{2,0},{3,1},{4,6},{5,7},{6,4},{7,5},{8,10},{9,11},{10,... | collective-permute-start | bytes 3145736 | tf_op jit(solution)/shard_map/ppermute | solution.py:125
  31.0 22.4 %collective-permute-start.15 = (bf16[256,2048]{1,0:T(8,128)(2,1)}, bf16[256,2048]{1,0:T(8,128)(2,1)}, u32[]{:S(2)}, u32[]{:S(2)}) collective-permute-start(bf16[256,2048]{1,0:T(8,128)(2,1)} %param.25), channel_id=1, source_target_pairs={{0,1},{1,0},{2,3},{3,2},{4,5},{5,4},{6,7},{7,6},{8,9},{9,8},{10,11... | collective-permute-start | bytes 3145736 | tf_op jit(solution)/shard_map/ppermute | solution.py:125
  31.6 101.0 %collective-permute-start.10 = (bf16[512,2048]{1,0:T(8,128)(2,1)}, bf16[512,2048]{1,0:T(8,128)(2,1)}, u32[]{:S(2)}, u32[]{:S(2)}) collective-permute-start(bf16[512,2048]{1,0:T(8,128)(2,1)} %param.29), channel_id=1, source_target_pairs={{0,2},{1,3},{2,0},{3,1},{4,6},{5,7},{6,4},{7,5},{8,10},{9,11},{10,... | collective-permute-start | bytes 6291464 | tf_op jit(solution)/shard_map/ppermute | solution.py:125
  41.0 17.2 %collective-permute-start.2 = (bf16[256,2048]{1,0:T(8,128)(2,1)S(1)}, bf16[256,2048]{1,0:T(8,128)(2,1)}, u32[]{:S(2)}, u32[]{:S(2)}) collective-permute-start(bf16[256,2048]{1,0:T(8,128)(2,1)S(1)} %collective-permute-done.1), channel_id=1, source_target_pairs={{0,1},{1,0},{2,3},{3,2},{4,5},{5,4},{6,7},{7,6},{8,9},{9,8},{10,11... | collective-permute-start | bytes 3145736 | tf_op jit(solution)/shard_map/ppermute | solution.py:125
  53.0 111.6 %collective-permute-start.9 = (bf16[512,2048]{1,0:T(8,128)(2,1)}, bf16[512,2048]{1,0:T(8,128)(2,1)}, u32[]{:S(2)}, u32[]{:S(2)}) collective-permute-start(bf16[512,2048]{1,0:T(8,128)(2,1)} %param.29), channel_id=1, source_target_pairs={{0,1},{1,0},{2,3},{3,2},{4,5},{5,4},{6,7},{7,6},{8,9},{9,8},{10,11... | collective-permute-start | bytes 6291464 | tf_op jit(solution)/shard_map/ppermute | solution.py:125
  53.5 87.1 %collective-permute-start.17 = (bf16[256,2048]{1,0:T(8,128)(2,1)}, bf16[256,2048]{1,0:T(8,128)(2,1)}, u32[]{:S(2)}, u32[]{:S(2)}) collective-permute-start(bf16[256,2048]{1,0:T(8,128)(2,1)} %collective-permute-done.16), channel_id=1, source_target_pairs={{0,1},{1,0},{2,3},{3,2},{4,5},{5,4},{6,7},{7,6},{8,9},{9,8},{10,11... | collective-permute-start | bytes 3145736 | tf_op jit(solution)/shard_map/ppermute | solution.py:125
  130.9 25.6 %collective-permute-start.7 = (bf16[1024,512]{1,0:T(8,128)(2,1)S(1)}, bf16[1024,512]{1,0:T(8,128)(2,1)S(1)}, u32[]{:S(2)}, u32[]{:S(2)}) collective-permute-start(bf16[1024,512]{1,0:T(8,128)(2,1)S(1)} %bitcast.486), channel_id=1, source_target_pairs={{0,2},{1,3},{2,0},{3,1},{4,6},{5,7},{6,4},{7,5},{8,10},{9,11},{10,... | collective-permute-start | bytes 3145736 | tf_op jit(solution)/shard_map/ppermute | solution.py:125
  132.4 29.2 %collective-permute-start.6 = (bf16[1024,512]{1,0:T(8,128)(2,1)S(1)}, bf16[1024,512]{1,0:T(8,128)(2,1)S(1)}, u32[]{:S(2)}, u32[]{:S(2)}) collective-permute-start(bf16[1024,512]{1,0:T(8,128)(2,1)S(1)} %bitcast.487), channel_id=1, source_target_pairs={{0,1},{1,0},{2,3},{3,2},{4,5},{5,4},{6,7},{7,6},{8,9},{9,8},{10,11... | collective-permute-start | bytes 3145736 | tf_op jit(solution)/shard_map/ppermute | solution.py:125
  132.6 32.0 %collective-permute-start.11 = (bf16[512,2048]{1,0:T(8,128)(2,1)}, bf16[512,2048]{1,0:T(8,128)(2,1)S(1)}, u32[]{:S(2)}, u32[]{:S(2)}) collective-permute-start(bf16[512,2048]{1,0:T(8,128)(2,1)} %collective-permute-done.10), channel_id=1, source_target_pairs={{0,1},{1,0},{2,3},{3,2},{4,5},{5,4},{6,7},{7,6},{8,9},{9,8},{10,11... | collective-permute-start | bytes 6291464 | tf_op jit(solution)/shard_map/ppermute | solution.py:125
  307.1 264.3 %collective-permute-start.70 = (bf16[1408,1024]{1,0:T(8,128)(2,1)}, bf16[1408,1024]{1,0:T(8,128)(2,1)}, u32[]{:S(2)}, u32[]{:S(2)}) collective-permute-start(bf16[1408,1024]{1,0:T(8,128)(2,1)} %convolution_convert_fusion.2), channel_id=1, source_target_pairs={{0,24},{4,28},{8,16},{12,20},{16,8},{20,12},{24,0},{28,4},{1,25},{... | collective-permute-start | bytes 8650760 | tf_op jit(solution)/shard_map/ppermute | solution.py:125
  318.2 316.4 %collective-permute-start.73 = (bf16[1408,1024]{1,0:T(8,128)(2,1)}, bf16[1408,1024]{1,0:T(8,128)(2,1)}, u32[]{:S(2)}, u32[]{:S(2)}) collective-permute-start(bf16[1408,1024]{1,0:T(8,128)(2,1)} %convolution_convert_fusion), channel_id=1, source_target_pairs={{0,24},{4,28},{8,16},{12,20},{16,8},{20,12},{24,0},{28,4},{1,25},{... | collective-permute-start | bytes 8650760 | tf_op jit(solution)/shard_map/ppermute | solution.py:125
  433.0 57.1 %collective-permute-start.19 = (bf16[256,2048]{1,0:T(8,128)(2,1)S(1)}, bf16[256,2048]{1,0:T(8,128)(2,1)S(1)}, u32[]{:S(2)}, u32[]{:S(2)}) collective-permute-start(bf16[256,2048]{1,0:T(8,128)(2,1)S(1)} %get-tuple-element.638), channel_id=1, source_target_pairs={{0,1},{1,0},{2,3},{3,2},{4,5},{5,4},{6,7},{7,6},{8,9},{9,8},{10,11... | collective-permute-start | bytes 3145736 | tf_op jit(solution)/shard_map/ppermute | solution.py:125
  433.0 70.2 %collective-permute-start.18 = (bf16[256,2048]{1,0:T(8,128)(2,1)S(1)}, bf16[256,2048]{1,0:T(8,128)(2,1)S(1)}, u32[]{:S(2)}, u32[]{:S(2)}) collective-permute-start(bf16[256,2048]{1,0:T(8,128)(2,1)S(1)} %get-tuple-element.637), channel_id=1, source_target_pairs={{0,1},{1,0},{2,3},{3,2},{4,5},{5,4},{6,7},{7,6},{8,9},{9,8},{10,11... | collective-permute-start | bytes 3145736 | tf_op jit(solution)/shard_map/ppermute | solution.py:125
  434.0 84.1 %collective-permute-start.13 = (bf16[256,2048]{1,0:T(8,128)(2,1)S(1)}, bf16[256,2048]{1,0:T(8,128)(2,1)S(1)}, u32[]{:S(2)}, u32[]{:S(2)}) collective-permute-start(bf16[256,2048]{1,0:T(8,128)(2,1)S(1)} %get-tuple-element.640), channel_id=1, source_target_pairs={{0,1},{1,0},{2,3},{3,2},{4,5},{5,4},{6,7},{7,6},{8,9},{9,8},{10,11... | collective-permute-start | bytes 3145736 | tf_op jit(solution)/shard_map/ppermute | solution.py:125
  490.4 25.1 %collective-permute-start.20 = (bf16[256,2048]{1,0:T(8,128)(2,1)S(1)}, bf16[256,2048]{1,0:T(8,128)(2,1)S(1)}, u32[]{:S(2)}, u32[]{:S(2)}) collective-permute-start(bf16[256,2048]{1,0:T(8,128)(2,1)S(1)} %fusion.148), channel_id=1, source_target_pairs={{0,2},{1,3},{2,0},{3,1},{4,6},{5,7},{6,4},{7,5},{8,10},{9,11},{10,... | collective-permute-start | bytes 3145736 | tf_op jit(solution)/shard_map/ppermute | solution.py:125
  503.2 55.7 %collective-permute-start.12 = (bf16[256,2048]{1,0:T(8,128)(2,1)S(1)}, bf16[256,2048]{1,0:T(8,128)(2,1)S(1)}, u32[]{:S(2)}, u32[]{:S(2)}) collective-permute-start(bf16[256,2048]{1,0:T(8,128)(2,1)S(1)} %get-tuple-element.639), channel_id=1, source_target_pairs={{0,1},{1,0},{2,3},{3,2},{4,5},{5,4},{6,7},{7,6},{8,9},{9,8},{10,11... | collective-permute-start | bytes 3145736 | tf_op jit(solution)/shard_map/ppermute | solution.py:125
  518.5 42.6 %collective-permute-start.14 = (bf16[256,2048]{1,0:T(8,128)(2,1)S(1)}, bf16[256,2048]{1,0:T(8,128)(2,1)S(1)}, u32[]{:S(2)}, u32[]{:S(2)}) collective-permute-start(bf16[256,2048]{1,0:T(8,128)(2,1)S(1)} %fusion.150), channel_id=1, source_target_pairs={{0,2},{1,3},{2,0},{3,1},{4,6},{5,7},{6,4},{7,5},{8,10},{9,11},{10,... | collective-permute-start | bytes 3145736 | tf_op jit(solution)/shard_map/ppermute | solution.py:125
  520.1 26.8 %collective-permute-start.45 = (f32[10,2048]{1,0:T(8,128)S(1)}, f32[10,2048]{1,0:T(8,128)S(1)}, u32[]{:S(2)}, u32[]{:S(2)}) collective-permute-start(f32[10,2048]{1,0:T(8,128)S(1)} %fusion.552), channel_id=1, source_target_pairs={{0,2},{1,3},{2,0},{3,1},{4,6},{5,7},{6,4},{7,5},{8,10},{9,11},{10,... | collective-permute-start | bytes 245768 | tf_op jit(solution)/shard_map/ppermute | solution.py:125
  558.2 79.6 %collective-permute-start.58 = (bf16[1024,1408]{1,0:T(8,128)(2,1)}, bf16[1024,1408]{1,0:T(8,128)(2,1)}, u32[]{:S(2)}, u32[]{:S(2)}) collective-permute-start(bf16[1024,1408]{1,0:T(8,128)(2,1)} %convolution_convert_fusion.10), channel_id=1, source_target_pairs={{0,4},{4,0},{8,12},{12,8},{16,20},{20,16},{24,28},{28,24},{1,5},{5... | collective-permute-start | bytes 8650760 | tf_op jit(solution)/shard_map/ppermute | solution.py:125
  558.9 82.6 %collective-permute-start.61 = (bf16[1024,1408]{1,0:T(8,128)(2,1)}, bf16[1024,1408]{1,0:T(8,128)(2,1)}, u32[]{:S(2)}, u32[]{:S(2)}) collective-permute-start(bf16[1024,1408]{1,0:T(8,128)(2,1)} %convolution_convert_fusion.8), channel_id=1, source_target_pairs={{0,8},{4,12},{8,0},{12,4},{16,24},{20,28},{24,16},{28,20},{1,9},{5... | collective-permute-start | bytes 8650760 | tf_op jit(solution)/shard_map/ppermute | solution.py:125
  568.8 116.9 %collective-permute-start.64 = (bf16[1024,1408]{1,0:T(8,128)(2,1)}, bf16[1024,1408]{1,0:T(8,128)(2,1)S(1)}, u32[]{:S(2)}, u32[]{:S(2)}) collective-permute-start(bf16[1024,1408]{1,0:T(8,128)(2,1)} %convolution_convert_fusion.6), channel_id=1, source_target_pairs={{0,4},{4,0},{8,12},{12,8},{16,20},{20,16},{24,28},{28,24},{1,5},{5... | collective-permute-start | bytes 8650760 | tf_op jit(solution)/shard_map/ppermute | solution.py:125
  571.3 184.8 %collective-permute-start.67 = (bf16[1024,1408]{1,0:T(8,128)(2,1)}, bf16[1024,1408]{1,0:T(8,128)(2,1)S(1)}, u32[]{:S(2)}, u32[]{:S(2)}) collective-permute-start(bf16[1024,1408]{1,0:T(8,128)(2,1)} %convolution_convert_fusion.4), channel_id=1, source_target_pairs={{0,8},{4,12},{8,0},{12,4},{16,24},{20,28},{24,16},{28,20},{1,9},{5... | collective-permute-start | bytes 8650760 | tf_op jit(solution)/shard_map/ppermute | solution.py:125
  634.6 123.2 %collective-permute-start.55 = (bf16[1408,1024]{1,0:T(8,128)(2,1)}, bf16[1408,1024]{1,0:T(8,128)(2,1)S(1)}, u32[]{:S(2)}, u32[]{:S(2)}) collective-permute-start(bf16[1408,1024]{1,0:T(8,128)(2,1)} %convolution_convert_fusion.12), channel_id=1, source_target_pairs={{0,24},{4,28},{8,16},{12,20},{16,8},{20,12},{24,0},{28,4},{1,25},{... | collective-permute-start | bytes 8650760 | tf_op jit(solution)/shard_map/ppermute | solution.py:125
  637.8 122.5 %collective-permute-start.49 = (bf16[1024,1408]{1,0:T(8,128)(2,1)S(1)}, bf16[1024,1408]{1,0:T(8,128)(2,1)S(1)}, u32[]{:S(2)}, u32[]{:S(2)}) collective-permute-start(bf16[1024,1408]{1,0:T(8,128)(2,1)S(1)} %copy-done.225), channel_id=1, source_target_pairs={{0,4},{4,0},{8,12},{12,8},{16,20},{20,16},{24,28},{28,24},{1,5},{5... | collective-permute-start | bytes 8650760 | tf_op jit(solution)/shard_map/ppermute | solution.py:125
  641.5 173.8 %collective-permute-start.52 = (bf16[1024,1408]{1,0:T(8,128)(2,1)}, bf16[1024,1408]{1,0:T(8,128)(2,1)S(1)}, u32[]{:S(2)}, u32[]{:S(2)}) collective-permute-start(bf16[1024,1408]{1,0:T(8,128)(2,1)} %convolution_convert_fusion.14), channel_id=1, source_target_pairs={{0,8},{4,12},{8,0},{12,4},{16,24},{20,28},{24,16},{28,20},{1,9},{5... | collective-permute-start | bytes 8650760 | tf_op jit(solution)/shard_map/ppermute | solution.py:125
  685.7 76.2 %collective-permute-start.22 = (bf16[256,2048]{1,0:T(8,128)(2,1)S(1)}, bf16[256,2048]{1,0:T(8,128)(2,1)S(1)}, u32[]{:S(2)}, u32[]{:S(2)}) collective-permute-start(bf16[256,2048]{1,0:T(8,128)(2,1)S(1)} %get-tuple-element.552), channel_id=1, source_target_pairs={{0,2},{1,3},{2,0},{3,1},{4,6},{5,7},{6,4},{7,5},{8,10},{9,11},{10,... | collective-permute-start | bytes 3145736 | tf_op jit(solution)/shard_map/ppermute | solution.py:125
  756.2 62.6 %collective-permute-start.21 = (bf16[256,2048]{1,0:T(8,128)(2,1)S(1)}, bf16[256,2048]{1,0:T(8,128)(2,1)S(1)}, u32[]{:S(2)}, u32[]{:S(2)}) collective-permute-start(bf16[256,2048]{1,0:T(8,128)(2,1)S(1)} %get-tuple-element.552), channel_id=1, source_target_pairs={{0,1},{1,0},{2,3},{3,2},{4,5},{5,4},{6,7},{7,6},{8,9},{9,8},{10,11... | collective-permute-start | bytes 3145736 | tf_op jit(solution)/shard_map/ppermute | solution.py:125
  757.9 198.6 %collective-permute-start.71 = (bf16[1408,512]{1,0:T(8,128)(2,1)}, bf16[1408,512]{1,0:T(8,128)(2,1)}, u32[]{:S(2)}, u32[]{:S(2)}) collective-permute-start(bf16[1408,512]{1,0:T(8,128)(2,1)} %add_convert_fusion.3), channel_id=1, source_target_pairs={{0,4},{4,0},{8,12},{12,8},{16,20},{20,16},{24,28},{28,24},{1,5},{5... | collective-permute-start | bytes 4325384 | tf_op jit(solution)/shard_map/ppermute | solution.py:125
  760.3 201.1 %collective-permute-start.74 = (bf16[1408,512]{1,0:T(8,128)(2,1)}, bf16[1408,512]{1,0:T(8,128)(2,1)}, u32[]{:S(2)}, u32[]{:S(2)}) collective-permute-start(bf16[1408,512]{1,0:T(8,128)(2,1)} %add_convert_fusion.2), channel_id=1, source_target_pairs={{0,4},{4,0},{8,12},{12,8},{16,20},{20,16},{24,28},{28,24},{1,5},{5... | collective-permute-start | bytes 4325384 | tf_op jit(solution)/shard_map/ppermute | solution.py:125
  761.9 57.0 %collective-permute-start.23 = (bf16[256,2048]{1,0:T(8,128)(2,1)S(1)}, bf16[256,2048]{1,0:T(8,128)(2,1)S(1)}, u32[]{:S(2)}, u32[]{:S(2)}) collective-permute-start(bf16[256,2048]{1,0:T(8,128)(2,1)S(1)} %collective-permute-done.22), channel_id=1, source_target_pairs={{0,1},{1,0},{2,3},{3,2},{4,5},{5,4},{6,7},{7,6},{8,9},{9,8},{10,11... | collective-permute-start | bytes 3145736 | tf_op jit(solution)/shard_map/ppermute | solution.py:125
  815.3 148.7 %collective-permute-start.59 = (bf16[512,1408]{1,0:T(8,128)(2,1)}, bf16[512,1408]{1,0:T(8,128)(2,1)}, u32[]{:S(2)}, u32[]{:S(2)}) collective-permute-start(bf16[512,1408]{1,0:T(8,128)(2,1)} %add_convert_fusion.7), channel_id=1, source_target_pairs={{0,8},{4,12},{8,0},{12,4},{16,24},{20,28},{24,16},{28,20},{1,9},{5... | collective-permute-start | bytes 4325384 | tf_op jit(solution)/shard_map/ppermute | solution.py:125
  818.8 149.6 %collective-permute-start.62 = (bf16[512,1408]{1,0:T(8,128)(2,1)}, bf16[512,1408]{1,0:T(8,128)(2,1)}, u32[]{:S(2)}, u32[]{:S(2)}) collective-permute-start(bf16[512,1408]{1,0:T(8,128)(2,1)} %add_convert_fusion.6), channel_id=1, source_target_pairs={{0,24},{4,28},{8,16},{12,20},{16,8},{20,12},{24,0},{28,4},{1,25},{... | collective-permute-start | bytes 4325384 | tf_op jit(solution)/shard_map/ppermute | solution.py:125
  818.9 152.8 %collective-permute-start.65 = (bf16[512,1408]{1,0:T(8,128)(2,1)}, bf16[512,1408]{1,0:T(8,128)(2,1)}, u32[]{:S(2)}, u32[]{:S(2)}) collective-permute-start(bf16[512,1408]{1,0:T(8,128)(2,1)} %add_convert_fusion.5), channel_id=1, source_target_pairs={{0,8},{4,12},{8,0},{12,4},{16,24},{20,28},{24,16},{28,20},{1,9},{5... | collective-permute-start | bytes 4325384 | tf_op jit(solution)/shard_map/ppermute | solution.py:125
  956.5 66.9 %collective-permute-start.68 = (bf16[512,1408]{1,0:T(8,128)(2,1)S(1)}, bf16[512,1408]{1,0:T(8,128)(2,1)S(1)}, u32[]{:S(2)}, u32[]{:S(2)}) collective-permute-start(bf16[512,1408]{1,0:T(8,128)(2,1)S(1)} %copy-done.80), channel_id=1, source_target_pairs={{0,24},{4,28},{8,16},{12,20},{16,8},{20,12},{24,0},{28,4},{1,25},{... | collective-permute-start | bytes 4325384 | tf_op jit(solution)/shard_map/ppermute | solution.py:125
  961.4 64.8 %collective-permute-start.56 = (bf16[1408,512]{1,0:T(8,128)(2,1)S(1)}, bf16[1408,512]{1,0:T(8,128)(2,1)S(1)}, u32[]{:S(2)}, u32[]{:S(2)}) collective-permute-start(bf16[1408,512]{1,0:T(8,128)(2,1)S(1)} %copy-done.81), channel_id=1, source_target_pairs={{0,4},{4,0},{8,12},{12,8},{16,20},{20,16},{24,28},{28,24},{1,5},{5... | collective-permute-start | bytes 4325384 | tf_op jit(solution)/shard_map/ppermute | solution.py:125
  964.0 64.3 %collective-permute-start.50 = (bf16[512,1408]{1,0:T(8,128)(2,1)S(1)}, bf16[512,1408]{1,0:T(8,128)(2,1)S(1)}, u32[]{:S(2)}, u32[]{:S(2)}) collective-permute-start(bf16[512,1408]{1,0:T(8,128)(2,1)S(1)} %copy-done.82), channel_id=1, source_target_pairs={{0,8},{4,12},{8,0},{12,4},{16,24},{20,28},{24,16},{28,20},{1,9},{5... | collective-permute-start | bytes 4325384 | tf_op jit(solution)/shard_map/ppermute | solution.py:125
  968.4 109.8 %collective-permute-start.53 = (bf16[512,1408]{1,0:T(8,128)(2,1)S(1)}, bf16[512,1408]{1,0:T(8,128)(2,1)S(1)}, u32[]{:S(2)}, u32[]{:S(2)}) collective-permute-start(bf16[512,1408]{1,0:T(8,128)(2,1)S(1)} %copy-done.83), channel_id=1, source_target_pairs={{0,24},{4,28},{8,16},{12,20},{16,8},{20,12},{24,0},{28,4},{1,25},{... | collective-permute-start | bytes 4325384 | tf_op jit(solution)/shard_map/ppermute | solution.py:125
  971.7 247.5 %collective-permute-start.41 = (bf16[512,1024]{1,0:T(8,128)(2,1)}, bf16[512,1024]{1,0:T(8,128)(2,1)}, u32[]{:S(2)}, u32[]{:S(2)}) collective-permute-start(bf16[512,1024]{1,0:T(8,128)(2,1)} %fusion.291), channel_id=1, source_target_pairs={{0,4},{4,0},{8,12},{12,8},{16,20},{20,16},{24,28},{28,24},{1,5},{5... | collective-permute-start | bytes 3145736 | tf_op jit(solution)/shard_map/ppermute | solution.py:125
  1023.4 197.6 %collective-permute-start.32 = (bf16[1024,512]{1,0:T(8,128)(2,1)}, bf16[1024,512]{1,0:T(8,128)(2,1)}, u32[]{:S(2)}, u32[]{:S(2)}) collective-permute-start(bf16[1024,512]{1,0:T(8,128)(2,1)} %fusion.309), channel_id=1, source_target_pairs={{0,4},{4,0},{8,12},{12,8},{16,20},{20,16},{24,28},{28,24},{1,5},{5... | collective-permute-start | bytes 3145736 | tf_op jit(solution)/shard_map/ppermute | solution.py:125
  1026.2 196.1 %collective-permute-start.35 = (bf16[1024,512]{1,0:T(8,128)(2,1)}, bf16[1024,512]{1,0:T(8,128)(2,1)}, u32[]{:S(2)}, u32[]{:S(2)}) collective-permute-start(bf16[1024,512]{1,0:T(8,128)(2,1)} %fusion.303), channel_id=1, source_target_pairs={{0,8},{4,12},{8,0},{12,4},{16,24},{20,28},{24,16},{28,20},{1,9},{5... | collective-permute-start | bytes 3145736 | tf_op jit(solution)/shard_map/ppermute | solution.py:125
  1028.3 64.6 %collective-permute-start.72 = (bf16[1408,256]{1,0:T(8,128)(2,1)}, bf16[1408,256]{1,0:T(8,128)(2,1)S(1)}, u32[]{:S(2)}, u32[]{:S(2)}) collective-permute-start(bf16[1408,256]{1,0:T(8,128)(2,1)} %add_convert_fusion.14), channel_id=1, source_target_pairs={{0,8},{4,12},{8,0},{12,4},{16,24},{20,28},{24,16},{28,20},{1,9},{5... | collective-permute-start | bytes 2162696 | tf_op jit(solution)/shard_map/ppermute | solution.py:125
  1078.2 30.2 %collective-permute-start.75 = (bf16[1408,256]{1,0:T(8,128)(2,1)S(1)}, bf16[1408,256]{1,0:T(8,128)(2,1)S(1)}, u32[]{:S(2)}, u32[]{:S(2)}) collective-permute-start(bf16[1408,256]{1,0:T(8,128)(2,1)S(1)} %add_convert_fusion.13), channel_id=1, source_target_pairs={{0,8},{4,12},{8,0},{12,4},{16,24},{20,28},{24,16},{28,20},{1,9},{5... | collective-permute-start | bytes 2162696 | tf_op jit(solution)/shard_map/ppermute | solution.py:125
  1092.9 44.3 %collective-permute-start.60 = (bf16[256,1408]{1,0:T(8,128)(2,1)}, bf16[256,1408]{1,0:T(8,128)(2,1)S(1)}, u32[]{:S(2)}, u32[]{:S(2)}) collective-permute-start(bf16[256,1408]{1,0:T(8,128)(2,1)} %add_convert_fusion.18), channel_id=1, source_target_pairs={{0,24},{4,28},{8,16},{12,20},{16,8},{20,12},{24,0},{28,4},{1,25},{... | collective-permute-start | bytes 2162696 | tf_op jit(solution)/shard_map/ppermute | solution.py:125
  1108.4 31.6 %collective-permute-start.63 = (bf16[256,1408]{1,0:T(8,128)(2,1)}, bf16[256,1408]{1,0:T(8,128)(2,1)S(1)}, u32[]{:S(2)}, u32[]{:S(2)}) collective-permute-start(bf16[256,1408]{1,0:T(8,128)(2,1)} %add_convert_fusion.17), channel_id=1, source_target_pairs={{0,4},{4,0},{8,12},{12,8},{16,20},{20,16},{24,28},{28,24},{1,5},{5... | collective-permute-start | bytes 2162696 | tf_op jit(solution)/shard_map/ppermute | solution.py:125
  1137.2 13.7 %collective-permute-start.66 = (bf16[256,1408]{1,0:T(8,128)(2,1)S(1)}, bf16[256,1408]{1,0:T(8,128)(2,1)S(1)}, u32[]{:S(2)}, u32[]{:S(2)}) collective-permute-start(bf16[256,1408]{1,0:T(8,128)(2,1)S(1)} %copy-done.106), channel_id=1, source_target_pairs={{0,24},{4,28},{8,16},{12,20},{16,8},{20,12},{24,0},{28,4},{1,25},{... | collective-permute-start | bytes 2162696 | tf_op jit(solution)/shard_map/ppermute | solution.py:125
  1140.0 12.6 collective-permute-start.69
  1150.9 19.1 %collective-permute-start.57 = (bf16[1408,256]{1,0:T(8,128)(2,1)S(1)}, bf16[1408,256]{1,0:T(8,128)(2,1)S(1)}, u32[]{:S(2)}, u32[]{:S(2)}) collective-permute-start(bf16[1408,256]{1,0:T(8,128)(2,1)S(1)} %add_convert_fusion.19), channel_id=1, source_target_pairs={{0,8},{4,12},{8,0},{12,4},{16,24},{20,28},{24,16},{28,20},{1,9},{5... | collective-permute-start | bytes 2162696 | tf_op jit(solution)/shard_map/ppermute | solution.py:125
  1152.6 54.6 %collective-permute-start.51 = (bf16[256,1408]{1,0:T(8,128)(2,1)}, bf16[256,1408]{1,0:T(8,128)(2,1)S(1)}, u32[]{:S(2)}, u32[]{:S(2)}) collective-permute-start(bf16[256,1408]{1,0:T(8,128)(2,1)} %add_convert_fusion.21), channel_id=1, source_target_pairs={{0,24},{4,28},{8,16},{12,20},{16,8},{20,12},{24,0},{28,4},{1,25},{... | collective-permute-start | bytes 2162696 | tf_op jit(solution)/shard_map/ppermute | solution.py:125
  1170.0 41.0 %collective-permute-start.54 = (bf16[256,1408]{1,0:T(8,128)(2,1)S(1)}, bf16[256,1408]{1,0:T(8,128)(2,1)S(1)}, u32[]{:S(2)}, u32[]{:S(2)}) collective-permute-start(bf16[256,1408]{1,0:T(8,128)(2,1)S(1)} %add_convert_fusion.20), channel_id=1, source_target_pairs={{0,4},{4,0},{8,12},{12,8},{16,20},{20,16},{24,28},{28,24},{1,5},{5... | collective-permute-start | bytes 2162696 | tf_op jit(solution)/shard_map/ppermute | solution.py:125
  1207.2 19.1 %collective-permute-start.38 = (bf16[1024,512]{1,0:T(8,128)(2,1)S(1)}, bf16[1024,512]{1,0:T(8,128)(2,1)S(1)}, u32[]{:S(2)}, u32[]{:S(2)}) collective-permute-start(bf16[1024,512]{1,0:T(8,128)(2,1)S(1)} %copy-done.228), channel_id=1, source_target_pairs={{0,24},{4,28},{8,16},{12,20},{16,8},{20,12},{24,0},{28,4},{1,25},{... | collective-permute-start | bytes 3145736 | tf_op jit(solution)/shard_map/ppermute | solution.py:125
  1211.0 17.1 %collective-permute-start.25 = (bf16[256,2048]{1,0:T(8,128)(2,1)S(1)}, bf16[256,2048]{1,0:T(8,128)(2,1)S(1)}, u32[]{:S(2)}, u32[]{:S(2)}) collective-permute-start(bf16[256,2048]{1,0:T(8,128)(2,1)S(1)} %copy-done.99), channel_id=1, source_target_pairs={{0,1},{1,0},{2,3},{3,2},{4,5},{5,4},{6,7},{7,6},{8,9},{9,8},{10,11... | collective-permute-start | bytes 3145736 | tf_op jit(solution)/shard_map/ppermute | solution.py:125
  1219.2 61.2 %collective-permute-start.24 = (bf16[256,2048]{1,0:T(8,128)(2,1)S(1)}, bf16[256,2048]{1,0:T(8,128)(2,1)S(1)}, u32[]{:S(2)}, u32[]{:S(2)}) collective-permute-start(bf16[256,2048]{1,0:T(8,128)(2,1)S(1)} %copy-done.98), channel_id=1, source_target_pairs={{0,1},{1,0},{2,3},{3,2},{4,5},{5,4},{6,7},{7,6},{8,9},{9,8},{10,11... | collective-permute-start | bytes 3145736 | tf_op jit(solution)/shard_map/ppermute | solution.py:125
  1221.0 14.8 %collective-permute-start.42 = (bf16[512,512]{1,0:T(8,128)(2,1)S(1)}, bf16[512,512]{1,0:T(8,128)(2,1)S(1)}, u32[]{:S(2)}, u32[]{:S(2)}) collective-permute-start(bf16[512,512]{1,0:T(8,128)(2,1)S(1)} %add_convert_fusion.22), channel_id=1, source_target_pairs={{0,8},{4,12},{8,0},{12,4},{16,24},{20,28},{24,16},{28,20},{1,9},{5... | collective-permute-start | bytes 1572872 | tf_op jit(solution)/shard_map/ppermute | solution.py:125
  1222.3 24.8 %collective-permute-start.33 = (bf16[512,512]{1,0:T(8,128)(2,1)S(1)}, bf16[512,512]{1,0:T(8,128)(2,1)S(1)}, u32[]{:S(2)}, u32[]{:S(2)}) collective-permute-start(bf16[512,512]{1,0:T(8,128)(2,1)S(1)} %add_convert_fusion.25), channel_id=1, source_target_pairs={{0,8},{4,12},{8,0},{12,4},{16,24},{20,28},{24,16},{28,20},{1,9},{5... | collective-permute-start | bytes 1572872 | tf_op jit(solution)/shard_map/ppermute | solution.py:125
  1226.3 21.9 %collective-permute-start.36 = (bf16[512,512]{1,0:T(8,128)(2,1)S(1)}, bf16[512,512]{1,0:T(8,128)(2,1)S(1)}, u32[]{:S(2)}, u32[]{:S(2)}) collective-permute-start(bf16[512,512]{1,0:T(8,128)(2,1)S(1)} %add_convert_fusion.24), channel_id=1, source_target_pairs={{0,24},{4,28},{8,16},{12,20},{16,8},{20,12},{24,0},{28,4},{1,25},{... | collective-permute-start | bytes 1572872 | tf_op jit(solution)/shard_map/ppermute | solution.py:125
  1228.1 23.2 %collective-permute-start.39 = (bf16[512,512]{1,0:T(8,128)(2,1)S(1)}, bf16[512,512]{1,0:T(8,128)(2,1)S(1)}, u32[]{:S(2)}, u32[]{:S(2)}) collective-permute-start(bf16[512,512]{1,0:T(8,128)(2,1)S(1)} %add_convert_fusion.23), channel_id=1, source_target_pairs={{0,4},{4,0},{8,12},{12,8},{16,20},{20,16},{24,28},{28,24},{1,5},{5... | collective-permute-start | bytes 1572872 | tf_op jit(solution)/shard_map/ppermute | solution.py:125
  1235.9 44.6 %collective-permute-start.26 = (bf16[256,2048]{1,0:T(8,128)(2,1)S(1)}, bf16[256,2048]{1,0:T(8,128)(2,1)S(1)}, u32[]{:S(2)}, u32[]{:S(2)}) collective-permute-start(bf16[256,2048]{1,0:T(8,128)(2,1)S(1)} %fusion.146), channel_id=1, source_target_pairs={{0,2},{1,3},{2,0},{3,1},{4,6},{5,7},{6,4},{7,5},{8,10},{9,11},{10,... | collective-permute-start | bytes 3145736 | tf_op jit(solution)/shard_map/ppermute | solution.py:125
  1247.1 26.8 %collective-permute-start.43 = (bf16[512,256]{1,0:T(8,128)(2,1)S(1)}, bf16[512,256]{1,0:T(8,128)(2,1)S(1)}, u32[]{:S(2)}, u32[]{:S(2)}) collective-permute-start(bf16[512,256]{1,0:T(8,128)(2,1)S(1)} %add_convert_fusion.26), channel_id=1, source_target_pairs={{0,24},{4,28},{8,16},{12,20},{16,8},{20,12},{24,0},{28,4},{1,25},{... | collective-permute-start | bytes 786440 | tf_op jit(solution)/shard_map/ppermute | solution.py:125
  1248.2 31.2 %collective-permute-start.34 = (bf16[256,512]{1,0:T(8,128)(2,1)S(1)}, bf16[256,512]{1,0:T(8,128)(2,1)S(1)}, u32[]{:S(2)}, u32[]{:S(2)}) collective-permute-start(bf16[256,512]{1,0:T(8,128)(2,1)S(1)} %add_convert_fusion.29), channel_id=1, source_target_pairs={{0,24},{4,28},{8,16},{12,20},{16,8},{20,12},{24,0},{28,4},{1,25},{... | collective-permute-start | bytes 786440 | tf_op jit(solution)/shard_map/ppermute | solution.py:125
  1251.3 30.3 %collective-permute-start.37 = (bf16[256,512]{1,0:T(8,128)(2,1)S(1)}, bf16[256,512]{1,0:T(8,128)(2,1)S(1)}, u32[]{:S(2)}, u32[]{:S(2)}) collective-permute-start(bf16[256,512]{1,0:T(8,128)(2,1)S(1)} %add_convert_fusion.28), channel_id=1, source_target_pairs={{0,4},{4,0},{8,12},{12,8},{16,20},{20,16},{24,28},{28,24},{1,5},{5... | collective-permute-start | bytes 786440 | tf_op jit(solution)/shard_map/ppermute | solution.py:125
  (285 other events, 3276.0 us)

commit v2 on v1

v2 whole, which is shorter than its diff:
```python
import functools
import math

import numpy as np

import jax
import jax.numpy as jnp
from jax import lax
from jax.experimental import pallas as pl
from jax.experimental.pallas import tpu as pltpu
from jax.sharding import PartitionSpec as P

HEAD_DIM = 128
TOP = 4
BRANCHES = 4
LEAVES = 2
LANES = 128

EPSILON = 1e-06
THETA = 1000000.0
NEGATIVE = -1e30
BF16 = jnp.bfloat16
F32 = jnp.float32
VMEM_LIMIT = 56 * 1024 * 1024


SECOND_FIRST = ('Su', '0g', '0d')
PLAN = {
    "Sg": "Sg+",
    "Su": "Su+",
    "Sd": "Sd+",
    "0g": "0g+",
    "0u": "0u+",
    "mix": "Sg- Su- 0d+",
    "back": "Sd- 0g- Sd+",
    "1g": "0u-",
    "n1": "1g+",
    "norm": "0d- Sg+",
    "1d": "Sd-",
    "h": "Sd+ 0d+ 0u+",
    "ab": "1g- 1u+ Sg- Sg+",
    "v": "Sd- 1g+ 0d- 0d+",
    "fin": " ".join(
        ["0u- q+ 1u- 1u+", "Sg- o+ 1g- 1g+", "0d- Su+ q- q+", "1u- 1u+ o- o+", "1g- 1d+ Su- Su+", "q- q+ 1u- 0u+", "o- o+ 1d- v+", "Su- 1d+ q- k+", "0u- 0g+ o- v-", "v+ 1d- 1d+ k-", "k+ 0g- 0g+ v-", "v+ 1d- k- k+", "0g- v- k-"]
    ),
}


def rms_scale(values):
    return lax.rsqrt(jnp.mean(values * values, axis=-1, keepdims=True) + EPSILON)


def dots(left, right, left_dim, right_dim):
    return lax.dot_general(
        left, right, (((left_dim,), (right_dim,)), ((), ())), preferred_element_type=F32
    )


def after(values, *earlier):
    return lax.optimization_barrier((values, earlier))[0]


def kernel_call(
    name, body, grid, in_specs, out_specs, out_shape, *operands, scratch=(), prefetch=0, aliases=None
):
    return pl.pallas_call(
        body,
        name=name,
        grid_spec=pltpu.PrefetchScalarGridSpec(
            num_scalar_prefetch=prefetch,
            grid=grid,
            in_specs=in_specs,
            out_specs=out_specs,
            scratch_shapes=list(scratch),
        ),
        out_shape=out_shape,
        input_output_aliases=aliases or {},
        compiler_params=pltpu.CompilerParams(vmem_limit_bytes=VMEM_LIMIT),
        cost_estimate=pl.CostEstimate(flops=1, bytes_accessed=1, transcendentals=0),
    )(*operands)


def whole(array):
    zeros = (0,) * len(array.shape)
    return pl.BlockSpec(array.shape, lambda *_: zeros, pipeline_mode=pl.Buffered(1))


def array_of(shape, dtype=BF16):
    return jax.ShapeDtypeStruct(shape, dtype)


def cube_of(count):
    digits, left = [], count
    while left > 1:
        size = 4 if left % 4 == 0 else 2
        digits.append(size)
        left //= size
    table = []
    for index in range(count):
        rest, corner, shift = index, 0, 0
        for size in reversed(digits):
            digit = rest % size
            rest //= size
            corner |= (digit ^ (digit >> 1)) << shift
            shift += int(math.log2(size))
        table.append(corner)
    return table


def swap(values, axis, table, bit):
    where = {corner: index for index, corner in enumerate(table)}
    pairs = [(index, where[corner ^ bit]) for index, corner in enumerate(table)]
    return lax.ppermute(values, axis, pairs)


def far_gather(own, count):
    table = list(range(count))
    blocks = {0: own}
    for place in range(2, count, 2):
        bit = max(1 << k for k in range(10) if place & (1 << k))
        blocks[place] = swap(blocks[place ^ bit], "expert", table, bit)
    return blocks


def near_gather(blocks, count):
    table = list(range(lax.axis_size("expert")))
    out = []
    for place in range(0, count, 2):
        out += [blocks[place], swap(blocks[place], "expert", table, 1)]
    return out


def group_gather(own, count, *earlier):
    table = list(range(count))
    blocks = far_gather(own, count)
    other = swap(own, "expert", table, 1)
    far = {p: after(block, *earlier) for p, block in blocks.items() if p}
    rest = near_gather({0: own, **far}, count)
    return [own, other, *rest[2:]]


def group_sum(blocks, pin=lambda values: values):
    for parts in group_steps(blocks, pin):
        pass
    return sum(value.astype(F32) for value in parts)


def group_steps(blocks, pin):
    count = len(blocks)
    table = list(range(count))
    parts = [[block] for block in blocks]
    bit = 1
    while bit < count:
        for p in range(0, count, 2 * bit):
            sent = parts[p + bit]
            if len(sent) > 1:
                sent = [sum(value.astype(F32) for value in sent).astype(BF16)]
            parts[p].append(swap(pin(sent[0]), "expert", table, bit))
        yield parts[0]
        bit *= 2


def prepare_kernel(width, rows_each, local, capacity, places, first, *refs):
    cosine, sine, col_meta, row_meta, hot = refs[width:]
    shape = (rows_each, rows_each)
    identity = jnp.where(
        lax.broadcasted_iota(jnp.int32, shape, 0) == lax.broadcasted_iota(jnp.int32, shape, 1),
        1.0,
        0.0,
    ).astype(BF16)
    by_col = [dots(identity, ref[...], 1, 1) for ref in refs[:width]]
    half_dim = HEAD_DIM // 2
    count_seg = 1 + BRANCHES * (1 + LEAVES)
    by_row = [ref[...].astype(F32) for ref in refs[:width]]
    lengths = [
        sum(jnp.sum(jnp.where(rows[0:1, :] == k, 1.0, 0.0)) for rows in by_row)
        for k in range(count_seg)
    ]
    lanes = lax.broadcasted_iota(jnp.int32, (1, HEAD_DIM), 1)
    frequency = jnp.exp(
        jnp.where(lanes < half_dim, lanes, lanes - half_dim).astype(F32)
        * F32(-2.0 * math.log(THETA) / HEAD_DIM)
    )
    sign = jnp.where(lanes < half_dim, F32(-1.0), F32(1.0))
    shape = (rows_each, LANES)
    lane_ids = lax.broadcasted_iota(jnp.int32, shape, 1)
    for p in range(width):
        at = slice(p * rows_each, (p + 1) * rows_each)
        cols = by_col[p]
        segment = jnp.broadcast_to(cols[:, 0:1], shape)
        start = jnp.zeros(shape, F32)
        above = jnp.zeros(shape, F32)
        parent = segment
        for k in range(count_seg):
            start = start + jnp.where(segment > k, lengths[k], 0.0)
            back = (k - 1) % (LEAVES + 1)
            if k > 0 and back > 0:
                leaf = segment == k
                parent = jnp.where(leaf, float(k - back), parent)
                above = above + jnp.where(leaf, lengths[k - back], 0.0)
        first_place = (places[p] * rows_each).astype(F32)
        place = lax.broadcasted_iota(jnp.int32, shape, 0).astype(F32) + first_place
        position = place - start + jnp.where(segment > 0, lengths[0], 0.0) + above
        angle = position * frequency
        cosine[at, :] = jnp.cos(angle)
        sine[at, :] = jnp.sin(angle) * sign
        col_meta[at, :] = jnp.where(
            lane_ids == 0, segment, jnp.where(lane_ids == 1, parent, place)
        )
        rows = by_row[p]
        row_places = (
            lax.broadcasted_iota(jnp.int32, rows.shape, 1).astype(F32) + first_place
        )
        sublanes = lax.broadcasted_iota(jnp.int32, rows.shape, 0)
        row_meta[:, at] = jnp.where(sublanes == 0, rows, row_places)
        before = jnp.where(cols[:, 1:2] < rows[1:2, :], 1.0, 0.0)
        for e in range(local):
            name = (first[0] + e).astype(F32)
            named_col = sum(jnp.where(cols[:, 2 + k : 3 + k] == name, 1.0, 0.0) for k in range(TOP))
            named_row = sum(jnp.where(rows[2 + k : 3 + k, :] == name, 1.0, 0.0) for k in range(TOP))
            slot = jnp.sum(before * named_col, axis=0, keepdims=True)
            kept = (named_row > 0.0) & (slot < capacity)
            slot = jnp.where(kept, slot, -1.0)
            ranks = lax.broadcasted_iota(jnp.int32, hot.shape[2:], 0).astype(F32)
            hot[p, e] = jnp.where(ranks == slot, 1.0, 0.0).astype(BF16)


def prepare(places, first, by_row, local, capacity, slots_each):
    width = len(by_row)
    rows_each = by_row[0].shape[1]
    rows = width * rows_each
    shapes = [
        array_of((rows, HEAD_DIM), F32),
        array_of((rows, HEAD_DIM), F32),
        array_of((rows, LANES), F32),
        array_of((by_row[0].shape[0], rows), F32),
        array_of((width, local, slots_each, rows_each)),
    ]
    return kernel_call(
        "prepare",
        functools.partial(prepare_kernel, width, rows_each, local, capacity),
        (1,),
        [whole(block) for block in by_row],
        [whole(shape) for shape in shapes],
        shapes,
        places,
        first,
        *by_row,
        prefetch=2,
    )


def turned(values):
    return pltpu.roll(values, HEAD_DIM // 2, 1)


def project_kernel(count, heads, rows_each, first, *refs):
    inputs = refs[:count]
    gain, weight, bias, cosine, sine = refs[count : count + 5]
    projected, normed = refs[-2:]
    j = pl.program_id(0)

    @pl.when(j == 0)
    def _():
        for k in range(count):
            values = inputs[k][...].astype(F32)
            normed[k * rows_each : (k + 1) * rows_each, :] = (
                values * rms_scale(values) * gain[...].astype(F32)
            ).astype(BF16)

    product = dots(normed[...], weight[0], 1, 0) + bias[0].astype(F32)

    @pl.when(j < 2)
    def _():
        for head in range(heads):
            at = slice(head * HEAD_DIM, (head + 1) * HEAD_DIM)
            part = product[:, at]
            projected[0, :, at] = (part * cosine[...] + turned(part) * sine[...]).astype(BF16)

    @pl.when(j == 2)
    def _():
        projected[0] = product.astype(BF16)


def project(input_blocks, gain, weight, bias, cosine, sine, part, parts, earlier):
    count = len(input_blocks)
    rows_each, dim = input_blocks[0].shape
    cols = weight.shape[2]
    rows = count * rows_each
    table = pl.BlockSpec((rows, HEAD_DIM), lambda j: (part, 0), pipeline_mode=pl.Buffered(1))
    operands = [*input_blocks, gain[None, :], weight, bias[:, None, :], cosine, sine]
    in_specs = [
        *[whole(block) for block in input_blocks],
        pl.BlockSpec((1, dim), lambda j: (0, 0)),
        pl.BlockSpec((1, dim, cols), lambda j: (j, 0, 0)),
        pl.BlockSpec((1, 1, cols), lambda j: (j, 0, 0)),
        table,
        table,
    ]
    aliases = {}
    if earlier is not None:
        aliases = {len(operands): 0, len(operands) + 1: 1}
        operands += list(earlier)
        in_specs += [pl.BlockSpec(memory_space=pl.ANY)] * 2
    return kernel_call(
        "project",
        functools.partial(project_kernel, count, cols // HEAD_DIM, rows_each, part),
        (3,),
        in_specs,
        [
            pl.BlockSpec((1, rows, cols), lambda j: (j, part, 0)),
            pl.BlockSpec((rows, dim), lambda j: (part, 0)),
        ],
        [array_of((3, parts * rows, cols)), array_of((parts * rows, dim))],
        *operands,
        aliases=aliases,
    )


def seen(col_meta, row_meta):
    query_seg, query_parent, query_place = (col_meta[:, k : k + 1] for k in range(3))
    key_seg, key_place = row_meta[0:1, :], row_meta[1:2, :]
    related = (key_seg == query_seg) | (key_seg == 0) | (key_seg == query_parent)
    return related & (key_place <= query_place)


def lane_fold(values, combine):
    total = values[:, :LANES]
    for k in range(1, values.shape[1] // LANES):
        total = combine(total, values[:, k * LANES : (k + 1) * LANES])
    return total


def attend_kernel(
    width, rows_each, heads, first, places, query, key, value, col_meta, row_meta, out, log_total,
    scores, peak, total, mixed,
):
    own_place = places[first + pl.program_id(0)]
    scale = 1.0 / math.sqrt(HEAD_DIM)
    peak[...] = jnp.full(peak.shape, NEGATIVE, F32)
    total[...] = jnp.zeros(total.shape, F32)
    mixed[...] = jnp.zeros(mixed.shape, F32)
    for k in range(width):
        at = slice(k * rows_each, (k + 1) * rows_each)

        @pl.when(places[k] <= own_place)
        def _():
            mask = seen(col_meta[...], row_meta[:, at])
            for h in range(heads):
                cols = slice(h * HEAD_DIM, (h + 1) * HEAD_DIM)
                raw = dots(query[0, :, cols], key[0, at, cols], 1, 1) * scale
                raw = jnp.where(mask, raw, NEGATIVE)
                scores[h, :, at] = raw
                peak[h] = jnp.maximum(peak[h], lane_fold(raw, jnp.maximum))

    for h in range(heads):
        peak[h] = jnp.broadcast_to(jnp.max(peak[h], axis=1, keepdims=True), peak.shape[1:])

    for k in range(width):
        at = slice(k * rows_each, (k + 1) * rows_each)

        @pl.when(places[k] <= own_place)
        def _():
            for h in range(heads):
                cols = slice(h * HEAD_DIM, (h + 1) * HEAD_DIM)
                weights = jnp.exp(scores[h, :, at] - peak[h][:, :1])
                total[h] += lane_fold(weights, jnp.add)
                mixed[h] += dots(weights.astype(BF16), value[0, at, cols], 1, 0)

    for h in range(heads):
        whole_sum = jnp.sum(total[h], axis=1, keepdims=True)
        out[:, h * HEAD_DIM : (h + 1) * HEAD_DIM] = (mixed[h] / whole_sum).astype(BF16)
        log_total[h] = peak[h][:, :1] + jnp.log(whole_sum)


def attend(places, projected, col_meta, row_meta, rows_each, first, count):
    _, rows, cols = projected.shape
    heads = cols // HEAD_DIM
    width = rows // rows_each

    def side(j):
        return pl.BlockSpec((1, rows, cols), lambda b, _: (j, 0, 0), pipeline_mode=pl.Buffered(1))

    return kernel_call(
        "attend",
        functools.partial(attend_kernel, width, rows_each, heads, first),
        (count,),
        [
            pl.BlockSpec((1, rows_each, cols), lambda b, _: (0, first + b, 0)),
            side(1),
            side(2),
            pl.BlockSpec((rows_each, LANES), lambda b, _: (first + b, 0)),
            whole(row_meta),
        ],
        [
            pl.BlockSpec((rows_each, cols), lambda b, _: (b, 0)),
            pl.BlockSpec((heads, rows_each, 1), lambda b, _: (0, b, 0)),
        ],
        [array_of((count * rows_each, cols)), array_of((heads, count * rows_each, 1), F32)],
        places,
        projected,
        projected,
        projected,
        col_meta,
        row_meta,
        scratch=[
            pltpu.VMEM((heads, rows_each, rows), F32),
            pltpu.VMEM((heads, rows_each, LANES), F32),
            pltpu.VMEM((heads, rows_each, LANES), F32),
            pltpu.VMEM((heads, rows_each, HEAD_DIM), F32),
        ],
        prefetch=1,
    )


def attend_back_kernel(
    width, rows_each, heads, places, query, key, value, out_grad, log_near, log_far, col_meta,
    row_meta, cosine_q, sine_q, cosine, sine, query_out, key_out, value_out, bias_out,
    weights, weight_grads, delta, query_grad, key_grad, value_grad, log_total,
):
    block = pl.program_id(0)
    own_place = places[block]
    scale = 1.0 / math.sqrt(HEAD_DIM)

    @pl.when(block == 0)
    def _():
        key_grad[...] = jnp.zeros(key_grad.shape, F32)
        value_grad[...] = jnp.zeros(value_grad.shape, F32)
        bias_out[...] = jnp.zeros(bias_out.shape, F32)

    @pl.when(block < width // 2)
    def _():
        log_total[...] = log_near[...]

    @pl.when(block >= width // 2)
    def _():
        log_total[...] = log_far[...]

    def add_bias(j, cols, low):
        bias_out[j, :, cols] += jnp.sum(low.astype(F32).reshape(-1, 8, HEAD_DIM), axis=0)

    delta[...] = jnp.zeros(delta.shape, F32)
    query_grad[...] = jnp.zeros(query_grad.shape, F32)
    for k in range(width):
        at = slice(k * rows_each, (k + 1) * rows_each)

        @pl.when(places[k] <= own_place)
        def _():
            mask = seen(col_meta[...], row_meta[:, at])
            for h in range(heads):
                cols = slice(h * HEAD_DIM, (h + 1) * HEAD_DIM)
                raw = dots(query[0, :, cols], key[0, at, cols], 1, 1) * scale
                part = jnp.exp(jnp.where(mask, raw - log_total[h], NEGATIVE))
                part_grad = dots(out_grad[:, cols], value[0, at, cols], 1, 1)
                delta[h] += lane_fold(part * part_grad, jnp.add)
                weights[h, :, at] = part
                weight_grads[h, :, at] = part_grad

    for h in range(heads):
        delta[h] = jnp.broadcast_to(jnp.sum(delta[h], axis=1, keepdims=True), delta.shape[1:])

    for k in range(width):
        at = slice(k * rows_each, (k + 1) * rows_each)

        @pl.when(places[k] <= own_place)
        def _():
            for h in range(heads):
                cols = slice(h * HEAD_DIM, (h + 1) * HEAD_DIM)
                part = weights[h, :, at]
                score_grad = (part * (weight_grads[h, :, at] - delta[h][:, :1])).astype(BF16)
                query_grad[h] += dots(score_grad, key[0, at, cols], 1, 0)
                key_grad[at, cols] += dots(score_grad, query[0, :, cols], 0, 0)
                value_grad[at, cols] += dots(part.astype(BF16), out_grad[:, cols], 0, 0)

    for h in range(heads):
        cols = slice(h * HEAD_DIM, (h + 1) * HEAD_DIM)
        grad = query_grad[h] * scale
        low = (grad * cosine_q[...] - turned(grad) * sine_q[...]).astype(BF16)
        query_out[:, cols] = low
        add_bias(0, cols, low)

    @pl.when(block == width - 1)
    def _():
        for h in range(heads):
            cols = slice(h * HEAD_DIM, (h + 1) * HEAD_DIM)
            grad = key_grad[:, cols] * scale
            low = (grad * cosine[...] - turned(grad) * sine[...]).astype(BF16)
            key_out[:, cols] = low
            add_bias(1, cols, low)
            low = value_grad[:, cols].astype(BF16)
            value_out[:, cols] = low
            add_bias(2, cols, low)


def attend_back(places, projected, out_grad, log_near, log_far, col_meta, row_meta, cosine, sine, rows_each):
    _, rows, cols = projected.shape
    heads = cols // HEAD_DIM
    width = rows // rows_each
    near = width // 2

    def side(j):
        return pl.BlockSpec((1, rows, cols), lambda b, _: (j, 0, 0), pipeline_mode=pl.Buffered(1))

    by_block = pl.BlockSpec((rows_each, LANES), lambda b, _: (b, 0))
    full_out = pl.BlockSpec((rows, cols), lambda b, _: (0, 0), pipeline_mode=pl.Buffered(1))
    log_shape = (heads, rows_each, 1)
    return kernel_call(
        "attend_back",
        functools.partial(attend_back_kernel, width, rows_each, heads),
        (width,),
        [
            pl.BlockSpec((1, rows_each, cols), lambda b, _: (0, b, 0)),
            side(1),
            side(2),
            pl.BlockSpec((rows_each, cols), lambda b, _: (b, 0)),
            pl.BlockSpec(log_shape, lambda b, _: (0, jnp.minimum(b, near - 1), 0)),
            pl.BlockSpec(log_shape, lambda b, _: (0, jnp.maximum(b - near, 0), 0)),
            by_block,
            whole(row_meta),
            by_block,
            by_block,
            whole(cosine),
            whole(sine),
        ],
        [
            pl.BlockSpec((rows_each, cols), lambda b, _: (b, 0)),
            full_out,
            full_out,
            pl.BlockSpec((3, 8, cols), lambda b, _: (0, 0, 0)),
        ],
        [array_of((rows, cols))] * 3 + [array_of((3, 8, cols), F32)],
        places,
        projected,
        projected,
        projected,
        out_grad,
        log_near,
        log_far,
        col_meta,
        row_meta,
        cosine,
        sine,
        cosine,
        sine,
        scratch=[
            pltpu.VMEM((heads, rows_each, rows), F32),
            pltpu.VMEM((heads, rows_each, rows), F32),
            pltpu.VMEM((heads, rows_each, LANES), F32),
            pltpu.VMEM((heads, rows_each, HEAD_DIM), F32),
            pltpu.VMEM((rows, cols), F32),
            pltpu.VMEM((rows, cols), F32),
            pltpu.VMEM(log_shape, F32),
        ],
        prefetch=1,
    )


def out_kernel(width, count, *refs):
    inputs = refs[:count]
    attended = refs[count : count + width]
    weights = refs[count + width : count + 2 * width]
    gain, side_weight = refs[count + 2 * width : count + 2 * width + 2]
    normed, side, hidden_own, hidden = refs[-4:]
    block = pl.program_id(0)
    for k in range(count):

        @pl.when(block == k)
        def _():
            hidden[...] = inputs[k][...].astype(F32)

    total = hidden[...]
    for p in range(width):
        total = total + dots(attended[p][...], weights[p][...], 1, 0)

    @pl.when(block == 0)
    def _():
        hidden_own[...] = total

    low = (total * rms_scale(total) * gain[...].astype(F32)).astype(BF16)
    normed[...] = low
    side[...] = dots(low, side_weight[...], 1, 0)


def out_project(input_blocks, attended, weights, gain, side_weight, part, earlier):
    count = len(input_blocks)
    width = len(attended)
    rows_each, dim = input_blocks[0].shape
    cols = attended[0].shape[1]

    def piece(p):
        return pl.BlockSpec((rows_each, cols), lambda b: (b ^ (p % count), 0))

    operands = [*input_blocks, *attended, *weights, gain[None, :], side_weight]
    in_specs = [
        *[whole(block) for block in input_blocks],
        *[piece(p) for p in range(width)],
        *[whole(weight) for weight in weights],
        pl.BlockSpec((1, dim), lambda b: (0, 0)),
        whole(side_weight),
    ]
    aliases = {}
    if earlier is not None:
        aliases = {len(operands): 0, len(operands) + 1: 1}
        operands += list(earlier)
        in_specs += [pl.BlockSpec(memory_space=pl.ANY)] * 2
    start = part * count
    return kernel_call(
        "out_project",
        functools.partial(out_kernel, width, count),
        (count,),
        in_specs,
        [
            pl.BlockSpec((rows_each, dim), lambda b: (start + b, 0)),
            pl.BlockSpec((rows_each, LANES), lambda b: (start + b, 0)),
            pl.BlockSpec((rows_each, dim), lambda b: (0, 0)),
        ],
        [
            array_of((width * rows_each, dim)),
            array_of((width * rows_each, LANES), F32),
            array_of((rows_each, dim), F32),
        ],
        *operands,
        scratch=[pltpu.VMEM((rows_each, dim), F32)],
        aliases=aliases,
    )


def pick(values, lane):
    lanes = lax.broadcasted_iota(jnp.int32, values.shape, 1)
    return jnp.sum(jnp.where(lanes == lane, values, 0.0), axis=1, keepdims=True)


def probabilities(side, expert_count):
    lanes = lax.broadcasted_iota(jnp.int32, side.shape, 1)
    logits = jnp.where(lanes < expert_count, side, NEGATIVE)
    raw = jnp.exp(logits - jnp.max(logits, axis=1, keepdims=True))
    return raw / jnp.sum(raw, axis=1, keepdims=True)


def inner(rows_in, grad_in, gate_up_ref, down_ref, act, gate_grad, up_grad):
    gate = dots(rows_in, gate_up_ref[0], 1, 0)
    up = dots(rows_in, gate_up_ref[1], 1, 0)
    act_grad = dots(grad_in, down_ref[...], 1, 1)
    sig = jax.nn.sigmoid(gate)
    silu = gate * sig
    act[...] = (silu * up).astype(BF16)
    gate_grad[...] = (act_grad * up * sig * (1.0 + gate * (1.0 - sig))).astype(BF16)
    up_grad[...] = (act_grad * silu).astype(BF16)


def shared_kernel(width, rows_each, expert_count, *refs):
    normed, side = refs[:2]
    cots = refs[2 : 2 + width]
    gate_up, down, act, gate_grad, up_grad, out_grad = refs[2 + width :]

    @pl.when(pl.program_id(0) == 0)
    def _():
        for p in range(width):
            at = slice(p * rows_each, (p + 1) * rows_each)
            gate = jax.nn.sigmoid(side[at, expert_count : expert_count + 1])
            out_grad[at, :] = (cots[p][...].astype(F32) * gate).astype(BF16)

    inner(normed[...], out_grad[...], gate_up, down, act, gate_grad, up_grad)


def tile_of(size):
    return min(256, size)


def shared_inner(normed, side, cots, gate_up, down, expert_count):
    rows, dim = normed.shape
    hidden = down.shape[0]
    tile = tile_of(hidden)
    width = len(cots)
    out = pl.BlockSpec((rows, tile), lambda i: (0, i))
    return kernel_call(
        "shared_inner",
        functools.partial(shared_kernel, width, rows // width, expert_count),
        (pl.cdiv(hidden, tile),),
        [
            whole(normed),
            whole(side),
            *[whole(cot) for cot in cots],
            pl.BlockSpec((2, dim, tile), lambda i: (0, 0, i)),
            pl.BlockSpec((tile, dim), lambda i: (i, 0)),
        ],
        [out, out, out, pl.BlockSpec((rows, dim), lambda i: (0, 0), pipeline_mode=pl.Buffered(1))],
        [array_of((rows, hidden))] * 3 + [array_of((rows, dim))],
        normed,
        side,
        *cots,
        gate_up,
        down,
    )


def expert_kernel(width, rows_each, capacity, expert_count, first, normed, side, hot, *refs):
    cots = refs[:width]
    gate_up, down, act, gate_grad, up_grad, rows_in, grad_in = refs[width:]

    @pl.when(pl.program_id(0) == 0)
    def _():
        for p in range(width):
            at = slice(p * rows_each, (p + 1) * rows_each)
            to = slice(p * capacity, (p + 1) * capacity)
            gate = pick(probabilities(side[at, :], expert_count), first)
            rows_in[to, :] = dots(hot[p, 0], normed[at, :], 1, 0).astype(BF16)
            scaled = (cots[p][...].astype(F32) * gate).astype(BF16)
            grad_in[to, :] = dots(hot[p, 0], scaled, 1, 0).astype(BF16)

    inner(rows_in[...], grad_in[...], gate_up.at[0], down.at[0], act, gate_grad, up_grad)


def expert_inner(lane, normed, side, hot, cots, gate_up, down, expert, expert_count):
    rows, dim = normed.shape
    hidden = down.shape[1]
    tile = tile_of(hidden)
    width = len(cots)
    capacity = hot.shape[2]
    slots = width * capacity
    out = pl.BlockSpec((slots, tile), lambda i, _: (0, i))
    kept = pl.BlockSpec((slots, dim), lambda i, _: (0, 0), pipeline_mode=pl.Buffered(1))

    def body(first, *refs):
        expert_kernel(width, rows // width, capacity, expert_count, first[0] + expert, *refs)

    return kernel_call(
        "expert_inner",
        body,
        (pl.cdiv(hidden, tile),),
        [
            whole(normed),
            whole(side),
            pl.BlockSpec((width, 1, *hot.shape[2:]), lambda i, _: (0, expert, 0, 0)),
            *[whole(cot) for cot in cots],
            pl.BlockSpec((1, 2, dim, tile), lambda i, _: (expert, 0, 0, i)),
            pl.BlockSpec((1, tile, dim), lambda i, _: (expert, i, 0)),
        ],
        [out, out, out, kept, kept],
        [array_of((slots, hidden))] * 3 + [array_of((slots, dim))] * 2,
        lane,
        normed,
        side,
        hot,
        *cots,
        gate_up,
        down,
        prefetch=1,
    )


def weight_kernel(half, count, dim_first, blocks, *refs):
    values = refs[:count]
    others = refs[count:-2]
    sent, kept = refs[-2:]
    each = values[0].shape[0]
    product = None
    for p in range(count):
        per_other = others[0].shape[0] // each
        row = (p % per_other) * each
        rows = others[p // per_other][row : row + each, :]
        part = (
            dots(values[p][...], rows, 0, 0) if dim_first else dots(rows, values[p][...], 0, 0)
        )
        product = part if product is None else product + part
    low = product.astype(BF16)

    @pl.when(pl.program_id(0) < half)
    def _():
        sent[...] = low

    @pl.when(pl.program_id(0) >= half)
    def _():
        kept[...] = low


def weight_product(blocks, values, other, block_dim, dim_first):
    values = values if isinstance(values, (list, tuple)) else [values]
    others = other if isinstance(other, (list, tuple)) else [other]
    count = blocks.shape[0]
    half = count // 2
    each = values[0].shape[0]
    cols = others[0].shape[1]
    if dim_first:
        shape = array_of((half * block_dim, cols))
        sent = pl.BlockSpec((block_dim, cols), lambda i, _: (jnp.minimum(i, half - 1), 0))
        kept = pl.BlockSpec((block_dim, cols), lambda i, _: (jnp.maximum(i - half, 0), 0))
    else:
        shape = array_of((cols, half * block_dim))
        sent = pl.BlockSpec((cols, block_dim), lambda i, _: (0, jnp.minimum(i, half - 1)))
        kept = pl.BlockSpec((cols, block_dim), lambda i, _: (0, jnp.maximum(i - half, 0)))
    return kernel_call(
        "weight_product",
        functools.partial(weight_kernel, half, len(values), dim_first),
        (count,),
        [
            *[pl.BlockSpec((each, block_dim), lambda i, at: (0, at[i])) for _ in values],
            *[whole(array) for array in others],
        ],
        [sent, kept],
        [shape, shape],
        blocks,
        *values,
        *others,
        prefetch=1,
    )


def mix_kernel(width, rows_each, local, expert_count, first, side, act, down, hot, *refs):
    acts, downs = refs[:local], refs[local : 2 * local]
    cots = refs[2 * local : 2 * local + width]
    mixed = refs[2 * local + width : 2 * local + 2 * width]
    totals = refs[2 * local + 2 * width]
    lanes = lax.broadcasted_iota(jnp.int32, (rows_each, LANES), 1)
    shared = dots(act[...], down[...], 1, 0)
    outputs = [
        dots(acts[e][...], downs[e][0], 1, 0).astype(BF16) for e in range(local)
    ]
    capacity = hot.shape[2]

    @pl.when(pl.program_id(0) == 0)
    def _():
        totals[...] = jnp.zeros(totals.shape, F32)

    for p in range(width):
        at = slice(p * rows_each, (p + 1) * rows_each)
        slots = slice(p * capacity, (p + 1) * capacity)
        pre = side[at, :]
        probs = probabilities(pre, expert_count)
        cot = cots[p][...].astype(F32)
        part = shared[at, :]
        sums = jnp.where(lanes == expert_count, jnp.sum(cot * part, axis=1, keepdims=True), 0.0)
        value = jax.nn.sigmoid(pre[:, expert_count : expert_count + 1]) * part
        for e in range(local):
            back = dots(hot[p, e], outputs[e][slots, :], 0, 0)
            lane = first[0] + e
            sums = sums + jnp.where(
                lanes == lane, jnp.sum(cot * back, axis=1, keepdims=True), 0.0
            )
            value = value + pick(probs, lane) * back
        totals[at, :] += sums
        mixed[p][...] = value.astype(BF16)


def mix(lane, side, act, down, hot, acts, expert_down, cots, expert_count):
    rows, hidden = act.shape
    dim = down.shape[1]
    width = len(cots)
    rows_each = rows // width
    local = len(acts)
    tile = tile_of(dim)

    def expert_tile(e):
        return pl.BlockSpec((1, expert_down.shape[1], tile), lambda i, _: (e, 0, i))

    return kernel_call(
        "mix",
        functools.partial(mix_kernel, width, rows_each, local, expert_count),
        (dim // tile,),
        [
            whole(side),
            whole(act),
            pl.BlockSpec((hidden, tile), lambda i, _: (0, i)),
            whole(hot),
            *[whole(values) for values in acts],
            *[expert_tile(e) for e in range(local)],
            *[pl.BlockSpec((rows_each, tile), lambda i, _: (0, i)) for _ in cots],
        ],
        [
            *[pl.BlockSpec((rows_each, tile), lambda i, _: (0, i)) for _ in cots],
            pl.BlockSpec((rows, LANES), lambda i, _: (0, 0)),
        ],
        [array_of((rows_each, dim)) for _ in cots] + [array_of((rows, LANES), F32)],
        lane,
        side,
        act,
        down,
        hot,
        *acts,
        *[expert_down] * local,
        *cots,
        prefetch=1,
    )


def back_kernel(width, rows_each, local, expert_count, side, totals, gate_grad, up_grad, gate_up, hot, *refs):
    grads = refs[: 2 * local]
    weights = refs[2 * local : 3 * local]
    normed, side_weight = refs[3 * local : 3 * local + 2]
    outs = refs[3 * local + 2 : 3 * local + 2 + width]
    side_sum, high, low = refs[3 * local + 2 + width :]
    capacity = hot.shape[2]

    @pl.when(pl.program_id(0) == 0)
    def _():
        pre = side[...]
        sums = totals[...]
        lanes = lax.broadcasted_iota(jnp.int32, pre.shape, 1)
        probs = probabilities(pre, expert_count)
        prob_grad = jnp.where(lanes < expert_count, sums, 0.0)
        logit_grad = probs * (prob_grad - jnp.sum(probs * prob_grad, axis=1, keepdims=True))
        gate = jax.nn.sigmoid(pre)
        value = jnp.where(lanes == expert_count, sums * gate * (1.0 - gate), logit_grad)
        value = jnp.where(lanes <= expert_count, value, 0.0)
        top = value.astype(BF16)
        high[...] = top
        low[...] = (value - top.astype(F32)).astype(BF16)

    side_sum[...] = dots(high[...], normed[...], 0, 0) + dots(low[...], normed[...], 0, 0)
    total = (
        dots(gate_grad[...], gate_up[0], 1, 1)
        + dots(up_grad[...], gate_up[1], 1, 1)
        + dots(high[...], side_weight[...], 1, 1)
        + dots(low[...], side_weight[...], 1, 1)
    )
    back = [
        (
            dots(grads[2 * e][...], weights[e][0, 0], 1, 1)
            + dots(grads[2 * e + 1][...], weights[e][0, 1], 1, 1)
        ).astype(BF16)
        for e in range(local)
    ]
    for p in range(width):
        at = slice(p * rows_each, (p + 1) * rows_each)
        slots = slice(p * capacity, (p + 1) * capacity)
        value = total[at, :]
        for e in range(local):
            value = value + dots(hot[p, e], back[e][slots, :], 0, 0)
        outs[p][...] = value.astype(BF16)


def back(side, totals, gate_grad, up_grad, gate_up, hot, grads, expert_gate_up, normed, side_weight, width, expert_count):
    rows, hidden = gate_grad.shape
    dim = normed.shape[1]
    rows_each = rows // width
    local = len(grads) // 2
    tile = tile_of(dim)

    def expert_tile(e):
        return pl.BlockSpec((1, 2, tile, expert_gate_up.shape[3]), lambda i: (e, 0, i, 0))

    return kernel_call(
        "back",
        functools.partial(back_kernel, width, rows_each, local, expert_count),
        (dim // tile,),
        [
            whole(side),
            whole(totals),
            whole(gate_grad),
            whole(up_grad),
            pl.BlockSpec((2, tile, hidden), lambda i: (0, i, 0)),
            whole(hot),
            *[whole(values) for values in grads],
            *[expert_tile(e) for e in range(local)],
            pl.BlockSpec((rows, tile), lambda i: (0, i)),
            pl.BlockSpec((tile, LANES), lambda i: (i, 0)),
        ],
        [
            *[pl.BlockSpec((rows_each, tile), lambda i: (0, i)) for _ in range(width)],
            pl.BlockSpec((LANES, tile), lambda i: (0, i)),
        ],
        [array_of((rows_each, dim)) for _ in range(width)] + [array_of((LANES, dim), F32)],
        side,
        totals,
        gate_grad,
        up_grad,
        gate_up,
        hot,
        *grads,
        *[expert_gate_up] * local,
        normed,
        side_weight,
        scratch=[pltpu.VMEM((rows, LANES), BF16), pltpu.VMEM((rows, LANES), BF16)],
    )


def attended_grad_kernel(rows_each, weight, *refs):
    out = refs[-1]
    for p, block in enumerate(refs[:-1]):
        out[p * rows_each : (p + 1) * rows_each, :] = dots(block[...], weight[...], 1, 1).astype(
            BF16
        )


def attended_gradient(weight, blocks):
    rows_each = blocks[0].shape[0]
    cols = weight.shape[0]
    shape = (rows_each * len(blocks), cols)
    return kernel_call(
        "attended_gradient",
        functools.partial(attended_grad_kernel, rows_each),
        (1,),
        [whole(weight), *[whole(block) for block in blocks]],
        pl.BlockSpec(shape, lambda i: (0, 0)),
        array_of(shape),
        weight,
        *blocks,
    )


def first_back_kernel(width, rows_each, grads, weight, *refs):
    inputs = refs[:width]
    scales = refs[width]
    outs = refs[width + 1 : 2 * width + 1]
    gain_sum = refs[2 * width + 1]
    total = sum(dots(grads[j][...], weight[j], 1, 1) for j in range(3))
    sums = jnp.zeros((8, total.shape[1]), F32)
    for p in range(width):
        at = slice(p * rows_each, (p + 1) * rows_each)
        value = total[at, :]
        outs[p][...] = value.astype(BF16)
        term = value * (inputs[p][...].astype(F32) * scales[at, :])
        sums = sums + jnp.sum(term.reshape(-1, 8, term.shape[1]), axis=0)
    gain_sum[...] = sums


def first_back(grads, weight, input_blocks, scales):
    rows, cols = grads[0].shape
    dim = weight.shape[1]
    width = len(input_blocks)
    rows_each = rows // width
    tile = tile_of(dim)

    def body(query, key, value, *refs):
        first_back_kernel(width, rows_each, (query, key, value), *refs)

    block = pl.BlockSpec((rows_each, tile), lambda i: (0, i))
    return kernel_call(
        "first_back",
        body,
        (dim // tile,),
        [
            *[whole(grad) for grad in grads],
            pl.BlockSpec((3, tile, cols), lambda i: (0, i, 0)),
            *[block] * width,
            whole(scales),
        ],
        [*[block] * width, pl.BlockSpec((8, tile), lambda i: (0, i))],
        [array_of((rows_each, dim)) for _ in range(width)] + [array_of((8, dim), F32)],
        *grads,
        weight,
        *input_blocks,
        scales,
    )


def per_device(
    block_input,
    segment_ids,
    expert_ids,
    priority,
    cotangent,
    norm1_gain,
    qkv_weight,
    qkv_bias,
    out_weight,
    norm2_gain,
    router_weight,
    shared_gate_vector,
    shared_gate_up,
    shared_down,
    expert_gate_up,
    expert_down,
):
    width = lax.axis_size("expert")
    member = lax.axis_index("expert")
    dp_count = lax.axis_size("dp")
    rows_each, dim = block_input.shape
    rows = rows_each * width
    head_cols = qkv_weight.shape[2]
    local = expert_gate_up.shape[0]
    expert_count = local * width
    capacity = (9 * rows_each * TOP + 8 * expert_count - 1) // (8 * expert_count)
    slots_each = -(-capacity // 16) * 16
    gain_one = norm1_gain.astype(F32)
    gain_two = norm2_gain.astype(F32)

    cube = cube_of(dp_count)
    cube_bits = int(math.log2(dp_count))
    half = dp_count // 2
    colours, orders = [], []
    for first in range(2):
        bits = [1 << k for k in range(cube_bits)]
        bits = bits[first::-1] + bits[first + 1 :] if cube_bits > 1 else bits
        order = [0]
        for bit in reversed(bits):
            order = order + [p | bit for p in order]
        colours.append(bits)
        orders.append(order[half:] + order[:half])
    at_corner = {corner: index for index, corner in enumerate(cube)}
    block_table = np.array(
        [
            [[at_corner[cube[index] ^ p] for p in order] for order in orders]
            for index in range(dp_count)
        ],
        np.int32,
    )
    my_blocks = jnp.asarray(block_table)[lax.axis_index("dp")]
    block_dim = dim // dp_count

    token = []

    def then(values):
        return after(values, *token) if token else values

    def mark(*arrays):
        token[:] = arrays

    class WeightSum:
        def __init__(self, colour, values, other, dim_first):
            self.bits = colours[colour]
            self.axis = 0 if dim_first else 1
            self.size = half
            self.came = []
            several = isinstance(other, (list, tuple))
            other = [then(other[0]), *other[1:]] if several else then(other)
            self.sent, self.own = weight_product(
                my_blocks[colour], values, other, block_dim, dim_first
            )
            mark(self.own)

        def part(self, first, last):
            total = 0.0
            for array in [self.own, *self.came]:
                piece = lax.slice_in_dim(
                    array, first * block_dim, last * block_dim, axis=self.axis
                )
                total = total + piece.astype(F32)
            return total

        def start(self):
            if self.sent is not None:
                bit = self.bits[len(self.came)]
                self.came.append(swap(then(self.sent), "dp", cube, bit))
                self.sent = None

        def collect(self):
            self.came[-1] = then(self.came[-1])
            if self.size > 1:
                self.size //= 2
                self.sent = self.part(self.size, 2 * self.size).astype(BF16)
                mark(self.sent)
            else:
                mark(self.came[-1])

        def result(self):
            self.start()
            while self.size > 1:
                self.collect()
                self.start()
            return self.part(0, 1)

    sums = {}

    def moves(place):
        if cube_bits != 3 or local != 2:
            return
        for step in PLAN.get(place, "").split():
            (sums[step[:-1]].start if step[-1] == "+" else sums[step[:-1]].collect)()

    def weight_total(name, *args):
        sums[name] = WeightSum(1 if name in SECOND_FIRST else 0, *args)
        moves(name)

    table = list(range(width))
    near = width // 2
    top = near
    block_places = member ^ jnp.arange(width, dtype=jnp.int32)
    lane = (member * local)[None].astype(jnp.int32)
    listed = jnp.concatenate([segment_ids[None, :], priority, expert_ids.T], axis=0).astype(BF16)
    listed = jnp.pad(listed, ((0, 8 - listed.shape[0]), (0, 0)))
    by_row = group_gather(listed, width)
    own_input = after(block_input, listed)
    input_far = far_gather(own_input, width)
    input_blocks = near_gather({0: own_input}, 2)
    cosine, sine, meta_cols, meta, hot = prepare(
        block_places, lane, by_row, local, capacity, slots_each
    )

    slice_rows = head_cols // dp_count
    far_blocks = far_gather(
        lax.dynamic_slice_in_dim(
            after(out_weight, by_row[-1]), lax.axis_index("dp") * slice_rows, slice_rows, 0
        ),
        width,
    )

    project_args = (norm1_gain, qkv_weight, qkv_bias, cosine, sine)
    if near > 2:
        input_blocks = near_gather(input_far, width)
    projected, normed_one = project(input_blocks[:near], *project_args, 0, 2, None)
    if near == 2:
        input_blocks += near_gather({0: after(input_far[2], normed_one)}, 2)
    cot_blocks = far_gather(after(cotangent, input_blocks[near]), width)
    far_all = lax.all_gather(
        jnp.stack([after(far_blocks[p], normed_one) for p in range(2, width, 2)]),
        "dp",
        axis=1,
        tiled=True,
    )
    projected, normed_one = project(
        input_blocks[near:], *project_args, 1, 2, (projected, normed_one)
    )
    attend_args = (block_places, projected, meta_cols, meta, rows_each)
    attended_far, log_far = attend(*attend_args, near, near)
    far_pieces = far_gather(after(attended_far, cot_blocks[near]), width)
    out_blocks = near_gather({0: out_weight}, 2)
    attended_near, log_near = attend(
        after(block_places, attended_far, cot_blocks[near], out_blocks[1]), *attend_args[1:], 0, near
    )
    far_pieces = near_gather(
        {p: after(block, attended_near) if p else block for p, block in far_pieces.items()}, width
    )
    far_all = after(far_all, attended_near)
    for place in range(2, width, 2):
        out_blocks += near_gather({0: far_all[place // 2 - 1]}, 2)
    near_far = far_gather(attended_near, width)
    near_pieces = near_gather({0: attended_near}, 2)

    side_weight = jnp.concatenate(
        [
            router_weight,
            shared_gate_vector[:, None],
            jnp.zeros((dim, LANES - expert_count - 1), BF16),
        ],
        axis=1,
    )
    if near > 2:
        near_pieces = near_gather(near_far, width)
    normed, side, hidden_own = out_project(
        input_blocks[:near], near_pieces[:near] + far_pieces[near:], out_blocks, norm2_gain,
        side_weight, 0, None,
    )
    if near == 2:
        near_pieces += near_gather({0: after(near_far[2], side)}, 2)
    normed, side, _ = out_project(
        input_blocks[near:], far_pieces[:near] + near_pieces[near:], out_blocks, norm2_gain,
        side_weight, 1, (normed, side),
    )
    mark(side)
    cot_blocks = near_gather({p: then(block) if p else block for p, block in cot_blocks.items()}, width)

    act, gate_grad, up_grad, out_grad = shared_inner(
        normed, side, cot_blocks, shared_gate_up, shared_down, expert_count
    )
    mark(act)
    weight_total("Sg", normed, gate_grad, True)
    weight_total("Su", normed, up_grad, True)
    weight_total("Sd", out_grad, act, False)
    acts, grads, expert_rows = [], [], []

    def expert_product(e, k):
        act_e, gate_e, up_e = acts[e], grads[2 * e], grads[2 * e + 1]
        rows_e, grad_e = expert_rows[e]
        args = ((rows_e, gate_e, True), (rows_e, up_e, True), (grad_e, act_e, False))[k]
        weight_total(f"{e}{'gud'[k]}", *args)

    for e in range(local):
        e_act, e_gate, e_up, *e_rows = expert_inner(
            lane, then(normed), side, hot, cot_blocks, expert_gate_up, expert_down, e, expert_count
        )
        mark(e_act)
        acts.append(e_act)
        grads += [e_gate, e_up]
        expert_rows.append(e_rows)
        moves(f"E{e}")
        if e == 0:
            for k in range(3):
                expert_product(0, k)

    *mixed_parts, totals = mix(
        lane, side, then(act), shared_down, hot, acts, expert_down, cot_blocks, expert_count
    )
    mark(totals)
    moves("mix")
    *grad_parts, side_sum = back(
        side, totals, then(gate_grad), up_grad, shared_gate_up, hot, grads, expert_gate_up,
        normed, side_weight, width, expert_count,
    )
    mark(side_sum)
    moves("back")

    def rest(k):
        for e in range(1, local):
            expert_product(e, k)

    steps = group_steps(grad_parts, then)
    next(steps)
    rest(0)
    for _ in range(int(math.log2(width)) - 1):
        parts = next(steps)
    moves("n1")
    rest(1)
    normed_grad = sum(value.astype(F32) for value in [*parts[:-1], then(parts[-1])])
    inv_two_own = rms_scale(hidden_own)
    hat_two = hidden_own * inv_two_own
    scaled_two = normed_grad * gain_two
    hidden_grad = cotangent.astype(F32) + inv_two_own * (
        scaled_two - hat_two * jnp.mean(scaled_two * hat_two, axis=-1, keepdims=True)
    )
    gain_two_grad = jnp.sum(normed_grad * hat_two, axis=0)
    hidden_low = hidden_grad.astype(BF16)
    hidden_far = far_gather(hidden_low, width)
    hidden_blocks = near_gather({0: hidden_low}, 2)
    mark(hidden_low)
    moves("norm")
    rest(2)
    hidden_far = {p: then(block) for p, block in hidden_far.items() if p}
    hidden_blocks += near_gather({p - 2: block for p, block in hidden_far.items()}, width - 2)
    moves("h")

    attended_grad = attended_gradient(then(out_weight), hidden_blocks)
    mark(attended_grad)
    moves("ag")
    *projected_grad, bias_parts = attend_back(
        block_places, projected, then(attended_grad), log_near, log_far, meta_cols, meta, cosine,
        sine, rows_each,
    )
    mark(bias_parts)
    moves("ab")
    for j, name in enumerate("qkv"):
        weight_total(name, normed_one, projected_grad[j], True)
    weight_total("o", hidden_blocks, [attended_near, attended_far], False)
    inv_one_all = jnp.concatenate(
        [rms_scale(block.astype(F32)) for block in input_blocks], axis=0
    )
    *first_parts, gain_one_parts = first_back(
        [then(projected_grad[0]), *projected_grad[1:]], qkv_weight, input_blocks, inv_one_all
    )
    mark(gain_one_parts)
    bias_full = lax.dynamic_update_slice_in_dim(
        jnp.zeros((3, dim), F32), jnp.sum(bias_parts, axis=1), member * head_cols, 1
    )
    small_sums = lax.psum(
        jnp.concatenate(
            [
                gain_two_grad[None, :],
                side_sum[: expert_count + 1],
                jnp.sum(gain_one_parts, axis=0)[None, :],
                bias_full,
            ],
            axis=0,
        ),
        ("dp", "expert"),
    )
    moves("fb")
    normed_one_grad = group_sum(first_parts)
    mixed_out = (hidden_own + group_sum(mixed_parts, then)).astype(BF16)
    inv_one = inv_one_all[:rows_each]
    hat_one = block_input.astype(F32) * inv_one
    scaled_one = normed_one_grad * gain_one
    input_grad = (
        hidden_grad
        + inv_one * (scaled_one - hat_one * jnp.mean(scaled_one * hat_one, axis=-1, keepdims=True))
    ).astype(BF16)
    moves("fin")
    small_sums = then(small_sums)

    expert_totals = [
        [sums[f"{e}{side}"].result() for side in "gud"] for e in range(local)
    ]
    return (
        mixed_out,
        input_grad,
        small_sums[expert_count + 2],
        jnp.stack([sums[name].result() for name in "qkv"]),
        small_sums[expert_count + 3 :],
        sums["o"].result(),
        small_sums[0],
        small_sums[1 : 1 + expert_count].T,
        small_sums[1 + expert_count],
        jnp.stack([sums["Sg"].result(), sums["Su"].result()]),
        sums["Sd"].result(),
        jnp.stack([jnp.stack(totals[:2]) for totals in expert_totals]),
        jnp.stack([totals[2] for totals in expert_totals]),
    )


def solution(mesh):
    return jax.shard_map(
        per_device,
        mesh=mesh,
        in_specs=(
            P(("dp", "expert"), None),
            P(("dp", "expert")),
            P(("dp", "expert"), None),
            P(("dp", "expert"), None),
            P(("dp", "expert"), None),
            P(),
            P(None, None, "expert"),
            P(None, "expert"),
            P("expert", None),
            P(),
            P(),
            P(),
            P(None, None, "expert"),
            P("expert", None),
            P("expert", None, None, None),
            P("expert", None, None),
        ),
        out_specs=(
            P(("dp", "expert"), None),
            P(("dp", "expert"), None),
            P(),
            P(None, "dp", "expert"),
            P(),
            P("expert", "dp"),
            P(),
            P(),
            P(),
            P(None, "dp", "expert"),
            P("expert", "dp"),
            P("expert", None, "dp", None),
            P("expert", None, "dp"),
        ),
        check_vma=False,
    )
```

time: 1310 us -> 1020 us (0.78)
  Pallas kernels: 0 us -> 407 us
  matrix products: 404 us -> 0 us
  other arithmetic: 182 us -> 82.7 us
  local copies, waits for them, and re-layouts: 109 us -> 21.6 us
  waiting for transfers between devices: 465 us -> 382 us
  starting transfers between devices: 120 us -> 100 us
    pallas_call x0 -> x28, Pallas kernels: none -> 407 us  [kernel_call(): pl.pallas_call(body, name=name, grid_spec=pltpu.PrefetchScalarGridSpec(nu...]
    dot_general x76 -> x0, matrix products: 404 us -> none  [the longest x14 127 us: dot(): return jnp.dot(left, right, preferred_element_type=F32)]
    ppermute x76 -> x69, waiting for transfers between devices: 465 us -> 382 us  [swap(): return lax.ppermute(values, axis, pairs)]
    convert_element_type x44 -> x31, other arithmetic: 88.8 us -> 44.7 us  [the longest x26 36.3 us: collect(): self.sent = self.part(self.size, 2 * self.size).astype(BF16)]
    dynamic_slice x16 -> x2, local copies, waits for them, and re-layouts: 24.1 us -> 1.65 us  [the longest x1 0.97 us: per_device(): lax.dynamic_slice_in_dim(after(out_weight, by_row[-1]), lax.axis_index('d...]
    unnamed x526 -> x133, local copies, waits for them, and re-layouts: 28.3 us -> 6.82 us
    ppermute x76 -> x69, starting transfers between devices: 120 us -> 100 us  [swap(): return lax.ppermute(values, axis, pairs)]
    another operation x24 -> x14, other arithmetic: 34.9 us -> 18.8 us  [the longest x2 4.19 us: per_device(): jnp.stack(totals[:2])]
  transfers between devices with their start and end apart: 76 -> 71, of which waited for: 25 -> 27; matrix products, arithmetic and copies ran while one was open for 41% -> 9% of each run, Pallas kernels for 0% -> 36%
where the time goes in v2:
time: 1020 us; the launch traced here: 1010 us
  Pallas kernels  407 us (40%)
  waiting for transfers between devices  382 us (37%)
  starting transfers between devices  100 us (10%)
  other arithmetic  82.7 us (8%)
  local copies, waits for them, and re-layouts  21.6 us (2%)
  between operations  15.5 us (2%)
    pallas_call x28, Pallas kernels, kernel_call(): pl.pallas_call(body, name=name, grid_spec=pltpu.PrefetchScalarGridSpec(nu...  407 us
    ppermute x69, waiting for transfers between devices, swap(): return lax.ppermute(values, axis, pairs)  382 us
    ppermute x69, starting transfers between devices, swap(): return lax.ppermute(values, axis, pairs)  100 us
    convert_element_type x26, other arithmetic, collect(): self.sent = self.part(self.size, 2 * self.size).astype(BF16)  36.3 us
  transfers between devices with their start and end apart: 71, of which 27 were waited for; matrix products, arithmetic and copies ran while one was open for 9% of the time, Pallas kernels for 36%

profile of v2, /device:TPU:8, one launch (start us, length us, event | category | flops | bytes accessed | tf_op | source)
XLA Modules:
  0.0 1009.0 jit_solution(10758514058020547789)
XLA Ops:
  20.5 7.0 prepare.1
  28.5 9.4 project.2
  38.8 24.8 %collective-permute-done.1.refs_0_.refs_3_ = bf16[256,2048]{1,0:T(8,128)(2,1)S(1)} collective-permute-done((bf16[256,2048]{1,0:T(8,128)(2,1)S(1)}, bf16[256,2048]{1,0:T(8,128)(2,1)S(1)}, u32[]{:S(2)}, u32[]{:S(2)}) %collective-permute-start.1) | collective-permute-done | bytes 1048608 | tf_op jit(solution)/shard_map/ppermute | solution.py:113
  67.3 9.8 project.3
  77.1 9.5 attend.2
  86.6 2.6 collective-permute-done.6.refs_4_.refs_5_.refs_6_
  89.3 6.7 attend.3
  96.0 3.5 collective-permute-start.9
  99.6 12.6 %collective-permute-done.9.refs_4_ = bf16[512,512]{1,0:T(8,128)(2,1)S(1)} collective-permute-done((bf16[512,512]{1,0:T(8,128)(2,1)}, bf16[512,512]{1,0:T(8,128)(2,1)S(1)}, u32[]{:S(2)}, u32[]{:S(2)}) %collective-permute-start.9) | collective-permute-done | bytes 524320 | tf_op jit(solution)/shard_map/ppermute | solution.py:113
  116.7 12.1 %out_project.2 = (bf16[1024,2048]{1,0:T(8,128)(2,1)}, f32[1024,128]{1,0:T(8,128)}, f32[256,2048]{1,0:T(8,128)}) custom-call(bf16[256,2048]{1,0:T(8,128)(2,1)} %refs_1_, bf16[256,2048]{1,0:T(8,128)(2,1)} %copy-done.11, bf16[512,512]{1,0:T(8,128)(2,1)} %get-tuple-element.320.refs_2_.refs_4_, bf16[512,512]{1,0:T(8,128)(2,1)} %collective-permute-done.8.refs_3_, ...), custom_call_target="tpu_custom_call" | custom-call | flops 1 | bytes 1 | tf_op jit(solution)/shard_map/out_project/pallas_call | solution.py:66
  131.7 11.9 %out_project.3 = (bf16[1024,2048]{1,0:T(8,128)(2,1)}, f32[1024,128]{1,0:T(8,128)}, f32[256,2048]{1,0:T(8,128)}) custom-call(bf16[256,2048]{1,0:T(8,128)(2,1)} %copy-done.8, bf16[256,2048]{1,0:T(8,128)(2,1)} %copy-done.9, bf16[512,512]{1,0:T(8,128)(2,1)} %get-tuple-element.220.refs_2_.refs_5_, ...), custom_call_target="tpu_custom_call", output_to_operand_aliasing={{0}: (12, {}), {1}: (13, {})} | custom-call | flops 1 | bytes 1 | tf_op jit(solution)/shard_map/out_project/pallas_call | solution.py:66
  146.6 28.9 %shared_inner.1 = (bf16[1024,1408]{1,0:T(8,128)(2,1)}, bf16[1024,1408]{1,0:T(8,128)(2,1)}, bf16[1024,1408]{1,0:T(8,128)(2,1)}, bf16[1024,2048]{1,0:T(8,128)(2,1)}) custom-call(bf16[1024,2048]{1,0:T(8,128)(2,1)} %get-tuple-element.255.refs_0_.refs_6_, f32[1024,128]{1,0:T(8,128)} %get-tuple-element.229.refs_1_.side, bf16[256,2048]{1,0:T(8,128)(2,1)} %refs_4_.1, ...), custom_call_target="tpu_custom_call" | custom-call | flops 1 | bytes 1 | tf_op jit(solution)/shard_map/shared_inner/pallas_call | solution.py:66
  175.4 13.2 %weight_product.13 = (bf16[1024,1408]{1,0:T(8,128)(2,1)}, bf16[1024,1408]{1,0:T(8,128)(2,1)}) custom-call(s32[8]{0:T(128)} %get-tuple-element.403.blocks, bf16[1024,2048]{1,0:T(8,128)(2,1)} %get-tuple-element.255.refs_0_.refs_6_, bf16[1024,1408]{1,0:T(8,128)(2,1)} %get-tuple-element.266.refs_1_.gate_grad), custom_call_target="tpu_custom_call" | custom-call | flops 1 | bytes 1 | tf_op jit(solution)/shard_map/weight_product/pallas_call | solution.py:66
  190.2 13.3 %weight_product.14 = (bf16[1024,1408]{1,0:T(8,128)(2,1)}, bf16[1024,1408]{1,0:T(8,128)(2,1)}) custom-call(s32[8]{0:T(128)} %get-tuple-element.404.blocks, bf16[1024,2048]{1,0:T(8,128)(2,1)} %get-tuple-element.255.refs_0_.refs_6_, bf16[1024,1408]{1,0:T(8,128)(2,1)} %get-tuple-element.238.refs_1_.up_grad), custom_call_target="tpu_custom_call" | custom-call | flops 1 | bytes 1 | tf_op jit(solution)/shard_map/weight_product/pallas_call | solution.py:66
  203.9 13.1 %weight_product.15 = (bf16[1408,1024]{1,0:T(8,128)(2,1)}, bf16[1408,1024]{1,0:T(8,128)(2,1)}) custom-call(s32[8]{0:T(128)} %get-tuple-element.403.blocks, bf16[1024,2048]{1,0:T(8,128)(2,1)} %get-tuple-element.233.refs_0_, bf16[1024,1408]{1,0:T(8,128)(2,1)} %get-tuple-element.257.refs_1_.act), custom_call_target="tpu_custom_call" | custom-call | flops 1 | bytes 1 | tf_op jit(solution)/shard_map/weight_product/pallas_call | solution.py:66
  217.3 21.4 %expert_inner.2 = (bf16[576,1408]{1,0:T(8,128)(2,1)}, bf16[576,1408]{1,0:T(8,128)(2,1)}, bf16[576,1408]{1,0:T(8,128)(2,1)}, bf16[576,2048]{1,0:T(8,128)(2,1)}, bf16[576,2048]{1,0:T(8,128)(2,1)}) custom-call(s32[1]{0:T(128)} %bitcast.2.first, bf16[1024,2048]{1,0:T(8,128)(2,1)} %get-tuple-element.255.refs_0_.refs_6_, ...), custom_call_target="tpu_custom_call" | custom-call | flops 1 | bytes 1 | tf_op jit(solution)/shard_map/expert_inner/pallas_call | solution.py:66
  238.7 11.5 %weight_product.16 = (bf16[1024,1408]{1,0:T(8,128)(2,1)}, bf16[1024,1408]{1,0:T(8,128)(2,1)}) custom-call(s32[8]{0:T(128)} %get-tuple-element.404.blocks, bf16[576,2048]{1,0:T(8,128)(2,1)} %get-tuple-element.246.refs_0_, bf16[576,1408]{1,0:T(8,128)(2,1)} %get-tuple-element.249.refs_1_.refs_0_), custom_call_target="tpu_custom_call" | custom-call | flops 1 | bytes 1 | tf_op jit(solution)/shard_map/weight_product/pallas_call | solution.py:66
  252.0 11.4 %weight_product.17 = (bf16[1024,1408]{1,0:T(8,128)(2,1)}, bf16[1024,1408]{1,0:T(8,128)(2,1)}) custom-call(s32[8]{0:T(128)} %get-tuple-element.403.blocks, bf16[576,2048]{1,0:T(8,128)(2,1)} %get-tuple-element.246.refs_0_, bf16[576,1408]{1,0:T(8,128)(2,1)} %get-tuple-element.251.refs_1_), custom_call_target="tpu_custom_call" | custom-call | flops 1 | bytes 1 | tf_op jit(solution)/shard_map/weight_product/pallas_call | solution.py:66
  264.9 11.5 %weight_product.18 = (bf16[1408,1024]{1,0:T(8,128)(2,1)}, bf16[1408,1024]{1,0:T(8,128)(2,1)}) custom-call(s32[8]{0:T(128)} %get-tuple-element.404.blocks, bf16[576,2048]{1,0:T(8,128)(2,1)} %get-tuple-element.244.refs_0_, bf16[576,1408]{1,0:T(8,128)(2,1)} %get-tuple-element.253.refs_1_.refs_0_), custom_call_target="tpu_custom_call" | custom-call | flops 1 | bytes 1 | tf_op jit(solution)/shard_map/weight_product/pallas_call | solution.py:66
  276.4 21.3 %expert_inner.3 = (bf16[576,1408]{1,0:T(8,128)(2,1)}, bf16[576,1408]{1,0:T(8,128)(2,1)}, bf16[576,1408]{1,0:T(8,128)(2,1)}, bf16[576,2048]{1,0:T(8,128)(2,1)}, bf16[576,2048]{1,0:T(8,128)(2,1)}) custom-call(s32[1]{0:T(128)} %bitcast.2.first, bf16[1024,2048]{1,0:T(8,128)(2,1)} %get-tuple-element.255.refs_0_.refs_6_, ...), custom_call_target="tpu_custom_call" | custom-call | flops 1 | bytes 1 | tf_op jit(solution)/shard_map/expert_inner/pallas_call | solution.py:66
  297.7 36.5 %mix.1 = (bf16[256,2048]{1,0:T(8,128)(2,1)}, bf16[256,2048]{1,0:T(8,128)(2,1)}, bf16[256,2048]{1,0:T(8,128)(2,1)}, bf16[256,2048]{1,0:T(8,128)(2,1)}, f32[1024,128]{1,0:T(8,128)}) custom-call(s32[1]{0:T(128)} %bitcast.2.first, f32[1024,128]{1,0:T(8,128)} %get-tuple-element.229.refs_1_.side, bf16[1024,1408]{1,0:T(8,128)(2,1)} %get-tuple-element.257.refs_1_.act, ...), custom_call_target="tpu_custom_call" | custom-call | flops 1 | bytes 1 | tf_op jit(solution)/shard_map/mix/pallas_call | solution.py:66
  334.2 2.9 add_convert_fusion.8
  337.2 2.8 add_convert_fusion.7
  340.0 47.0 %back.1 = (bf16[256,2048]{1,0:T(8,128)(2,1)}, bf16[256,2048]{1,0:T(8,128)(2,1)}, bf16[256,2048]{1,0:T(8,128)(2,1)}, bf16[256,2048]{1,0:T(8,128)(2,1)}, f32[128,2048]{1,0:T(8,128)}) custom-call(f32[1024,128]{1,0:T(8,128)} %get-tuple-element.229.refs_1_.side, f32[1024,128]{1,0:T(8,128)} %get-tuple-element.261.totals, ...), custom_call_target="tpu_custom_call" | custom-call | flops 1 | bytes 1 | tf_op jit(solution)/shard_map/back/pallas_call | solution.py:66
  387.0 3.2 add_convert_fusion.6
  392.8 11.6 %weight_product.19 = (bf16[1024,1408]{1,0:T(8,128)(2,1)}, bf16[1024,1408]{1,0:T(8,128)(2,1)}) custom-call(s32[8]{0:T(128)} %get-tuple-element.403.blocks, bf16[576,2048]{1,0:T(8,128)(2,1)} %get-tuple-element.284.refs_0_, bf16[576,1408]{1,0:T(8,128)(2,1)} %get-tuple-element.285.refs_2_.refs_1_), custom_call_target="tpu_custom_call" | custom-call | flops 1 | bytes 1 | tf_op jit(solution)/shard_map/weight_product/pallas_call | solution.py:66
  404.4 2.9 add_convert_fusion.4
  412.7 11.6 %weight_product.20 = (bf16[1024,1408]{1,0:T(8,128)(2,1)}, bf16[1024,1408]{1,0:T(8,128)(2,1)}) custom-call(s32[8]{0:T(128)} %get-tuple-element.403.blocks, bf16[576,2048]{1,0:T(8,128)(2,1)} %get-tuple-element.284.refs_0_, bf16[576,1408]{1,0:T(8,128)(2,1)} %get-tuple-element.289.refs_3_.refs_1_), custom_call_target="tpu_custom_call" | custom-call | flops 1 | bytes 1 | tf_op jit(solution)/shard_map/weight_product/pallas_call | solution.py:66
  424.8 9.3 collective-permute-done.27
  436.6 4.5 fusion.5
  441.4 16.5 %collective-permute-done.23 = bf16[1408,1024]{1,0:T(8,128)(2,1)} collective-permute-done((bf16[1408,1024]{1,0:T(8,128)(2,1)}, bf16[1408,1024]{1,0:T(8,128)(2,1)}, u32[]{:S(2)}, u32[]{:S(2)}) %collective-permute-start.23) | collective-permute-done | bytes 2883616 | tf_op jit(solution)/shard_map/ppermute | solution.py:113
  457.9 3.1 add_convert_fusion.3
  461.0 11.4 %weight_product.21 = (bf16[1408,1024]{1,0:T(8,128)(2,1)}, bf16[1408,1024]{1,0:T(8,128)(2,1)}) custom-call(s32[8]{0:T(128)} %get-tuple-element.403.blocks, bf16[576,2048]{1,0:T(8,128)(2,1)} %get-tuple-element.274.refs_0_, bf16[576,1408]{1,0:T(8,128)(2,1)} %get-tuple-element.293.refs_1_), custom_call_target="tpu_custom_call" | custom-call | flops 1 | bytes 1 | tf_op jit(solution)/shard_map/weight_product/pallas_call | solution.py:66
  472.4 15.9 %collective-permute-done.22 = bf16[1408,512]{1,0:T(8,128)(2,1)} collective-permute-done((bf16[1408,512]{1,0:T(8,128)(2,1)S(1)}, bf16[1408,512]{1,0:T(8,128)(2,1)}, u32[]{:S(2)}, u32[]{:S(2)}) %collective-permute-start.22) | collective-permute-done | bytes 1441824 | tf_op jit(solution)/shard_map/ppermute | solution.py:113
  488.4 2.7 add_convert_fusion.22
  495.2 2.9 collective-permute-start.32
  499.4 6.2 attended_gradient.1.out_grad
  505.6 22.3 %attend_back.1 = (bf16[1024,512]{1,0:T(8,128)(2,1)}, bf16[1024,512]{1,0:T(8,128)(2,1)}, bf16[1024,512]{1,0:T(8,128)(2,1)}, f32[3,8,512]{2,1,0:T(8,128)}) custom-call(s32[4]{0:T(128)} %iota_xor_fusion.places, bf16[3,1024,512]{2,1,0:T(8,128)(2,1)} %get-tuple-element.213.query.key.value, bf16[3,1024,512]{2,1,0:T(8,128)(2,1)} %get-tuple-element.213.query.key.value, ...), custom_call_target="tpu_custom_call" | custom-call | flops 1 | bytes 1 | tf_op jit(solution)/shard_map/attend_back/pallas_call | solution.py:66
  534.5 2.7 add_convert_fusion.21
  537.1 9.0 weight_product.22
  546.1 9.0 weight_product.23
  555.1 9.0 weight_product.24
  564.1 2.7 add_convert_fusion.20
  566.8 9.3 weight_product.25
  576.1 12.6 %first_back.1 = (bf16[256,2048]{1,0:T(8,128)(2,1)}, bf16[256,2048]{1,0:T(8,128)(2,1)}, bf16[256,2048]{1,0:T(8,128)(2,1)}, bf16[256,2048]{1,0:T(8,128)(2,1)}, f32[8,2048]{1,0:T(8,128)}) custom-call(bf16[1024,512]{1,0:T(8,128)(2,1)} %get-tuple-element.322.refs_1_.query, bf16[1024,512]{1,0:T(8,128)(2,1)} %get-tuple-element.314.refs_1_.key, ...), custom_call_target="tpu_custom_call" | custom-call | flops 1 | bytes 1 | tf_op jit(solution)/shard_map/first_back/pallas_call | solution.py:66
  594.9 3.2 convert_add_fusion.1
  604.1 9.0 collective-permute-start.45
  613.7 12.4 %collective-permute-done.37 = bf16[256,2048]{1,0:T(8,128)(2,1)S(1)} collective-permute-done((bf16[256,2048]{1,0:T(8,128)(2,1)S(1)}, bf16[256,2048]{1,0:T(8,128)(2,1)S(1)}, u32[]{:S(2)}, u32[]{:S(2)}) %collective-permute-start.37) | collective-permute-done | bytes 1048608 | tf_op jit(solution)/shard_map/ppermute | solution.py:113
  628.5 19.7 %collective-permute-done.40 = bf16[256,2048]{1,0:T(8,128)(2,1)S(1)} collective-permute-done((bf16[256,2048]{1,0:T(8,128)(2,1)S(1)}, bf16[256,2048]{1,0:T(8,128)(2,1)S(1)}, u32[]{:S(2)}, u32[]{:S(2)}) %collective-permute-start.40) | collective-permute-done | bytes 1048608 | tf_op jit(solution)/shard_map/ppermute | solution.py:113
  648.2 8.4 collective-permute-start.43
  660.1 12.3 %collective-permute-done.43 = bf16[1408,256]{1,0:T(8,128)(2,1)S(1)} collective-permute-done((bf16[1408,256]{1,0:T(8,128)(2,1)S(1)}, bf16[1408,256]{1,0:T(8,128)(2,1)S(1)}, u32[]{:S(2)}, u32[]{:S(2)}) %collective-permute-start.43) | collective-permute-done | bytes 720928 | tf_op jit(solution)/shard_map/ppermute | solution.py:113
  675.0 5.4 collective-permute-done.51
  684.4 20.4 %collective-permute-done.49 = bf16[256,1408]{1,0:T(8,128)(2,1)S(1)} collective-permute-done((bf16[256,1408]{1,0:T(8,128)(2,1)S(1)}, bf16[256,1408]{1,0:T(8,128)(2,1)S(1)}, u32[]{:S(2)}, u32[]{:S(2)}) %collective-permute-start.49) | collective-permute-done | bytes 720928 | tf_op jit(solution)/shard_map/ppermute | solution.py:113
  707.4 19.9 %collective-permute-start.47 = (bf16[512,512]{1,0:T(8,128)(2,1)S(1)}, bf16[512,512]{1,0:T(8,128)(2,1)S(1)}, u32[]{:S(2)}, u32[]{:S(2)}) collective-permute-start(bf16[512,512]{1,0:T(8,128)(2,1)S(1)} %add_convert_fusion.26), channel_id=1, source_target_pairs={{0,8},{4,12},{8,0},{12,4},{16,24},{20,28},{24,16},{28,20},{1,9},{5... | collective-permute-start | bytes 1572872 | tf_op jit(solution)/shard_map/ppermute | solution.py:113
  727.3 12.3 %collective-permute-start.55 = (bf16[512,512]{1,0:T(8,128)(2,1)S(1)}, bf16[512,512]{1,0:T(8,128)(2,1)S(1)}, u32[]{:S(2)}, u32[]{:S(2)}) collective-permute-start(bf16[512,512]{1,0:T(8,128)(2,1)S(1)} %add_convert_fusion.25), channel_id=1, source_target_pairs={{0,8},{4,12},{8,0},{12,4},{16,24},{20,28},{24,16},{28,20},{1,9},{5... | collective-permute-start | bytes 1572872 | tf_op jit(solution)/shard_map/ppermute | solution.py:113
  739.6 2.9 collective-permute-start.56
  746.1 71.2 %collective-permute-done.56 = bf16[256,1408]{1,0:T(8,128)(2,1)S(1)} collective-permute-done((bf16[256,1408]{1,0:T(8,128)(2,1)S(1)}, bf16[256,1408]{1,0:T(8,128)(2,1)S(1)}, u32[]{:S(2)}, u32[]{:S(2)}) %collective-permute-start.56) | collective-permute-done | bytes 720928 | tf_op jit(solution)/shard_map/ppermute | solution.py:113
  824.2 14.2 %collective-permute-done.53 = bf16[256,1408]{1,0:T(8,128)(2,1)S(1)} collective-permute-done((bf16[256,1408]{1,0:T(8,128)(2,1)S(1)}, bf16[256,1408]{1,0:T(8,128)(2,1)S(1)}, u32[]{:S(2)}, u32[]{:S(2)}) %collective-permute-start.53) | collective-permute-done | bytes 720928 | tf_op jit(solution)/shard_map/ppermute | solution.py:113
  841.5 14.1 %collective-permute-done.61 = bf16[256,1408]{1,0:T(8,128)(2,1)S(1)} collective-permute-done((bf16[256,1408]{1,0:T(8,128)(2,1)S(1)}, bf16[256,1408]{1,0:T(8,128)(2,1)S(1)}, u32[]{:S(2)}, u32[]{:S(2)}) %collective-permute-start.61) | collective-permute-done | bytes 720928 | tf_op jit(solution)/shard_map/ppermute | solution.py:113
  860.8 9.3 collective-permute-done.58
  870.6 38.6 %collective-permute-done.57 = bf16[1024,512]{1,0:T(8,128)(2,1)S(1)} collective-permute-done((bf16[1024,512]{1,0:T(8,128)(2,1)S(1)}, bf16[1024,512]{1,0:T(8,128)(2,1)S(1)}, u32[]{:S(2)}, u32[]{:S(2)}) %collective-permute-start.57) | collective-permute-done | bytes 1048608 | tf_op jit(solution)/shard_map/ppermute | solution.py:113
  913.7 57.3 %collective-permute-done.63 = bf16[1408,256]{1,0:T(8,128)(2,1)S(1)} collective-permute-done((bf16[1408,256]{1,0:T(8,128)(2,1)S(1)}, bf16[1408,256]{1,0:T(8,128)(2,1)S(1)}, u32[]{:S(2)}, u32[]{:S(2)}) %collective-permute-start.63) | collective-permute-done | bytes 720928 | tf_op jit(solution)/shard_map/ppermute | solution.py:113
  973.4 11.4 %collective-permute-done.68 = bf16[256,1408]{1,0:T(8,128)(2,1)S(1)} collective-permute-done((bf16[256,1408]{1,0:T(8,128)(2,1)S(1)}, bf16[256,1408]{1,0:T(8,128)(2,1)S(1)}, u32[]{:S(2)}, u32[]{:S(2)}) %collective-permute-start.68) | collective-permute-done | bytes 720928 | tf_op jit(solution)/shard_map/ppermute | solution.py:113
  990.8 2.9 pad_maximum_fusion
  (330 shorter events, 125.7 us)
Async XLA Ops:
  7.2 88.8 %all-gather.3.cloned.1.call-start = ((), (), s32[]{:S(2)}) async-start(), calls=%async_computation.1 | async-start | bytes 2359296 | tf_op jit(solution)/shard_map/all_gather | solution.py:1195
  9.3 18.2 %collective-permute-start = (bf16[256,2048]{1,0:T(8,128)(2,1)}, bf16[256,2048]{1,0:T(8,128)(2,1)S(1)}, u32[]{:S(2)}, u32[]{:S(2)}) collective-permute-start(bf16[256,2048]{1,0:T(8,128)(2,1)} %refs_1_), channel_id=1, source_target_pairs={{0,1},{1,0},{2,3},{3,2},{4,5},{5,4},{6,7},{7,6},{8,9},{9,8},{10,11... | collective-permute-start | bytes 3145736 | tf_op jit(solution)/shard_map/ppermute | solution.py:113
  15.2 22.7 %collective-permute-start.11 = (bf16[64,2048]{1,0:T(8,128)(2,1)S(1)}, bf16[64,2048]{1,0:T(8,128)(2,1)}, u32[]{:S(2)}, u32[]{:S(2)}) collective-permute-start(bf16[64,2048]{1,0:T(8,128)(2,1)S(1)} %constant_dynamic-slice_fusion.1), channel_id=1, source_target_pairs={{0,2},{1,3},{2,0},{3,1},{4,6},{5,7},{6,4},{7,5},{8,10},{9,11},{10,... | collective-permute-start | bytes 786440 | tf_op jit(solution)/shard_map/ppermute | solution.py:113
  38.0 957.9 %all-reduce.3.cloned.1.call-start = ((), (), s32[]{:S(2)}) async-start(), calls=%async_computation | async-start | bytes 262144 | tf_op jit(solution)/shard_map/psum | solution.py:1334
  38.0 25.6 %collective-permute-start.1 = (bf16[256,2048]{1,0:T(8,128)(2,1)S(1)}, bf16[256,2048]{1,0:T(8,128)(2,1)S(1)}, u32[]{:S(2)}, u32[]{:S(2)}) collective-permute-start(bf16[256,2048]{1,0:T(8,128)(2,1)S(1)} %copy-done), channel_id=1, source_target_pairs={{0,2},{1,3},{2,0},{3,1},{4,6},{5,7},{6,4},{7,5},{8,10},{9,11},{10,... | collective-permute-start | bytes 3145736 | tf_op jit(solution)/shard_map/ppermute | solution.py:113
  38.6 48.0 %collective-permute-start.7 = (bf16[512,2048]{1,0:T(8,128)(2,1)}, bf16[512,2048]{1,0:T(8,128)(2,1)S(1)}, u32[]{:S(2)}, u32[]{:S(2)}) collective-permute-start(bf16[512,2048]{1,0:T(8,128)(2,1)} %weight), channel_id=1, source_target_pairs={{0,1},{1,0},{2,3},{3,2},{4,5},{5,4},{6,7},{7,6},{8,9},{9,8},{10,11... | collective-permute-start | bytes 6291464 | tf_op jit(solution)/shard_map/ppermute | solution.py:113
  63.7 25.6 %collective-permute-start.6 = (bf16[256,2048]{1,0:T(8,128)(2,1)S(1)}, bf16[256,2048]{1,0:T(8,128)(2,1)S(1)}, u32[]{:S(2)}, u32[]{:S(2)}) collective-permute-start(bf16[256,2048]{1,0:T(8,128)(2,1)S(1)} %copy-done.4), channel_id=1, source_target_pairs={{0,2},{1,3},{2,0},{3,1},{4,6},{5,7},{6,4},{7,5},{8,10},{9,11},{10,... | collective-permute-start | bytes 3145736 | tf_op jit(solution)/shard_map/ppermute | solution.py:113
  95.9 20.7 %collective-permute-start.12 = (bf16[512,2048]{1,0:T(8,128)(2,1)}, bf16[512,2048]{1,0:T(8,128)(2,1)}, u32[]{:S(2)}, u32[]{:S(2)}) collective-permute-start(bf16[512,2048]{1,0:T(8,128)(2,1)} %all-gather.3.cloned.1.call-done), channel_id=1, source_target_pairs={{0,1},{1,0},{2,3},{3,2},{4,5},{5,4},{6,7},{7,6},{8,9},{9,8},{10,11... | collective-permute-start | bytes 6291464 | tf_op jit(solution)/shard_map/ppermute | solution.py:113
  96.0 16.3 %collective-permute-start.9 = (bf16[512,512]{1,0:T(8,128)(2,1)}, bf16[512,512]{1,0:T(8,128)(2,1)S(1)}, u32[]{:S(2)}, u32[]{:S(2)}) collective-permute-start(bf16[512,512]{1,0:T(8,128)(2,1)} %get-tuple-element.220.refs_2_.refs_5_), channel_id=1, source_target_pairs={{0,2},{1,3},{2,0},{3,1},{4,6},{5,7},{6,4},{7,5},{8,10},{9,11},{10,... | collective-permute-start | bytes 1572872 | tf_op jit(solution)/shard_map/ppermute | solution.py:113
  99.5 17.2 %collective-permute-start.8 = (bf16[512,512]{1,0:T(8,128)(2,1)}, bf16[512,512]{1,0:T(8,128)(2,1)}, u32[]{:S(2)}, u32[]{:S(2)}) collective-permute-start(bf16[512,512]{1,0:T(8,128)(2,1)} %get-tuple-element.320.refs_2_.refs_4_), channel_id=1, source_target_pairs={{0,1},{1,0},{2,3},{3,2},{4,5},{5,4},{6,7},{7,6},{8,9},{9,8},{10,11... | collective-permute-start | bytes 1572872 | tf_op jit(solution)/shard_map/ppermute | solution.py:113
  112.2 16.5 %collective-permute-start.14 = (bf16[512,512]{1,0:T(8,128)(2,1)}, bf16[512,512]{1,0:T(8,128)(2,1)}, u32[]{:S(2)}, u32[]{:S(2)}) collective-permute-start(bf16[512,512]{1,0:T(8,128)(2,1)} %get-tuple-element.320.refs_2_.refs_4_), channel_id=1, source_target_pairs={{0,2},{1,3},{2,0},{3,1},{4,6},{5,7},{6,4},{7,5},{8,10},{9,11},{10,... | collective-permute-start | bytes 1572872 | tf_op jit(solution)/shard_map/ppermute | solution.py:113
  116.4 12.9 %collective-permute-start.13 = (bf16[512,512]{1,0:T(8,128)(2,1)}, bf16[512,512]{1,0:T(8,128)(2,1)S(1)}, u32[]{:S(2)}, u32[]{:S(2)}) collective-permute-start(bf16[512,512]{1,0:T(8,128)(2,1)} %get-tuple-element.220.refs_2_.refs_5_), channel_id=1, source_target_pairs={{0,1},{1,0},{2,3},{3,2},{4,5},{5,4},{6,7},{7,6},{8,9},{9,8},{10,11... | collective-permute-start | bytes 1572872 | tf_op jit(solution)/shard_map/ppermute | solution.py:113
  129.1 16.1 %collective-permute-start.16 = (bf16[256,2048]{1,0:T(8,128)(2,1)S(1)}, bf16[256,2048]{1,0:T(8,128)(2,1)S(1)}, u32[]{:S(2)}, u32[]{:S(2)}) collective-permute-start(bf16[256,2048]{1,0:T(8,128)(2,1)S(1)} %copy-done.4), channel_id=1, source_target_pairs={{0,1},{1,0},{2,3},{3,2},{4,5},{5,4},{6,7},{7,6},{8,9},{9,8},{10,11... | collective-permute-start | bytes 3145736 | tf_op jit(solution)/shard_map/ppermute | solution.py:113
  188.7 145.5 %collective-permute-start.20 = (bf16[1024,1408]{1,0:T(8,128)(2,1)}, bf16[1024,1408]{1,0:T(8,128)(2,1)}, u32[]{:S(2)}, u32[]{:S(2)}) collective-permute-start(bf16[1024,1408]{1,0:T(8,128)(2,1)} %get-tuple-element.263), channel_id=1, source_target_pairs={{0,4},{4,0},{8,12},{12,8},{16,20},{20,16},{24,28},{28,24},{1,5},{5... | collective-permute-start | bytes 8650760 | tf_op jit(solution)/shard_map/ppermute | solution.py:113
  203.5 133.7 %collective-permute-start.19 = (bf16[1024,1408]{1,0:T(8,128)(2,1)}, bf16[1024,1408]{1,0:T(8,128)(2,1)}, u32[]{:S(2)}, u32[]{:S(2)}) collective-permute-start(bf16[1024,1408]{1,0:T(8,128)(2,1)} %get-tuple-element.262), channel_id=1, source_target_pairs={{0,8},{4,12},{8,0},{12,4},{16,24},{20,28},{24,16},{28,20},{1,9},{5... | collective-permute-start | bytes 8650760 | tf_op jit(solution)/shard_map/ppermute | solution.py:113
  217.0 170.0 %collective-permute-start.18 = (bf16[1408,1024]{1,0:T(8,128)(2,1)}, bf16[1408,1024]{1,0:T(8,128)(2,1)}, u32[]{:S(2)}, u32[]{:S(2)}) collective-permute-start(bf16[1408,1024]{1,0:T(8,128)(2,1)} %get-tuple-element.260), channel_id=1, source_target_pairs={{0,4},{4,0},{8,12},{12,8},{16,20},{20,16},{24,28},{28,24},{1,5},{5... | collective-permute-start | bytes 8650760 | tf_op jit(solution)/shard_map/ppermute | solution.py:113
  250.2 140.0 %collective-permute-start.21 = (bf16[1024,1408]{1,0:T(8,128)(2,1)}, bf16[1024,1408]{1,0:T(8,128)(2,1)S(1)}, u32[]{:S(2)}, u32[]{:S(2)}) collective-permute-start(bf16[1024,1408]{1,0:T(8,128)(2,1)} %get-tuple-element.271), channel_id=1, source_target_pairs={{0,8},{4,12},{8,0},{12,4},{16,24},{20,28},{24,16},{28,20},{1,9},{5... | collective-permute-start | bytes 8650760 | tf_op jit(solution)/shard_map/ppermute | solution.py:113
  263.4 140.9 %collective-permute-start.26 = (bf16[1024,1408]{1,0:T(8,128)(2,1)}, bf16[1024,1408]{1,0:T(8,128)(2,1)}, u32[]{:S(2)}, u32[]{:S(2)}) collective-permute-start(bf16[1024,1408]{1,0:T(8,128)(2,1)} %get-tuple-element.283), channel_id=1, source_target_pairs={{0,4},{4,0},{8,12},{12,8},{16,20},{20,16},{24,28},{28,24},{1,5},{5... | collective-permute-start | bytes 8650760 | tf_op jit(solution)/shard_map/ppermute | solution.py:113
  392.2 15.0 %collective-permute-start.25 = (bf16[256,2048]{1,0:T(8,128)(2,1)S(1)}, bf16[256,2048]{1,0:T(8,128)(2,1)S(1)}, u32[]{:S(2)}, u32[]{:S(2)}) collective-permute-start(bf16[256,2048]{1,0:T(8,128)(2,1)S(1)} %copy-done.65), channel_id=1, source_target_pairs={{0,1},{1,0},{2,3},{3,2},{4,5},{5,4},{6,7},{7,6},{8,9},{9,8},{10,11... | collective-permute-start | bytes 3145736 | tf_op jit(solution)/shard_map/ppermute | solution.py:113
  392.2 65.7 %collective-permute-start.23 = (bf16[1408,1024]{1,0:T(8,128)(2,1)}, bf16[1408,1024]{1,0:T(8,128)(2,1)}, u32[]{:S(2)}, u32[]{:S(2)}) collective-permute-start(bf16[1408,1024]{1,0:T(8,128)(2,1)} %get-tuple-element.276), channel_id=1, source_target_pairs={{0,8},{4,12},{8,0},{12,4},{16,24},{20,28},{24,16},{28,20},{1,9},{5... | collective-permute-start | bytes 8650760 | tf_op jit(solution)/shard_map/ppermute | solution.py:113
  408.7 25.4 %collective-permute-start.27 = (bf16[256,2048]{1,0:T(8,128)(2,1)}, bf16[256,2048]{1,0:T(8,128)(2,1)}, u32[]{:S(2)}, u32[]{:S(2)}) collective-permute-start(bf16[256,2048]{1,0:T(8,128)(2,1)} %add_convert_fusion.13), channel_id=1, source_target_pairs={{0,2},{1,3},{2,0},{3,1},{4,6},{5,7},{6,4},{7,5},{8,10},{9,11},{10,... | collective-permute-start | bytes 3145736 | tf_op jit(solution)/shard_map/ppermute | solution.py:113
  409.0 25.1 %collective-permute-start.24 = (bf16[256,2048]{1,0:T(8,128)(2,1)}, bf16[256,2048]{1,0:T(8,128)(2,1)}, u32[]{:S(2)}, u32[]{:S(2)}) collective-permute-start(bf16[256,2048]{1,0:T(8,128)(2,1)} %get-tuple-element.279), channel_id=1, source_target_pairs={{0,1},{1,0},{2,3},{3,2},{4,5},{5,4},{6,7},{7,6},{8,9},{9,8},{10,11... | collective-permute-start | bytes 3145736 | tf_op jit(solution)/shard_map/ppermute | solution.py:113
  411.2 77.2 %collective-permute-start.22 = (bf16[1408,512]{1,0:T(8,128)(2,1)S(1)}, bf16[1408,512]{1,0:T(8,128)(2,1)}, u32[]{:S(2)}, u32[]{:S(2)}) collective-permute-start(bf16[1408,512]{1,0:T(8,128)(2,1)S(1)} %copy-done.34), channel_id=1, source_target_pairs={{0,8},{4,12},{8,0},{12,4},{16,24},{20,28},{24,16},{28,20},{1,9},{5... | collective-permute-start | bytes 4325384 | tf_op jit(solution)/shard_map/ppermute | solution.py:113
  424.3 103.6 %collective-permute-start.34 = (bf16[1024,1408]{1,0:T(8,128)(2,1)}, bf16[1024,1408]{1,0:T(8,128)(2,1)}, u32[]{:S(2)}, u32[]{:S(2)}) collective-permute-start(bf16[1024,1408]{1,0:T(8,128)(2,1)} %get-tuple-element.308), channel_id=1, source_target_pairs={{0,4},{4,0},{8,12},{12,8},{16,20},{20,16},{24,28},{28,24},{1,5},{5... | collective-permute-start | bytes 8650760 | tf_op jit(solution)/shard_map/ppermute | solution.py:113
  441.2 49.9 %collective-permute-start.29 = (bf16[256,2048]{1,0:T(8,128)(2,1)}, bf16[256,2048]{1,0:T(8,128)(2,1)S(1)}, u32[]{:S(2)}, u32[]{:S(2)}) collective-permute-start(bf16[256,2048]{1,0:T(8,128)(2,1)} %get-tuple-element.398.refs_0_), channel_id=1, source_target_pairs={{0,2},{1,3},{2,0},{3,1},{4,6},{5,7},{6,4},{7,5},{8,10},{9,11},{10,... | collective-permute-start | bytes 3145736 | tf_op jit(solution)/shard_map/ppermute | solution.py:113
  441.4 53.7 %collective-permute-start.28 = (bf16[256,2048]{1,0:T(8,128)(2,1)}, bf16[256,2048]{1,0:T(8,128)(2,1)}, u32[]{:S(2)}, u32[]{:S(2)}) collective-permute-start(bf16[256,2048]{1,0:T(8,128)(2,1)} %get-tuple-element.398.refs_0_), channel_id=1, source_target_pairs={{0,1},{1,0},{2,3},{3,2},{4,5},{5,4},{6,7},{7,6},{8,9},{9,8},{10,11... | collective-permute-start | bytes 3145736 | tf_op jit(solution)/shard_map/ppermute | solution.py:113
  491.0 7.0 collective-permute-start.30
  491.4 43.1 %collective-permute-start.33 = (bf16[512,1408]{1,0:T(8,128)(2,1)}, bf16[512,1408]{1,0:T(8,128)(2,1)}, u32[]{:S(2)}, u32[]{:S(2)}) collective-permute-start(bf16[512,1408]{1,0:T(8,128)(2,1)} %add_convert_fusion.8), channel_id=1, source_target_pairs={{0,8},{4,12},{8,0},{12,4},{16,24},{20,28},{24,16},{28,20},{1,9},{5... | collective-permute-start | bytes 4325384 | tf_op jit(solution)/shard_map/ppermute | solution.py:113
  492.2 71.9 %collective-permute-start.31 = (bf16[1408,512]{1,0:T(8,128)(2,1)}, bf16[1408,512]{1,0:T(8,128)(2,1)}, u32[]{:S(2)}, u32[]{:S(2)}) collective-permute-start(bf16[1408,512]{1,0:T(8,128)(2,1)} %add_convert_fusion.3), channel_id=1, source_target_pairs={{0,4},{4,0},{8,12},{12,8},{16,20},{20,16},{24,28},{28,24},{1,5},{5... | collective-permute-start | bytes 4325384 | tf_op jit(solution)/shard_map/ppermute | solution.py:113
  495.2 68.9 %collective-permute-start.32 = (bf16[1408,256]{1,0:T(8,128)(2,1)}, bf16[1408,256]{1,0:T(8,128)(2,1)}, u32[]{:S(2)}, u32[]{:S(2)}) collective-permute-start(bf16[1408,256]{1,0:T(8,128)(2,1)} %add_convert_fusion.22), channel_id=1, source_target_pairs={{0,24},{4,28},{8,16},{12,20},{16,8},{20,12},{24,0},{28,4},{1,25},{... | collective-permute-start | bytes 2162696 | tf_op jit(solution)/shard_map/ppermute | solution.py:113
  498.1 92.1 %collective-permute-start.41 = (bf16[512,1408]{1,0:T(8,128)(2,1)}, bf16[512,1408]{1,0:T(8,128)(2,1)}, u32[]{:S(2)}, u32[]{:S(2)}) collective-permute-start(bf16[512,1408]{1,0:T(8,128)(2,1)} %add_convert_fusion.4), channel_id=1, source_target_pairs={{0,8},{4,12},{8,0},{12,4},{16,24},{20,28},{24,16},{28,20},{1,9},{5... | collective-permute-start | bytes 4325384 | tf_op jit(solution)/shard_map/ppermute | solution.py:113
  531.0 69.5 %collective-permute-start.46 = (bf16[1024,1408]{1,0:T(8,128)(2,1)}, bf16[1024,1408]{1,0:T(8,128)(2,1)}, u32[]{:S(2)}, u32[]{:S(2)}) collective-permute-start(bf16[1024,1408]{1,0:T(8,128)(2,1)} %get-tuple-element.342), channel_id=1, source_target_pairs={{0,4},{4,0},{8,12},{12,8},{16,20},{20,16},{24,28},{28,24},{1,5},{5... | collective-permute-start | bytes 8650760 | tf_op jit(solution)/shard_map/ppermute | solution.py:113
  591.9 6.2 collective-permute-start.36
  593.9 10.2 %collective-permute-start.35 = (bf16[256,2048]{1,0:T(8,128)(2,1)S(1)}, bf16[256,2048]{1,0:T(8,128)(2,1)S(1)}, u32[]{:S(2)}, u32[]{:S(2)}) collective-permute-start(bf16[256,2048]{1,0:T(8,128)(2,1)S(1)} %copy-done.59), channel_id=1, source_target_pairs={{0,1},{1,0},{2,3},{3,2},{4,5},{5,4},{6,7},{7,6},{8,9},{9,8},{10,11... | collective-permute-start | bytes 3145736 | tf_op jit(solution)/shard_map/ppermute | solution.py:113
  594.3 18.8 %collective-permute-start.38 = (bf16[256,2048]{1,0:T(8,128)(2,1)S(1)}, bf16[256,2048]{1,0:T(8,128)(2,1)S(1)}, u32[]{:S(2)}, u32[]{:S(2)}) collective-permute-start(bf16[256,2048]{1,0:T(8,128)(2,1)S(1)} %copy-done.64), channel_id=1, source_target_pairs={{0,1},{1,0},{2,3},{3,2},{4,5},{5,4},{6,7},{7,6},{8,9},{9,8},{10,11... | collective-permute-start | bytes 3145736 | tf_op jit(solution)/shard_map/ppermute | solution.py:113
  594.5 5.4 collective-permute-start.39
  598.1 59.3 %collective-permute-start.44 = (bf16[512,1408]{1,0:T(8,128)(2,1)S(1)}, bf16[512,1408]{1,0:T(8,128)(2,1)S(1)}, u32[]{:S(2)}, u32[]{:S(2)}) collective-permute-start(bf16[512,1408]{1,0:T(8,128)(2,1)S(1)} %add_convert_fusion.2), channel_id=1, source_target_pairs={{0,8},{4,12},{8,0},{12,4},{16,24},{20,28},{24,16},{28,20},{1,9},{5... | collective-permute-start | bytes 4325384 | tf_op jit(solution)/shard_map/ppermute | solution.py:113
  599.8 26.3 %collective-permute-start.37 = (bf16[256,2048]{1,0:T(8,128)(2,1)S(1)}, bf16[256,2048]{1,0:T(8,128)(2,1)S(1)}, u32[]{:S(2)}, u32[]{:S(2)}) collective-permute-start(bf16[256,2048]{1,0:T(8,128)(2,1)S(1)} %add_convert_fusion.12), channel_id=1, source_target_pairs={{0,2},{1,3},{2,0},{3,1},{4,6},{5,7},{6,4},{7,5},{8,10},{9,11},{10,... | collective-permute-start | bytes 3145736 | tf_op jit(solution)/shard_map/ppermute | solution.py:113
  600.6 47.6 %collective-permute-start.40 = (bf16[256,2048]{1,0:T(8,128)(2,1)S(1)}, bf16[256,2048]{1,0:T(8,128)(2,1)S(1)}, u32[]{:S(2)}, u32[]{:S(2)}) collective-permute-start(bf16[256,2048]{1,0:T(8,128)(2,1)S(1)} %add_convert_fusion.10), channel_id=1, source_target_pairs={{0,2},{1,3},{2,0},{3,1},{4,6},{5,7},{6,4},{7,5},{8,10},{9,11},{10,... | collective-permute-start | bytes 3145736 | tf_op jit(solution)/shard_map/ppermute | solution.py:113
  604.1 53.3 %collective-permute-start.45 = (bf16[256,1408]{1,0:T(8,128)(2,1)S(1)}, bf16[256,1408]{1,0:T(8,128)(2,1)S(1)}, u32[]{:S(2)}, u32[]{:S(2)}) collective-permute-start(bf16[256,1408]{1,0:T(8,128)(2,1)S(1)} %copy-done.43), channel_id=1, source_target_pairs={{0,24},{4,28},{8,16},{12,20},{16,8},{20,12},{24,0},{28,4},{1,25},{... | collective-permute-start | bytes 2162696 | tf_op jit(solution)/shard_map/ppermute | solution.py:113
  613.1 59.3 %collective-permute-start.42 = (bf16[1024,512]{1,0:T(8,128)(2,1)S(1)}, bf16[1024,512]{1,0:T(8,128)(2,1)S(1)}, u32[]{:S(2)}, u32[]{:S(2)}) collective-permute-start(bf16[1024,512]{1,0:T(8,128)(2,1)S(1)} %copy-done.62), channel_id=1, source_target_pairs={{0,4},{4,0},{8,12},{12,8},{16,20},{20,16},{24,28},{28,24},{1,5},{5... | collective-permute-start | bytes 3145736 | tf_op jit(solution)/shard_map/ppermute | solution.py:113
  626.1 54.3 %collective-permute-start.51 = (bf16[512,1408]{1,0:T(8,128)(2,1)S(1)}, bf16[512,1408]{1,0:T(8,128)(2,1)S(1)}, u32[]{:S(2)}, u32[]{:S(2)}) collective-permute-start(bf16[512,1408]{1,0:T(8,128)(2,1)S(1)} %add_convert_fusion.1), channel_id=1, source_target_pairs={{0,8},{4,12},{8,0},{12,4},{16,24},{20,28},{24,16},{28,20},{1,9},{5... | collective-permute-start | bytes 4325384 | tf_op jit(solution)/shard_map/ppermute | solution.py:113
  648.2 24.3 %collective-permute-start.43 = (bf16[1408,256]{1,0:T(8,128)(2,1)S(1)}, bf16[1408,256]{1,0:T(8,128)(2,1)S(1)}, u32[]{:S(2)}, u32[]{:S(2)}) collective-permute-start(bf16[1408,256]{1,0:T(8,128)(2,1)S(1)} %copy-done.44), channel_id=1, source_target_pairs={{0,24},{4,28},{8,16},{12,20},{16,8},{20,12},{24,0},{28,4},{1,25},{... | collective-permute-start | bytes 2162696 | tf_op jit(solution)/shard_map/ppermute | solution.py:113
  657.8 26.4 %collective-permute-start.50 = (bf16[512,1024]{1,0:T(8,128)(2,1)S(1)}, bf16[512,1024]{1,0:T(8,128)(2,1)S(1)}, u32[]{:S(2)}, u32[]{:S(2)}) collective-permute-start(bf16[512,1024]{1,0:T(8,128)(2,1)S(1)} %copy-done.63), channel_id=1, source_target_pairs={{0,4},{4,0},{8,12},{12,8},{16,20},{20,16},{24,28},{28,24},{1,5},{5... | collective-permute-start | bytes 3145736 | tf_op jit(solution)/shard_map/ppermute | solution.py:113
  672.4 32.3 %collective-permute-start.49 = (bf16[256,1408]{1,0:T(8,128)(2,1)S(1)}, bf16[256,1408]{1,0:T(8,128)(2,1)S(1)}, u32[]{:S(2)}, u32[]{:S(2)}) collective-permute-start(bf16[256,1408]{1,0:T(8,128)(2,1)S(1)} %add_convert_fusion.18), channel_id=1, source_target_pairs={{0,24},{4,28},{8,16},{12,20},{16,8},{20,12},{24,0},{28,4},{1,25},{... | collective-permute-start | bytes 2162696 | tf_op jit(solution)/shard_map/ppermute | solution.py:113
  674.2 53.1 %collective-permute-start.48 = (bf16[512,1408]{1,0:T(8,128)(2,1)S(1)}, bf16[512,1408]{1,0:T(8,128)(2,1)S(1)}, u32[]{:S(2)}, u32[]{:S(2)}) collective-permute-start(bf16[512,1408]{1,0:T(8,128)(2,1)S(1)} %copy-done.33), channel_id=1, source_target_pairs={{0,4},{4,0},{8,12},{12,8},{16,20},{20,16},{24,28},{28,24},{1,5},{5... | collective-permute-start | bytes 4325384 | tf_op jit(solution)/shard_map/ppermute | solution.py:113
  704.8 117.1 %collective-permute-start.54 = (bf16[1408,1024]{1,0:T(8,128)(2,1)S(1)}, bf16[1408,1024]{1,0:T(8,128)(2,1)S(1)}, u32[]{:S(2)}, u32[]{:S(2)}) collective-permute-start(bf16[1408,1024]{1,0:T(8,128)(2,1)S(1)} %copy-done.58), channel_id=1, source_target_pairs={{0,4},{4,0},{8,12},{12,8},{16,20},{20,16},{24,28},{28,24},{1,5},{5... | collective-permute-start | bytes 8650760 | tf_op jit(solution)/shard_map/ppermute | solution.py:113
  707.4 36.5 %collective-permute-start.47 = (bf16[512,512]{1,0:T(8,128)(2,1)S(1)}, bf16[512,512]{1,0:T(8,128)(2,1)S(1)}, u32[]{:S(2)}, u32[]{:S(2)}) collective-permute-start(bf16[512,512]{1,0:T(8,128)(2,1)S(1)} %add_convert_fusion.26), channel_id=1, source_target_pairs={{0,8},{4,12},{8,0},{12,4},{16,24},{20,28},{24,16},{28,20},{1,9},{5... | collective-permute-start | bytes 1572872 | tf_op jit(solution)/shard_map/ppermute | solution.py:113
  727.3 90.1 %collective-permute-start.55 = (bf16[512,512]{1,0:T(8,128)(2,1)S(1)}, bf16[512,512]{1,0:T(8,128)(2,1)S(1)}, u32[]{:S(2)}, u32[]{:S(2)}) collective-permute-start(bf16[512,512]{1,0:T(8,128)(2,1)S(1)} %add_convert_fusion.25), channel_id=1, source_target_pairs={{0,8},{4,12},{8,0},{12,4},{16,24},{20,28},{24,16},{28,20},{1,9},{5... | collective-permute-start | bytes 1572872 | tf_op jit(solution)/shard_map/ppermute | solution.py:113
  739.6 77.7 %collective-permute-start.56 = (bf16[256,1408]{1,0:T(8,128)(2,1)S(1)}, bf16[256,1408]{1,0:T(8,128)(2,1)S(1)}, u32[]{:S(2)}, u32[]{:S(2)}) collective-permute-start(bf16[256,1408]{1,0:T(8,128)(2,1)S(1)} %add_convert_fusion.17), channel_id=1, source_target_pairs={{0,24},{4,28},{8,16},{12,20},{16,8},{20,12},{24,0},{28,4},{1,25},{... | collective-permute-start | bytes 2162696 | tf_op jit(solution)/shard_map/ppermute | solution.py:113
  744.0 97.5 %collective-permute-start.52 = (bf16[256,512]{1,0:T(8,128)(2,1)S(1)}, bf16[256,512]{1,0:T(8,128)(2,1)S(1)}, u32[]{:S(2)}, u32[]{:S(2)}) collective-permute-start(bf16[256,512]{1,0:T(8,128)(2,1)S(1)} %add_convert_fusion.30), channel_id=1, source_target_pairs={{0,24},{4,28},{8,16},{12,20},{16,8},{20,12},{24,0},{28,4},{1,25},{... | collective-permute-start | bytes 786440 | tf_op jit(solution)/shard_map/ppermute | solution.py:113
  744.1 94.3 %collective-permute-start.53 = (bf16[256,1408]{1,0:T(8,128)(2,1)S(1)}, bf16[256,1408]{1,0:T(8,128)(2,1)S(1)}, u32[]{:S(2)}, u32[]{:S(2)}) collective-permute-start(bf16[256,1408]{1,0:T(8,128)(2,1)S(1)} %add_convert_fusion.16), channel_id=1, source_target_pairs={{0,24},{4,28},{8,16},{12,20},{16,8},{20,12},{24,0},{28,4},{1,25},{... | collective-permute-start | bytes 2162696 | tf_op jit(solution)/shard_map/ppermute | solution.py:113
  817.5 40.6 %collective-permute-start.60 = (bf16[512,256]{1,0:T(8,128)(2,1)S(1)}, bf16[512,256]{1,0:T(8,128)(2,1)S(1)}, u32[]{:S(2)}, u32[]{:S(2)}) collective-permute-start(bf16[512,256]{1,0:T(8,128)(2,1)S(1)} %add_convert_fusion.29), channel_id=1, source_target_pairs={{0,24},{4,28},{8,16},{12,20},{16,8},{20,12},{24,0},{28,4},{1,25},{... | collective-permute-start | bytes 786440 | tf_op jit(solution)/shard_map/ppermute | solution.py:113
  819.6 36.0 %collective-permute-start.61 = (bf16[256,1408]{1,0:T(8,128)(2,1)S(1)}, bf16[256,1408]{1,0:T(8,128)(2,1)S(1)}, u32[]{:S(2)}, u32[]{:S(2)}) collective-permute-start(bf16[256,1408]{1,0:T(8,128)(2,1)S(1)} %add_convert_fusion.19), channel_id=1, source_target_pairs={{0,24},{4,28},{8,16},{12,20},{16,8},{20,12},{24,0},{28,4},{1,25},{... | collective-permute-start | bytes 2162696 | tf_op jit(solution)/shard_map/ppermute | solution.py:113
  838.4 22.1 %collective-permute-start.59 = (bf16[1024,512]{1,0:T(8,128)(2,1)S(1)}, bf16[1024,512]{1,0:T(8,128)(2,1)S(1)}, u32[]{:S(2)}, u32[]{:S(2)}) collective-permute-start(bf16[1024,512]{1,0:T(8,128)(2,1)S(1)} %copy-done.61), channel_id=1, source_target_pairs={{0,4},{4,0},{8,12},{12,8},{16,20},{20,16},{24,28},{28,24},{1,5},{5... | collective-permute-start | bytes 3145736 | tf_op jit(solution)/shard_map/ppermute | solution.py:113
  839.0 31.1 %collective-permute-start.58 = (bf16[1408,512]{1,0:T(8,128)(2,1)S(1)}, bf16[1408,512]{1,0:T(8,128)(2,1)S(1)}, u32[]{:S(2)}, u32[]{:S(2)}) collective-permute-start(bf16[1408,512]{1,0:T(8,128)(2,1)S(1)} %add_convert_fusion), channel_id=1, source_target_pairs={{0,8},{4,12},{8,0},{12,4},{16,24},{20,28},{24,16},{28,20},{1,9},{5... | collective-permute-start | bytes 4325384 | tf_op jit(solution)/shard_map/ppermute | solution.py:113
  855.6 53.7 %collective-permute-start.65 = (bf16[512,1408]{1,0:T(8,128)(2,1)S(1)}, bf16[512,1408]{1,0:T(8,128)(2,1)S(1)}, u32[]{:S(2)}, u32[]{:S(2)}) collective-permute-start(bf16[512,1408]{1,0:T(8,128)(2,1)S(1)} %copy-done.32), channel_id=1, source_target_pairs={{0,4},{4,0},{8,12},{12,8},{16,20},{20,16},{24,28},{28,24},{1,5},{5... | collective-permute-start | bytes 4325384 | tf_op jit(solution)/shard_map/ppermute | solution.py:113
  858.1 51.0 %collective-permute-start.57 = (bf16[1024,512]{1,0:T(8,128)(2,1)S(1)}, bf16[1024,512]{1,0:T(8,128)(2,1)S(1)}, u32[]{:S(2)}, u32[]{:S(2)}) collective-permute-start(bf16[1024,512]{1,0:T(8,128)(2,1)S(1)} %copy-done.60), channel_id=1, source_target_pairs={{0,4},{4,0},{8,12},{12,8},{16,20},{20,16},{24,28},{28,24},{1,5},{5... | collective-permute-start | bytes 3145736 | tf_op jit(solution)/shard_map/ppermute | solution.py:113
  860.7 51.4 %collective-permute-start.64 = (bf16[512,512]{1,0:T(8,128)(2,1)S(1)}, bf16[512,512]{1,0:T(8,128)(2,1)S(1)}, u32[]{:S(2)}, u32[]{:S(2)}) collective-permute-start(bf16[512,512]{1,0:T(8,128)(2,1)S(1)} %add_convert_fusion.24), channel_id=1, source_target_pairs={{0,8},{4,12},{8,0},{12,4},{16,24},{20,28},{24,16},{28,20},{1,9},{5... | collective-permute-start | bytes 1572872 | tf_op jit(solution)/shard_map/ppermute | solution.py:113
  909.3 61.6 %collective-permute-start.62 = (bf16[512,512]{1,0:T(8,128)(2,1)S(1)}, bf16[512,512]{1,0:T(8,128)(2,1)S(1)}, u32[]{:S(2)}, u32[]{:S(2)}) collective-permute-start(bf16[512,512]{1,0:T(8,128)(2,1)S(1)} %add_convert_fusion.23), channel_id=1, source_target_pairs={{0,8},{4,12},{8,0},{12,4},{16,24},{20,28},{24,16},{28,20},{1,9},{5... | collective-permute-start | bytes 1572872 | tf_op jit(solution)/shard_map/ppermute | solution.py:113
  909.7 61.3 %collective-permute-start.63 = (bf16[1408,256]{1,0:T(8,128)(2,1)S(1)}, bf16[1408,256]{1,0:T(8,128)(2,1)S(1)}, u32[]{:S(2)}, u32[]{:S(2)}) collective-permute-start(bf16[1408,256]{1,0:T(8,128)(2,1)S(1)} %add_convert_fusion.15), channel_id=1, source_target_pairs={{0,24},{4,28},{8,16},{12,20},{16,8},{20,12},{24,0},{28,4},{1,25},{... | collective-permute-start | bytes 2162696 | tf_op jit(solution)/shard_map/ppermute | solution.py:113
  911.4 73.4 %collective-permute-start.68 = (bf16[256,1408]{1,0:T(8,128)(2,1)S(1)}, bf16[256,1408]{1,0:T(8,128)(2,1)S(1)}, u32[]{:S(2)}, u32[]{:S(2)}) collective-permute-start(bf16[256,1408]{1,0:T(8,128)(2,1)S(1)} %add_convert_fusion.14), channel_id=1, source_target_pairs={{0,24},{4,28},{8,16},{12,20},{16,8},{20,12},{24,0},{28,4},{1,25},{... | collective-permute-start | bytes 2162696 | tf_op jit(solution)/shard_map/ppermute | solution.py:113
  912.2 77.0 %collective-permute-start.67 = (bf16[256,512]{1,0:T(8,128)(2,1)S(1)}, bf16[256,512]{1,0:T(8,128)(2,1)S(1)}, u32[]{:S(2)}, u32[]{:S(2)}) collective-permute-start(bf16[256,512]{1,0:T(8,128)(2,1)S(1)} %add_convert_fusion.28), channel_id=1, source_target_pairs={{0,24},{4,28},{8,16},{12,20},{16,8},{20,12},{24,0},{28,4},{1,25},{... | collective-permute-start | bytes 786440 | tf_op jit(solution)/shard_map/ppermute | solution.py:113
  989.2 6.4 collective-permute-start.66
  (73 other events, 1082.4 us)
Sparse Core Ops, SparseCore 0:
  38.1 49.6 all-gather.2
  592.0 161.2 all-reduce.2

commit v3 on v2

--- a/solution.py
+++ b/solution.py
@@ -24,25 +24,27 @@
 VMEM_LIMIT = 56 * 1024 * 1024
 
 
-SECOND_FIRST = ('Su', '0g', '0d')
+WHOLE = ("Sg", "1u")
+SECOND_FIRST = ()
 PLAN = {
+    "Sd": "Sd+",
+    "Su": "Su+",
+    "0g": "0g+",
+    "E1": "Sd- Sd+",
+    "mix": " ".join(["Sg- Su- Su+ Sd-", "Sd+ 0u+"]),
+    "back": "Su- Su+",
+    "1g": "0g- Sd- 0g+",
+    "n1": "0d+",
+    "norm": "Su-",
+    "h": " ".join(["0u- 0u+ 0g- 0g+", "1g+"]),
+    "q": "0u- 0u+",
+    "o": "0d- 1d+ 0g- 0d+",
     "Sg": "Sg+",
-    "Su": "Su+",
-    "Sd": "Sd+",
-    "0g": "0g+",
-    "0u": "0u+",
-    "mix": "Sg- Su- 0d+",
-    "back": "Sd- 0g- Sd+",
-    "1g": "0u-",
-    "n1": "1g+",
-    "norm": "0d- Sg+",
-    "1d": "Sd-",
-    "h": "Sd+ 0d+ 0u+",
-    "ab": "1g- 1u+ Sg- Sg+",
-    "v": "Sd- 1g+ 0d- 0d+",
-    "fin": " ".join(
-        ["0u- q+ 1u- 1u+", "Sg- o+ 1g- 1g+", "0d- Su+ q- q+", "1u- 1u+ o- o+", "1g- 1d+ Su- Su+", "q- q+ 1u- 0u+", "o- o+ 1d- v+", "Su- 1d+ q- k+", "0u- 0g+ o- v-", "v+ 1d- 1d+ k-", "k+ 0g- 0g+ v-", "v+ 1d- k- k+", "0g- v- k-"]
-    ),
+    "1u": "1u+",
+    "fb": "1u-",
+    "r1": "0u- 0d- 0d+",
+    "r2": "1g- 1g+ q+",
+    "fin": " ".join(["0d- 1g- 1g+ 1d-", "1d+ o+ 1g- 1d-", "1d+ q- q+ 1d-", "o- o+ q- q+", "o- o+ q- o-"]),
 }
 
 
@@ -139,7 +141,7 @@
     return [own, other, *rest[2:]]
 
 
-def group_sum(blocks, pin=lambda values: values):
+def group_sum(blocks, pin):
     for parts in group_steps(blocks, pin):
         pass
     return sum(value.astype(F32) for value in parts)
@@ -751,8 +753,8 @@
 
 def weight_kernel(half, count, dim_first, blocks, *refs):
     values = refs[:count]
-    others = refs[count:-2]
-    sent, kept = refs[-2:]
+    outs = 2 if half else 1
+    others = refs[count:-outs]
     each = values[0].shape[0]
     product = None
     for p in range(count):
@@ -764,31 +766,41 @@
         )
         product = part if product is None else product + part
     low = product.astype(BF16)
+    if not half:
+        refs[-1][...] = low
+        return
 
     @pl.when(pl.program_id(0) < half)
     def _():
-        sent[...] = low
+        refs[-2][...] = low
 
     @pl.when(pl.program_id(0) >= half)
     def _():
-        kept[...] = low
-
-
-def weight_product(blocks, values, other, block_dim, dim_first):
+        refs[-1][...] = low
+
+
+def weight_product(blocks, values, other, block_dim, dim_first, split=True):
     values = values if isinstance(values, (list, tuple)) else [values]
     others = other if isinstance(other, (list, tuple)) else [other]
     count = blocks.shape[0]
-    half = count // 2
+    half = count // 2 if split else 0
     each = values[0].shape[0]
     cols = others[0].shape[1]
-    if dim_first:
-        shape = array_of((half * block_dim, cols))
-        sent = pl.BlockSpec((block_dim, cols), lambda i, _: (jnp.minimum(i, half - 1), 0))
-        kept = pl.BlockSpec((block_dim, cols), lambda i, _: (jnp.maximum(i - half, 0), 0))
+    if not split:
+        outs = [pl.BlockSpec((block_dim, cols), lambda i, _: (i, 0))]
+        shapes = [array_of((count * block_dim, cols))]
+    elif dim_first:
+        shapes = [array_of((half * block_dim, cols))] * 2
+        outs = [
+            pl.BlockSpec((block_dim, cols), lambda i, _: (jnp.minimum(i, half - 1), 0)),
+            pl.BlockSpec((block_dim, cols), lambda i, _: (jnp.maximum(i - half, 0), 0)),
+        ]
     else:
-        shape = array_of((cols, half * block_dim))
-        sent = pl.BlockSpec((cols, block_dim), lambda i, _: (0, jnp.minimum(i, half - 1)))
-        kept = pl.BlockSpec((cols, block_dim), lambda i, _: (0, jnp.maximum(i - half, 0)))
+        shapes = [array_of((cols, half * block_dim))] * 2
+        outs = [
+            pl.BlockSpec((cols, block_dim), lambda i, _: (0, jnp.minimum(i, half - 1))),
+            pl.BlockSpec((cols, block_dim), lambda i, _: (0, jnp.maximum(i - half, 0))),
+        ]
     return kernel_call(
         "weight_product",
         functools.partial(weight_kernel, half, len(values), dim_first),
@@ -797,8 +809,8 @@
             *[pl.BlockSpec((each, block_dim), lambda i, at: (0, at[i])) for _ in values],
             *[whole(array) for array in others],
         ],
-        [sent, kept],
-        [shape, shape],
+        outs,
+        shapes,
         blocks,
         *values,
         *others,
@@ -1078,24 +1090,19 @@
     cube = cube_of(dp_count)
     cube_bits = int(math.log2(dp_count))
     half = dp_count // 2
-    colours, orders = [], []
-    for first in range(2):
-        bits = [1 << k for k in range(cube_bits)]
-        bits = bits[first::-1] + bits[first + 1 :] if cube_bits > 1 else bits
+    at_corner = {corner: index for index, corner in enumerate(cube)}
+    orders = []
+    for bits in ([1 << k for k in range(cube_bits)],) * 2:
+        if orders and cube_bits > 1:
+            bits = [bits[1], bits[0], *bits[2:]]
         order = [0]
         for bit in reversed(bits):
             order = order + [p | bit for p in order]
-        colours.append(bits)
-        orders.append(order[half:] + order[:half])
-    at_corner = {corner: index for index, corner in enumerate(cube)}
-    block_table = np.array(
-        [
-            [[at_corner[cube[index] ^ p] for p in order] for order in orders]
-            for index in range(dp_count)
-        ],
-        np.int32,
-    )
-    my_blocks = jnp.asarray(block_table)[lax.axis_index("dp")]
+        order = order[half:] + order[:half]
+        blocks = np.array(
+            [[at_corner[cube[index] ^ p] for p in order] for index in range(dp_count)], np.int32
+        )
+        orders.append((bits, jnp.asarray(blocks)[lax.axis_index("dp")]))
     block_dim = dim // dp_count
 
     token = []
@@ -1107,16 +1114,14 @@
         token[:] = arrays
 
     class WeightSum:
-        def __init__(self, colour, values, other, dim_first):
-            self.bits = colours[colour]
+        def __init__(self, values, other, dim_first, second):
+            self.bits, blocks = orders[second]
             self.axis = 0 if dim_first else 1
             self.size = half
             self.came = []
             several = isinstance(other, (list, tuple))
             other = [then(other[0]), *other[1:]] if several else then(other)
-            self.sent, self.own = weight_product(
-                my_blocks[colour], values, other, block_dim, dim_first
-            )
+            self.sent, self.own = weight_product(blocks, values, other, block_dim, dim_first)
             mark(self.own)
 
         def part(self, first, last):
@@ -1150,6 +1155,25 @@
                 self.start()
             return self.part(0, 1)
 
+    class WholeSum:
+        def __init__(self, values, other, _, __):
+            blocks = jnp.arange(dp_count, dtype=jnp.int32)
+            (self.sent,) = weight_product(blocks, values, then(other), block_dim, True, False)
+            mark(self.sent)
+
+        def start(self):
+            self.out = lax.psum_scatter(then(self.sent), "dp", scatter_dimension=0, tiled=True)
+            self.sent = None
+
+        def collect(self):
+            self.out = then(self.out)
+            mark(self.out)
+
+        def result(self):
+            if self.sent is not None:
+                self.start()
+            return self.out.astype(F32)
+
     sums = {}
 
     def moves(place):
@@ -1159,7 +1183,9 @@
             (sums[step[:-1]].start if step[-1] == "+" else sums[step[:-1]].collect)()
 
     def weight_total(name, *args):
-        sums[name] = WeightSum(1 if name in SECOND_FIRST else 0, *args)
+        sums[name] = (WholeSum if name in WHOLE else WeightSum)(
+            *args, cube_bits > 1 and name in SECOND_FIRST
+        )
         moves(name)
 
     table = list(range(width))
@@ -1170,34 +1196,33 @@
     listed = jnp.concatenate([segment_ids[None, :], priority, expert_ids.T], axis=0).astype(BF16)
     listed = jnp.pad(listed, ((0, 8 - listed.shape[0]), (0, 0)))
     by_row = group_gather(listed, width)
-    own_input = after(block_input, listed)
+    slice_rows = head_cols // dp_count
+    out_slice = lax.dynamic_slice_in_dim(
+        out_weight, lax.axis_index("dp") * slice_rows, slice_rows, 0
+    )
+    far_blocks = far_gather(out_slice, width)
+    far_all = lax.all_gather(
+        jnp.stack([after(far_blocks[p], by_row[-1]) for p in range(2, width, 2)]),
+        "dp",
+        axis=1,
+        tiled=True,
+    )
+    own_input = after(block_input, listed, out_slice)
     input_far = far_gather(own_input, width)
     input_blocks = near_gather({0: own_input}, 2)
     cosine, sine, meta_cols, meta, hot = prepare(
         block_places, lane, by_row, local, capacity, slots_each
     )
 
-    slice_rows = head_cols // dp_count
-    far_blocks = far_gather(
-        lax.dynamic_slice_in_dim(
-            after(out_weight, by_row[-1]), lax.axis_index("dp") * slice_rows, slice_rows, 0
-        ),
-        width,
-    )
-
     project_args = (norm1_gain, qkv_weight, qkv_bias, cosine, sine)
     if near > 2:
         input_blocks = near_gather(input_far, width)
+    input_far = {p: after(block, cosine) if p else block for p, block in input_far.items()}
+    input_blocks[0] = after(input_blocks[0], *input_far.values())
     projected, normed_one = project(input_blocks[:near], *project_args, 0, 2, None)
     if near == 2:
-        input_blocks += near_gather({0: after(input_far[2], normed_one)}, 2)
+        input_blocks += near_gather({0: input_far[2]}, 2)
     cot_blocks = far_gather(after(cotangent, input_blocks[near]), width)
-    far_all = lax.all_gather(
-        jnp.stack([after(far_blocks[p], normed_one) for p in range(2, width, 2)]),
-        "dp",
-        axis=1,
-        tiled=True,
-    )
     projected, normed_one = project(
         input_blocks[near:], *project_args, 1, 2, (projected, normed_one)
     )
@@ -1244,9 +1269,9 @@
         normed, side, cot_blocks, shared_gate_up, shared_down, expert_count
     )
     mark(act)
+    weight_total("Sd", out_grad, act, False)
     weight_total("Sg", normed, gate_grad, True)
     weight_total("Su", normed, up_grad, True)
-    weight_total("Sd", out_grad, act, False)
     acts, grads, expert_rows = [], [], []
 
     def expert_product(e, k):
@@ -1309,17 +1334,22 @@
     hidden_blocks += near_gather({p - 2: block for p, block in hidden_far.items()}, width - 2)
     moves("h")
 
+    mixed_steps = group_steps(mixed_parts, then)
+    next(mixed_steps)
     attended_grad = attended_gradient(then(out_weight), hidden_blocks)
     mark(attended_grad)
     moves("ag")
+    for _ in range(int(math.log2(width)) - 1):
+        mixed_sums = next(mixed_steps)
     *projected_grad, bias_parts = attend_back(
         block_places, projected, then(attended_grad), log_near, log_far, meta_cols, meta, cosine,
         sine, rows_each,
     )
     mark(bias_parts)
+    mixed_sums = [*mixed_sums[:-1], then(mixed_sums[-1])]
+    mixed_out = (hidden_own + sum(value.astype(F32) for value in mixed_sums)).astype(BF16)
     moves("ab")
-    for j, name in enumerate("qkv"):
-        weight_total(name, normed_one, projected_grad[j], True)
+    weight_total("q", normed_one, jnp.concatenate(projected_grad, axis=1), True)
     weight_total("o", hidden_blocks, [attended_near, attended_far], False)
     inv_one_all = jnp.concatenate(
         [rms_scale(block.astype(F32)) for block in input_blocks], axis=0
@@ -1331,10 +1361,11 @@
     bias_full = lax.dynamic_update_slice_in_dim(
         jnp.zeros((3, dim), F32), jnp.sum(bias_parts, axis=1), member * head_cols, 1
     )
+    moves("fb")
     small_sums = lax.psum(
         jnp.concatenate(
             [
-                gain_two_grad[None, :],
+                then(gain_two_grad[None, :]),
                 side_sum[: expert_count + 1],
                 jnp.sum(gain_one_parts, axis=0)[None, :],
                 bias_full,
@@ -1343,9 +1374,14 @@
         ),
         ("dp", "expert"),
     )
-    moves("fb")
-    normed_one_grad = group_sum(first_parts)
-    mixed_out = (hidden_own + group_sum(mixed_parts, then)).astype(BF16)
+    first_steps = group_steps(first_parts, then)
+    first_total = next(first_steps)
+    for _ in range(int(math.log2(width)) - 1):
+        moves("r1")
+        first_total = next(first_steps)
+    moves("r2")
+    first_total = [*first_total[:-1], then(first_total[-1])]
+    normed_one_grad = sum(value.astype(F32) for value in first_total)
     inv_one = inv_one_all[:rows_each]
     hat_one = block_input.astype(F32) * inv_one
     scaled_one = normed_one_grad * gain_one
@@ -1363,7 +1399,7 @@
         mixed_out,
         input_grad,
         small_sums[expert_count + 2],
-        jnp.stack([sums[name].result() for name in "qkv"]),
+        sums["q"].result().reshape(block_dim, 3, head_cols).swapaxes(0, 1),
         small_sums[expert_count + 3 :],
         sums["o"].result(),
         small_sums[0],

time: 1020 us -> 917 us (0.90)
  waiting for transfers between devices: 382 us -> 314 us
  starting transfers between devices: 100 us -> 76.6 us
  Pallas kernels: 407 us -> 393 us
    ppermute x69 -> x57, waiting for transfers between devices: 382 us -> 295 us  [swap(): return lax.ppermute(values, axis, pairs)]
    ppermute x69 -> x57, starting transfers between devices: 100 us -> 76.4 us  [swap(): return lax.ppermute(values, axis, pairs)]
    reduce_scatter x0 -> x2, waiting for transfers between devices: none -> 18.5 us  [start(): lax.psum_scatter(then(self.sent), 'dp', scatter_dimension=0, tiled=True)]
    pallas_call x28 -> x26, Pallas kernels: 407 us -> 393 us  [kernel_call(): pl.pallas_call(body, name=name, grid_spec=pltpu.PrefetchScalarGridSpec(nu...]
    convert_element_type x26 -> x18, other arithmetic: 36.3 us -> 34.2 us  [collect(): self.sent = self.part(self.size, 2 * self.size).astype(BF16)]
  transfers between devices with their start and end apart: 71 -> 61, of which waited for: 27 -> 26; matrix products, arithmetic and copies ran while one was open for 9% -> 10% of each run, Pallas kernels for 36% -> 36%
where the time goes in v3:
time: 917 us; the launch traced here: 908 us
  Pallas kernels  393 us (43%)
  waiting for transfers between devices  314 us (34%)
  other arithmetic  84 us (9%)
  starting transfers between devices  76.6 us (8%)
  local copies, waits for them, and re-layouts  25.9 us (3%)
  between operations  14.6 us (2%)
    pallas_call x26, Pallas kernels, kernel_call(): pl.pallas_call(body, name=name, grid_spec=pltpu.PrefetchScalarGridSpec(nu...  393 us
    ppermute x57, waiting for transfers between devices, swap(): return lax.ppermute(values, axis, pairs)  295 us
    ppermute x57, starting transfers between devices, swap(): return lax.ppermute(values, axis, pairs)  76.4 us
    convert_element_type x18, other arithmetic, collect(): self.sent = self.part(self.size, 2 * self.size).astype(BF16)  34.2 us
    reduce_scatter x2, waiting for transfers between devices, start(): lax.psum_scatter(then(self.sent), 'dp', scatter_dimension=0, tiled=True)  18.5 us
  transfers between devices with their start and end apart: 61, of which 26 were waited for; matrix products, arithmetic and copies ran while one was open for 10% of the time, Pallas kernels for 36%

profile of v3, /device:TPU:8, one launch (start us, length us, event | category | flops | bytes accessed | tf_op | source)
XLA Modules:
  0.0 908.2 jit_solution(5860168683597299560)
XLA Ops:
  12.4 4.0 collective-permute-done.2.refs_2_
  21.0 2.8 collective-permute-done.1.refs_1_
  24.3 7.0 prepare.1
  31.3 12.5 %collective-permute-done.refs_0_.refs_3_ = bf16[256,2048]{1,0:T(8,128)(2,1)S(1)} collective-permute-done((bf16[256,2048]{1,0:T(8,128)(2,1)}, bf16[256,2048]{1,0:T(8,128)(2,1)S(1)}, u32[]{:S(2)}, u32[]{:S(2)}) %collective-permute-start) | collective-permute-done | bytes 1048608 | tf_op jit(solution)/shard_map/ppermute | solution.py:115
  48.9 9.7 %project.2 = (bf16[3,1024,512]{2,1,0:T(8,128)(2,1)}, bf16[1024,2048]{1,0:T(8,128)(2,1)}) custom-call(bf16[256,2048]{1,0:T(8,128)(2,1)} %refs_1_, bf16[256,2048]{1,0:T(8,128)(2,1)} %copy-done.11, bf16[1,2048]{1,0:T(2,128)(2,1)} %broadcast_in_dim.45.refs_2_, bf16[3,2048,512]{2,1,0:T(8,128)(2,1)} %refs_0_.3, bf16[3,1,512]{2,1,0:T(2,128)(2,1)} %copy.47.refs_4_, ...), custom_call_target="tpu_custom_call" | custom-call | flops 1 | bytes 1 | tf_op jit(solution)/shard_map/project/pallas_call | solution.py:68
  59.7 9.4 %project.3 = (bf16[3,1024,512]{2,1,0:T(8,128)(2,1)}, bf16[1024,2048]{1,0:T(8,128)(2,1)}) custom-call(bf16[256,2048]{1,0:T(8,128)(2,1)} %copy-done.7, bf16[256,2048]{1,0:T(8,128)(2,1)} %copy-done.9, bf16[1,2048]{1,0:T(2,128)(2,1)} %broadcast_in_dim.45.refs_2_, bf16[3,2048,512]{2,1,0:T(8,128)(2,1)} %refs_0_.3, ...), custom_call_target="tpu_custom_call", output_to_operand_aliasing={{0}: (7, {}), {1}: (8, {})} | custom-call | flops 1 | bytes 1 | tf_op jit(solution)/shard_map/project/pallas_call | solution.py:68
  69.1 9.5 %attend.2 = (bf16[512,512]{1,0:T(8,128)(2,1)}, f32[4,512,1]{2,1,0:T(8,128)}) custom-call(s32[4]{0:T(128)} %iota_xor_fusion.places, bf16[3,1024,512]{2,1,0:T(8,128)(2,1)} %get-tuple-element.191.query.key.value, bf16[3,1024,512]{2,1,0:T(8,128)(2,1)} %get-tuple-element.191.query.key.value, bf16[3,1024,512]{2,1,0:T(8,128)(2,1)} %get-tuple-element.191.query.key.value, ...), custom_call_target="tpu_custom_call" | custom-call | flops 1 | bytes 1 | tf_op jit(solution)/shard_map/attend/pallas_call | solution.py:68
  78.7 6.7 attend.3
  86.2 13.7 %collective-permute-done.9.refs_4_ = bf16[512,512]{1,0:T(8,128)(2,1)S(1)} collective-permute-done((bf16[512,512]{1,0:T(8,128)(2,1)}, bf16[512,512]{1,0:T(8,128)(2,1)S(1)}, u32[]{:S(2)}, u32[]{:S(2)}) %collective-permute-start.9) | collective-permute-done | bytes 524320 | tf_op jit(solution)/shard_map/ppermute | solution.py:115
  103.8 12.2 %out_project.2 = (bf16[1024,2048]{1,0:T(8,128)(2,1)}, f32[1024,128]{1,0:T(8,128)}, f32[256,2048]{1,0:T(8,128)}) custom-call(bf16[256,2048]{1,0:T(8,128)(2,1)} %refs_1_, bf16[256,2048]{1,0:T(8,128)(2,1)} %copy-done.11, bf16[512,512]{1,0:T(8,128)(2,1)} %get-tuple-element.300.refs_2_.refs_4_, bf16[512,512]{1,0:T(8,128)(2,1)} %copy-done.45, ...), custom_call_target="tpu_custom_call" | custom-call | flops 1 | bytes 1 | tf_op jit(solution)/shard_map/out_project/pallas_call | solution.py:68
  119.0 11.9 %out_project.3 = (bf16[1024,2048]{1,0:T(8,128)(2,1)}, f32[1024,128]{1,0:T(8,128)}, f32[256,2048]{1,0:T(8,128)}) custom-call(bf16[256,2048]{1,0:T(8,128)(2,1)} %copy-done.7, bf16[256,2048]{1,0:T(8,128)(2,1)} %copy-done.9, bf16[512,512]{1,0:T(8,128)(2,1)} %get-tuple-element.198.refs_2_.refs_5_, ...), custom_call_target="tpu_custom_call", output_to_operand_aliasing={{0}: (12, {}), {1}: (13, {})} | custom-call | flops 1 | bytes 1 | tf_op jit(solution)/shard_map/out_project/pallas_call | solution.py:68
  133.8 29.0 %shared_inner.1 = (bf16[1024,1408]{1,0:T(8,128)(2,1)}, bf16[1024,1408]{1,0:T(8,128)(2,1)}, bf16[1024,1408]{1,0:T(8,128)(2,1)}, bf16[1024,2048]{1,0:T(8,128)(2,1)}) custom-call(bf16[1024,2048]{1,0:T(8,128)(2,1)} %get-tuple-element.232.refs_0_.refs_6_, f32[1024,128]{1,0:T(8,128)} %get-tuple-element.206.refs_1_.side, bf16[256,2048]{1,0:T(8,128)(2,1)} %refs_4_.1, ...), custom_call_target="tpu_custom_call" | custom-call | flops 1 | bytes 1 | tf_op jit(solution)/shard_map/shared_inner/pallas_call | solution.py:68
  162.7 13.1 %weight_product.11 = (bf16[1408,1024]{1,0:T(8,128)(2,1)}, bf16[1408,1024]{1,0:T(8,128)(2,1)}) custom-call(s32[8]{0:T(128)} %fusion.5.blocks, bf16[1024,2048]{1,0:T(8,128)(2,1)} %get-tuple-element.210.refs_0_, bf16[1024,1408]{1,0:T(8,128)(2,1)} %get-tuple-element.235.refs_1_.act), custom_call_target="tpu_custom_call" | custom-call | flops 1 | bytes 1 | tf_op jit(solution)/shard_map/weight_product/pallas_call | solution.py:68
  176.4 12.7 %weight_product.12 = bf16[2048,1408]{1,0:T(8,128)(2,1)} custom-call(s32[8]{0:T(128)} %iota.10.blocks, bf16[1024,2048]{1,0:T(8,128)(2,1)} %get-tuple-element.232.refs_0_.refs_6_, bf16[1024,1408]{1,0:T(8,128)(2,1)} %get-tuple-element.249.refs_1_.gate_grad), custom_call_target="tpu_custom_call" | custom-call | flops 1 | bytes 1 | tf_op jit(solution)/shard_map/weight_product/pallas_call | solution.py:68
  190.8 13.7 %weight_product.13 = (bf16[1024,1408]{1,0:T(8,128)(2,1)}, bf16[1024,1408]{1,0:T(8,128)(2,1)}) custom-call(s32[8]{0:T(128)} %fusion.5.blocks, bf16[1024,2048]{1,0:T(8,128)(2,1)} %get-tuple-element.232.refs_0_.refs_6_, bf16[1024,1408]{1,0:T(8,128)(2,1)} %get-tuple-element.217.refs_1_.up_grad), custom_call_target="tpu_custom_call" | custom-call | flops 1 | bytes 1 | tf_op jit(solution)/shard_map/weight_product/pallas_call | solution.py:68
  204.9 21.4 %expert_inner.2 = (bf16[576,1408]{1,0:T(8,128)(2,1)}, bf16[576,1408]{1,0:T(8,128)(2,1)}, bf16[576,1408]{1,0:T(8,128)(2,1)}, bf16[576,2048]{1,0:T(8,128)(2,1)}, bf16[576,2048]{1,0:T(8,128)(2,1)}) custom-call(s32[1]{0:T(128)} %bitcast.1.first, bf16[1024,2048]{1,0:T(8,128)(2,1)} %get-tuple-element.232.refs_0_.refs_6_, ...), custom_call_target="tpu_custom_call" | custom-call | flops 1 | bytes 1 | tf_op jit(solution)/shard_map/expert_inner/pallas_call | solution.py:68
  226.3 11.6 %weight_product.14 = (bf16[1024,1408]{1,0:T(8,128)(2,1)}, bf16[1024,1408]{1,0:T(8,128)(2,1)}) custom-call(s32[8]{0:T(128)} %fusion.5.blocks, bf16[576,2048]{1,0:T(8,128)(2,1)} %get-tuple-element.223.refs_0_, bf16[576,1408]{1,0:T(8,128)(2,1)} %get-tuple-element.226.refs_1_.refs_0_), custom_call_target="tpu_custom_call" | custom-call | flops 1 | bytes 1 | tf_op jit(solution)/shard_map/weight_product/pallas_call | solution.py:68
  239.5 11.5 %weight_product.15 = (bf16[1024,1408]{1,0:T(8,128)(2,1)}, bf16[1024,1408]{1,0:T(8,128)(2,1)}) custom-call(s32[8]{0:T(128)} %fusion.5.blocks, bf16[576,2048]{1,0:T(8,128)(2,1)} %get-tuple-element.223.refs_0_, bf16[576,1408]{1,0:T(8,128)(2,1)} %get-tuple-element.228.refs_1_), custom_call_target="tpu_custom_call" | custom-call | flops 1 | bytes 1 | tf_op jit(solution)/shard_map/weight_product/pallas_call | solution.py:68
  251.0 11.5 %weight_product.16 = (bf16[1408,1024]{1,0:T(8,128)(2,1)}, bf16[1408,1024]{1,0:T(8,128)(2,1)}) custom-call(s32[8]{0:T(128)} %fusion.5.blocks, bf16[576,2048]{1,0:T(8,128)(2,1)} %get-tuple-element.221.refs_0_, bf16[576,1408]{1,0:T(8,128)(2,1)} %get-tuple-element.230.refs_1_.refs_0_), custom_call_target="tpu_custom_call" | custom-call | flops 1 | bytes 1 | tf_op jit(solution)/shard_map/weight_product/pallas_call | solution.py:68
  262.5 21.4 %expert_inner.3 = (bf16[576,1408]{1,0:T(8,128)(2,1)}, bf16[576,1408]{1,0:T(8,128)(2,1)}, bf16[576,1408]{1,0:T(8,128)(2,1)}, bf16[576,2048]{1,0:T(8,128)(2,1)}, bf16[576,2048]{1,0:T(8,128)(2,1)}) custom-call(s32[1]{0:T(128)} %bitcast.1.first, bf16[1024,2048]{1,0:T(8,128)(2,1)} %get-tuple-element.232.refs_0_.refs_6_, ...), custom_call_target="tpu_custom_call" | custom-call | flops 1 | bytes 1 | tf_op jit(solution)/shard_map/expert_inner/pallas_call | solution.py:68
  285.7 3.0 add_convert_fusion.7
  289.0 36.1 %mix.1 = (bf16[256,2048]{1,0:T(8,128)(2,1)}, bf16[256,2048]{1,0:T(8,128)(2,1)}, bf16[256,2048]{1,0:T(8,128)(2,1)}, bf16[256,2048]{1,0:T(8,128)(2,1)}, f32[1024,128]{1,0:T(8,128)}) custom-call(s32[1]{0:T(128)} %bitcast.1.first, f32[1024,128]{1,0:T(8,128)} %get-tuple-element.206.refs_1_.side, bf16[1024,1408]{1,0:T(8,128)(2,1)} %get-tuple-element.235.refs_1_.act, ...), custom_call_target="tpu_custom_call" | custom-call | flops 1 | bytes 1 | tf_op jit(solution)/shard_map/mix/pallas_call | solution.py:68
  325.1 18.5 %reduce-scatter.3.cloned.1.call-done = bf16[256,1408]{1,0:T(8,128)(2,1)} async-done(((bf16[2048,1408]{1,0:T(8,128)(2,1)}), bf16[256,1408]{1,0:T(8,128)(2,1)}) %reduce-scatter.3.cloned.1.call-update) | async-done | bytes 720912 | tf_op jit(solution)/shard_map/reduce_scatter | solution.py:1165
  343.6 11.6 %collective-permute-done.20 = bf16[1024,1408]{1,0:T(8,128)(2,1)} collective-permute-done((bf16[1024,1408]{1,0:T(8,128)(2,1)}, bf16[1024,1408]{1,0:T(8,128)(2,1)}, u32[]{:S(2)}, u32[]{:S(2)}) %collective-permute-start.20) | collective-permute-done | bytes 2883616 | tf_op jit(solution)/shard_map/ppermute | solution.py:115
  359.6 3.0 collective-permute-start.23
  362.5 47.0 %back.1 = (bf16[256,2048]{1,0:T(8,128)(2,1)}, bf16[256,2048]{1,0:T(8,128)(2,1)}, bf16[256,2048]{1,0:T(8,128)(2,1)}, bf16[256,2048]{1,0:T(8,128)(2,1)}, f32[128,2048]{1,0:T(8,128)}) custom-call(f32[1024,128]{1,0:T(8,128)} %get-tuple-element.206.refs_1_.side, f32[1024,128]{1,0:T(8,128)} %get-tuple-element.243.totals, ...), custom_call_target="tpu_custom_call" | custom-call | flops 1 | bytes 1 | tf_op jit(solution)/shard_map/back/pallas_call | solution.py:68
  413.1 11.6 %weight_product.17 = (bf16[1024,1408]{1,0:T(8,128)(2,1)}, bf16[1024,1408]{1,0:T(8,128)(2,1)}) custom-call(s32[8]{0:T(128)} %fusion.5.blocks, bf16[576,2048]{1,0:T(8,128)(2,1)} %get-tuple-element.239.refs_0_, bf16[576,1408]{1,0:T(8,128)(2,1)} %get-tuple-element.253.refs_2_.refs_1_), custom_call_target="tpu_custom_call" | custom-call | flops 1 | bytes 1 | tf_op jit(solution)/shard_map/weight_product/pallas_call | solution.py:68
  428.3 10.8 %weight_product.18 = bf16[2048,1408]{1,0:T(8,128)(2,1)} custom-call(s32[8]{0:T(128)} %iota.11.blocks, bf16[576,2048]{1,0:T(8,128)(2,1)} %get-tuple-element.239.refs_0_, bf16[576,1408]{1,0:T(8,128)(2,1)} %get-tuple-element.270.refs_3_.refs_1_), custom_call_target="tpu_custom_call" | custom-call | flops 1 | bytes 1 | tf_op jit(solution)/shard_map/weight_product/pallas_call | solution.py:68
  443.0 2.7 add_convert_fusion.12
  452.5 19.1 %collective-permute-done.29 = bf16[256,2048]{1,0:T(8,128)(2,1)} collective-permute-done((bf16[256,2048]{1,0:T(8,128)(2,1)}, bf16[256,2048]{1,0:T(8,128)(2,1)}, u32[]{:S(2)}, u32[]{:S(2)}) %collective-permute-start.29) | collective-permute-done | bytes 1048608 | tf_op jit(solution)/shard_map/ppermute | solution.py:115
  474.7 4.0 fusion.6
  480.1 33.2 %collective-permute-done.26 = bf16[256,1408]{1,0:T(8,128)(2,1)S(1)} collective-permute-done((bf16[256,1408]{1,0:T(8,128)(2,1)S(1)}, bf16[256,1408]{1,0:T(8,128)(2,1)S(1)}, u32[]{:S(2)}, u32[]{:S(2)}) %collective-permute-start.26) | collective-permute-done | bytes 720928 | tf_op jit(solution)/shard_map/ppermute | solution.py:115
  513.3 11.8 %weight_product.19 = (bf16[1408,1024]{1,0:T(8,128)(2,1)}, bf16[1408,1024]{1,0:T(8,128)(2,1)}) custom-call(s32[8]{0:T(128)} %fusion.5.blocks, bf16[576,2048]{1,0:T(8,128)(2,1)} %get-tuple-element.261.refs_0_, bf16[576,1408]{1,0:T(8,128)(2,1)} %get-tuple-element.273.refs_1_), custom_call_target="tpu_custom_call" | custom-call | flops 1 | bytes 1 | tf_op jit(solution)/shard_map/weight_product/pallas_call | solution.py:68
  525.2 3.2 add_convert_fusion.4
  528.4 11.1 %collective-permute-done.24 = bf16[512,1408]{1,0:T(8,128)(2,1)} collective-permute-done((bf16[512,1408]{1,0:T(8,128)(2,1)S(1)}, bf16[512,1408]{1,0:T(8,128)(2,1)}, u32[]{:S(2)}, u32[]{:S(2)}) %collective-permute-start.24) | collective-permute-done | bytes 1441824 | tf_op jit(solution)/shard_map/ppermute | solution.py:115
  539.5 2.7 add_convert_fusion.18
  545.0 3.4 convert_add_fusion.2
  552.8 6.4 attended_gradient.1.out_grad
  559.2 21.8 %attend_back.1 = (bf16[1024,512]{1,0:T(8,128)(2,1)}, bf16[1024,512]{1,0:T(8,128)(2,1)}, bf16[1024,512]{1,0:T(8,128)(2,1)}, f32[3,8,512]{2,1,0:T(8,128)}) custom-call(s32[4]{0:T(128)} %iota_xor_fusion.places, bf16[3,1024,512]{2,1,0:T(8,128)(2,1)} %get-tuple-element.191.query.key.value, bf16[3,1024,512]{2,1,0:T(8,128)(2,1)} %get-tuple-element.191.query.key.value, ...), custom_call_target="tpu_custom_call" | custom-call | flops 1 | bytes 1 | tf_op jit(solution)/shard_map/attend_back/pallas_call | solution.py:68
  581.0 3.7 pad_maximum_fusion.1.refs_1_
  584.8 13.6 %weight_product.20 = (bf16[1024,1536]{1,0:T(8,128)(2,1)}, bf16[1024,1536]{1,0:T(8,128)(2,1)}) custom-call(s32[8]{0:T(128)} %fusion.5.blocks, bf16[1024,2048]{1,0:T(8,128)(2,1)} %get-tuple-element.294.refs_0_, bf16[1024,1536]{1,0:T(8,128)(2,1)} %pad_maximum_fusion.1.refs_1_), custom_call_target="tpu_custom_call" | custom-call | flops 1 | bytes 1 | tf_op jit(solution)/shard_map/weight_product/pallas_call | solution.py:68
  599.9 2.7 add_convert_fusion.17
  602.6 9.6 %weight_product.21 = (bf16[512,1024]{1,0:T(8,128)(2,1)}, bf16[512,1024]{1,0:T(8,128)(2,1)}) custom-call(s32[8]{0:T(128)} %fusion.5.blocks, bf16[256,2048]{1,0:T(8,128)(2,1)} %copy-done.13, bf16[256,2048]{1,0:T(8,128)(2,1)} %copy-done.18, bf16[256,2048]{1,0:T(8,128)(2,1)} %copy-done.17, bf16[256,2048]{1,0:T(8,128)(2,1)} %copy-done.19, ...), custom_call_target="tpu_custom_call" | custom-call | flops 1 | bytes 1 | tf_op jit(solution)/shard_map/weight_product/pallas_call | solution.py:68
  612.2 3.2 add_convert_fusion.3
  619.8 12.5 %first_back.1 = (bf16[256,2048]{1,0:T(8,128)(2,1)}, bf16[256,2048]{1,0:T(8,128)(2,1)}, bf16[256,2048]{1,0:T(8,128)(2,1)}, bf16[256,2048]{1,0:T(8,128)(2,1)}, f32[8,2048]{1,0:T(8,128)}) custom-call(bf16[1024,512]{1,0:T(8,128)(2,1)} %get-tuple-element.304.query, bf16[1024,512]{1,0:T(8,128)(2,1)} %get-tuple-element.295.key, ...), custom_call_target="tpu_custom_call" | custom-call | flops 1 | bytes 1 | tf_op jit(solution)/shard_map/first_back/pallas_call | solution.py:68
  634.6 3.5 add_convert_fusion.10
  638.2 12.0 %collective-permute-done.41 = bf16[1408,512]{1,0:T(8,128)(2,1)} collective-permute-done((bf16[1408,512]{1,0:T(8,128)(2,1)}, bf16[1408,512]{1,0:T(8,128)(2,1)}, u32[]{:S(2)}, u32[]{:S(2)}) %collective-permute-start.41) | collective-permute-done | bytes 1441824 | tf_op jit(solution)/shard_map/ppermute | solution.py:115
  650.2 2.7 add_convert_fusion.16
  652.9 16.5 %collective-permute-done.44 = bf16[1024,1408]{1,0:T(8,128)(2,1)} collective-permute-done((bf16[1024,1408]{1,0:T(8,128)(2,1)}, bf16[1024,1408]{1,0:T(8,128)(2,1)}, u32[]{:S(2)}, u32[]{:S(2)}) %collective-permute-start.44) | collective-permute-done | bytes 2883616 | tf_op jit(solution)/shard_map/ppermute | solution.py:115
  669.3 2.8 add_convert_fusion.2
  674.9 3.4 add_bitcast_fusion.3
  678.4 15.2 %collective-permute-done.47 = bf16[1408,256]{1,0:T(8,128)(2,1)S(1)} collective-permute-done((bf16[1408,256]{1,0:T(8,128)(2,1)}, bf16[1408,256]{1,0:T(8,128)(2,1)S(1)}, u32[]{:S(2)}, u32[]{:S(2)}) %collective-permute-start.47) | collective-permute-done | bytes 720928 | tf_op jit(solution)/shard_map/ppermute | solution.py:115
  698.3 9.4 %collective-permute-done.46 = bf16[512,1408]{1,0:T(8,128)(2,1)S(1)} collective-permute-done((bf16[512,1408]{1,0:T(8,128)(2,1)}, bf16[512,1408]{1,0:T(8,128)(2,1)S(1)}, u32[]{:S(2)}, u32[]{:S(2)}) %collective-permute-start.46) | collective-permute-done | bytes 1441824 | tf_op jit(solution)/shard_map/ppermute | solution.py:115
  709.0 22.5 %collective-permute-done.45 = bf16[1408,1024]{1,0:T(8,128)(2,1)} collective-permute-done((bf16[1408,1024]{1,0:T(8,128)(2,1)}, bf16[1408,1024]{1,0:T(8,128)(2,1)}, u32[]{:S(2)}, u32[]{:S(2)}) %collective-permute-start.45) | collective-permute-done | bytes 2883616 | tf_op jit(solution)/shard_map/ppermute | solution.py:115
  741.4 8.8 collective-permute-done.50
  750.3 21.4 %collective-permute-done.49 = bf16[1408,512]{1,0:T(8,128)(2,1)S(1)} collective-permute-done((bf16[1408,512]{1,0:T(8,128)(2,1)S(1)}, bf16[1408,512]{1,0:T(8,128)(2,1)S(1)}, u32[]{:S(2)}, u32[]{:S(2)}) %collective-permute-start.49) | collective-permute-done | bytes 1441824 | tf_op jit(solution)/shard_map/ppermute | solution.py:115
  773.2 26.2 %collective-permute-done.52 = bf16[1024,1536]{1,0:T(8,128)(2,1)S(1)} collective-permute-done((bf16[1024,1536]{1,0:T(8,128)(2,1)S(1)}, bf16[1024,1536]{1,0:T(8,128)(2,1)S(1)}, u32[]{:S(2)}, u32[]{:S(2)}) %collective-permute-start.52) | collective-permute-done | bytes 3145760 | tf_op jit(solution)/shard_map/ppermute | solution.py:115
  803.3 2.9 pad_maximum_fusion
  806.2 11.4 %collective-permute-done.51 = bf16[1408,256]{1,0:T(8,128)(2,1)S(1)} collective-permute-done((bf16[1408,256]{1,0:T(8,128)(2,1)S(1)}, bf16[1408,256]{1,0:T(8,128)(2,1)S(1)}, u32[]{:S(2)}, u32[]{:S(2)}) %collective-permute-start.51) | collective-permute-done | bytes 720928 | tf_op jit(solution)/shard_map/ppermute | solution.py:115
  817.6 2.7 collective-permute-done.48
  820.6 29.7 %collective-permute-start.53 = (bf16[512,512]{1,0:T(8,128)(2,1)S(1)}, bf16[512,512]{1,0:T(8,128)(2,1)S(1)}, u32[]{:S(2)}, u32[]{:S(2)}) collective-permute-start(bf16[512,512]{1,0:T(8,128)(2,1)S(1)} %add_convert_fusion.21), channel_id=1, source_target_pairs={{0,8},{4,12},{8,0},{12,4},{16,24},{20,28},{24,16},{28,20},{1,9},{5... | collective-permute-start | bytes 1572872 | tf_op jit(solution)/shard_map/ppermute | solution.py:115
  850.6 3.5 collective-permute-start.56
  858.4 20.2 %collective-permute-done.53 = bf16[512,512]{1,0:T(8,128)(2,1)S(1)} collective-permute-done((bf16[512,512]{1,0:T(8,128)(2,1)S(1)}, bf16[512,512]{1,0:T(8,128)(2,1)S(1)}, u32[]{:S(2)}, u32[]{:S(2)}) %collective-permute-start.53) | collective-permute-done | bytes 524320 | tf_op jit(solution)/shard_map/ppermute | solution.py:115
  878.9 12.2 %collective-permute-done.56 = bf16[256,1536]{1,0:T(8,128)(2,1)S(1)} collective-permute-done((bf16[256,1536]{1,0:T(8,128)(2,1)S(1)}, bf16[256,1536]{1,0:T(8,128)(2,1)S(1)}, u32[]{:S(2)}, u32[]{:S(2)}) %collective-permute-start.56) | collective-permute-done | bytes 786464 | tf_op jit(solution)/shard_map/ppermute | solution.py:115
  (294 shorter events, 114.9 us)
Async XLA Ops:
  7.2 78.2 %all-gather.3.cloned.1.call-start = ((), (), s32[]{:S(2)}) async-start(), calls=%async_computation.5 | async-start | bytes 2359296 | tf_op jit(solution)/shard_map/all_gather | solution.py:1204
  8.2 9.4 %collective-permute-start.11 = (bf16[64,2048]{1,0:T(8,128)(2,1)S(1)}, bf16[64,2048]{1,0:T(8,128)(2,1)S(1)}, u32[]{:S(2)}, u32[]{:S(2)}) collective-permute-start(bf16[64,2048]{1,0:T(8,128)(2,1)S(1)} %constant_dynamic-slice_fusion.1), channel_id=1, source_target_pairs={{0,2},{1,3},{2,0},{3,1},{4,6},{5,7},{6,4},{7,5},{8,10},{9,11},{10,... | collective-permute-start | bytes 786440 | tf_op jit(solution)/shard_map/ppermute | solution.py:115
  11.9 4.5 collective-permute-start.2
  16.4 1.2 collective-permute-start.3
  18.3 325.3 %reduce-scatter.3.cloned.1.call-start = ((), (), s32[]{:S(2)}) async-start(), calls=%async_computation.2 | async-start | bytes 6488064 | tf_op jit(solution)/shard_map/reduce_scatter | solution.py:1165
  18.4 25.5 %collective-permute-start = (bf16[256,2048]{1,0:T(8,128)(2,1)}, bf16[256,2048]{1,0:T(8,128)(2,1)S(1)}, u32[]{:S(2)}, u32[]{:S(2)}) collective-permute-start(bf16[256,2048]{1,0:T(8,128)(2,1)} %refs_1_), channel_id=1, source_target_pairs={{0,2},{1,3},{2,0},{3,1},{4,6},{5,7},{6,4},{7,5},{8,10},{9,11},{10,... | collective-permute-start | bytes 3145736 | tf_op jit(solution)/shard_map/ppermute | solution.py:115
  19.9 58.7 %collective-permute-start.7 = (bf16[512,2048]{1,0:T(8,128)(2,1)}, bf16[512,2048]{1,0:T(8,128)(2,1)}, u32[]{:S(2)}, u32[]{:S(2)}) collective-permute-start(bf16[512,2048]{1,0:T(8,128)(2,1)} %weight), channel_id=1, source_target_pairs={{0,1},{1,0},{2,3},{3,2},{4,5},{5,4},{6,7},{7,6},{8,9},{9,8},{10,11... | collective-permute-start | bytes 6291464 | tf_op jit(solution)/shard_map/ppermute | solution.py:115
  19.9 3.8 collective-permute-start.1
  20.5 27.5 %collective-permute-start.4 = (bf16[256,2048]{1,0:T(8,128)(2,1)}, bf16[256,2048]{1,0:T(8,128)(2,1)S(1)}, u32[]{:S(2)}, u32[]{:S(2)}) collective-permute-start(bf16[256,2048]{1,0:T(8,128)(2,1)} %refs_1_), channel_id=1, source_target_pairs={{0,1},{1,0},{2,3},{3,2},{4,5},{5,4},{6,7},{7,6},{8,9},{9,8},{10,11... | collective-permute-start | bytes 3145736 | tf_op jit(solution)/shard_map/ppermute | solution.py:115
  43.9 14.8 %collective-permute-start.5 = (bf16[256,2048]{1,0:T(8,128)(2,1)S(1)}, bf16[256,2048]{1,0:T(8,128)(2,1)S(1)}, u32[]{:S(2)}, u32[]{:S(2)}) collective-permute-start(bf16[256,2048]{1,0:T(8,128)(2,1)S(1)} %collective-permute-done.refs_0_.refs_3_), channel_id=1, source_target_pairs={{0,1},{1,0},{2,3},{3,2},{4,5},{5,4},{6,7},{7,6},{8,9},{9,8},{10,11... | collective-permute-start | bytes 3145736 | tf_op jit(solution)/shard_map/ppermute | solution.py:115
  43.9 34.7 %collective-permute-start.6 = (bf16[256,2048]{1,0:T(8,128)(2,1)}, bf16[256,2048]{1,0:T(8,128)(2,1)S(1)}, u32[]{:S(2)}, u32[]{:S(2)}) collective-permute-start(bf16[256,2048]{1,0:T(8,128)(2,1)} %refs_4_.1), channel_id=1, source_target_pairs={{0,2},{1,3},{2,0},{3,1},{4,6},{5,7},{6,4},{7,5},{8,10},{9,11},{10,... | collective-permute-start | bytes 3145736 | tf_op jit(solution)/shard_map/ppermute | solution.py:115
  78.6 52.3 %copy-start.5 = (bf16[256,2048]{1,0:T(8,128)(2,1)}, bf16[256,2048]{1,0:T(8,128)(2,1)S(1)}, u32[]{:S(2)}) copy-start(bf16[256,2048]{1,0:T(8,128)(2,1)S(1)} %collective-permute-done.6.refs_4_.refs_5_.refs_6_) | copy-start | bytes 3145732
  85.3 17.7 %collective-permute-start.12 = (bf16[512,2048]{1,0:T(8,128)(2,1)}, bf16[512,2048]{1,0:T(8,128)(2,1)}, u32[]{:S(2)}, u32[]{:S(2)}) collective-permute-start(bf16[512,2048]{1,0:T(8,128)(2,1)} %all-gather.3.cloned.1.call-done), channel_id=1, source_target_pairs={{0,1},{1,0},{2,3},{3,2},{4,5},{5,4},{6,7},{7,6},{8,9},{9,8},{10,11... | collective-permute-start | bytes 6291464 | tf_op jit(solution)/shard_map/ppermute | solution.py:115
  85.6 14.2 %collective-permute-start.9 = (bf16[512,512]{1,0:T(8,128)(2,1)}, bf16[512,512]{1,0:T(8,128)(2,1)S(1)}, u32[]{:S(2)}, u32[]{:S(2)}) collective-permute-start(bf16[512,512]{1,0:T(8,128)(2,1)} %get-tuple-element.198.refs_2_.refs_5_), channel_id=1, source_target_pairs={{0,2},{1,3},{2,0},{3,1},{4,6},{5,7},{6,4},{7,5},{8,10},{9,11},{10,... | collective-permute-start | bytes 1572872 | tf_op jit(solution)/shard_map/ppermute | solution.py:115
  86.2 16.8 %collective-permute-start.8 = (bf16[512,512]{1,0:T(8,128)(2,1)}, bf16[512,512]{1,0:T(8,128)(2,1)S(1)}, u32[]{:S(2)}, u32[]{:S(2)}) collective-permute-start(bf16[512,512]{1,0:T(8,128)(2,1)} %get-tuple-element.300.refs_2_.refs_4_), channel_id=1, source_target_pairs={{0,1},{1,0},{2,3},{3,2},{4,5},{5,4},{6,7},{7,6},{8,9},{9,8},{10,11... | collective-permute-start | bytes 1572872 | tf_op jit(solution)/shard_map/ppermute | solution.py:115
  99.9 3.1 collective-permute-start.10
  99.9 16.1 %collective-permute-start.14 = (bf16[512,512]{1,0:T(8,128)(2,1)}, bf16[512,512]{1,0:T(8,128)(2,1)}, u32[]{:S(2)}, u32[]{:S(2)}) collective-permute-start(bf16[512,512]{1,0:T(8,128)(2,1)} %get-tuple-element.300.refs_2_.refs_4_), channel_id=1, source_target_pairs={{0,2},{1,3},{2,0},{3,1},{4,6},{5,7},{6,4},{7,5},{8,10},{9,11},{10,... | collective-permute-start | bytes 1572872 | tf_op jit(solution)/shard_map/ppermute | solution.py:115
  102.8 13.8 %collective-permute-start.13 = (bf16[512,512]{1,0:T(8,128)(2,1)}, bf16[512,512]{1,0:T(8,128)(2,1)S(1)}, u32[]{:S(2)}, u32[]{:S(2)}) collective-permute-start(bf16[512,512]{1,0:T(8,128)(2,1)} %get-tuple-element.198.refs_2_.refs_5_), channel_id=1, source_target_pairs={{0,1},{1,0},{2,3},{3,2},{4,5},{5,4},{6,7},{7,6},{8,9},{9,8},{10,11... | collective-permute-start | bytes 1572872 | tf_op jit(solution)/shard_map/ppermute | solution.py:115
  116.0 2.2 collective-permute-start.15
  116.3 16.1 %collective-permute-start.16 = (bf16[256,2048]{1,0:T(8,128)(2,1)S(1)}, bf16[256,2048]{1,0:T(8,128)(2,1)S(1)}, u32[]{:S(2)}, u32[]{:S(2)}) collective-permute-start(bf16[256,2048]{1,0:T(8,128)(2,1)S(1)} %copy-done.3), channel_id=1, source_target_pairs={{0,1},{1,0},{2,3},{3,2},{4,5},{5,4},{6,7},{7,6},{8,9},{9,8},{10,11... | collective-permute-start | bytes 3145736 | tf_op jit(solution)/shard_map/ppermute | solution.py:115
  130.9 2.9 collective-permute-start.17
  189.1 449.0 %reduce-scatter.5.cloned.1.call-start = ((), (), s32[]{:S(2)}) async-start(), calls=%async_computation.3 | async-start | bytes 6488064 | tf_op jit(solution)/shard_map/reduce_scatter | solution.py:1165
  189.1 96.6 %collective-permute-start.18 = (bf16[1408,1024]{1,0:T(8,128)(2,1)}, bf16[1408,1024]{1,0:T(8,128)(2,1)}, u32[]{:S(2)}, u32[]{:S(2)}) collective-permute-start(bf16[1408,1024]{1,0:T(8,128)(2,1)} %get-tuple-element.213), channel_id=1, source_target_pairs={{0,4},{4,0},{8,12},{12,8},{16,20},{20,16},{24,28},{28,24},{1,5},{5... | collective-permute-start | bytes 8650760 | tf_op jit(solution)/shard_map/ppermute | solution.py:115
  204.5 150.7 %collective-permute-start.20 = (bf16[1024,1408]{1,0:T(8,128)(2,1)}, bf16[1024,1408]{1,0:T(8,128)(2,1)}, u32[]{:S(2)}, u32[]{:S(2)}) collective-permute-start(bf16[1024,1408]{1,0:T(8,128)(2,1)} %get-tuple-element.241), channel_id=1, source_target_pairs={{0,4},{4,0},{8,12},{12,8},{16,20},{20,16},{24,28},{28,24},{1,5},{5... | collective-permute-start | bytes 8650760 | tf_op jit(solution)/shard_map/ppermute | solution.py:115
  237.9 186.9 %collective-permute-start.19 = (bf16[1024,1408]{1,0:T(8,128)(2,1)}, bf16[1024,1408]{1,0:T(8,128)(2,1)S(1)}, u32[]{:S(2)}, u32[]{:S(2)}) collective-permute-start(bf16[1024,1408]{1,0:T(8,128)(2,1)} %get-tuple-element.238), channel_id=1, source_target_pairs={{0,4},{4,0},{8,12},{12,8},{16,20},{20,16},{24,28},{28,24},{1,5},{5... | collective-permute-start | bytes 8650760 | tf_op jit(solution)/shard_map/ppermute | solution.py:115
  288.8 69.0 %collective-permute-start.22 = (bf16[1408,512]{1,0:T(8,128)(2,1)}, bf16[1408,512]{1,0:T(8,128)(2,1)}, u32[]{:S(2)}, u32[]{:S(2)}) collective-permute-start(bf16[1408,512]{1,0:T(8,128)(2,1)} %add_convert_fusion.7), channel_id=1, source_target_pairs={{0,8},{4,12},{8,0},{12,4},{16,24},{20,28},{24,16},{28,20},{1,9},{5... | collective-permute-start | bytes 4325384 | tf_op jit(solution)/shard_map/ppermute | solution.py:115
  357.4 52.2 %collective-permute-start.21 = (bf16[512,1408]{1,0:T(8,128)(2,1)S(1)}, bf16[512,1408]{1,0:T(8,128)(2,1)S(1)}, u32[]{:S(2)}, u32[]{:S(2)}) collective-permute-start(bf16[512,1408]{1,0:T(8,128)(2,1)S(1)} %add_convert_fusion.6), channel_id=1, source_target_pairs={{0,8},{4,12},{8,0},{12,4},{16,24},{20,28},{24,16},{28,20},{1,9},{5... | collective-permute-start | bytes 4325384 | tf_op jit(solution)/shard_map/ppermute | solution.py:115
  359.6 67.3 %collective-permute-start.23 = (bf16[1408,256]{1,0:T(8,128)(2,1)S(1)}, bf16[1408,256]{1,0:T(8,128)(2,1)S(1)}, u32[]{:S(2)}, u32[]{:S(2)}) collective-permute-start(bf16[1408,256]{1,0:T(8,128)(2,1)S(1)} %add_convert_fusion.20), channel_id=1, source_target_pairs={{0,24},{4,28},{8,16},{12,20},{16,8},{20,12},{24,0},{28,4},{1,25},{... | collective-permute-start | bytes 2162696 | tf_op jit(solution)/shard_map/ppermute | solution.py:115
  439.2 455.7 %all-reduce.3.cloned.1.call-start = ((), (), s32[]{:S(2)}) async-start(), calls=%async_computation.4 | async-start | bytes 262144 | tf_op jit(solution)/shard_map/psum | solution.py:1365
  439.2 3.8 collective-permute-start.28
  441.3 83.9 %collective-permute-start.25 = (bf16[1024,1408]{1,0:T(8,128)(2,1)}, bf16[1024,1408]{1,0:T(8,128)(2,1)}, u32[]{:S(2)}, u32[]{:S(2)}) collective-permute-start(bf16[1024,1408]{1,0:T(8,128)(2,1)} %get-tuple-element.260), channel_id=1, source_target_pairs={{0,4},{4,0},{8,12},{12,8},{16,20},{20,16},{24,28},{28,24},{1,5},{5... | collective-permute-start | bytes 8650760 | tf_op jit(solution)/shard_map/ppermute | solution.py:115
  443.0 29.2 %collective-permute-start.27 = (bf16[256,2048]{1,0:T(8,128)(2,1)}, bf16[256,2048]{1,0:T(8,128)(2,1)}, u32[]{:S(2)}, u32[]{:S(2)}) collective-permute-start(bf16[256,2048]{1,0:T(8,128)(2,1)} %get-tuple-element.265), channel_id=1, source_target_pairs={{0,1},{1,0},{2,3},{3,2},{4,5},{5,4},{6,7},{7,6},{8,9},{9,8},{10,11... | collective-permute-start | bytes 3145736 | tf_op jit(solution)/shard_map/ppermute | solution.py:115
  445.8 25.9 %collective-permute-start.29 = (bf16[256,2048]{1,0:T(8,128)(2,1)}, bf16[256,2048]{1,0:T(8,128)(2,1)}, u32[]{:S(2)}, u32[]{:S(2)}) collective-permute-start(bf16[256,2048]{1,0:T(8,128)(2,1)} %add_convert_fusion.12), channel_id=1, source_target_pairs={{0,2},{1,3},{2,0},{3,1},{4,6},{5,7},{6,4},{7,5},{8,10},{9,11},{10,... | collective-permute-start | bytes 3145736 | tf_op jit(solution)/shard_map/ppermute | solution.py:115
  449.7 63.6 %collective-permute-start.26 = (bf16[256,1408]{1,0:T(8,128)(2,1)S(1)}, bf16[256,1408]{1,0:T(8,128)(2,1)S(1)}, u32[]{:S(2)}, u32[]{:S(2)}) collective-permute-start(bf16[256,1408]{1,0:T(8,128)(2,1)S(1)} %copy-done.42), channel_id=1, source_target_pairs={{0,24},{4,28},{8,16},{12,20},{16,8},{20,12},{24,0},{28,4},{1,25},{... | collective-permute-start | bytes 2162696 | tf_op jit(solution)/shard_map/ppermute | solution.py:115
  450.1 89.4 %collective-permute-start.24 = (bf16[512,1408]{1,0:T(8,128)(2,1)S(1)}, bf16[512,1408]{1,0:T(8,128)(2,1)}, u32[]{:S(2)}, u32[]{:S(2)}) collective-permute-start(bf16[512,1408]{1,0:T(8,128)(2,1)S(1)} %copy-done.28), channel_id=1, source_target_pairs={{0,8},{4,12},{8,0},{12,4},{16,24},{20,28},{24,16},{28,20},{1,9},{5... | collective-permute-start | bytes 4325384 | tf_op jit(solution)/shard_map/ppermute | solution.py:115
  471.6 140.5 %collective-permute-start.37 = (bf16[1408,1024]{1,0:T(8,128)(2,1)}, bf16[1408,1024]{1,0:T(8,128)(2,1)}, u32[]{:S(2)}, u32[]{:S(2)}) collective-permute-start(bf16[1408,1024]{1,0:T(8,128)(2,1)} %get-tuple-element.292), channel_id=1, source_target_pairs={{0,4},{4,0},{8,12},{12,8},{16,20},{20,16},{24,28},{28,24},{1,5},{5... | collective-permute-start | bytes 8650760 | tf_op jit(solution)/shard_map/ppermute | solution.py:115
  478.7 63.6 %copy-start.13 = (bf16[256,2048]{1,0:T(8,128)(2,1)}, bf16[256,2048]{1,0:T(8,128)(2,1)S(1)}, u32[]{:S(2)}) copy-start(bf16[256,2048]{1,0:T(8,128)(2,1)S(1)} %get-tuple-element.380.refs_0_) | copy-start | bytes 3145732
  478.7 66.2 %collective-permute-start.33 = (bf16[256,2048]{1,0:T(8,128)(2,1)S(1)}, bf16[256,2048]{1,0:T(8,128)(2,1)S(1)}, u32[]{:S(2)}, u32[]{:S(2)}) collective-permute-start(bf16[256,2048]{1,0:T(8,128)(2,1)S(1)} %get-tuple-element.380.refs_0_), channel_id=1, source_target_pairs={{0,2},{1,3},{2,0},{3,1},{4,6},{5,7},{6,4},{7,5},{8,10},{9,11},{10,... | collective-permute-start | bytes 3145736 | tf_op jit(solution)/shard_map/ppermute | solution.py:115
  542.2 6.2 collective-permute-start.31
  542.3 9.0 collective-permute-start.32
  542.9 55.5 %collective-permute-start.38 = (bf16[512,1408]{1,0:T(8,128)(2,1)}, bf16[512,1408]{1,0:T(8,128)(2,1)}, u32[]{:S(2)}, u32[]{:S(2)}) collective-permute-start(bf16[512,1408]{1,0:T(8,128)(2,1)} %add_convert_fusion.4), channel_id=1, source_target_pairs={{0,8},{4,12},{8,0},{12,4},{16,24},{20,28},{24,16},{28,20},{1,9},{5... | collective-permute-start | bytes 4325384 | tf_op jit(solution)/shard_map/ppermute | solution.py:115
  544.9 6.3 collective-permute-start.34
  548.4 67.0 %collective-permute-start.36 = (bf16[256,1408]{1,0:T(8,128)(2,1)}, bf16[256,1408]{1,0:T(8,128)(2,1)}, u32[]{:S(2)}, u32[]{:S(2)}) collective-permute-start(bf16[256,1408]{1,0:T(8,128)(2,1)} %add_convert_fusion.18), channel_id=1, source_target_pairs={{0,24},{4,28},{8,16},{12,20},{16,8},{20,12},{24,0},{28,4},{1,25},{... | collective-permute-start | bytes 2162696 | tf_op jit(solution)/shard_map/ppermute | solution.py:115
  551.3 83.4 %collective-permute-start.30 = (bf16[256,2048]{1,0:T(8,128)(2,1)}, bf16[256,2048]{1,0:T(8,128)(2,1)}, u32[]{:S(2)}, u32[]{:S(2)}) collective-permute-start(bf16[256,2048]{1,0:T(8,128)(2,1)} %get-tuple-element.277), channel_id=1, source_target_pairs={{0,1},{1,0},{2,3},{3,2},{4,5},{5,4},{6,7},{7,6},{8,9},{9,8},{10,11... | collective-permute-start | bytes 3145736 | tf_op jit(solution)/shard_map/ppermute | solution.py:115
  551.3 118.0 %collective-permute-start.44 = (bf16[1024,1408]{1,0:T(8,128)(2,1)}, bf16[1024,1408]{1,0:T(8,128)(2,1)}, u32[]{:S(2)}, u32[]{:S(2)}) collective-permute-start(bf16[1024,1408]{1,0:T(8,128)(2,1)} %get-tuple-element.320), channel_id=1, source_target_pairs={{0,4},{4,0},{8,12},{12,8},{16,20},{20,16},{24,28},{28,24},{1,5},{5... | collective-permute-start | bytes 8650760 | tf_op jit(solution)/shard_map/ppermute | solution.py:115
  598.3 34.9 %collective-permute-start.35 = (bf16[256,2048]{1,0:T(8,128)(2,1)S(1)}, bf16[256,2048]{1,0:T(8,128)(2,1)}, u32[]{:S(2)}, u32[]{:S(2)}) collective-permute-start(bf16[256,2048]{1,0:T(8,128)(2,1)S(1)} %copy-done.33), channel_id=1, source_target_pairs={{0,2},{1,3},{2,0},{3,1},{4,6},{5,7},{6,4},{7,5},{8,10},{9,11},{10,... | collective-permute-start | bytes 3145736 | tf_op jit(solution)/shard_map/ppermute | solution.py:115
  615.4 34.8 %collective-permute-start.41 = (bf16[1408,512]{1,0:T(8,128)(2,1)}, bf16[1408,512]{1,0:T(8,128)(2,1)}, u32[]{:S(2)}, u32[]{:S(2)}) collective-permute-start(bf16[1408,512]{1,0:T(8,128)(2,1)} %add_convert_fusion.3), channel_id=1, source_target_pairs={{0,8},{4,12},{8,0},{12,4},{16,24},{20,28},{24,16},{28,20},{1,9},{5... | collective-permute-start | bytes 4325384 | tf_op jit(solution)/shard_map/ppermute | solution.py:115
  617.8 20.4 %collective-permute-start.42 = (bf16[256,1408]{1,0:T(8,128)(2,1)}, bf16[256,1408]{1,0:T(8,128)(2,1)}, u32[]{:S(2)}, u32[]{:S(2)}) collective-permute-start(bf16[256,1408]{1,0:T(8,128)(2,1)} %add_convert_fusion.17), channel_id=1, source_target_pairs={{0,24},{4,28},{8,16},{12,20},{16,8},{20,12},{24,0},{28,4},{1,25},{... | collective-permute-start | bytes 2162696 | tf_op jit(solution)/shard_map/ppermute | solution.py:115
  633.3 98.3 %collective-permute-start.45 = (bf16[1408,1024]{1,0:T(8,128)(2,1)}, bf16[1408,1024]{1,0:T(8,128)(2,1)}, u32[]{:S(2)}, u32[]{:S(2)}) collective-permute-start(bf16[1408,1024]{1,0:T(8,128)(2,1)} %get-tuple-element.326), channel_id=1, source_target_pairs={{0,4},{4,0},{8,12},{12,8},{16,20},{20,16},{24,28},{28,24},{1,5},{5... | collective-permute-start | bytes 8650760 | tf_op jit(solution)/shard_map/ppermute | solution.py:115
  638.1 57.1 %collective-permute-start.40 = (bf16[256,2048]{1,0:T(8,128)(2,1)}, bf16[256,2048]{1,0:T(8,128)(2,1)}, u32[]{:S(2)}, u32[]{:S(2)}) collective-permute-start(bf16[256,2048]{1,0:T(8,128)(2,1)} %get-tuple-element.313), channel_id=1, source_target_pairs={{0,1},{1,0},{2,3},{3,2},{4,5},{5,4},{6,7},{7,6},{8,9},{9,8},{10,11... | collective-permute-start | bytes 3145736 | tf_op jit(solution)/shard_map/ppermute | solution.py:115
  672.2 35.4 %collective-permute-start.46 = (bf16[512,1408]{1,0:T(8,128)(2,1)}, bf16[512,1408]{1,0:T(8,128)(2,1)S(1)}, u32[]{:S(2)}, u32[]{:S(2)}) collective-permute-start(bf16[512,1408]{1,0:T(8,128)(2,1)} %add_convert_fusion.2), channel_id=1, source_target_pairs={{0,8},{4,12},{8,0},{12,4},{16,24},{20,28},{24,16},{28,20},{1,9},{5... | collective-permute-start | bytes 4325384 | tf_op jit(solution)/shard_map/ppermute | solution.py:115
  674.4 63.3 %collective-permute-start.39 = (bf16[256,2048]{1,0:T(8,128)(2,1)}, bf16[256,2048]{1,0:T(8,128)(2,1)S(1)}, u32[]{:S(2)}, u32[]{:S(2)}) collective-permute-start(bf16[256,2048]{1,0:T(8,128)(2,1)} %get-tuple-element.310), channel_id=1, source_target_pairs={{0,1},{1,0},{2,3},{3,2},{4,5},{5,4},{6,7},{7,6},{8,9},{9,8},{10,11... | collective-permute-start | bytes 3145736 | tf_op jit(solution)/shard_map/ppermute | solution.py:115
  674.4 19.2 %collective-permute-start.47 = (bf16[1408,256]{1,0:T(8,128)(2,1)}, bf16[1408,256]{1,0:T(8,128)(2,1)S(1)}, u32[]{:S(2)}, u32[]{:S(2)}) collective-permute-start(bf16[1408,256]{1,0:T(8,128)(2,1)} %add_convert_fusion.16), channel_id=1, source_target_pairs={{0,24},{4,28},{8,16},{12,20},{16,8},{20,12},{24,0},{28,4},{1,25},{... | collective-permute-start | bytes 2162696 | tf_op jit(solution)/shard_map/ppermute | solution.py:115
  693.6 105.8 %collective-permute-start.52 = (bf16[1024,1536]{1,0:T(8,128)(2,1)S(1)}, bf16[1024,1536]{1,0:T(8,128)(2,1)S(1)}, u32[]{:S(2)}, u32[]{:S(2)}) collective-permute-start(bf16[1024,1536]{1,0:T(8,128)(2,1)S(1)} %copy-done.57), channel_id=1, source_target_pairs={{0,4},{4,0},{8,12},{12,8},{16,20},{20,16},{24,28},{28,24},{1,5},{5... | collective-permute-start | bytes 9437192 | tf_op jit(solution)/shard_map/ppermute | solution.py:115
  696.9 38.8 %collective-permute-start.43 = (bf16[256,2048]{1,0:T(8,128)(2,1)S(1)}, bf16[256,2048]{1,0:T(8,128)(2,1)S(1)}, u32[]{:S(2)}, u32[]{:S(2)}) collective-permute-start(bf16[256,2048]{1,0:T(8,128)(2,1)S(1)} %add_convert_fusion.9), channel_id=1, source_target_pairs={{0,2},{1,3},{2,0},{3,1},{4,6},{5,7},{6,4},{7,5},{8,10},{9,11},{10,... | collective-permute-start | bytes 3145736 | tf_op jit(solution)/shard_map/ppermute | solution.py:115
  733.5 38.2 %collective-permute-start.49 = (bf16[1408,512]{1,0:T(8,128)(2,1)S(1)}, bf16[1408,512]{1,0:T(8,128)(2,1)S(1)}, u32[]{:S(2)}, u32[]{:S(2)}) collective-permute-start(bf16[1408,512]{1,0:T(8,128)(2,1)S(1)} %add_convert_fusion.1), channel_id=1, source_target_pairs={{0,8},{4,12},{8,0},{12,4},{16,24},{20,28},{24,16},{28,20},{1,9},{5... | collective-permute-start | bytes 4325384 | tf_op jit(solution)/shard_map/ppermute | solution.py:115
  735.1 15.1 %collective-permute-start.50 = (bf16[256,1408]{1,0:T(8,128)(2,1)S(1)}, bf16[256,1408]{1,0:T(8,128)(2,1)S(1)}, u32[]{:S(2)}, u32[]{:S(2)}) collective-permute-start(bf16[256,1408]{1,0:T(8,128)(2,1)S(1)} %add_convert_fusion.15), channel_id=1, source_target_pairs={{0,24},{4,28},{8,16},{12,20},{16,8},{20,12},{24,0},{28,4},{1,25},{... | collective-permute-start | bytes 2162696 | tf_op jit(solution)/shard_map/ppermute | solution.py:115
  736.2 84.2 %collective-permute-start.48 = (bf16[512,1024]{1,0:T(8,128)(2,1)S(1)}, bf16[512,1024]{1,0:T(8,128)(2,1)S(1)}, u32[]{:S(2)}, u32[]{:S(2)}) collective-permute-start(bf16[512,1024]{1,0:T(8,128)(2,1)S(1)} %copy-done.58), channel_id=1, source_target_pairs={{0,4},{4,0},{8,12},{12,8},{16,20},{20,16},{24,28},{28,24},{1,5},{5... | collective-permute-start | bytes 3145736 | tf_op jit(solution)/shard_map/ppermute | solution.py:115
  739.3 60.1 %copy-start.20 = (bf16[1024,1536]{1,0:T(8,128)(2,1)S(1)}, bf16[1024,1536]{1,0:T(8,128)(2,1)}, u32[]{:S(2)}) copy-start(bf16[1024,1536]{1,0:T(8,128)(2,1)} %get-tuple-element.298) | copy-start | bytes 9437188
  799.8 50.5 %collective-permute-start.54 = (bf16[512,1536]{1,0:T(8,128)(2,1)S(1)}, bf16[512,1536]{1,0:T(8,128)(2,1)S(1)}, u32[]{:S(2)}, u32[]{:S(2)}) collective-permute-start(bf16[512,1536]{1,0:T(8,128)(2,1)S(1)} %add_convert_fusion), channel_id=1, source_target_pairs={{0,8},{4,12},{8,0},{12,4},{16,24},{20,28},{24,16},{28,20},{1,9},{5... | collective-permute-start | bytes 4718600 | tf_op jit(solution)/shard_map/ppermute | solution.py:115
  802.7 15.0 %collective-permute-start.51 = (bf16[1408,256]{1,0:T(8,128)(2,1)S(1)}, bf16[1408,256]{1,0:T(8,128)(2,1)S(1)}, u32[]{:S(2)}, u32[]{:S(2)}) collective-permute-start(bf16[1408,256]{1,0:T(8,128)(2,1)S(1)} %add_convert_fusion.14), channel_id=1, source_target_pairs={{0,24},{4,28},{8,16},{12,20},{16,8},{20,12},{24,0},{28,4},{1,25},{... | collective-permute-start | bytes 2162696 | tf_op jit(solution)/shard_map/ppermute | solution.py:115
  820.6 58.1 %collective-permute-start.53 = (bf16[512,512]{1,0:T(8,128)(2,1)S(1)}, bf16[512,512]{1,0:T(8,128)(2,1)S(1)}, u32[]{:S(2)}, u32[]{:S(2)}) collective-permute-start(bf16[512,512]{1,0:T(8,128)(2,1)S(1)} %add_convert_fusion.21), channel_id=1, source_target_pairs={{0,8},{4,12},{8,0},{12,4},{16,24},{20,28},{24,16},{28,20},{1,9},{5... | collective-permute-start | bytes 1572872 | tf_op jit(solution)/shard_map/ppermute | solution.py:115
  850.6 40.5 %collective-permute-start.56 = (bf16[256,1536]{1,0:T(8,128)(2,1)S(1)}, bf16[256,1536]{1,0:T(8,128)(2,1)S(1)}, u32[]{:S(2)}, u32[]{:S(2)}) collective-permute-start(bf16[256,1536]{1,0:T(8,128)(2,1)S(1)} %add_convert_fusion.13), channel_id=1, source_target_pairs={{0,24},{4,28},{8,16},{12,20},{16,8},{20,12},{24,0},{28,4},{1,25},{... | collective-permute-start | bytes 2359304 | tf_op jit(solution)/shard_map/ppermute | solution.py:115
  878.8 15.1 %collective-permute-start.55 = (bf16[512,256]{1,0:T(8,128)(2,1)S(1)}, bf16[512,256]{1,0:T(8,128)(2,1)S(1)}, u32[]{:S(2)}, u32[]{:S(2)}) collective-permute-start(bf16[512,256]{1,0:T(8,128)(2,1)S(1)} %add_convert_fusion.22), channel_id=1, source_target_pairs={{0,24},{4,28},{8,16},{12,20},{16,8},{20,12},{24,0},{28,4},{1,25},{... | collective-permute-start | bytes 786440 | tf_op jit(solution)/shard_map/ppermute | solution.py:115
  (57 other events, 513.9 us)
Sparse Core Ops, SparseCore 0:
  18.4 50.5 all-gather.2
  189.2 154.3 reduce-scatter.2
  439.3 177.8 reduce-scatter.4
  674.5 139.5 all-reduce.2

commit v4 on v3

--- a/solution.py
+++ b/solution.py
@@ -25,8 +25,9 @@
 
 
 WHOLE = ("Sg", "1u")
-SECOND_FIRST = ()
+SECOND_FIRST = ("q",)
 PLAN = {
+    "Sg": "Sg+",
     "Sd": "Sd+",
     "Su": "Su+",
     "0g": "0g+",
@@ -35,16 +36,17 @@
     "back": "Su- Su+",
     "1g": "0g- Sd- 0g+",
     "n1": "0d+",
-    "norm": "Su-",
-    "h": " ".join(["0u- 0u+ 0g- 0g+", "1g+"]),
+    "1u": "1u+",
+    "norm": "Su- 0u- 0u+",
+    "h": "0g- 0g+ 1g+",
     "q": "0u- 0u+",
-    "o": "0d- 1d+ 0g- 0d+",
-    "Sg": "Sg+",
-    "1u": "1u+",
+    "o": " ".join(["0d- 0g- 1d+ q+", "0d+"]),
     "fb": "1u-",
-    "r1": "0u- 0d- 0d+",
-    "r2": "1g- 1g+ q+",
-    "fin": " ".join(["0d- 1g- 1g+ 1d-", "1d+ o+ 1g- 1d-", "1d+ q- q+ 1d-", "o- o+ q- q+", "o- o+ q- o-"]),
+    "r1": "0u- 0d-",
+    "r2": "1g- 1g+ 0d+",
+    "fin": " ".join(
+        ["q- q+ o+ 0d-", "1g- 1g+ 1d- 1d+", "1g- q- q+ 1d-", "1d+ o- o+ q-", "1d- o- o+ o-"]
+    ),
 }
 
 
@@ -640,14 +642,21 @@
 
 
 def inner(rows_in, grad_in, gate_up_ref, down_ref, act, gate_grad, up_grad):
-    gate = dots(rows_in, gate_up_ref[0], 1, 0)
-    up = dots(rows_in, gate_up_ref[1], 1, 0)
-    act_grad = dots(grad_in, down_ref[...], 1, 1)
-    sig = jax.nn.sigmoid(gate)
-    silu = gate * sig
-    act[...] = (silu * up).astype(BF16)
-    gate_grad[...] = (act_grad * up * sig * (1.0 + gate * (1.0 - sig))).astype(BF16)
-    up_grad[...] = (act_grad * silu).astype(BF16)
+    rows = rows_in.shape[0]
+    chunk = max(size for size in range(16, 257, 16) if rows % size == 0)
+
+    def body(start, length):
+        at = pl.ds(start, length)
+        gate = dots(rows_in[at, :], gate_up_ref[0], 1, 0)
+        up = dots(rows_in[at, :], gate_up_ref[1], 1, 0)
+        act_grad = dots(grad_in[at, :], down_ref[...], 1, 1)
+        sig = jax.nn.sigmoid(gate)
+        silu = gate * sig
+        act[at, :] = (silu * up).astype(BF16)
+        gate_grad[at, :] = (act_grad * up * sig * (1.0 + gate * (1.0 - sig))).astype(BF16)
+        up_grad[at, :] = (act_grad * silu).astype(BF16)
+
+    by_tiles(rows, chunk, body)
 
 
 def shared_kernel(width, rows_each, expert_count, *refs):
@@ -662,7 +671,7 @@
             gate = jax.nn.sigmoid(side[at, expert_count : expert_count + 1])
             out_grad[at, :] = (cots[p][...].astype(F32) * gate).astype(BF16)
 
-    inner(normed[...], out_grad[...], gate_up, down, act, gate_grad, up_grad)
+    inner(normed, out_grad, gate_up, down, act, gate_grad, up_grad)
 
 
 def tile_of(size):
@@ -710,7 +719,7 @@
             scaled = (cots[p][...].astype(F32) * gate).astype(BF16)
             grad_in[to, :] = dots(hot[p, 0], scaled, 1, 0).astype(BF16)
 
-    inner(rows_in[...], grad_in[...], gate_up.at[0], down.at[0], act, gate_grad, up_grad)
+    inner(rows_in, grad_in, gate_up.at[0], down.at[0], act, gate_grad, up_grad)
 
 
 def expert_inner(lane, normed, side, hot, cots, gate_up, down, expert, expert_count):
@@ -751,32 +760,53 @@
     )
 
 
+def by_tiles(size, tile, body):
+    count = size // tile
+    if count:
+
+        def step(i, carry):
+            body(pl.multiple_of(i * tile, tile), tile)
+            return carry
+
+        lax.fori_loop(0, count, step, 0)
+    if size % tile:
+        body(count * tile, size % tile)
+
+
 def weight_kernel(half, count, dim_first, blocks, *refs):
     values = refs[:count]
     outs = 2 if half else 1
     others = refs[count:-outs]
     each = values[0].shape[0]
-    product = None
-    for p in range(count):
-        per_other = others[0].shape[0] // each
-        row = (p % per_other) * each
-        rows = others[p // per_other][row : row + each, :]
-        part = (
-            dots(values[p][...], rows, 0, 0) if dim_first else dots(rows, values[p][...], 0, 0)
-        )
-        product = part if product is None else product + part
-    low = product.astype(BF16)
+    per_other = others[0].shape[0] // each
+
+    def fill(out):
+        def tile(start, length):
+            product = None
+            for p in range(count):
+                row = (p % per_other) * each
+                rows = others[p // per_other][row : row + each, pl.ds(start, length)]
+                left, right = (values[p][...], rows) if dim_first else (rows, values[p][...])
+                part = dots(left, right, 0, 0)
+                product = part if product is None else product + part
+            if dim_first:
+                out[:, pl.ds(start, length)] = product.astype(BF16)
+            else:
+                out[pl.ds(start, length), :] = product.astype(BF16)
+
+        by_tiles(others[0].shape[1], 256, tile)
+
     if not half:
-        refs[-1][...] = low
+        fill(refs[-1])
         return
 
     @pl.when(pl.program_id(0) < half)
     def _():
-        refs[-2][...] = low
+        fill(refs[-2])
 
     @pl.when(pl.program_id(0) >= half)
     def _():
-        refs[-1][...] = low
+        fill(refs[-1])
 
 
 def weight_product(blocks, values, other, block_dim, dim_first, split=True):
@@ -1269,8 +1299,8 @@
         normed, side, cot_blocks, shared_gate_up, shared_down, expert_count
     )
     mark(act)
+    weight_total("Sg", normed, gate_grad, True)
     weight_total("Sd", out_grad, act, False)
-    weight_total("Sg", normed, gate_grad, True)
     weight_total("Su", normed, up_grad, True)
     acts, grads, expert_rows = [], [], []
 

time: 917 us -> 971 us (1.059)
  Pallas kernels: 393 us -> 480 us
  waiting for transfers between devices: 314 us -> 290 us
  starting transfers between devices: 76.6 us -> 55.8 us
    pallas_call x26, Pallas kernels: 393 us -> 480 us  [kernel_call(): pl.pallas_call(body, name=name, grid_spec=pltpu.PrefetchScalarGridSpec(nu...]
    ppermute x57, starting transfers between devices: 76.4 us -> 55.7 us  [swap(): return lax.ppermute(values, axis, pairs)]
    reduce_scatter x2, waiting for transfers between devices: 18.5 us -> 0.02 us  [start(): lax.psum_scatter(then(self.sent), 'dp', scatter_dimension=0, tiled=True)]
  transfers between devices with their start and end apart: 61 -> 61, of which waited for: 26 -> 21; matrix products, arithmetic and copies ran while one was open for 10% -> 11% of each run, Pallas kernels for 36% -> 42%
where the time goes in v4:
time: 971 us; the launch traced here: 963 us
  Pallas kernels  480 us (49%)
  waiting for transfers between devices  290 us (30%)
  other arithmetic  91.4 us (9%)
  starting transfers between devices  55.8 us (6%)
  local copies, waits for them, and re-layouts  31.7 us (3%)
  between operations  14.8 us (2%)
    pallas_call x26, Pallas kernels, kernel_call(): pl.pallas_call(body, name=name, grid_spec=pltpu.PrefetchScalarGridSpec(nu...  480 us
    ppermute x57, waiting for transfers between devices, swap(): return lax.ppermute(values, axis, pairs)  290 us
    ppermute x57, starting transfers between devices, swap(): return lax.ppermute(values, axis, pairs)  55.7 us
    convert_element_type x18, other arithmetic, collect(): self.sent = self.part(self.size, 2 * self.size).astype(BF16)  39.1 us
  transfers between devices with their start and end apart: 61, of which 21 were waited for; matrix products, arithmetic and copies ran while one was open for 11% of the time, Pallas kernels for 42%

profile of v4, /device:TPU:8, one launch (start us, length us, event | category | flops | bytes accessed | tf_op | source)
XLA Modules:
  0.0 962.9 jit_solution(2464290019211168832)
XLA Ops:
  12.4 4.0 collective-permute-done.2.refs_2_
  21.0 2.7 collective-permute-done.1.refs_1_
  24.3 7.0 prepare.1
  31.3 12.5 %collective-permute-done.refs_0_.refs_3_ = bf16[256,2048]{1,0:T(8,128)(2,1)S(1)} collective-permute-done((bf16[256,2048]{1,0:T(8,128)(2,1)}, bf16[256,2048]{1,0:T(8,128)(2,1)S(1)}, u32[]{:S(2)}, u32[]{:S(2)}) %collective-permute-start) | collective-permute-done | bytes 1048608 | tf_op jit(solution)/shard_map/ppermute | solution.py:117
  48.9 9.4 project.2
  59.4 9.4 project.3
  68.8 9.5 attend.2
  78.4 6.7 attend.3
  85.9 13.5 %collective-permute-done.9.refs_4_ = bf16[512,512]{1,0:T(8,128)(2,1)S(1)} collective-permute-done((bf16[512,512]{1,0:T(8,128)(2,1)S(1)}, bf16[512,512]{1,0:T(8,128)(2,1)S(1)}, u32[]{:S(2)}, u32[]{:S(2)}) %collective-permute-start.9) | collective-permute-done | bytes 524320 | tf_op jit(solution)/shard_map/ppermute | solution.py:117
  102.7 12.1 %out_project.2 = (bf16[1024,2048]{1,0:T(8,128)(2,1)}, f32[1024,128]{1,0:T(8,128)}, f32[256,2048]{1,0:T(8,128)}) custom-call(bf16[256,2048]{1,0:T(8,128)(2,1)} %refs_1_, bf16[256,2048]{1,0:T(8,128)(2,1)} %copy-done.12, bf16[512,512]{1,0:T(8,128)(2,1)} %get-tuple-element.300.refs_2_.refs_4_, bf16[512,512]{1,0:T(8,128)(2,1)} %collective-permute-done.8.refs_3_, ...), custom_call_target="tpu_custom_call" | custom-call | flops 1 | bytes 1 | tf_op jit(solution)/shard_map/out_project/pallas_call | solution.py:70
  117.6 11.9 %out_project.3 = (bf16[1024,2048]{1,0:T(8,128)(2,1)}, f32[1024,128]{1,0:T(8,128)}, f32[256,2048]{1,0:T(8,128)}) custom-call(bf16[256,2048]{1,0:T(8,128)(2,1)} %copy-done.8, bf16[256,2048]{1,0:T(8,128)(2,1)} %copy-done.10, bf16[512,512]{1,0:T(8,128)(2,1)} %get-tuple-element.198.refs_2_.refs_5_, ...), custom_call_target="tpu_custom_call", output_to_operand_aliasing={{0}: (12, {}), {1}: (13, {})} | custom-call | flops 1 | bytes 1 | tf_op jit(solution)/shard_map/out_project/pallas_call | solution.py:70
  129.9 2.4 collective-permute-done.17.refs_5_.refs_6_.refs_7_
  133.3 32.0 %shared_inner.1 = (bf16[1024,1408]{1,0:T(8,128)(2,1)}, bf16[1024,1408]{1,0:T(8,128)(2,1)}, bf16[1024,1408]{1,0:T(8,128)(2,1)}, bf16[1024,2048]{1,0:T(8,128)(2,1)}) custom-call(bf16[1024,2048]{1,0:T(8,128)(2,1)} %get-tuple-element.232.refs_0_.refs_6_, f32[1024,128]{1,0:T(8,128)} %get-tuple-element.206.refs_1_.side, bf16[256,2048]{1,0:T(8,128)(2,1)} %refs_4_.1, ...), custom_call_target="tpu_custom_call" | custom-call | flops 1 | bytes 1 | tf_op jit(solution)/shard_map/shared_inner/pallas_call | solution.py:70
  165.8 20.5 %weight_product.11 = bf16[2048,1408]{1,0:T(8,128)(2,1)} custom-call(s32[8]{0:T(128)} %iota.10.blocks, bf16[1024,2048]{1,0:T(8,128)(2,1)} %get-tuple-element.232.refs_0_.refs_6_, bf16[1024,1408]{1,0:T(8,128)(2,1)} %get-tuple-element.249.refs_1_.gate_grad), custom_call_target="tpu_custom_call" | custom-call | flops 1 | bytes 1 | tf_op jit(solution)/shard_map/weight_product/pallas_call | solution.py:70
  187.6 20.9 %weight_product.12 = (bf16[1408,1024]{1,0:T(8,128)(2,1)}, bf16[1408,1024]{1,0:T(8,128)(2,1)}) custom-call(s32[8]{0:T(128)} %fusion.5.blocks, bf16[1024,2048]{1,0:T(8,128)(2,1)} %get-tuple-element.210.refs_0_, bf16[1024,1408]{1,0:T(8,128)(2,1)} %get-tuple-element.235.refs_1_.act), custom_call_target="tpu_custom_call" | custom-call | flops 1 | bytes 1 | tf_op jit(solution)/shard_map/weight_product/pallas_call | solution.py:70
  210.0 21.2 %weight_product.13 = (bf16[1024,1408]{1,0:T(8,128)(2,1)}, bf16[1024,1408]{1,0:T(8,128)(2,1)}) custom-call(s32[8]{0:T(128)} %fusion.5.blocks, bf16[1024,2048]{1,0:T(8,128)(2,1)} %get-tuple-element.232.refs_0_.refs_6_, bf16[1024,1408]{1,0:T(8,128)(2,1)} %get-tuple-element.217.refs_1_.up_grad), custom_call_target="tpu_custom_call" | custom-call | flops 1 | bytes 1 | tf_op jit(solution)/shard_map/weight_product/pallas_call | solution.py:70
  231.6 25.9 %expert_inner.2 = (bf16[576,1408]{1,0:T(8,128)(2,1)}, bf16[576,1408]{1,0:T(8,128)(2,1)}, bf16[576,1408]{1,0:T(8,128)(2,1)}, bf16[576,2048]{1,0:T(8,128)(2,1)}, bf16[576,2048]{1,0:T(8,128)(2,1)}) custom-call(s32[1]{0:T(128)} %bitcast.1.first, bf16[1024,2048]{1,0:T(8,128)(2,1)} %get-tuple-element.232.refs_0_.refs_6_, ...), custom_call_target="tpu_custom_call" | custom-call | flops 1 | bytes 1 | tf_op jit(solution)/shard_map/expert_inner/pallas_call | solution.py:70
  257.5 18.7 %weight_product.14 = (bf16[1024,1408]{1,0:T(8,128)(2,1)}, bf16[1024,1408]{1,0:T(8,128)(2,1)}) custom-call(s32[8]{0:T(128)} %fusion.5.blocks, bf16[576,2048]{1,0:T(8,128)(2,1)} %get-tuple-element.223.refs_0_, bf16[576,1408]{1,0:T(8,128)(2,1)} %get-tuple-element.226.refs_1_.refs_0_), custom_call_target="tpu_custom_call" | custom-call | flops 1 | bytes 1 | tf_op jit(solution)/shard_map/weight_product/pallas_call | solution.py:70
  277.9 18.7 %weight_product.15 = (bf16[1024,1408]{1,0:T(8,128)(2,1)}, bf16[1024,1408]{1,0:T(8,128)(2,1)}) custom-call(s32[8]{0:T(128)} %fusion.5.blocks, bf16[576,2048]{1,0:T(8,128)(2,1)} %get-tuple-element.223.refs_0_, bf16[576,1408]{1,0:T(8,128)(2,1)} %get-tuple-element.228.refs_1_), custom_call_target="tpu_custom_call" | custom-call | flops 1 | bytes 1 | tf_op jit(solution)/shard_map/weight_product/pallas_call | solution.py:70
  296.5 18.4 %weight_product.16 = (bf16[1408,1024]{1,0:T(8,128)(2,1)}, bf16[1408,1024]{1,0:T(8,128)(2,1)}) custom-call(s32[8]{0:T(128)} %fusion.5.blocks, bf16[576,2048]{1,0:T(8,128)(2,1)} %get-tuple-element.221.refs_0_, bf16[576,1408]{1,0:T(8,128)(2,1)} %get-tuple-element.230.refs_1_.refs_0_), custom_call_target="tpu_custom_call" | custom-call | flops 1 | bytes 1 | tf_op jit(solution)/shard_map/weight_product/pallas_call | solution.py:70
  314.9 26.0 %expert_inner.3 = (bf16[576,1408]{1,0:T(8,128)(2,1)}, bf16[576,1408]{1,0:T(8,128)(2,1)}, bf16[576,1408]{1,0:T(8,128)(2,1)}, bf16[576,2048]{1,0:T(8,128)(2,1)}, bf16[576,2048]{1,0:T(8,128)(2,1)}) custom-call(s32[1]{0:T(128)} %bitcast.1.first, bf16[1024,2048]{1,0:T(8,128)(2,1)} %get-tuple-element.232.refs_0_.refs_6_, ...), custom_call_target="tpu_custom_call" | custom-call | flops 1 | bytes 1 | tf_op jit(solution)/shard_map/expert_inner/pallas_call | solution.py:70
  341.0 3.0 add_convert_fusion.7
  344.3 36.2 %mix.1 = (bf16[256,2048]{1,0:T(8,128)(2,1)}, bf16[256,2048]{1,0:T(8,128)(2,1)}, bf16[256,2048]{1,0:T(8,128)(2,1)}, bf16[256,2048]{1,0:T(8,128)(2,1)}, f32[1024,128]{1,0:T(8,128)}) custom-call(s32[1]{0:T(128)} %bitcast.1.first, f32[1024,128]{1,0:T(8,128)} %get-tuple-element.206.refs_1_.side, bf16[1024,1408]{1,0:T(8,128)(2,1)} %get-tuple-element.235.refs_1_.act, ...), custom_call_target="tpu_custom_call" | custom-call | flops 1 | bytes 1 | tf_op jit(solution)/shard_map/mix/pallas_call | solution.py:70
  388.0 46.8 %back.1 = (bf16[256,2048]{1,0:T(8,128)(2,1)}, bf16[256,2048]{1,0:T(8,128)(2,1)}, bf16[256,2048]{1,0:T(8,128)(2,1)}, bf16[256,2048]{1,0:T(8,128)(2,1)}, f32[128,2048]{1,0:T(8,128)}) custom-call(f32[1024,128]{1,0:T(8,128)} %get-tuple-element.206.refs_1_.side, f32[1024,128]{1,0:T(8,128)} %get-tuple-element.243.totals, ...), custom_call_target="tpu_custom_call" | custom-call | flops 1 | bytes 1 | tf_op jit(solution)/shard_map/back/pallas_call | solution.py:70
  436.0 2.5 add_convert_fusion.19
  438.4 18.9 %weight_product.17 = (bf16[1024,1408]{1,0:T(8,128)(2,1)}, bf16[1024,1408]{1,0:T(8,128)(2,1)}) custom-call(s32[8]{0:T(128)} %fusion.5.blocks, bf16[576,2048]{1,0:T(8,128)(2,1)} %get-tuple-element.239.refs_0_, bf16[576,1408]{1,0:T(8,128)(2,1)} %get-tuple-element.253.refs_2_.refs_1_), custom_call_target="tpu_custom_call" | custom-call | flops 1 | bytes 1 | tf_op jit(solution)/shard_map/weight_product/pallas_call | solution.py:70
  460.7 18.2 %weight_product.18 = bf16[2048,1408]{1,0:T(8,128)(2,1)} custom-call(s32[8]{0:T(128)} %iota.11.blocks, bf16[576,2048]{1,0:T(8,128)(2,1)} %get-tuple-element.239.refs_0_, bf16[576,1408]{1,0:T(8,128)(2,1)} %get-tuple-element.270.refs_3_.refs_1_), custom_call_target="tpu_custom_call" | custom-call | flops 1 | bytes 1 | tf_op jit(solution)/shard_map/weight_product/pallas_call | solution.py:70
  489.0 2.3 collective-permute-start.24
  491.3 18.3 %collective-permute-done.29 = bf16[256,2048]{1,0:T(8,128)(2,1)} collective-permute-done((bf16[256,2048]{1,0:T(8,128)(2,1)}, bf16[256,2048]{1,0:T(8,128)(2,1)}, u32[]{:S(2)}, u32[]{:S(2)}) %collective-permute-start.29) | collective-permute-done | bytes 1048608 | tf_op jit(solution)/shard_map/ppermute | solution.py:117
  511.4 2.5 multiply_reduce_fusion
  513.9 4.1 fusion.7
  519.4 33.0 %collective-permute-done.26 = bf16[256,1408]{1,0:T(8,128)(2,1)S(1)} collective-permute-done((bf16[256,1408]{1,0:T(8,128)(2,1)S(1)}, bf16[256,1408]{1,0:T(8,128)(2,1)S(1)}, u32[]{:S(2)}, u32[]{:S(2)}) %collective-permute-start.26) | collective-permute-done | bytes 720928 | tf_op jit(solution)/shard_map/ppermute | solution.py:117
  552.4 10.7 %collective-permute-done.25 = bf16[1024,1408]{1,0:T(8,128)(2,1)} collective-permute-done((bf16[1024,1408]{1,0:T(8,128)(2,1)}, bf16[1024,1408]{1,0:T(8,128)(2,1)}, u32[]{:S(2)}, u32[]{:S(2)}) %collective-permute-start.25) | collective-permute-done | bytes 2883616 | tf_op jit(solution)/shard_map/ppermute | solution.py:117
  563.1 2.8 add_convert_fusion.4
  566.0 18.8 %weight_product.19 = (bf16[1408,1024]{1,0:T(8,128)(2,1)}, bf16[1408,1024]{1,0:T(8,128)(2,1)}) custom-call(s32[8]{0:T(128)} %fusion.5.blocks, bf16[576,2048]{1,0:T(8,128)(2,1)} %get-tuple-element.259.refs_0_, bf16[576,1408]{1,0:T(8,128)(2,1)} %get-tuple-element.274.refs_1_), custom_call_target="tpu_custom_call" | custom-call | flops 1 | bytes 1 | tf_op jit(solution)/shard_map/weight_product/pallas_call | solution.py:70
  584.8 2.8 add_convert_fusion.18
  590.4 3.4 convert_add_fusion.2
  596.7 6.2 attended_gradient.1.out_grad
  602.9 21.9 %attend_back.1 = (bf16[1024,512]{1,0:T(8,128)(2,1)}, bf16[1024,512]{1,0:T(8,128)(2,1)}, bf16[1024,512]{1,0:T(8,128)(2,1)}, f32[3,8,512]{2,1,0:T(8,128)}) custom-call(s32[4]{0:T(128)} %iota_xor_fusion.places, bf16[3,1024,512]{2,1,0:T(8,128)(2,1)} %get-tuple-element.191.query.key.value, bf16[3,1024,512]{2,1,0:T(8,128)(2,1)} %get-tuple-element.191.query.key.value, ...), custom_call_target="tpu_custom_call" | custom-call | flops 1 | bytes 1 | tf_op jit(solution)/shard_map/attend_back/pallas_call | solution.py:70
  624.7 3.2 pad_maximum_fusion.1.refs_1_
  627.9 21.3 %weight_product.20 = (bf16[1024,1536]{1,0:T(8,128)(2,1)}, bf16[1024,1536]{1,0:T(8,128)(2,1)}) custom-call(s32[8]{0:T(128)} %fusion.6.blocks, bf16[1024,2048]{1,0:T(8,128)(2,1)} %get-tuple-element.294.refs_0_, bf16[1024,1536]{1,0:T(8,128)(2,1)} %pad_maximum_fusion.1.refs_1_), custom_call_target="tpu_custom_call" | custom-call | flops 1 | bytes 1 | tf_op jit(solution)/shard_map/weight_product/pallas_call | solution.py:70
  650.7 2.7 add_convert_fusion.17
  653.3 10.5 %weight_product.21 = (bf16[512,1024]{1,0:T(8,128)(2,1)}, bf16[512,1024]{1,0:T(8,128)(2,1)}) custom-call(s32[8]{0:T(128)} %fusion.5.blocks, bf16[256,2048]{1,0:T(8,128)(2,1)} %copy-done.14, bf16[256,2048]{1,0:T(8,128)(2,1)} %copy-done.19, bf16[256,2048]{1,0:T(8,128)(2,1)} %copy-done.18, bf16[256,2048]{1,0:T(8,128)(2,1)} %copy-done.20, ...), custom_call_target="tpu_custom_call" | custom-call | flops 1 | bytes 1 | tf_op jit(solution)/shard_map/weight_product/pallas_call | solution.py:70
  670.7 4.1 collective-permute-done.35
  677.8 12.5 %first_back.1 = (bf16[256,2048]{1,0:T(8,128)(2,1)}, bf16[256,2048]{1,0:T(8,128)(2,1)}, bf16[256,2048]{1,0:T(8,128)(2,1)}, bf16[256,2048]{1,0:T(8,128)(2,1)}, f32[8,2048]{1,0:T(8,128)}) custom-call(bf16[1024,512]{1,0:T(8,128)(2,1)} %get-tuple-element.304.query, bf16[1024,512]{1,0:T(8,128)(2,1)} %get-tuple-element.295.key, ...), custom_call_target="tpu_custom_call" | custom-call | flops 1 | bytes 1 | tf_op jit(solution)/shard_map/first_back/pallas_call | solution.py:70
  695.8 3.5 add_convert_fusion.10
  700.6 2.7 add_convert_fusion.16
  703.3 6.6 collective-permute-done.44
  709.9 3.3 add_bitcast_fusion.3
  713.2 2.8 add_convert_fusion.2
  718.1 8.9 collective-permute-start.49
  727.0 57.9 %collective-permute-done.45 = bf16[1024,1536]{1,0:T(8,128)(2,1)} collective-permute-done((bf16[1024,1536]{1,0:T(8,128)(2,1)}, bf16[1024,1536]{1,0:T(8,128)(2,1)}, u32[]{:S(2)}, u32[]{:S(2)}) %collective-permute-start.45) | collective-permute-done | bytes 3145760 | tf_op jit(solution)/shard_map/ppermute | solution.py:117
  784.9 2.3 add_convert_fusion
  792.0 38.8 %collective-permute-done.48 = bf16[512,1408]{1,0:T(8,128)(2,1)S(1)} collective-permute-done((bf16[512,1408]{1,0:T(8,128)(2,1)}, bf16[512,1408]{1,0:T(8,128)(2,1)S(1)}, u32[]{:S(2)}, u32[]{:S(2)}) %collective-permute-start.48) | collective-permute-done | bytes 1441824 | tf_op jit(solution)/shard_map/ppermute | solution.py:117
  836.8 18.6 %collective-permute-done.43 = bf16[256,2048]{1,0:T(8,128)(2,1)S(1)} collective-permute-done((bf16[256,2048]{1,0:T(8,128)(2,1)S(1)}, bf16[256,2048]{1,0:T(8,128)(2,1)S(1)}, u32[]{:S(2)}, u32[]{:S(2)}) %collective-permute-start.43) | collective-permute-done | bytes 1048608 | tf_op jit(solution)/shard_map/ppermute | solution.py:117
  855.4 2.4 collective-permute-start.50
  861.6 4.2 collective-permute-done.52
  870.7 2.9 pad_maximum_fusion
  873.6 38.8 %collective-permute-done.50 = bf16[1408,512]{1,0:T(8,128)(2,1)S(1)} collective-permute-done((bf16[1408,512]{1,0:T(8,128)(2,1)S(1)}, bf16[1408,512]{1,0:T(8,128)(2,1)S(1)}, u32[]{:S(2)}, u32[]{:S(2)}) %collective-permute-start.50) | collective-permute-done | bytes 1441824 | tf_op jit(solution)/shard_map/ppermute | solution.py:117
  912.4 2.9 add_convert_fusion.14
  916.4 2.6 collective-permute-start.53
  922.7 16.2 %collective-permute-done.54 = bf16[1408,256]{1,0:T(8,128)(2,1)} collective-permute-done((bf16[1408,256]{1,0:T(8,128)(2,1)}, bf16[1408,256]{1,0:T(8,128)(2,1)}, u32[]{:S(2)}, u32[]{:S(2)}) %collective-permute-start.54) | collective-permute-done | bytes 720928 | tf_op jit(solution)/shard_map/ppermute | solution.py:117
  938.9 3.1 add_bitcast_fusion
  946.6 3.1 collective-permute-done.56
  (315 shorter events, 116.3 us)
Async XLA Ops:
  7.2 77.9 %all-gather.3.cloned.1.call-start = ((), (), s32[]{:S(2)}) async-start(), calls=%async_computation.5 | async-start | bytes 2359296 | tf_op jit(solution)/shard_map/all_gather | solution.py:1234
  8.2 9.4 collective-permute-start.11
  11.9 4.5 collective-permute-start.2
  16.4 1.2 collective-permute-start.3
  18.3 362.2 %reduce-scatter.3.cloned.1.call-start = ((), (), s32[]{:S(2)}) async-start(), calls=%async_computation.2 | async-start | bytes 6488064 | tf_op jit(solution)/shard_map/reduce_scatter | solution.py:1195
  18.4 25.5 %collective-permute-start = (bf16[256,2048]{1,0:T(8,128)(2,1)}, bf16[256,2048]{1,0:T(8,128)(2,1)S(1)}, u32[]{:S(2)}, u32[]{:S(2)}) collective-permute-start(bf16[256,2048]{1,0:T(8,128)(2,1)} %refs_1_), channel_id=1, source_target_pairs={{0,2},{1,3},{2,0},{3,1},{4,6},{5,7},{6,4},{7,5},{8,10},{9,11},{10,... | collective-permute-start | bytes 3145736 | tf_op jit(solution)/shard_map/ppermute | solution.py:117
  19.9 58.3 %collective-permute-start.7 = (bf16[512,2048]{1,0:T(8,128)(2,1)}, bf16[512,2048]{1,0:T(8,128)(2,1)}, u32[]{:S(2)}, u32[]{:S(2)}) collective-permute-start(bf16[512,2048]{1,0:T(8,128)(2,1)} %weight), channel_id=1, source_target_pairs={{0,1},{1,0},{2,3},{3,2},{4,5},{5,4},{6,7},{7,6},{8,9},{9,8},{10,11... | collective-permute-start | bytes 6291464 | tf_op jit(solution)/shard_map/ppermute | solution.py:117
  19.9 3.8 collective-permute-start.1
  20.5 27.5 %collective-permute-start.4 = (bf16[256,2048]{1,0:T(8,128)(2,1)}, bf16[256,2048]{1,0:T(8,128)(2,1)S(1)}, u32[]{:S(2)}, u32[]{:S(2)}) collective-permute-start(bf16[256,2048]{1,0:T(8,128)(2,1)} %refs_1_), channel_id=1, source_target_pairs={{0,1},{1,0},{2,3},{3,2},{4,5},{5,4},{6,7},{7,6},{8,9},{9,8},{10,11... | collective-permute-start | bytes 3145736 | tf_op jit(solution)/shard_map/ppermute | solution.py:117
  43.9 14.5 %collective-permute-start.5 = (bf16[256,2048]{1,0:T(8,128)(2,1)S(1)}, bf16[256,2048]{1,0:T(8,128)(2,1)S(1)}, u32[]{:S(2)}, u32[]{:S(2)}) collective-permute-start(bf16[256,2048]{1,0:T(8,128)(2,1)S(1)} %collective-permute-done.refs_0_.refs_3_), channel_id=1, source_target_pairs={{0,1},{1,0},{2,3},{3,2},{4,5},{5,4},{6,7},{7,6},{8,9},{9,8},{10,11... | collective-permute-start | bytes 3145736 | tf_op jit(solution)/shard_map/ppermute | solution.py:117
  43.9 34.4 %collective-permute-start.6 = (bf16[256,2048]{1,0:T(8,128)(2,1)}, bf16[256,2048]{1,0:T(8,128)(2,1)S(1)}, u32[]{:S(2)}, u32[]{:S(2)}) collective-permute-start(bf16[256,2048]{1,0:T(8,128)(2,1)} %refs_4_.1), channel_id=1, source_target_pairs={{0,2},{1,3},{2,0},{3,1},{4,6},{5,7},{6,4},{7,5},{8,10},{9,11},{10,... | collective-permute-start | bytes 3145736 | tf_op jit(solution)/shard_map/ppermute | solution.py:117
  78.3 51.3 %copy-start.5 = (bf16[256,2048]{1,0:T(8,128)(2,1)}, bf16[256,2048]{1,0:T(8,128)(2,1)S(1)}, u32[]{:S(2)}) copy-start(bf16[256,2048]{1,0:T(8,128)(2,1)S(1)} %collective-permute-done.6.refs_4_.refs_5_.refs_6_) | copy-start | bytes 3145732
  85.1 17.6 %collective-permute-start.12 = (bf16[512,2048]{1,0:T(8,128)(2,1)}, bf16[512,2048]{1,0:T(8,128)(2,1)}, u32[]{:S(2)}, u32[]{:S(2)}) collective-permute-start(bf16[512,2048]{1,0:T(8,128)(2,1)} %all-gather.3.cloned.1.call-done), channel_id=1, source_target_pairs={{0,1},{1,0},{2,3},{3,2},{4,5},{5,4},{6,7},{7,6},{8,9},{9,8},{10,11... | collective-permute-start | bytes 6291464 | tf_op jit(solution)/shard_map/ppermute | solution.py:117
  85.4 14.0 %collective-permute-start.9 = (bf16[512,512]{1,0:T(8,128)(2,1)S(1)}, bf16[512,512]{1,0:T(8,128)(2,1)S(1)}, u32[]{:S(2)}, u32[]{:S(2)}) collective-permute-start(bf16[512,512]{1,0:T(8,128)(2,1)S(1)} %copy-done.30), channel_id=1, source_target_pairs={{0,2},{1,3},{2,0},{3,1},{4,6},{5,7},{6,4},{7,5},{8,10},{9,11},{10,... | collective-permute-start | bytes 1572872 | tf_op jit(solution)/shard_map/ppermute | solution.py:117
  85.9 16.8 %collective-permute-start.8 = (bf16[512,512]{1,0:T(8,128)(2,1)}, bf16[512,512]{1,0:T(8,128)(2,1)}, u32[]{:S(2)}, u32[]{:S(2)}) collective-permute-start(bf16[512,512]{1,0:T(8,128)(2,1)} %get-tuple-element.300.refs_2_.refs_4_), channel_id=1, source_target_pairs={{0,1},{1,0},{2,3},{3,2},{4,5},{5,4},{6,7},{7,6},{8,9},{9,8},{10,11... | collective-permute-start | bytes 1572872 | tf_op jit(solution)/shard_map/ppermute | solution.py:117
  99.4 3.2 collective-permute-start.10
  99.4 15.4 %collective-permute-start.14 = (bf16[512,512]{1,0:T(8,128)(2,1)}, bf16[512,512]{1,0:T(8,128)(2,1)S(1)}, u32[]{:S(2)}, u32[]{:S(2)}) collective-permute-start(bf16[512,512]{1,0:T(8,128)(2,1)} %get-tuple-element.300.refs_2_.refs_4_), channel_id=1, source_target_pairs={{0,2},{1,3},{2,0},{3,1},{4,6},{5,7},{6,4},{7,5},{8,10},{9,11},{10,... | collective-permute-start | bytes 1572872 | tf_op jit(solution)/shard_map/ppermute | solution.py:117
  102.4 13.0 %collective-permute-start.13 = (bf16[512,512]{1,0:T(8,128)(2,1)S(1)}, bf16[512,512]{1,0:T(8,128)(2,1)S(1)}, u32[]{:S(2)}, u32[]{:S(2)}) collective-permute-start(bf16[512,512]{1,0:T(8,128)(2,1)S(1)} %copy-done.30), channel_id=1, source_target_pairs={{0,1},{1,0},{2,3},{3,2},{4,5},{5,4},{6,7},{7,6},{8,9},{9,8},{10,11... | collective-permute-start | bytes 1572872 | tf_op jit(solution)/shard_map/ppermute | solution.py:117
  114.8 2.0 collective-permute-start.15
  115.2 14.7 %collective-permute-start.16 = (bf16[256,2048]{1,0:T(8,128)(2,1)S(1)}, bf16[256,2048]{1,0:T(8,128)(2,1)S(1)}, u32[]{:S(2)}, u32[]{:S(2)}) collective-permute-start(bf16[256,2048]{1,0:T(8,128)(2,1)S(1)} %copy-done.3), channel_id=1, source_target_pairs={{0,1},{1,0},{2,3},{3,2},{4,5},{5,4},{6,7},{7,6},{8,9},{9,8},{10,11... | collective-permute-start | bytes 3145736 | tf_op jit(solution)/shard_map/ppermute | solution.py:117
  129.6 2.7 collective-permute-start.17
  186.3 513.0 %reduce-scatter.5.cloned.1.call-start = ((), (), s32[]{:S(2)}) async-start(), calls=%async_computation.3 | async-start | bytes 6488064 | tf_op jit(solution)/shard_map/reduce_scatter | solution.py:1195
  208.4 132.5 %collective-permute-start.18 = (bf16[1408,1024]{1,0:T(8,128)(2,1)}, bf16[1408,1024]{1,0:T(8,128)(2,1)}, u32[]{:S(2)}, u32[]{:S(2)}) collective-permute-start(bf16[1408,1024]{1,0:T(8,128)(2,1)} %get-tuple-element.215), channel_id=1, source_target_pairs={{0,4},{4,0},{8,12},{12,8},{16,20},{20,16},{24,28},{28,24},{1,5},{5... | collective-permute-start | bytes 8650760 | tf_op jit(solution)/shard_map/ppermute | solution.py:117
  231.2 149.4 %collective-permute-start.20 = (bf16[1024,1408]{1,0:T(8,128)(2,1)}, bf16[1024,1408]{1,0:T(8,128)(2,1)}, u32[]{:S(2)}, u32[]{:S(2)}) collective-permute-start(bf16[1024,1408]{1,0:T(8,128)(2,1)} %get-tuple-element.241), channel_id=1, source_target_pairs={{0,4},{4,0},{8,12},{12,8},{16,20},{20,16},{24,28},{28,24},{1,5},{5... | collective-permute-start | bytes 8650760 | tf_op jit(solution)/shard_map/ppermute | solution.py:117
  276.2 181.1 %collective-permute-start.19 = (bf16[1024,1408]{1,0:T(8,128)(2,1)}, bf16[1024,1408]{1,0:T(8,128)(2,1)S(1)}, u32[]{:S(2)}, u32[]{:S(2)}) collective-permute-start(bf16[1024,1408]{1,0:T(8,128)(2,1)} %get-tuple-element.238), channel_id=1, source_target_pairs={{0,4},{4,0},{8,12},{12,8},{16,20},{20,16},{24,28},{28,24},{1,5},{5... | collective-permute-start | bytes 8650760 | tf_op jit(solution)/shard_map/ppermute | solution.py:117
  344.0 40.5 %collective-permute-start.22 = (bf16[1408,512]{1,0:T(8,128)(2,1)}, bf16[1408,512]{1,0:T(8,128)(2,1)}, u32[]{:S(2)}, u32[]{:S(2)}) collective-permute-start(bf16[1408,512]{1,0:T(8,128)(2,1)} %add_convert_fusion.7), channel_id=1, source_target_pairs={{0,8},{4,12},{8,0},{12,4},{16,24},{20,28},{24,16},{28,20},{1,9},{5... | collective-permute-start | bytes 4325384 | tf_op jit(solution)/shard_map/ppermute | solution.py:117
  382.7 52.2 %collective-permute-start.21 = (bf16[512,1408]{1,0:T(8,128)(2,1)S(1)}, bf16[512,1408]{1,0:T(8,128)(2,1)S(1)}, u32[]{:S(2)}, u32[]{:S(2)}) collective-permute-start(bf16[512,1408]{1,0:T(8,128)(2,1)S(1)} %add_convert_fusion.6), channel_id=1, source_target_pairs={{0,8},{4,12},{8,0},{12,4},{16,24},{20,28},{24,16},{28,20},{1,9},{5... | collective-permute-start | bytes 4325384 | tf_op jit(solution)/shard_map/ppermute | solution.py:117
  386.3 73.0 %collective-permute-start.23 = (bf16[1408,256]{1,0:T(8,128)(2,1)S(1)}, bf16[1408,256]{1,0:T(8,128)(2,1)S(1)}, u32[]{:S(2)}, u32[]{:S(2)}) collective-permute-start(bf16[1408,256]{1,0:T(8,128)(2,1)S(1)} %add_convert_fusion.20), channel_id=1, source_target_pairs={{0,24},{4,28},{8,16},{12,20},{16,8},{20,12},{24,0},{28,4},{1,25},{... | collective-permute-start | bytes 2162696 | tf_op jit(solution)/shard_map/ppermute | solution.py:117
  478.9 472.7 %all-reduce.3.cloned.1.call-start = ((), (), s32[]{:S(2)}) async-start(), calls=%async_computation.4 | async-start | bytes 262144 | tf_op jit(solution)/shard_map/psum | solution.py:1395
  479.6 2.9 collective-permute-start.28
  482.0 81.1 %collective-permute-start.25 = (bf16[1024,1408]{1,0:T(8,128)(2,1)}, bf16[1024,1408]{1,0:T(8,128)(2,1)}, u32[]{:S(2)}, u32[]{:S(2)}) collective-permute-start(bf16[1024,1408]{1,0:T(8,128)(2,1)} %get-tuple-element.261), channel_id=1, source_target_pairs={{0,4},{4,0},{8,12},{12,8},{16,20},{20,16},{24,28},{28,24},{1,5},{5... | collective-permute-start | bytes 8650760 | tf_op jit(solution)/shard_map/ppermute | solution.py:117
  482.4 29.0 %collective-permute-start.27 = (bf16[256,2048]{1,0:T(8,128)(2,1)}, bf16[256,2048]{1,0:T(8,128)(2,1)}, u32[]{:S(2)}, u32[]{:S(2)}) collective-permute-start(bf16[256,2048]{1,0:T(8,128)(2,1)} %get-tuple-element.265), channel_id=1, source_target_pairs={{0,1},{1,0},{2,3},{3,2},{4,5},{5,4},{6,7},{7,6},{8,9},{9,8},{10,11... | collective-permute-start | bytes 3145736 | tf_op jit(solution)/shard_map/ppermute | solution.py:117
  483.8 25.8 %collective-permute-start.29 = (bf16[256,2048]{1,0:T(8,128)(2,1)}, bf16[256,2048]{1,0:T(8,128)(2,1)}, u32[]{:S(2)}, u32[]{:S(2)}) collective-permute-start(bf16[256,2048]{1,0:T(8,128)(2,1)} %add_convert_fusion.12), channel_id=1, source_target_pairs={{0,2},{1,3},{2,0},{3,1},{4,6},{5,7},{6,4},{7,5},{8,10},{9,11},{10,... | collective-permute-start | bytes 3145736 | tf_op jit(solution)/shard_map/ppermute | solution.py:117
  488.6 63.8 %collective-permute-start.26 = (bf16[256,1408]{1,0:T(8,128)(2,1)S(1)}, bf16[256,1408]{1,0:T(8,128)(2,1)S(1)}, u32[]{:S(2)}, u32[]{:S(2)}) collective-permute-start(bf16[256,1408]{1,0:T(8,128)(2,1)S(1)} %copy-done.50), channel_id=1, source_target_pairs={{0,24},{4,28},{8,16},{12,20},{16,8},{20,12},{24,0},{28,4},{1,25},{... | collective-permute-start | bytes 2162696 | tf_op jit(solution)/shard_map/ppermute | solution.py:117
  489.0 95.8 %collective-permute-start.24 = (bf16[512,1408]{1,0:T(8,128)(2,1)S(1)}, bf16[512,1408]{1,0:T(8,128)(2,1)}, u32[]{:S(2)}, u32[]{:S(2)}) collective-permute-start(bf16[512,1408]{1,0:T(8,128)(2,1)S(1)} %copy-done.31), channel_id=1, source_target_pairs={{0,8},{4,12},{8,0},{12,4},{16,24},{20,28},{24,16},{28,20},{1,9},{5... | collective-permute-start | bytes 4325384 | tf_op jit(solution)/shard_map/ppermute | solution.py:117
  509.6 154.2 %collective-permute-start.37 = (bf16[1408,1024]{1,0:T(8,128)(2,1)}, bf16[1408,1024]{1,0:T(8,128)(2,1)}, u32[]{:S(2)}, u32[]{:S(2)}) collective-permute-start(bf16[1408,1024]{1,0:T(8,128)(2,1)} %get-tuple-element.292), channel_id=1, source_target_pairs={{0,4},{4,0},{8,12},{12,8},{16,20},{20,16},{24,28},{28,24},{1,5},{5... | collective-permute-start | bytes 8650760 | tf_op jit(solution)/shard_map/ppermute | solution.py:117
  513.9 49.3 %copy-start.27 = (bf16[1024,1408]{1,0:T(8,128)(2,1)S(1)}, bf16[1024,1408]{1,0:T(8,128)(2,1)}, u32[]{:S(2)}) copy-start(bf16[1024,1408]{1,0:T(8,128)(2,1)} %get-tuple-element.229) | copy-start | bytes 8650756
  518.0 69.8 %copy-start.14 = (bf16[256,2048]{1,0:T(8,128)(2,1)}, bf16[256,2048]{1,0:T(8,128)(2,1)S(1)}, u32[]{:S(2)}) copy-start(bf16[256,2048]{1,0:T(8,128)(2,1)S(1)} %get-tuple-element.380.refs_0_) | copy-start | bytes 3145732
  518.0 72.4 %collective-permute-start.33 = (bf16[256,2048]{1,0:T(8,128)(2,1)S(1)}, bf16[256,2048]{1,0:T(8,128)(2,1)S(1)}, u32[]{:S(2)}, u32[]{:S(2)}) collective-permute-start(bf16[256,2048]{1,0:T(8,128)(2,1)S(1)} %get-tuple-element.380.refs_0_), channel_id=1, source_target_pairs={{0,2},{1,3},{2,0},{3,1},{4,6},{5,7},{6,4},{7,5},{8,10},{9,11},{10,... | collective-permute-start | bytes 3145736 | tf_op jit(solution)/shard_map/ppermute | solution.py:117
  587.7 6.2 collective-permute-start.31
  587.8 7.5 collective-permute-start.32
  588.4 60.8 %collective-permute-start.38 = (bf16[512,1408]{1,0:T(8,128)(2,1)}, bf16[512,1408]{1,0:T(8,128)(2,1)}, u32[]{:S(2)}, u32[]{:S(2)}) collective-permute-start(bf16[512,1408]{1,0:T(8,128)(2,1)} %add_convert_fusion.4), channel_id=1, source_target_pairs={{0,8},{4,12},{8,0},{12,4},{16,24},{20,28},{24,16},{28,20},{1,9},{5... | collective-permute-start | bytes 4325384 | tf_op jit(solution)/shard_map/ppermute | solution.py:117
  590.4 5.1 collective-permute-start.34
  593.9 72.1 %collective-permute-start.36 = (bf16[256,1408]{1,0:T(8,128)(2,1)}, bf16[256,1408]{1,0:T(8,128)(2,1)}, u32[]{:S(2)}, u32[]{:S(2)}) collective-permute-start(bf16[256,1408]{1,0:T(8,128)(2,1)} %add_convert_fusion.18), channel_id=1, source_target_pairs={{0,24},{4,28},{8,16},{12,20},{16,8},{20,12},{24,0},{28,4},{1,25},{... | collective-permute-start | bytes 2162696 | tf_op jit(solution)/shard_map/ppermute | solution.py:117
  595.3 99.8 %collective-permute-start.30 = (bf16[256,2048]{1,0:T(8,128)(2,1)}, bf16[256,2048]{1,0:T(8,128)(2,1)}, u32[]{:S(2)}, u32[]{:S(2)}) collective-permute-start(bf16[256,2048]{1,0:T(8,128)(2,1)} %get-tuple-element.277), channel_id=1, source_target_pairs={{0,1},{1,0},{2,3},{3,2},{4,5},{5,4},{6,7},{7,6},{8,9},{9,8},{10,11... | collective-permute-start | bytes 3145736 | tf_op jit(solution)/shard_map/ppermute | solution.py:117
  595.5 114.4 %collective-permute-start.44 = (bf16[1024,1408]{1,0:T(8,128)(2,1)}, bf16[1024,1408]{1,0:T(8,128)(2,1)}, u32[]{:S(2)}, u32[]{:S(2)}) collective-permute-start(bf16[1024,1408]{1,0:T(8,128)(2,1)} %get-tuple-element.320), channel_id=1, source_target_pairs={{0,4},{4,0},{8,12},{12,8},{16,20},{20,16},{24,28},{28,24},{1,5},{5... | collective-permute-start | bytes 8650760 | tf_op jit(solution)/shard_map/ppermute | solution.py:117
  649.2 25.6 %collective-permute-start.35 = (bf16[256,2048]{1,0:T(8,128)(2,1)}, bf16[256,2048]{1,0:T(8,128)(2,1)}, u32[]{:S(2)}, u32[]{:S(2)}) collective-permute-start(bf16[256,2048]{1,0:T(8,128)(2,1)} %add_convert_fusion.11), channel_id=1, source_target_pairs={{0,2},{1,3},{2,0},{3,1},{4,6},{5,7},{6,4},{7,5},{8,10},{9,11},{10,... | collective-permute-start | bytes 3145736 | tf_op jit(solution)/shard_map/ppermute | solution.py:117
  666.0 34.6 %collective-permute-start.41 = (bf16[1408,512]{1,0:T(8,128)(2,1)S(1)}, bf16[1408,512]{1,0:T(8,128)(2,1)}, u32[]{:S(2)}, u32[]{:S(2)}) collective-permute-start(bf16[1408,512]{1,0:T(8,128)(2,1)S(1)} %add_convert_fusion.3), channel_id=1, source_target_pairs={{0,8},{4,12},{8,0},{12,4},{16,24},{20,28},{24,16},{28,20},{1,9},{5... | collective-permute-start | bytes 4325384 | tf_op jit(solution)/shard_map/ppermute | solution.py:117
  669.0 30.2 %collective-permute-start.42 = (bf16[256,1408]{1,0:T(8,128)(2,1)}, bf16[256,1408]{1,0:T(8,128)(2,1)}, u32[]{:S(2)}, u32[]{:S(2)}) collective-permute-start(bf16[256,1408]{1,0:T(8,128)(2,1)} %add_convert_fusion.17), channel_id=1, source_target_pairs={{0,24},{4,28},{8,16},{12,20},{16,8},{20,12},{24,0},{28,4},{1,25},{... | collective-permute-start | bytes 2162696 | tf_op jit(solution)/shard_map/ppermute | solution.py:117
  674.8 110.0 %collective-permute-start.45 = (bf16[1024,1536]{1,0:T(8,128)(2,1)}, bf16[1024,1536]{1,0:T(8,128)(2,1)}, u32[]{:S(2)}, u32[]{:S(2)}) collective-permute-start(bf16[1024,1536]{1,0:T(8,128)(2,1)} %get-tuple-element.326), channel_id=1, source_target_pairs={{0,8},{4,12},{8,0},{12,4},{16,24},{20,28},{24,16},{28,20},{1,9},{5... | collective-permute-start | bytes 9437192 | tf_op jit(solution)/shard_map/ppermute | solution.py:117
  695.1 137.8 %collective-permute-start.47 = (bf16[1408,1024]{1,0:T(8,128)(2,1)}, bf16[1408,1024]{1,0:T(8,128)(2,1)}, u32[]{:S(2)}, u32[]{:S(2)}) collective-permute-start(bf16[1408,1024]{1,0:T(8,128)(2,1)} %get-tuple-element.330), channel_id=1, source_target_pairs={{0,4},{4,0},{8,12},{12,8},{16,20},{20,16},{24,28},{28,24},{1,5},{5... | collective-permute-start | bytes 8650760 | tf_op jit(solution)/shard_map/ppermute | solution.py:117
  717.5 140.3 %collective-permute-start.39 = (bf16[256,2048]{1,0:T(8,128)(2,1)}, bf16[256,2048]{1,0:T(8,128)(2,1)S(1)}, u32[]{:S(2)}, u32[]{:S(2)}) collective-permute-start(bf16[256,2048]{1,0:T(8,128)(2,1)} %get-tuple-element.310), channel_id=1, source_target_pairs={{0,1},{1,0},{2,3},{3,2},{4,5},{5,4},{6,7},{7,6},{8,9},{9,8},{10,11... | collective-permute-start | bytes 3145736 | tf_op jit(solution)/shard_map/ppermute | solution.py:117
  717.6 72.7 %collective-permute-start.40 = (bf16[256,2048]{1,0:T(8,128)(2,1)}, bf16[256,2048]{1,0:T(8,128)(2,1)S(1)}, u32[]{:S(2)}, u32[]{:S(2)}) collective-permute-start(bf16[256,2048]{1,0:T(8,128)(2,1)} %get-tuple-element.313), channel_id=1, source_target_pairs={{0,1},{1,0},{2,3},{3,2},{4,5},{5,4},{6,7},{7,6},{8,9},{9,8},{10,11... | collective-permute-start | bytes 3145736 | tf_op jit(solution)/shard_map/ppermute | solution.py:117
  718.1 70.4 %collective-permute-start.49 = (bf16[1408,256]{1,0:T(8,128)(2,1)}, bf16[1408,256]{1,0:T(8,128)(2,1)S(1)}, u32[]{:S(2)}, u32[]{:S(2)}) collective-permute-start(bf16[1408,256]{1,0:T(8,128)(2,1)} %add_convert_fusion.16), channel_id=1, source_target_pairs={{0,24},{4,28},{8,16},{12,20},{16,8},{20,12},{24,0},{28,4},{1,25},{... | collective-permute-start | bytes 2162696 | tf_op jit(solution)/shard_map/ppermute | solution.py:117
  784.8 46.0 %collective-permute-start.48 = (bf16[512,1408]{1,0:T(8,128)(2,1)}, bf16[512,1408]{1,0:T(8,128)(2,1)S(1)}, u32[]{:S(2)}, u32[]{:S(2)}) collective-permute-start(bf16[512,1408]{1,0:T(8,128)(2,1)} %add_convert_fusion.2), channel_id=1, source_target_pairs={{0,8},{4,12},{8,0},{12,4},{16,24},{20,28},{24,16},{28,20},{1,9},{5... | collective-permute-start | bytes 4325384 | tf_op jit(solution)/shard_map/ppermute | solution.py:117
  789.6 125.7 %collective-permute-start.46 = (bf16[512,1024]{1,0:T(8,128)(2,1)S(1)}, bf16[512,1024]{1,0:T(8,128)(2,1)S(1)}, u32[]{:S(2)}, u32[]{:S(2)}) collective-permute-start(bf16[512,1024]{1,0:T(8,128)(2,1)S(1)} %copy-done.68), channel_id=1, source_target_pairs={{0,4},{4,0},{8,12},{12,8},{16,20},{20,16},{24,28},{28,24},{1,5},{5... | collective-permute-start | bytes 3145736 | tf_op jit(solution)/shard_map/ppermute | solution.py:117
  790.3 75.5 %collective-permute-start.51 = (bf16[512,1536]{1,0:T(8,128)(2,1)S(1)}, bf16[512,1536]{1,0:T(8,128)(2,1)S(1)}, u32[]{:S(2)}, u32[]{:S(2)}) collective-permute-start(bf16[512,1536]{1,0:T(8,128)(2,1)S(1)} %add_convert_fusion), channel_id=1, source_target_pairs={{0,4},{4,0},{8,12},{12,8},{16,20},{20,16},{24,28},{28,24},{1,5},{5... | collective-permute-start | bytes 4718600 | tf_op jit(solution)/shard_map/ppermute | solution.py:117
  830.8 24.6 %collective-permute-start.43 = (bf16[256,2048]{1,0:T(8,128)(2,1)S(1)}, bf16[256,2048]{1,0:T(8,128)(2,1)S(1)}, u32[]{:S(2)}, u32[]{:S(2)}) collective-permute-start(bf16[256,2048]{1,0:T(8,128)(2,1)S(1)} %add_convert_fusion.9), channel_id=1, source_target_pairs={{0,2},{1,3},{2,0},{3,1},{4,6},{5,7},{6,4},{7,5},{8,10},{9,11},{10,... | collective-permute-start | bytes 3145736 | tf_op jit(solution)/shard_map/ppermute | solution.py:117
  832.9 32.9 %collective-permute-start.52 = (bf16[256,1408]{1,0:T(8,128)(2,1)S(1)}, bf16[256,1408]{1,0:T(8,128)(2,1)S(1)}, u32[]{:S(2)}, u32[]{:S(2)}) collective-permute-start(bf16[256,1408]{1,0:T(8,128)(2,1)S(1)} %add_convert_fusion.15), channel_id=1, source_target_pairs={{0,24},{4,28},{8,16},{12,20},{16,8},{20,12},{24,0},{28,4},{1,25},{... | collective-permute-start | bytes 2162696 | tf_op jit(solution)/shard_map/ppermute | solution.py:117
  855.4 57.0 %collective-permute-start.50 = (bf16[1408,512]{1,0:T(8,128)(2,1)S(1)}, bf16[1408,512]{1,0:T(8,128)(2,1)S(1)}, u32[]{:S(2)}, u32[]{:S(2)}) collective-permute-start(bf16[1408,512]{1,0:T(8,128)(2,1)S(1)} %add_convert_fusion.1), channel_id=1, source_target_pairs={{0,8},{4,12},{8,0},{12,4},{16,24},{20,28},{24,16},{28,20},{1,9},{5... | collective-permute-start | bytes 4325384 | tf_op jit(solution)/shard_map/ppermute | solution.py:117
  867.2 51.8 %collective-permute-start.55 = (bf16[256,1536]{1,0:T(8,128)(2,1)S(1)}, bf16[256,1536]{1,0:T(8,128)(2,1)S(1)}, u32[]{:S(2)}, u32[]{:S(2)}) collective-permute-start(bf16[256,1536]{1,0:T(8,128)(2,1)S(1)} %add_convert_fusion.13), channel_id=1, source_target_pairs={{0,24},{4,28},{8,16},{12,20},{16,8},{20,12},{24,0},{28,4},{1,25},{... | collective-permute-start | bytes 2359304 | tf_op jit(solution)/shard_map/ppermute | solution.py:117
  915.3 23.6 %collective-permute-start.54 = (bf16[1408,256]{1,0:T(8,128)(2,1)}, bf16[1408,256]{1,0:T(8,128)(2,1)}, u32[]{:S(2)}, u32[]{:S(2)}) collective-permute-start(bf16[1408,256]{1,0:T(8,128)(2,1)} %add_convert_fusion.14), channel_id=1, source_target_pairs={{0,24},{4,28},{8,16},{12,20},{16,8},{20,12},{24,0},{28,4},{1,25},{... | collective-permute-start | bytes 2162696 | tf_op jit(solution)/shard_map/ppermute | solution.py:117
  916.4 25.6 %collective-permute-start.53 = (bf16[512,512]{1,0:T(8,128)(2,1)}, bf16[512,512]{1,0:T(8,128)(2,1)}, u32[]{:S(2)}, u32[]{:S(2)}) collective-permute-start(bf16[512,512]{1,0:T(8,128)(2,1)} %add_convert_fusion.21), channel_id=1, source_target_pairs={{0,8},{4,12},{8,0},{12,4},{16,24},{20,28},{24,16},{28,20},{1,9},{5... | collective-permute-start | bytes 1572872 | tf_op jit(solution)/shard_map/ppermute | solution.py:117
  943.1 6.6 collective-permute-start.56
  (67 other events, 639.4 us)
Sparse Core Ops, SparseCore 0:
  18.4 50.5 all-gather.2
  186.4 133.3 reduce-scatter.2
  479.0 183.1 reduce-scatter.4
  717.6 151.6 all-reduce.2

commit v5 on v3

--- a/solution.py
+++ b/solution.py
@@ -27,6 +27,7 @@
 WHOLE = ("Sg", "1u")
 SECOND_FIRST = ()
 PLAN = {
+    "Sg": "Sg+",
     "Sd": "Sd+",
     "Su": "Su+",
     "0g": "0g+",
@@ -35,16 +36,15 @@
     "back": "Su- Su+",
     "1g": "0g- Sd- 0g+",
     "n1": "0d+",
+    "1u": "1u+",
     "norm": "Su-",
     "h": " ".join(["0u- 0u+ 0g- 0g+", "1g+"]),
-    "q": "0u- 0u+",
-    "o": "0d- 1d+ 0g- 0d+",
-    "Sg": "Sg+",
-    "1u": "1u+",
+    "q": " ".join(["0u- 0u+ 0d- q+", "0g- 0d+"]),
     "fb": "1u-",
-    "r1": "0u- 0d- 0d+",
-    "r2": "1g- 1g+ q+",
-    "fin": " ".join(["0d- 1g- 1g+ 1d-", "1d+ o+ 1g- 1d-", "1d+ q- q+ 1d-", "o- o+ q- q+", "o- o+ q- o-"]),
+    "r1": "0u- 1d+ 0d-",
+    "r2": "0d+ 1g- 1g+",
+    "fin": " ".join(["0d- o+ 1g- 1g+", "q- q+ 1g- q-", "q+ 1d- 1d+ q-"]),
+    "end": " ".join(["o- o+ 1d- 1d+", "o- o+ 1d- o-"]),
 }
 
 
@@ -1269,8 +1269,8 @@
         normed, side, cot_blocks, shared_gate_up, shared_down, expert_count
     )
     mark(act)
+    weight_total("Sg", normed, gate_grad, True)
     weight_total("Sd", out_grad, act, False)
-    weight_total("Sg", normed, gate_grad, True)
     weight_total("Su", normed, up_grad, True)
     acts, grads, expert_rows = [], [], []
 
@@ -1391,6 +1391,8 @@
     ).astype(BF16)
     moves("fin")
     small_sums = then(small_sums)
+    mark(small_sums)
+    moves("end")
 
     expert_totals = [
         [sums[f"{e}{side}"].result() for side in "gud"] for e in range(local)

time: 917 us -> 908 us (level)
  starting transfers between devices: 76.6 us -> 50.7 us
    ppermute x57, waiting for transfers between devices: 295 us -> 323 us  [swap(): return lax.ppermute(values, axis, pairs)]
    ppermute x57, starting transfers between devices: 76.4 us -> 50.5 us  [swap(): return lax.ppermute(values, axis, pairs)]
    reduce_scatter x2, waiting for transfers between devices: 18.5 us -> 0.02 us  [start(): lax.psum_scatter(then(self.sent), 'dp', scatter_dimension=0, tiled=True)]
  transfers between devices with their start and end apart: 61 -> 61, of which waited for: 26 -> 24; matrix products, arithmetic and copies ran while one was open for 10% -> 11% of each run, Pallas kernels for 36% -> 38%
where the time goes in v5:
time: 908 us; the launch traced here: 900 us
  Pallas kernels  394 us (43%)
  waiting for transfers between devices  323 us (36%)
  other arithmetic  92.6 us (10%)
  starting transfers between devices  50.7 us (6%)
  local copies, waits for them, and re-layouts  25.2 us (3%)
  between operations  14.7 us (2%)
    pallas_call x26, Pallas kernels, kernel_call(): pl.pallas_call(body, name=name, grid_spec=pltpu.PrefetchScalarGridSpec(nu...  394 us
    ppermute x57, waiting for transfers between devices, swap(): return lax.ppermute(values, axis, pairs)  323 us
    ppermute x57, starting transfers between devices, swap(): return lax.ppermute(values, axis, pairs)  50.5 us
    convert_element_type x18, other arithmetic, collect(): self.sent = self.part(self.size, 2 * self.size).astype(BF16)  40 us
  transfers between devices with their start and end apart: 61, of which 24 were waited for; matrix products, arithmetic and copies ran while one was open for 11% of the time, Pallas kernels for 38%

profile of v5, /device:TPU:8, one launch (start us, length us, event | category | flops | bytes accessed | tf_op | source)
XLA Modules:
  0.0 900.0 jit_solution(12183692666929566372)
XLA Ops:
  12.4 4.0 collective-permute-done.2.refs_2_
  21.0 2.8 collective-permute-done.1.refs_1_
  24.3 7.0 prepare.1
  31.3 12.5 %collective-permute-done.refs_0_.refs_3_ = bf16[256,2048]{1,0:T(8,128)(2,1)S(1)} collective-permute-done((bf16[256,2048]{1,0:T(8,128)(2,1)}, bf16[256,2048]{1,0:T(8,128)(2,1)S(1)}, u32[]{:S(2)}, u32[]{:S(2)}) %collective-permute-start) | collective-permute-done | bytes 1048608 | tf_op jit(solution)/shard_map/ppermute | solution.py:115
  48.9 9.8 %project.2 = (bf16[3,1024,512]{2,1,0:T(8,128)(2,1)}, bf16[1024,2048]{1,0:T(8,128)(2,1)}) custom-call(bf16[256,2048]{1,0:T(8,128)(2,1)} %refs_1_, bf16[256,2048]{1,0:T(8,128)(2,1)} %copy-done.12, bf16[1,2048]{1,0:T(2,128)(2,1)} %broadcast_in_dim.45.refs_2_, bf16[3,2048,512]{2,1,0:T(8,128)(2,1)} %refs_0_.3, bf16[3,1,512]{2,1,0:T(2,128)(2,1)} %copy.47.refs_4_, ...), custom_call_target="tpu_custom_call" | custom-call | flops 1 | bytes 1 | tf_op jit(solution)/shard_map/project/pallas_call | solution.py:68
  59.7 9.4 %project.3 = (bf16[3,1024,512]{2,1,0:T(8,128)(2,1)}, bf16[1024,2048]{1,0:T(8,128)(2,1)}) custom-call(bf16[256,2048]{1,0:T(8,128)(2,1)} %copy-done.8, bf16[256,2048]{1,0:T(8,128)(2,1)} %copy-done.10, bf16[1,2048]{1,0:T(2,128)(2,1)} %broadcast_in_dim.45.refs_2_, bf16[3,2048,512]{2,1,0:T(8,128)(2,1)} %refs_0_.3, ...), custom_call_target="tpu_custom_call", output_to_operand_aliasing={{0}: (7, {}), {1}: (8, {})} | custom-call | flops 1 | bytes 1 | tf_op jit(solution)/shard_map/project/pallas_call | solution.py:68
  69.1 9.5 %attend.2 = (bf16[512,512]{1,0:T(8,128)(2,1)}, f32[4,512,1]{2,1,0:T(8,128)}) custom-call(s32[4]{0:T(128)} %iota_xor_fusion.places, bf16[3,1024,512]{2,1,0:T(8,128)(2,1)} %get-tuple-element.191.query.key.value, bf16[3,1024,512]{2,1,0:T(8,128)(2,1)} %get-tuple-element.191.query.key.value, bf16[3,1024,512]{2,1,0:T(8,128)(2,1)} %get-tuple-element.191.query.key.value, ...), custom_call_target="tpu_custom_call" | custom-call | flops 1 | bytes 1 | tf_op jit(solution)/shard_map/attend/pallas_call | solution.py:68
  78.7 6.7 attend.3
  86.3 13.5 %collective-permute-done.9.refs_4_ = bf16[512,512]{1,0:T(8,128)(2,1)S(1)} collective-permute-done((bf16[512,512]{1,0:T(8,128)(2,1)S(1)}, bf16[512,512]{1,0:T(8,128)(2,1)S(1)}, u32[]{:S(2)}, u32[]{:S(2)}) %collective-permute-start.9) | collective-permute-done | bytes 524320 | tf_op jit(solution)/shard_map/ppermute | solution.py:115
  103.0 12.1 %out_project.2 = (bf16[1024,2048]{1,0:T(8,128)(2,1)}, f32[1024,128]{1,0:T(8,128)}, f32[256,2048]{1,0:T(8,128)}) custom-call(bf16[256,2048]{1,0:T(8,128)(2,1)} %refs_1_, bf16[256,2048]{1,0:T(8,128)(2,1)} %copy-done.12, bf16[512,512]{1,0:T(8,128)(2,1)} %get-tuple-element.302.refs_2_.refs_4_, bf16[512,512]{1,0:T(8,128)(2,1)} %collective-permute-done.8.refs_3_, ...), custom_call_target="tpu_custom_call" | custom-call | flops 1 | bytes 1 | tf_op jit(solution)/shard_map/out_project/pallas_call | solution.py:68
  117.9 11.9 %out_project.3 = (bf16[1024,2048]{1,0:T(8,128)(2,1)}, f32[1024,128]{1,0:T(8,128)}, f32[256,2048]{1,0:T(8,128)}) custom-call(bf16[256,2048]{1,0:T(8,128)(2,1)} %copy-done.8, bf16[256,2048]{1,0:T(8,128)(2,1)} %copy-done.10, bf16[512,512]{1,0:T(8,128)(2,1)} %get-tuple-element.198.refs_2_.refs_5_, ...), custom_call_target="tpu_custom_call", output_to_operand_aliasing={{0}: (12, {}), {1}: (13, {})} | custom-call | flops 1 | bytes 1 | tf_op jit(solution)/shard_map/out_project/pallas_call | solution.py:68
  133.6 29.0 %shared_inner.1 = (bf16[1024,1408]{1,0:T(8,128)(2,1)}, bf16[1024,1408]{1,0:T(8,128)(2,1)}, bf16[1024,1408]{1,0:T(8,128)(2,1)}, bf16[1024,2048]{1,0:T(8,128)(2,1)}) custom-call(bf16[1024,2048]{1,0:T(8,128)(2,1)} %get-tuple-element.232.refs_0_.refs_6_, f32[1024,128]{1,0:T(8,128)} %get-tuple-element.206.refs_1_.side, bf16[256,2048]{1,0:T(8,128)(2,1)} %refs_4_.1, ...), custom_call_target="tpu_custom_call" | custom-call | flops 1 | bytes 1 | tf_op jit(solution)/shard_map/shared_inner/pallas_call | solution.py:68
  163.1 12.7 %weight_product.11 = bf16[2048,1408]{1,0:T(8,128)(2,1)} custom-call(s32[8]{0:T(128)} %iota.10.blocks, bf16[1024,2048]{1,0:T(8,128)(2,1)} %get-tuple-element.232.refs_0_.refs_6_, bf16[1024,1408]{1,0:T(8,128)(2,1)} %get-tuple-element.249.refs_1_.gate_grad), custom_call_target="tpu_custom_call" | custom-call | flops 1 | bytes 1 | tf_op jit(solution)/shard_map/weight_product/pallas_call | solution.py:68
  177.0 13.6 %weight_product.12 = (bf16[1408,1024]{1,0:T(8,128)(2,1)}, bf16[1408,1024]{1,0:T(8,128)(2,1)}) custom-call(s32[8]{0:T(128)} %fusion.5.blocks, bf16[1024,2048]{1,0:T(8,128)(2,1)} %get-tuple-element.210.refs_0_, bf16[1024,1408]{1,0:T(8,128)(2,1)} %get-tuple-element.235.refs_1_.act), custom_call_target="tpu_custom_call" | custom-call | flops 1 | bytes 1 | tf_op jit(solution)/shard_map/weight_product/pallas_call | solution.py:68
  192.2 13.3 %weight_product.13 = (bf16[1024,1408]{1,0:T(8,128)(2,1)}, bf16[1024,1408]{1,0:T(8,128)(2,1)}) custom-call(s32[8]{0:T(128)} %fusion.5.blocks, bf16[1024,2048]{1,0:T(8,128)(2,1)} %get-tuple-element.232.refs_0_.refs_6_, bf16[1024,1408]{1,0:T(8,128)(2,1)} %get-tuple-element.217.refs_1_.up_grad), custom_call_target="tpu_custom_call" | custom-call | flops 1 | bytes 1 | tf_op jit(solution)/shard_map/weight_product/pallas_call | solution.py:68
  205.9 21.6 %expert_inner.2 = (bf16[576,1408]{1,0:T(8,128)(2,1)}, bf16[576,1408]{1,0:T(8,128)(2,1)}, bf16[576,1408]{1,0:T(8,128)(2,1)}, bf16[576,2048]{1,0:T(8,128)(2,1)}, bf16[576,2048]{1,0:T(8,128)(2,1)}) custom-call(s32[1]{0:T(128)} %bitcast.1.first, bf16[1024,2048]{1,0:T(8,128)(2,1)} %get-tuple-element.232.refs_0_.refs_6_, ...), custom_call_target="tpu_custom_call" | custom-call | flops 1 | bytes 1 | tf_op jit(solution)/shard_map/expert_inner/pallas_call | solution.py:68
  227.5 11.5 %weight_product.14 = (bf16[1024,1408]{1,0:T(8,128)(2,1)}, bf16[1024,1408]{1,0:T(8,128)(2,1)}) custom-call(s32[8]{0:T(128)} %fusion.5.blocks, bf16[576,2048]{1,0:T(8,128)(2,1)} %get-tuple-element.223.refs_0_, bf16[576,1408]{1,0:T(8,128)(2,1)} %get-tuple-element.226.refs_1_.refs_0_), custom_call_target="tpu_custom_call" | custom-call | flops 1 | bytes 1 | tf_op jit(solution)/shard_map/weight_product/pallas_call | solution.py:68
  240.6 11.5 %weight_product.15 = (bf16[1024,1408]{1,0:T(8,128)(2,1)}, bf16[1024,1408]{1,0:T(8,128)(2,1)}) custom-call(s32[8]{0:T(128)} %fusion.5.blocks, bf16[576,2048]{1,0:T(8,128)(2,1)} %get-tuple-element.223.refs_0_, bf16[576,1408]{1,0:T(8,128)(2,1)} %get-tuple-element.228.refs_1_), custom_call_target="tpu_custom_call" | custom-call | flops 1 | bytes 1 | tf_op jit(solution)/shard_map/weight_product/pallas_call | solution.py:68
  252.1 11.4 %weight_product.16 = (bf16[1408,1024]{1,0:T(8,128)(2,1)}, bf16[1408,1024]{1,0:T(8,128)(2,1)}) custom-call(s32[8]{0:T(128)} %fusion.5.blocks, bf16[576,2048]{1,0:T(8,128)(2,1)} %get-tuple-element.221.refs_0_, bf16[576,1408]{1,0:T(8,128)(2,1)} %get-tuple-element.230.refs_1_.refs_0_), custom_call_target="tpu_custom_call" | custom-call | flops 1 | bytes 1 | tf_op jit(solution)/shard_map/weight_product/pallas_call | solution.py:68
  263.5 22.0 %expert_inner.3 = (bf16[576,1408]{1,0:T(8,128)(2,1)}, bf16[576,1408]{1,0:T(8,128)(2,1)}, bf16[576,1408]{1,0:T(8,128)(2,1)}, bf16[576,2048]{1,0:T(8,128)(2,1)}, bf16[576,2048]{1,0:T(8,128)(2,1)}) custom-call(s32[1]{0:T(128)} %bitcast.1.first, bf16[1024,2048]{1,0:T(8,128)(2,1)} %get-tuple-element.232.refs_0_.refs_6_, ...), custom_call_target="tpu_custom_call" | custom-call | flops 1 | bytes 1 | tf_op jit(solution)/shard_map/expert_inner/pallas_call | solution.py:68
  285.6 3.0 add_convert_fusion.7
  289.1 35.9 %mix.1 = (bf16[256,2048]{1,0:T(8,128)(2,1)}, bf16[256,2048]{1,0:T(8,128)(2,1)}, bf16[256,2048]{1,0:T(8,128)(2,1)}, bf16[256,2048]{1,0:T(8,128)(2,1)}, f32[1024,128]{1,0:T(8,128)}) custom-call(s32[1]{0:T(128)} %bitcast.1.first, f32[1024,128]{1,0:T(8,128)} %get-tuple-element.206.refs_1_.side, bf16[1024,1408]{1,0:T(8,128)(2,1)} %get-tuple-element.235.refs_1_.act, ...), custom_call_target="tpu_custom_call" | custom-call | flops 1 | bytes 1 | tf_op jit(solution)/shard_map/mix/pallas_call | solution.py:68
  325.1 23.9 %collective-permute-done.20 = bf16[1024,1408]{1,0:T(8,128)(2,1)} collective-permute-done((bf16[1024,1408]{1,0:T(8,128)(2,1)}, bf16[1024,1408]{1,0:T(8,128)(2,1)}, u32[]{:S(2)}, u32[]{:S(2)}) %collective-permute-start.20) | collective-permute-done | bytes 2883616 | tf_op jit(solution)/shard_map/ppermute | solution.py:115
  353.3 2.9 collective-permute-start.23
  356.2 46.9 %back.1 = (bf16[256,2048]{1,0:T(8,128)(2,1)}, bf16[256,2048]{1,0:T(8,128)(2,1)}, bf16[256,2048]{1,0:T(8,128)(2,1)}, bf16[256,2048]{1,0:T(8,128)(2,1)}, f32[128,2048]{1,0:T(8,128)}) custom-call(f32[1024,128]{1,0:T(8,128)} %get-tuple-element.206.refs_1_.side, f32[1024,128]{1,0:T(8,128)} %get-tuple-element.243.totals, ...), custom_call_target="tpu_custom_call" | custom-call | flops 1 | bytes 1 | tf_op jit(solution)/shard_map/back/pallas_call | solution.py:68
  406.7 11.6 %weight_product.17 = (bf16[1024,1408]{1,0:T(8,128)(2,1)}, bf16[1024,1408]{1,0:T(8,128)(2,1)}) custom-call(s32[8]{0:T(128)} %fusion.5.blocks, bf16[576,2048]{1,0:T(8,128)(2,1)} %get-tuple-element.239.refs_0_, bf16[576,1408]{1,0:T(8,128)(2,1)} %get-tuple-element.253.refs_2_.refs_1_), custom_call_target="tpu_custom_call" | custom-call | flops 1 | bytes 1 | tf_op jit(solution)/shard_map/weight_product/pallas_call | solution.py:68
  421.8 10.8 %weight_product.18 = bf16[2048,1408]{1,0:T(8,128)(2,1)} custom-call(s32[8]{0:T(128)} %iota.11.blocks, bf16[576,2048]{1,0:T(8,128)(2,1)} %get-tuple-element.239.refs_0_, bf16[576,1408]{1,0:T(8,128)(2,1)} %get-tuple-element.270.refs_3_.refs_1_), custom_call_target="tpu_custom_call" | custom-call | flops 1 | bytes 1 | tf_op jit(solution)/shard_map/weight_product/pallas_call | solution.py:68
  436.5 2.7 add_convert_fusion.12
  446.5 18.6 %collective-permute-done.29 = bf16[256,2048]{1,0:T(8,128)(2,1)} collective-permute-done((bf16[256,2048]{1,0:T(8,128)(2,1)}, bf16[256,2048]{1,0:T(8,128)(2,1)}, u32[]{:S(2)}, u32[]{:S(2)}) %collective-permute-start.29) | collective-permute-done | bytes 1048608 | tf_op jit(solution)/shard_map/ppermute | solution.py:115
  468.2 3.9 fusion.6
  473.5 33.5 %collective-permute-done.26 = bf16[256,1408]{1,0:T(8,128)(2,1)S(1)} collective-permute-done((bf16[256,1408]{1,0:T(8,128)(2,1)S(1)}, bf16[256,1408]{1,0:T(8,128)(2,1)S(1)}, u32[]{:S(2)}, u32[]{:S(2)}) %collective-permute-start.26) | collective-permute-done | bytes 720928 | tf_op jit(solution)/shard_map/ppermute | solution.py:115
  507.0 11.8 %weight_product.19 = (bf16[1408,1024]{1,0:T(8,128)(2,1)}, bf16[1408,1024]{1,0:T(8,128)(2,1)}) custom-call(s32[8]{0:T(128)} %fusion.5.blocks, bf16[576,2048]{1,0:T(8,128)(2,1)} %get-tuple-element.261.refs_0_, bf16[576,1408]{1,0:T(8,128)(2,1)} %get-tuple-element.273.refs_1_), custom_call_target="tpu_custom_call" | custom-call | flops 1 | bytes 1 | tf_op jit(solution)/shard_map/weight_product/pallas_call | solution.py:68
  521.1 11.8 %collective-permute-done.24 = bf16[512,1408]{1,0:T(8,128)(2,1)} collective-permute-done((bf16[512,1408]{1,0:T(8,128)(2,1)S(1)}, bf16[512,1408]{1,0:T(8,128)(2,1)}, u32[]{:S(2)}, u32[]{:S(2)}) %collective-permute-start.24) | collective-permute-done | bytes 1441824 | tf_op jit(solution)/shard_map/ppermute | solution.py:115
  532.9 2.7 add_convert_fusion.18
  538.4 3.4 convert_add_fusion.2
  547.2 6.3 attended_gradient.1.out_grad
  553.5 22.0 %attend_back.1 = (bf16[1024,512]{1,0:T(8,128)(2,1)}, bf16[1024,512]{1,0:T(8,128)(2,1)}, bf16[1024,512]{1,0:T(8,128)(2,1)}, f32[3,8,512]{2,1,0:T(8,128)}) custom-call(s32[4]{0:T(128)} %iota_xor_fusion.places, bf16[3,1024,512]{2,1,0:T(8,128)(2,1)} %get-tuple-element.191.query.key.value, bf16[3,1024,512]{2,1,0:T(8,128)(2,1)} %get-tuple-element.191.query.key.value, ...), custom_call_target="tpu_custom_call" | custom-call | flops 1 | bytes 1 | tf_op jit(solution)/shard_map/attend_back/pallas_call | solution.py:68
  575.5 3.4 pad_maximum_fusion.1.refs_1_
  578.9 13.4 %weight_product.20 = (bf16[1024,1536]{1,0:T(8,128)(2,1)}, bf16[1024,1536]{1,0:T(8,128)(2,1)}) custom-call(s32[8]{0:T(128)} %fusion.5.blocks, bf16[1024,2048]{1,0:T(8,128)(2,1)} %get-tuple-element.294.refs_0_, bf16[1024,1536]{1,0:T(8,128)(2,1)} %pad_maximum_fusion.1.refs_1_), custom_call_target="tpu_custom_call" | custom-call | flops 1 | bytes 1 | tf_op jit(solution)/shard_map/weight_product/pallas_call | solution.py:68
  593.9 2.7 add_convert_fusion.17
  596.6 4.4 collective-permute-done.37
  601.0 3.1 add_convert_fusion.3
  609.3 9.4 %weight_product.21 = (bf16[512,1024]{1,0:T(8,128)(2,1)}, bf16[512,1024]{1,0:T(8,128)(2,1)}) custom-call(s32[8]{0:T(128)} %fusion.5.blocks, bf16[256,2048]{1,0:T(8,128)(2,1)} %copy-done.14, bf16[256,2048]{1,0:T(8,128)(2,1)} %copy-done.19, bf16[256,2048]{1,0:T(8,128)(2,1)} %copy-done.18, bf16[256,2048]{1,0:T(8,128)(2,1)} %copy-done.20, ...), custom_call_target="tpu_custom_call" | custom-call | flops 1 | bytes 1 | tf_op jit(solution)/shard_map/weight_product/pallas_call | solution.py:68
  618.7 12.6 %first_back.1 = (bf16[256,2048]{1,0:T(8,128)(2,1)}, bf16[256,2048]{1,0:T(8,128)(2,1)}, bf16[256,2048]{1,0:T(8,128)(2,1)}, bf16[256,2048]{1,0:T(8,128)(2,1)}, f32[8,2048]{1,0:T(8,128)}) custom-call(bf16[1024,512]{1,0:T(8,128)(2,1)} %get-tuple-element.304.query, bf16[1024,512]{1,0:T(8,128)(2,1)} %get-tuple-element.295.key, ...), custom_call_target="tpu_custom_call" | custom-call | flops 1 | bytes 1 | tf_op jit(solution)/shard_map/first_back/pallas_call | solution.py:68
  633.9 3.1 add_convert_fusion.10
  637.1 4.2 collective-permute-done.41
  641.3 2.7 add_convert_fusion.16
  643.9 18.9 %collective-permute-done.44 = bf16[1024,1408]{1,0:T(8,128)(2,1)} collective-permute-done((bf16[1024,1408]{1,0:T(8,128)(2,1)}, bf16[1024,1408]{1,0:T(8,128)(2,1)}, u32[]{:S(2)}, u32[]{:S(2)}) %collective-permute-start.44) | collective-permute-done | bytes 2883616 | tf_op jit(solution)/shard_map/ppermute | solution.py:115
  662.8 2.8 add_convert_fusion.2
  666.9 3.3 add_bitcast_fusion.3
  672.7 17.5 %collective-permute-done.47 = bf16[1408,256]{1,0:T(8,128)(2,1)S(1)} collective-permute-done((bf16[1408,256]{1,0:T(8,128)(2,1)}, bf16[1408,256]{1,0:T(8,128)(2,1)S(1)}, u32[]{:S(2)}, u32[]{:S(2)}) %collective-permute-start.47) | collective-permute-done | bytes 720928 | tf_op jit(solution)/shard_map/ppermute | solution.py:115
  694.0 17.9 %collective-permute-done.46 = bf16[512,1408]{1,0:T(8,128)(2,1)} collective-permute-done((bf16[512,1408]{1,0:T(8,128)(2,1)}, bf16[512,1408]{1,0:T(8,128)(2,1)}, u32[]{:S(2)}, u32[]{:S(2)}) %collective-permute-start.46) | collective-permute-done | bytes 1441824 | tf_op jit(solution)/shard_map/ppermute | solution.py:115
  715.0 15.9 %collective-permute-done.45 = bf16[1024,1536]{1,0:T(8,128)(2,1)} collective-permute-done((bf16[1024,1536]{1,0:T(8,128)(2,1)}, bf16[1024,1536]{1,0:T(8,128)(2,1)}, u32[]{:S(2)}, u32[]{:S(2)}) %collective-permute-start.45) | collective-permute-done | bytes 3145760 | tf_op jit(solution)/shard_map/ppermute | solution.py:115
  732.7 5.3 collective-permute-start.48
  741.8 19.9 %collective-permute-done.49 = bf16[256,1408]{1,0:T(8,128)(2,1)S(1)} collective-permute-done((bf16[256,1408]{1,0:T(8,128)(2,1)S(1)}, bf16[256,1408]{1,0:T(8,128)(2,1)S(1)}, u32[]{:S(2)}, u32[]{:S(2)}) %collective-permute-start.49) | collective-permute-done | bytes 720928 | tf_op jit(solution)/shard_map/ppermute | solution.py:115
  763.4 17.5 %collective-permute-done.48 = bf16[512,1536]{1,0:T(8,128)(2,1)S(1)} collective-permute-done((bf16[512,1536]{1,0:T(8,128)(2,1)S(1)}, bf16[512,1536]{1,0:T(8,128)(2,1)S(1)}, u32[]{:S(2)}, u32[]{:S(2)}) %collective-permute-start.48) | collective-permute-done | bytes 1572896 | tf_op jit(solution)/shard_map/ppermute | solution.py:115
  782.3 10.6 %collective-permute-done.51 = bf16[1408,1024]{1,0:T(8,128)(2,1)S(1)} collective-permute-done((bf16[1408,1024]{1,0:T(8,128)(2,1)S(1)}, bf16[1408,1024]{1,0:T(8,128)(2,1)S(1)}, u32[]{:S(2)}, u32[]{:S(2)}) %collective-permute-start.51) | collective-permute-done | bytes 2883616 | tf_op jit(solution)/shard_map/ppermute | solution.py:115
  797.5 2.9 pad_maximum_fusion
  800.4 26.2 %collective-permute-done.50 = bf16[256,1536]{1,0:T(8,128)(2,1)} collective-permute-done((bf16[256,1536]{1,0:T(8,128)(2,1)S(1)}, bf16[256,1536]{1,0:T(8,128)(2,1)}, u32[]{:S(2)}, u32[]{:S(2)}) %collective-permute-start.50) | collective-permute-done | bytes 786464 | tf_op jit(solution)/shard_map/ppermute | solution.py:115
  830.6 14.6 %collective-permute-done.54 = bf16[1408,512]{1,0:T(8,128)(2,1)} collective-permute-done((bf16[1408,512]{1,0:T(8,128)(2,1)}, bf16[1408,512]{1,0:T(8,128)(2,1)}, u32[]{:S(2)}, u32[]{:S(2)}) %collective-permute-start.54) | collective-permute-done | bytes 1441824 | tf_op jit(solution)/shard_map/ppermute | solution.py:115
  845.2 2.7 add_convert_fusion.14
  853.5 2.7 collective-permute-done.53
  859.0 27.2 %collective-permute-done.56 = bf16[1408,256]{1,0:T(8,128)(2,1)} collective-permute-done((bf16[1408,256]{1,0:T(8,128)(2,1)}, bf16[1408,256]{1,0:T(8,128)(2,1)}, u32[]{:S(2)}, u32[]{:S(2)}) %collective-permute-start.56) | collective-permute-done | bytes 720928 | tf_op jit(solution)/shard_map/ppermute | solution.py:115
  886.2 3.3 add_bitcast_fusion
  (310 shorter events, 119.7 us)
Async XLA Ops:
  7.2 78.2 %all-gather.3.cloned.1.call-start = ((), (), s32[]{:S(2)}) async-start(), calls=%async_computation.5 | async-start | bytes 2359296 | tf_op jit(solution)/shard_map/all_gather | solution.py:1204
  8.2 9.4 %collective-permute-start.11 = (bf16[64,2048]{1,0:T(8,128)(2,1)S(1)}, bf16[64,2048]{1,0:T(8,128)(2,1)S(1)}, u32[]{:S(2)}, u32[]{:S(2)}) collective-permute-start(bf16[64,2048]{1,0:T(8,128)(2,1)S(1)} %constant_dynamic-slice_fusion.1), channel_id=1, source_target_pairs={{0,2},{1,3},{2,0},{3,1},{4,6},{5,7},{6,4},{7,5},{8,10},{9,11},{10,... | collective-permute-start | bytes 786440 | tf_op jit(solution)/shard_map/ppermute | solution.py:115
  11.9 4.5 collective-permute-start.2
  16.4 1.2 collective-permute-start.3
  18.3 306.7 %reduce-scatter.3.cloned.1.call-start = ((), (), s32[]{:S(2)}) async-start(), calls=%async_computation.2 | async-start | bytes 6488064 | tf_op jit(solution)/shard_map/reduce_scatter | solution.py:1165
  18.4 25.5 %collective-permute-start = (bf16[256,2048]{1,0:T(8,128)(2,1)}, bf16[256,2048]{1,0:T(8,128)(2,1)S(1)}, u32[]{:S(2)}, u32[]{:S(2)}) collective-permute-start(bf16[256,2048]{1,0:T(8,128)(2,1)} %refs_1_), channel_id=1, source_target_pairs={{0,2},{1,3},{2,0},{3,1},{4,6},{5,7},{6,4},{7,5},{8,10},{9,11},{10,... | collective-permute-start | bytes 3145736 | tf_op jit(solution)/shard_map/ppermute | solution.py:115
  19.9 58.7 %collective-permute-start.7 = (bf16[512,2048]{1,0:T(8,128)(2,1)}, bf16[512,2048]{1,0:T(8,128)(2,1)}, u32[]{:S(2)}, u32[]{:S(2)}) collective-permute-start(bf16[512,2048]{1,0:T(8,128)(2,1)} %weight), channel_id=1, source_target_pairs={{0,1},{1,0},{2,3},{3,2},{4,5},{5,4},{6,7},{7,6},{8,9},{9,8},{10,11... | collective-permute-start | bytes 6291464 | tf_op jit(solution)/shard_map/ppermute | solution.py:115
  19.9 3.8 collective-permute-start.1
  20.5 27.5 %collective-permute-start.4 = (bf16[256,2048]{1,0:T(8,128)(2,1)}, bf16[256,2048]{1,0:T(8,128)(2,1)S(1)}, u32[]{:S(2)}, u32[]{:S(2)}) collective-permute-start(bf16[256,2048]{1,0:T(8,128)(2,1)} %refs_1_), channel_id=1, source_target_pairs={{0,1},{1,0},{2,3},{3,2},{4,5},{5,4},{6,7},{7,6},{8,9},{9,8},{10,11... | collective-permute-start | bytes 3145736 | tf_op jit(solution)/shard_map/ppermute | solution.py:115
  43.9 14.9 %collective-permute-start.5 = (bf16[256,2048]{1,0:T(8,128)(2,1)S(1)}, bf16[256,2048]{1,0:T(8,128)(2,1)S(1)}, u32[]{:S(2)}, u32[]{:S(2)}) collective-permute-start(bf16[256,2048]{1,0:T(8,128)(2,1)S(1)} %collective-permute-done.refs_0_.refs_3_), channel_id=1, source_target_pairs={{0,1},{1,0},{2,3},{3,2},{4,5},{5,4},{6,7},{7,6},{8,9},{9,8},{10,11... | collective-permute-start | bytes 3145736 | tf_op jit(solution)/shard_map/ppermute | solution.py:115
  43.9 34.8 %collective-permute-start.6 = (bf16[256,2048]{1,0:T(8,128)(2,1)}, bf16[256,2048]{1,0:T(8,128)(2,1)S(1)}, u32[]{:S(2)}, u32[]{:S(2)}) collective-permute-start(bf16[256,2048]{1,0:T(8,128)(2,1)} %refs_4_.1), channel_id=1, source_target_pairs={{0,2},{1,3},{2,0},{3,1},{4,6},{5,7},{6,4},{7,5},{8,10},{9,11},{10,... | collective-permute-start | bytes 3145736 | tf_op jit(solution)/shard_map/ppermute | solution.py:115
  78.7 51.2 %copy-start.5 = (bf16[256,2048]{1,0:T(8,128)(2,1)}, bf16[256,2048]{1,0:T(8,128)(2,1)S(1)}, u32[]{:S(2)}) copy-start(bf16[256,2048]{1,0:T(8,128)(2,1)S(1)} %collective-permute-done.6.refs_4_.refs_5_.refs_6_) | copy-start | bytes 3145732
  85.4 17.5 %collective-permute-start.12 = (bf16[512,2048]{1,0:T(8,128)(2,1)}, bf16[512,2048]{1,0:T(8,128)(2,1)}, u32[]{:S(2)}, u32[]{:S(2)}) collective-permute-start(bf16[512,2048]{1,0:T(8,128)(2,1)} %all-gather.3.cloned.1.call-done), channel_id=1, source_target_pairs={{0,1},{1,0},{2,3},{3,2},{4,5},{5,4},{6,7},{7,6},{8,9},{9,8},{10,11... | collective-permute-start | bytes 6291464 | tf_op jit(solution)/shard_map/ppermute | solution.py:115
  85.8 14.0 %collective-permute-start.9 = (bf16[512,512]{1,0:T(8,128)(2,1)S(1)}, bf16[512,512]{1,0:T(8,128)(2,1)S(1)}, u32[]{:S(2)}, u32[]{:S(2)}) collective-permute-start(bf16[512,512]{1,0:T(8,128)(2,1)S(1)} %copy-done.30), channel_id=1, source_target_pairs={{0,2},{1,3},{2,0},{3,1},{4,6},{5,7},{6,4},{7,5},{8,10},{9,11},{10,... | collective-permute-start | bytes 1572872 | tf_op jit(solution)/shard_map/ppermute | solution.py:115
  86.3 16.6 %collective-permute-start.8 = (bf16[512,512]{1,0:T(8,128)(2,1)}, bf16[512,512]{1,0:T(8,128)(2,1)}, u32[]{:S(2)}, u32[]{:S(2)}) collective-permute-start(bf16[512,512]{1,0:T(8,128)(2,1)} %get-tuple-element.302.refs_2_.refs_4_), channel_id=1, source_target_pairs={{0,1},{1,0},{2,3},{3,2},{4,5},{5,4},{6,7},{7,6},{8,9},{9,8},{10,11... | collective-permute-start | bytes 1572872 | tf_op jit(solution)/shard_map/ppermute | solution.py:115
  99.8 3.2 collective-permute-start.10
  99.8 15.3 %collective-permute-start.14 = (bf16[512,512]{1,0:T(8,128)(2,1)}, bf16[512,512]{1,0:T(8,128)(2,1)S(1)}, u32[]{:S(2)}, u32[]{:S(2)}) collective-permute-start(bf16[512,512]{1,0:T(8,128)(2,1)} %get-tuple-element.302.refs_2_.refs_4_), channel_id=1, source_target_pairs={{0,2},{1,3},{2,0},{3,1},{4,6},{5,7},{6,4},{7,5},{8,10},{9,11},{10,... | collective-permute-start | bytes 1572872 | tf_op jit(solution)/shard_map/ppermute | solution.py:115
  102.7 13.0 %collective-permute-start.13 = (bf16[512,512]{1,0:T(8,128)(2,1)S(1)}, bf16[512,512]{1,0:T(8,128)(2,1)S(1)}, u32[]{:S(2)}, u32[]{:S(2)}) collective-permute-start(bf16[512,512]{1,0:T(8,128)(2,1)S(1)} %copy-done.30), channel_id=1, source_target_pairs={{0,1},{1,0},{2,3},{3,2},{4,5},{5,4},{6,7},{7,6},{8,9},{9,8},{10,11... | collective-permute-start | bytes 1572872 | tf_op jit(solution)/shard_map/ppermute | solution.py:115
  115.1 2.0 collective-permute-start.15
  115.5 14.7 %collective-permute-start.16 = (bf16[256,2048]{1,0:T(8,128)(2,1)S(1)}, bf16[256,2048]{1,0:T(8,128)(2,1)S(1)}, u32[]{:S(2)}, u32[]{:S(2)}) collective-permute-start(bf16[256,2048]{1,0:T(8,128)(2,1)S(1)} %copy-done.3), channel_id=1, source_target_pairs={{0,1},{1,0},{2,3},{3,2},{4,5},{5,4},{6,7},{7,6},{8,9},{9,8},{10,11... | collective-permute-start | bytes 3145736 | tf_op jit(solution)/shard_map/ppermute | solution.py:115
  129.8 2.7 collective-permute-start.17
  175.8 461.2 %reduce-scatter.5.cloned.1.call-start = ((), (), s32[]{:S(2)}) async-start(), calls=%async_computation.3 | async-start | bytes 6488064 | tf_op jit(solution)/shard_map/reduce_scatter | solution.py:1165
  190.6 95.0 %collective-permute-start.18 = (bf16[1408,1024]{1,0:T(8,128)(2,1)}, bf16[1408,1024]{1,0:T(8,128)(2,1)}, u32[]{:S(2)}, u32[]{:S(2)}) collective-permute-start(bf16[1408,1024]{1,0:T(8,128)(2,1)} %get-tuple-element.215), channel_id=1, source_target_pairs={{0,4},{4,0},{8,12},{12,8},{16,20},{20,16},{24,28},{28,24},{1,5},{5... | collective-permute-start | bytes 8650760 | tf_op jit(solution)/shard_map/ppermute | solution.py:115
  205.6 143.4 %collective-permute-start.20 = (bf16[1024,1408]{1,0:T(8,128)(2,1)}, bf16[1024,1408]{1,0:T(8,128)(2,1)}, u32[]{:S(2)}, u32[]{:S(2)}) collective-permute-start(bf16[1024,1408]{1,0:T(8,128)(2,1)} %get-tuple-element.241), channel_id=1, source_target_pairs={{0,4},{4,0},{8,12},{12,8},{16,20},{20,16},{24,28},{28,24},{1,5},{5... | collective-permute-start | bytes 8650760 | tf_op jit(solution)/shard_map/ppermute | solution.py:115
  239.0 179.3 %collective-permute-start.19 = (bf16[1024,1408]{1,0:T(8,128)(2,1)}, bf16[1024,1408]{1,0:T(8,128)(2,1)S(1)}, u32[]{:S(2)}, u32[]{:S(2)}) collective-permute-start(bf16[1024,1408]{1,0:T(8,128)(2,1)} %get-tuple-element.238), channel_id=1, source_target_pairs={{0,4},{4,0},{8,12},{12,8},{16,20},{20,16},{24,28},{28,24},{1,5},{5... | collective-permute-start | bytes 8650760 | tf_op jit(solution)/shard_map/ppermute | solution.py:115
  288.6 62.9 %collective-permute-start.22 = (bf16[1408,512]{1,0:T(8,128)(2,1)}, bf16[1408,512]{1,0:T(8,128)(2,1)}, u32[]{:S(2)}, u32[]{:S(2)}) collective-permute-start(bf16[1408,512]{1,0:T(8,128)(2,1)} %add_convert_fusion.7), channel_id=1, source_target_pairs={{0,8},{4,12},{8,0},{12,4},{16,24},{20,28},{24,16},{28,20},{1,9},{5... | collective-permute-start | bytes 4325384 | tf_op jit(solution)/shard_map/ppermute | solution.py:115
  351.1 52.0 %collective-permute-start.21 = (bf16[512,1408]{1,0:T(8,128)(2,1)S(1)}, bf16[512,1408]{1,0:T(8,128)(2,1)S(1)}, u32[]{:S(2)}, u32[]{:S(2)}) collective-permute-start(bf16[512,1408]{1,0:T(8,128)(2,1)S(1)} %add_convert_fusion.6), channel_id=1, source_target_pairs={{0,8},{4,12},{8,0},{12,4},{16,24},{20,28},{24,16},{28,20},{1,9},{5... | collective-permute-start | bytes 4325384 | tf_op jit(solution)/shard_map/ppermute | solution.py:115
  353.3 67.1 %collective-permute-start.23 = (bf16[1408,256]{1,0:T(8,128)(2,1)S(1)}, bf16[1408,256]{1,0:T(8,128)(2,1)S(1)}, u32[]{:S(2)}, u32[]{:S(2)}) collective-permute-start(bf16[1408,256]{1,0:T(8,128)(2,1)S(1)} %add_convert_fusion.20), channel_id=1, source_target_pairs={{0,24},{4,28},{8,16},{12,20},{16,8},{20,12},{24,0},{28,4},{1,25},{... | collective-permute-start | bytes 2162696 | tf_op jit(solution)/shard_map/ppermute | solution.py:115
  432.6 394.0 %all-reduce.3.cloned.1.call-start = ((), (), s32[]{:S(2)}) async-start(), calls=%async_computation.4 | async-start | bytes 262144 | tf_op jit(solution)/shard_map/psum | solution.py:1365
  432.7 3.8 collective-permute-start.28
  434.8 84.1 %collective-permute-start.25 = (bf16[1024,1408]{1,0:T(8,128)(2,1)}, bf16[1024,1408]{1,0:T(8,128)(2,1)}, u32[]{:S(2)}, u32[]{:S(2)}) collective-permute-start(bf16[1024,1408]{1,0:T(8,128)(2,1)} %get-tuple-element.260), channel_id=1, source_target_pairs={{0,4},{4,0},{8,12},{12,8},{16,20},{20,16},{24,28},{28,24},{1,5},{5... | collective-permute-start | bytes 8650760 | tf_op jit(solution)/shard_map/ppermute | solution.py:115
  436.5 29.2 %collective-permute-start.27 = (bf16[256,2048]{1,0:T(8,128)(2,1)}, bf16[256,2048]{1,0:T(8,128)(2,1)}, u32[]{:S(2)}, u32[]{:S(2)}) collective-permute-start(bf16[256,2048]{1,0:T(8,128)(2,1)} %get-tuple-element.265), channel_id=1, source_target_pairs={{0,1},{1,0},{2,3},{3,2},{4,5},{5,4},{6,7},{7,6},{8,9},{9,8},{10,11... | collective-permute-start | bytes 3145736 | tf_op jit(solution)/shard_map/ppermute | solution.py:115
  439.2 25.9 %collective-permute-start.29 = (bf16[256,2048]{1,0:T(8,128)(2,1)}, bf16[256,2048]{1,0:T(8,128)(2,1)}, u32[]{:S(2)}, u32[]{:S(2)}) collective-permute-start(bf16[256,2048]{1,0:T(8,128)(2,1)} %add_convert_fusion.12), channel_id=1, source_target_pairs={{0,2},{1,3},{2,0},{3,1},{4,6},{5,7},{6,4},{7,5},{8,10},{9,11},{10,... | collective-permute-start | bytes 3145736 | tf_op jit(solution)/shard_map/ppermute | solution.py:115
  443.8 63.2 %collective-permute-start.26 = (bf16[256,1408]{1,0:T(8,128)(2,1)S(1)}, bf16[256,1408]{1,0:T(8,128)(2,1)S(1)}, u32[]{:S(2)}, u32[]{:S(2)}) collective-permute-start(bf16[256,1408]{1,0:T(8,128)(2,1)S(1)} %copy-done.47), channel_id=1, source_target_pairs={{0,24},{4,28},{8,16},{12,20},{16,8},{20,12},{24,0},{28,4},{1,25},{... | collective-permute-start | bytes 2162696 | tf_op jit(solution)/shard_map/ppermute | solution.py:115
  443.9 89.1 %collective-permute-start.24 = (bf16[512,1408]{1,0:T(8,128)(2,1)S(1)}, bf16[512,1408]{1,0:T(8,128)(2,1)}, u32[]{:S(2)}, u32[]{:S(2)}) collective-permute-start(bf16[512,1408]{1,0:T(8,128)(2,1)S(1)} %copy-done.31), channel_id=1, source_target_pairs={{0,8},{4,12},{8,0},{12,4},{16,24},{20,28},{24,16},{28,20},{1,9},{5... | collective-permute-start | bytes 4325384 | tf_op jit(solution)/shard_map/ppermute | solution.py:115
  465.1 135.9 %collective-permute-start.37 = (bf16[1408,1024]{1,0:T(8,128)(2,1)}, bf16[1408,1024]{1,0:T(8,128)(2,1)}, u32[]{:S(2)}, u32[]{:S(2)}) collective-permute-start(bf16[1408,1024]{1,0:T(8,128)(2,1)} %get-tuple-element.292), channel_id=1, source_target_pairs={{0,4},{4,0},{8,12},{12,8},{16,20},{20,16},{24,28},{28,24},{1,5},{5... | collective-permute-start | bytes 8650760 | tf_op jit(solution)/shard_map/ppermute | solution.py:115
  472.1 63.6 %copy-start.14 = (bf16[256,2048]{1,0:T(8,128)(2,1)}, bf16[256,2048]{1,0:T(8,128)(2,1)S(1)}, u32[]{:S(2)}) copy-start(bf16[256,2048]{1,0:T(8,128)(2,1)S(1)} %get-tuple-element.380.refs_0_) | copy-start | bytes 3145732
  472.1 66.3 %collective-permute-start.33 = (bf16[256,2048]{1,0:T(8,128)(2,1)S(1)}, bf16[256,2048]{1,0:T(8,128)(2,1)S(1)}, u32[]{:S(2)}, u32[]{:S(2)}) collective-permute-start(bf16[256,2048]{1,0:T(8,128)(2,1)S(1)} %get-tuple-element.380.refs_0_), channel_id=1, source_target_pairs={{0,2},{1,3},{2,0},{3,1},{4,6},{5,7},{6,4},{7,5},{8,10},{9,11},{10,... | collective-permute-start | bytes 3145736 | tf_op jit(solution)/shard_map/ppermute | solution.py:115
  535.6 6.2 collective-permute-start.31
  535.7 9.1 %collective-permute-start.32 = (bf16[256,2048]{1,0:T(8,128)(2,1)S(1)}, bf16[256,2048]{1,0:T(8,128)(2,1)S(1)}, u32[]{:S(2)}, u32[]{:S(2)}) collective-permute-start(bf16[256,2048]{1,0:T(8,128)(2,1)S(1)} %get-tuple-element.380.refs_0_), channel_id=1, source_target_pairs={{0,1},{1,0},{2,3},{3,2},{4,5},{5,4},{6,7},{7,6},{8,9},{9,8},{10,11... | collective-permute-start | bytes 3145736 | tf_op jit(solution)/shard_map/ppermute | solution.py:115
  536.3 56.0 %collective-permute-start.38 = (bf16[512,1408]{1,0:T(8,128)(2,1)S(1)}, bf16[512,1408]{1,0:T(8,128)(2,1)}, u32[]{:S(2)}, u32[]{:S(2)}) collective-permute-start(bf16[512,1408]{1,0:T(8,128)(2,1)S(1)} %add_convert_fusion.4), channel_id=1, source_target_pairs={{0,8},{4,12},{8,0},{12,4},{16,24},{20,28},{24,16},{28,20},{1,9},{5... | collective-permute-start | bytes 4325384 | tf_op jit(solution)/shard_map/ppermute | solution.py:115
  538.4 6.5 collective-permute-start.34
  541.8 62.4 %collective-permute-start.36 = (bf16[256,1408]{1,0:T(8,128)(2,1)}, bf16[256,1408]{1,0:T(8,128)(2,1)}, u32[]{:S(2)}, u32[]{:S(2)}) collective-permute-start(bf16[256,1408]{1,0:T(8,128)(2,1)} %add_convert_fusion.18), channel_id=1, source_target_pairs={{0,24},{4,28},{8,16},{12,20},{16,8},{20,12},{24,0},{28,4},{1,25},{... | collective-permute-start | bytes 2162696 | tf_op jit(solution)/shard_map/ppermute | solution.py:115
  544.9 89.0 %collective-permute-start.30 = (bf16[256,2048]{1,0:T(8,128)(2,1)}, bf16[256,2048]{1,0:T(8,128)(2,1)}, u32[]{:S(2)}, u32[]{:S(2)}) collective-permute-start(bf16[256,2048]{1,0:T(8,128)(2,1)} %get-tuple-element.277), channel_id=1, source_target_pairs={{0,1},{1,0},{2,3},{3,2},{4,5},{5,4},{6,7},{7,6},{8,9},{9,8},{10,11... | collective-permute-start | bytes 3145736 | tf_op jit(solution)/shard_map/ppermute | solution.py:115
  545.9 116.9 %collective-permute-start.44 = (bf16[1024,1408]{1,0:T(8,128)(2,1)}, bf16[1024,1408]{1,0:T(8,128)(2,1)}, u32[]{:S(2)}, u32[]{:S(2)}) collective-permute-start(bf16[1024,1408]{1,0:T(8,128)(2,1)} %get-tuple-element.320), channel_id=1, source_target_pairs={{0,4},{4,0},{8,12},{12,8},{16,20},{20,16},{24,28},{28,24},{1,5},{5... | collective-permute-start | bytes 8650760 | tf_op jit(solution)/shard_map/ppermute | solution.py:115
  592.3 39.9 %collective-permute-start.35 = (bf16[256,2048]{1,0:T(8,128)(2,1)}, bf16[256,2048]{1,0:T(8,128)(2,1)}, u32[]{:S(2)}, u32[]{:S(2)}) collective-permute-start(bf16[256,2048]{1,0:T(8,128)(2,1)} %add_convert_fusion.11), channel_id=1, source_target_pairs={{0,2},{1,3},{2,0},{3,1},{4,6},{5,7},{6,4},{7,5},{8,10},{9,11},{10,... | collective-permute-start | bytes 3145736 | tf_op jit(solution)/shard_map/ppermute | solution.py:115
  604.1 37.1 %collective-permute-start.41 = (bf16[1408,512]{1,0:T(8,128)(2,1)}, bf16[1408,512]{1,0:T(8,128)(2,1)}, u32[]{:S(2)}, u32[]{:S(2)}) collective-permute-start(bf16[1408,512]{1,0:T(8,128)(2,1)} %add_convert_fusion.3), channel_id=1, source_target_pairs={{0,8},{4,12},{8,0},{12,4},{16,24},{20,28},{24,16},{28,20},{1,9},{5... | collective-permute-start | bytes 4325384 | tf_op jit(solution)/shard_map/ppermute | solution.py:115
  608.9 28.1 %collective-permute-start.42 = (bf16[256,1408]{1,0:T(8,128)(2,1)}, bf16[256,1408]{1,0:T(8,128)(2,1)}, u32[]{:S(2)}, u32[]{:S(2)}) collective-permute-start(bf16[256,1408]{1,0:T(8,128)(2,1)} %add_convert_fusion.17), channel_id=1, source_target_pairs={{0,24},{4,28},{8,16},{12,20},{16,8},{20,12},{24,0},{28,4},{1,25},{... | collective-permute-start | bytes 2162696 | tf_op jit(solution)/shard_map/ppermute | solution.py:115
  632.2 98.6 %collective-permute-start.45 = (bf16[1024,1536]{1,0:T(8,128)(2,1)}, bf16[1024,1536]{1,0:T(8,128)(2,1)}, u32[]{:S(2)}, u32[]{:S(2)}) collective-permute-start(bf16[1024,1536]{1,0:T(8,128)(2,1)} %get-tuple-element.325), channel_id=1, source_target_pairs={{0,4},{4,0},{8,12},{12,8},{16,20},{20,16},{24,28},{28,24},{1,5},{5... | collective-permute-start | bytes 9437192 | tf_op jit(solution)/shard_map/ppermute | solution.py:115
  637.0 54.7 %collective-permute-start.40 = (bf16[256,2048]{1,0:T(8,128)(2,1)}, bf16[256,2048]{1,0:T(8,128)(2,1)}, u32[]{:S(2)}, u32[]{:S(2)}) collective-permute-start(bf16[256,2048]{1,0:T(8,128)(2,1)} %get-tuple-element.313), channel_id=1, source_target_pairs={{0,1},{1,0},{2,3},{3,2},{4,5},{5,4},{6,7},{7,6},{8,9},{9,8},{10,11... | collective-permute-start | bytes 3145736 | tf_op jit(solution)/shard_map/ppermute | solution.py:115
  665.6 46.3 %collective-permute-start.46 = (bf16[512,1408]{1,0:T(8,128)(2,1)}, bf16[512,1408]{1,0:T(8,128)(2,1)}, u32[]{:S(2)}, u32[]{:S(2)}) collective-permute-start(bf16[512,1408]{1,0:T(8,128)(2,1)} %add_convert_fusion.2), channel_id=1, source_target_pairs={{0,8},{4,12},{8,0},{12,4},{16,24},{20,28},{24,16},{28,20},{1,9},{5... | collective-permute-start | bytes 4325384 | tf_op jit(solution)/shard_map/ppermute | solution.py:115
  670.9 67.0 %collective-permute-start.39 = (bf16[256,2048]{1,0:T(8,128)(2,1)}, bf16[256,2048]{1,0:T(8,128)(2,1)S(1)}, u32[]{:S(2)}, u32[]{:S(2)}) collective-permute-start(bf16[256,2048]{1,0:T(8,128)(2,1)} %get-tuple-element.310), channel_id=1, source_target_pairs={{0,1},{1,0},{2,3},{3,2},{4,5},{5,4},{6,7},{7,6},{8,9},{9,8},{10,11... | collective-permute-start | bytes 3145736 | tf_op jit(solution)/shard_map/ppermute | solution.py:115
  671.0 19.2 %collective-permute-start.47 = (bf16[1408,256]{1,0:T(8,128)(2,1)}, bf16[1408,256]{1,0:T(8,128)(2,1)S(1)}, u32[]{:S(2)}, u32[]{:S(2)}) collective-permute-start(bf16[1408,256]{1,0:T(8,128)(2,1)} %add_convert_fusion.16), channel_id=1, source_target_pairs={{0,24},{4,28},{8,16},{12,20},{16,8},{20,12},{24,0},{28,4},{1,25},{... | collective-permute-start | bytes 2162696 | tf_op jit(solution)/shard_map/ppermute | solution.py:115
  672.7 40.6 %copy-start.24 = (bf16[1024,1408]{1,0:T(8,128)(2,1)S(1)}, bf16[1024,1408]{1,0:T(8,128)(2,1)}, u32[]{:S(2)}) copy-start(bf16[1024,1408]{1,0:T(8,128)(2,1)} %get-tuple-element.254) | copy-start | bytes 8650756
  690.2 102.7 %collective-permute-start.51 = (bf16[1408,1024]{1,0:T(8,128)(2,1)S(1)}, bf16[1408,1024]{1,0:T(8,128)(2,1)S(1)}, u32[]{:S(2)}, u32[]{:S(2)}) collective-permute-start(bf16[1408,1024]{1,0:T(8,128)(2,1)S(1)} %copy-done.66), channel_id=1, source_target_pairs={{0,4},{4,0},{8,12},{12,8},{16,20},{20,16},{24,28},{28,24},{1,5},{5... | collective-permute-start | bytes 8650760 | tf_op jit(solution)/shard_map/ppermute | solution.py:115
  691.8 134.9 %collective-permute-start.52 = (bf16[512,1024]{1,0:T(8,128)(2,1)}, bf16[512,1024]{1,0:T(8,128)(2,1)}, u32[]{:S(2)}, u32[]{:S(2)}) collective-permute-start(bf16[512,1024]{1,0:T(8,128)(2,1)} %get-tuple-element.342), channel_id=1, source_target_pairs={{0,4},{4,0},{8,12},{12,8},{16,20},{20,16},{24,28},{28,24},{1,5},{5... | collective-permute-start | bytes 3145736 | tf_op jit(solution)/shard_map/ppermute | solution.py:115
  711.9 20.8 %collective-permute-start.43 = (bf16[256,2048]{1,0:T(8,128)(2,1)S(1)}, bf16[256,2048]{1,0:T(8,128)(2,1)S(1)}, u32[]{:S(2)}, u32[]{:S(2)}) collective-permute-start(bf16[256,2048]{1,0:T(8,128)(2,1)S(1)} %add_convert_fusion.9), channel_id=1, source_target_pairs={{0,2},{1,3},{2,0},{3,1},{4,6},{5,7},{6,4},{7,5},{8,10},{9,11},{10,... | collective-permute-start | bytes 3145736 | tf_op jit(solution)/shard_map/ppermute | solution.py:115
  730.8 30.9 %collective-permute-start.49 = (bf16[256,1408]{1,0:T(8,128)(2,1)S(1)}, bf16[256,1408]{1,0:T(8,128)(2,1)S(1)}, u32[]{:S(2)}, u32[]{:S(2)}) collective-permute-start(bf16[256,1408]{1,0:T(8,128)(2,1)S(1)} %add_convert_fusion.15), channel_id=1, source_target_pairs={{0,24},{4,28},{8,16},{12,20},{16,8},{20,12},{24,0},{28,4},{1,25},{... | collective-permute-start | bytes 2162696 | tf_op jit(solution)/shard_map/ppermute | solution.py:115
  732.7 48.2 %collective-permute-start.48 = (bf16[512,1536]{1,0:T(8,128)(2,1)S(1)}, bf16[512,1536]{1,0:T(8,128)(2,1)S(1)}, u32[]{:S(2)}, u32[]{:S(2)}) collective-permute-start(bf16[512,1536]{1,0:T(8,128)(2,1)S(1)} %add_convert_fusion), channel_id=1, source_target_pairs={{0,8},{4,12},{8,0},{12,4},{16,24},{20,28},{24,16},{28,20},{1,9},{5... | collective-permute-start | bytes 4718600 | tf_op jit(solution)/shard_map/ppermute | solution.py:115
  792.9 33.7 %collective-permute-start.50 = (bf16[256,1536]{1,0:T(8,128)(2,1)S(1)}, bf16[256,1536]{1,0:T(8,128)(2,1)}, u32[]{:S(2)}, u32[]{:S(2)}) collective-permute-start(bf16[256,1536]{1,0:T(8,128)(2,1)S(1)} %add_convert_fusion.13), channel_id=1, source_target_pairs={{0,24},{4,28},{8,16},{12,20},{16,8},{20,12},{24,0},{28,4},{1,25},{... | collective-permute-start | bytes 2359304 | tf_op jit(solution)/shard_map/ppermute | solution.py:115
  794.9 50.3 %collective-permute-start.54 = (bf16[1408,512]{1,0:T(8,128)(2,1)}, bf16[1408,512]{1,0:T(8,128)(2,1)}, u32[]{:S(2)}, u32[]{:S(2)}) collective-permute-start(bf16[1408,512]{1,0:T(8,128)(2,1)} %add_convert_fusion.1), channel_id=1, source_target_pairs={{0,8},{4,12},{8,0},{12,4},{16,24},{20,28},{24,16},{28,20},{1,9},{5... | collective-permute-start | bytes 4325384 | tf_op jit(solution)/shard_map/ppermute | solution.py:115
  828.6 27.6 %collective-permute-start.53 = (bf16[512,512]{1,0:T(8,128)(2,1)}, bf16[512,512]{1,0:T(8,128)(2,1)}, u32[]{:S(2)}, u32[]{:S(2)}) collective-permute-start(bf16[512,512]{1,0:T(8,128)(2,1)} %add_convert_fusion.21), channel_id=1, source_target_pairs={{0,8},{4,12},{8,0},{12,4},{16,24},{20,28},{24,16},{28,20},{1,9},{5... | collective-permute-start | bytes 1572872 | tf_op jit(solution)/shard_map/ppermute | solution.py:115
  847.9 38.4 %collective-permute-start.56 = (bf16[1408,256]{1,0:T(8,128)(2,1)}, bf16[1408,256]{1,0:T(8,128)(2,1)}, u32[]{:S(2)}, u32[]{:S(2)}) collective-permute-start(bf16[1408,256]{1,0:T(8,128)(2,1)} %add_convert_fusion.14), channel_id=1, source_target_pairs={{0,24},{4,28},{8,16},{12,20},{16,8},{20,12},{24,0},{28,4},{1,25},{... | collective-permute-start | bytes 2162696 | tf_op jit(solution)/shard_map/ppermute | solution.py:115
  857.3 32.2 %collective-permute-start.55 = (bf16[512,256]{1,0:T(8,128)(2,1)S(1)}, bf16[512,256]{1,0:T(8,128)(2,1)S(1)}, u32[]{:S(2)}, u32[]{:S(2)}) collective-permute-start(bf16[512,256]{1,0:T(8,128)(2,1)S(1)} %add_convert_fusion.22), channel_id=1, source_target_pairs={{0,24},{4,28},{8,16},{12,20},{16,8},{20,12},{24,0},{28,4},{1,25},{... | collective-permute-start | bytes 786440 | tf_op jit(solution)/shard_map/ppermute | solution.py:115
  (65 other events, 652.1 us)
Sparse Core Ops, SparseCore 0:
  18.4 50.5 all-gather.2
  175.9 141.8 reduce-scatter.2
  432.7 181.9 reduce-scatter.4
  671.1 149.1 all-reduce.2

commit v6 on v5

--- a/solution.py
+++ b/solution.py
@@ -32,13 +32,13 @@
     "Su": "Su+",
     "0g": "0g+",
     "E1": "Sd- Sd+",
-    "mix": " ".join(["Sg- Su- Su+ Sd-", "Sd+ 0u+"]),
+    "mix": "Sg- Sd- Sd+ 0u+",
     "back": "Su- Su+",
-    "1g": "0g- Sd- 0g+",
+    "1g": "Sd-",
     "n1": "0d+",
-    "1u": "1u+",
-    "norm": "Su-",
-    "h": " ".join(["0u- 0u+ 0g- 0g+", "1g+"]),
+    "1u": "1u+ 0g- 0g+",
+    "norm": "Su- Su+",
+    "h": " ".join(["0u- 0u+ 0g- 0g+", "Su- 1g+"]),
     "q": " ".join(["0u- 0u+ 0d- q+", "0g- 0d+"]),
     "fb": "1u-",
     "r1": "0u- 1d+ 0d-",
@@ -1309,13 +1309,13 @@
         for e in range(1, local):
             expert_product(e, k)
 
+    rest(0)
+    rest(1)
     steps = group_steps(grad_parts, then)
     next(steps)
-    rest(0)
     for _ in range(int(math.log2(width)) - 1):
         parts = next(steps)
     moves("n1")
-    rest(1)
     normed_grad = sum(value.astype(F32) for value in [*parts[:-1], then(parts[-1])])
     inv_two_own = rms_scale(hidden_own)
     hat_two = hidden_own * inv_two_own

time: 908 us -> 910 us (level)
  starting transfers between devices: 50.7 us -> 95.3 us
  waiting for transfers between devices: 323 us -> 279 us
    ppermute x57, waiting for transfers between devices: 323 us -> 262 us  [swap(): return lax.ppermute(values, axis, pairs)]
    ppermute x57, starting transfers between devices: 50.5 us -> 95.1 us  [swap(): return lax.ppermute(values, axis, pairs)]
    psum x1, waiting for transfers between devices: 0.01 us -> 16.9 us  [per_device(): lax.psum(jnp.concatenate([then(gain_two_grad[None, :]), side_sum[:expert_...]
  transfers between devices with their start and end apart: 61 -> 61, of which waited for: 24 -> 21; matrix products, arithmetic and copies ran while one was open for 11% -> 11% of each run, Pallas kernels for 38% -> 39%
where the time goes in v6:
time: 910 us; the launch traced here: 902 us
  Pallas kernels  393 us (43%)
  waiting for transfers between devices  279 us (31%)
  starting transfers between devices  95.3 us (10%)
  other arithmetic  95 us (10%)
  local copies, waits for them, and re-layouts  25 us (3%)
  between operations  14.8 us (2%)
    pallas_call x26, Pallas kernels, kernel_call(): pl.pallas_call(body, name=name, grid_spec=pltpu.PrefetchScalarGridSpec(nu...  393 us
    ppermute x57, waiting for transfers between devices, swap(): return lax.ppermute(values, axis, pairs)  262 us
    ppermute x57, starting transfers between devices, swap(): return lax.ppermute(values, axis, pairs)  95.1 us
    convert_element_type x18, other arithmetic, collect(): self.sent = self.part(self.size, 2 * self.size).astype(BF16)  41.9 us
  transfers between devices with their start and end apart: 61, of which 21 were waited for; matrix products, arithmetic and copies ran while one was open for 11% of the time, Pallas kernels for 39%

profile of v6, /device:TPU:8, one launch (start us, length us, event | category | flops | bytes accessed | tf_op | source)
XLA Modules:
  0.0 901.6 jit_solution(13066697197453017156)
XLA Ops:
  12.4 4.0 collective-permute-done.2.refs_2_
  24.3 7.0 prepare.1
  31.3 12.5 %collective-permute-done.refs_0_.refs_3_ = bf16[256,2048]{1,0:T(8,128)(2,1)S(1)} collective-permute-done((bf16[256,2048]{1,0:T(8,128)(2,1)}, bf16[256,2048]{1,0:T(8,128)(2,1)S(1)}, u32[]{:S(2)}, u32[]{:S(2)}) %collective-permute-start) | collective-permute-done | bytes 1048608 | tf_op jit(solution)/shard_map/ppermute | solution.py:115
  48.9 9.8 %project.2 = (bf16[3,1024,512]{2,1,0:T(8,128)(2,1)}, bf16[1024,2048]{1,0:T(8,128)(2,1)}) custom-call(bf16[256,2048]{1,0:T(8,128)(2,1)} %refs_1_, bf16[256,2048]{1,0:T(8,128)(2,1)} %copy-done.12, bf16[1,2048]{1,0:T(2,128)(2,1)} %broadcast_in_dim.45.refs_2_, bf16[3,2048,512]{2,1,0:T(8,128)(2,1)} %refs_0_.3, bf16[3,1,512]{2,1,0:T(2,128)(2,1)} %copy.47.refs_4_, ...), custom_call_target="tpu_custom_call" | custom-call | flops 1 | bytes 1 | tf_op jit(solution)/shard_map/project/pallas_call | solution.py:68
  59.8 9.4 %project.3 = (bf16[3,1024,512]{2,1,0:T(8,128)(2,1)}, bf16[1024,2048]{1,0:T(8,128)(2,1)}) custom-call(bf16[256,2048]{1,0:T(8,128)(2,1)} %copy-done.8, bf16[256,2048]{1,0:T(8,128)(2,1)} %copy-done.10, bf16[1,2048]{1,0:T(2,128)(2,1)} %broadcast_in_dim.45.refs_2_, bf16[3,2048,512]{2,1,0:T(8,128)(2,1)} %refs_0_.3, ...), custom_call_target="tpu_custom_call", output_to_operand_aliasing={{0}: (7, {}), {1}: (8, {})} | custom-call | flops 1 | bytes 1 | tf_op jit(solution)/shard_map/project/pallas_call | solution.py:68
  69.2 9.5 %attend.2 = (bf16[512,512]{1,0:T(8,128)(2,1)}, f32[4,512,1]{2,1,0:T(8,128)}) custom-call(s32[4]{0:T(128)} %iota_xor_fusion.places, bf16[3,1024,512]{2,1,0:T(8,128)(2,1)} %get-tuple-element.191.query.key.value, bf16[3,1024,512]{2,1,0:T(8,128)(2,1)} %get-tuple-element.191.query.key.value, bf16[3,1024,512]{2,1,0:T(8,128)(2,1)} %get-tuple-element.191.query.key.value, ...), custom_call_target="tpu_custom_call" | custom-call | flops 1 | bytes 1 | tf_op jit(solution)/shard_map/attend/pallas_call | solution.py:68
  78.8 6.7 attend.3
  86.4 13.5 %collective-permute-done.9.refs_4_ = bf16[512,512]{1,0:T(8,128)(2,1)S(1)} collective-permute-done((bf16[512,512]{1,0:T(8,128)(2,1)S(1)}, bf16[512,512]{1,0:T(8,128)(2,1)S(1)}, u32[]{:S(2)}, u32[]{:S(2)}) %collective-permute-start.9) | collective-permute-done | bytes 524320 | tf_op jit(solution)/shard_map/ppermute | solution.py:115
  103.1 12.1 %out_project.2 = (bf16[1024,2048]{1,0:T(8,128)(2,1)}, f32[1024,128]{1,0:T(8,128)}, f32[256,2048]{1,0:T(8,128)}) custom-call(bf16[256,2048]{1,0:T(8,128)(2,1)} %refs_1_, bf16[256,2048]{1,0:T(8,128)(2,1)} %copy-done.12, bf16[512,512]{1,0:T(8,128)(2,1)} %get-tuple-element.302.refs_2_.refs_4_, bf16[512,512]{1,0:T(8,128)(2,1)} %collective-permute-done.8.refs_3_, ...), custom_call_target="tpu_custom_call" | custom-call | flops 1 | bytes 1 | tf_op jit(solution)/shard_map/out_project/pallas_call | solution.py:68
  118.0 11.9 %out_project.3 = (bf16[1024,2048]{1,0:T(8,128)(2,1)}, f32[1024,128]{1,0:T(8,128)}, f32[256,2048]{1,0:T(8,128)}) custom-call(bf16[256,2048]{1,0:T(8,128)(2,1)} %copy-done.8, bf16[256,2048]{1,0:T(8,128)(2,1)} %copy-done.10, bf16[512,512]{1,0:T(8,128)(2,1)} %get-tuple-element.198.refs_2_.refs_5_, ...), custom_call_target="tpu_custom_call", output_to_operand_aliasing={{0}: (12, {}), {1}: (13, {})} | custom-call | flops 1 | bytes 1 | tf_op jit(solution)/shard_map/out_project/pallas_call | solution.py:68
  133.6 29.0 %shared_inner.1 = (bf16[1024,1408]{1,0:T(8,128)(2,1)}, bf16[1024,1408]{1,0:T(8,128)(2,1)}, bf16[1024,1408]{1,0:T(8,128)(2,1)}, bf16[1024,2048]{1,0:T(8,128)(2,1)}) custom-call(bf16[1024,2048]{1,0:T(8,128)(2,1)} %get-tuple-element.232.refs_0_.refs_6_, f32[1024,128]{1,0:T(8,128)} %get-tuple-element.206.refs_1_.side, bf16[256,2048]{1,0:T(8,128)(2,1)} %refs_4_.1, ...), custom_call_target="tpu_custom_call" | custom-call | flops 1 | bytes 1 | tf_op jit(solution)/shard_map/shared_inner/pallas_call | solution.py:68
  163.1 12.7 %weight_product.11 = bf16[2048,1408]{1,0:T(8,128)(2,1)} custom-call(s32[8]{0:T(128)} %iota.10.blocks, bf16[1024,2048]{1,0:T(8,128)(2,1)} %get-tuple-element.232.refs_0_.refs_6_, bf16[1024,1408]{1,0:T(8,128)(2,1)} %get-tuple-element.244.refs_1_.gate_grad), custom_call_target="tpu_custom_call" | custom-call | flops 1 | bytes 1 | tf_op jit(solution)/shard_map/weight_product/pallas_call | solution.py:68
  177.1 13.6 %weight_product.12 = (bf16[1408,1024]{1,0:T(8,128)(2,1)}, bf16[1408,1024]{1,0:T(8,128)(2,1)}) custom-call(s32[8]{0:T(128)} %fusion.5.blocks, bf16[1024,2048]{1,0:T(8,128)(2,1)} %get-tuple-element.210.refs_0_, bf16[1024,1408]{1,0:T(8,128)(2,1)} %get-tuple-element.235.refs_1_.act), custom_call_target="tpu_custom_call" | custom-call | flops 1 | bytes 1 | tf_op jit(solution)/shard_map/weight_product/pallas_call | solution.py:68
  192.2 13.3 %weight_product.13 = (bf16[1024,1408]{1,0:T(8,128)(2,1)}, bf16[1024,1408]{1,0:T(8,128)(2,1)}) custom-call(s32[8]{0:T(128)} %fusion.5.blocks, bf16[1024,2048]{1,0:T(8,128)(2,1)} %get-tuple-element.232.refs_0_.refs_6_, bf16[1024,1408]{1,0:T(8,128)(2,1)} %get-tuple-element.217.refs_1_.up_grad), custom_call_target="tpu_custom_call" | custom-call | flops 1 | bytes 1 | tf_op jit(solution)/shard_map/weight_product/pallas_call | solution.py:68
  205.9 21.6 %expert_inner.2 = (bf16[576,1408]{1,0:T(8,128)(2,1)}, bf16[576,1408]{1,0:T(8,128)(2,1)}, bf16[576,1408]{1,0:T(8,128)(2,1)}, bf16[576,2048]{1,0:T(8,128)(2,1)}, bf16[576,2048]{1,0:T(8,128)(2,1)}) custom-call(s32[1]{0:T(128)} %bitcast.1.first, bf16[1024,2048]{1,0:T(8,128)(2,1)} %get-tuple-element.232.refs_0_.refs_6_, ...), custom_call_target="tpu_custom_call" | custom-call | flops 1 | bytes 1 | tf_op jit(solution)/shard_map/expert_inner/pallas_call | solution.py:68
  227.5 11.5 %weight_product.14 = (bf16[1024,1408]{1,0:T(8,128)(2,1)}, bf16[1024,1408]{1,0:T(8,128)(2,1)}) custom-call(s32[8]{0:T(128)} %fusion.5.blocks, bf16[576,2048]{1,0:T(8,128)(2,1)} %get-tuple-element.223.refs_0_, bf16[576,1408]{1,0:T(8,128)(2,1)} %get-tuple-element.226.refs_1_.refs_0_), custom_call_target="tpu_custom_call" | custom-call | flops 1 | bytes 1 | tf_op jit(solution)/shard_map/weight_product/pallas_call | solution.py:68
  239.0 11.5 %weight_product.15 = (bf16[1024,1408]{1,0:T(8,128)(2,1)}, bf16[1024,1408]{1,0:T(8,128)(2,1)}) custom-call(s32[8]{0:T(128)} %fusion.5.blocks, bf16[576,2048]{1,0:T(8,128)(2,1)} %get-tuple-element.223.refs_0_, bf16[576,1408]{1,0:T(8,128)(2,1)} %get-tuple-element.228.refs_1_), custom_call_target="tpu_custom_call" | custom-call | flops 1 | bytes 1 | tf_op jit(solution)/shard_map/weight_product/pallas_call | solution.py:68
  250.5 11.5 %weight_product.16 = (bf16[1408,1024]{1,0:T(8,128)(2,1)}, bf16[1408,1024]{1,0:T(8,128)(2,1)}) custom-call(s32[8]{0:T(128)} %fusion.5.blocks, bf16[576,2048]{1,0:T(8,128)(2,1)} %get-tuple-element.221.refs_0_, bf16[576,1408]{1,0:T(8,128)(2,1)} %get-tuple-element.230.refs_1_.refs_0_), custom_call_target="tpu_custom_call" | custom-call | flops 1 | bytes 1 | tf_op jit(solution)/shard_map/weight_product/pallas_call | solution.py:68
  262.0 21.5 %expert_inner.3 = (bf16[576,1408]{1,0:T(8,128)(2,1)}, bf16[576,1408]{1,0:T(8,128)(2,1)}, bf16[576,1408]{1,0:T(8,128)(2,1)}, bf16[576,2048]{1,0:T(8,128)(2,1)}, bf16[576,2048]{1,0:T(8,128)(2,1)}) custom-call(s32[1]{0:T(128)} %bitcast.1.first, bf16[1024,2048]{1,0:T(8,128)(2,1)} %get-tuple-element.232.refs_0_.refs_6_, ...), custom_call_target="tpu_custom_call" | custom-call | flops 1 | bytes 1 | tf_op jit(solution)/shard_map/expert_inner/pallas_call | solution.py:68
  283.5 3.0 add_convert_fusion.7
  288.5 35.9 %mix.1 = (bf16[256,2048]{1,0:T(8,128)(2,1)}, bf16[256,2048]{1,0:T(8,128)(2,1)}, bf16[256,2048]{1,0:T(8,128)(2,1)}, bf16[256,2048]{1,0:T(8,128)(2,1)}, f32[1024,128]{1,0:T(8,128)}) custom-call(s32[1]{0:T(128)} %bitcast.1.first, f32[1024,128]{1,0:T(8,128)} %get-tuple-element.206.refs_1_.side, bf16[1024,1408]{1,0:T(8,128)(2,1)} %get-tuple-element.235.refs_1_.act, ...), custom_call_target="tpu_custom_call" | custom-call | flops 1 | bytes 1 | tf_op jit(solution)/shard_map/mix/pallas_call | solution.py:68
  324.5 9.1 %collective-permute-done.20 = bf16[1408,512]{1,0:T(8,128)(2,1)} collective-permute-done((bf16[1408,512]{1,0:T(8,128)(2,1)}, bf16[1408,512]{1,0:T(8,128)(2,1)}, u32[]{:S(2)}, u32[]{:S(2)}) %collective-permute-start.20) | collective-permute-done | bytes 1441824 | tf_op jit(solution)/shard_map/ppermute | solution.py:115
  337.1 47.0 %back.1 = (bf16[256,2048]{1,0:T(8,128)(2,1)}, bf16[256,2048]{1,0:T(8,128)(2,1)}, bf16[256,2048]{1,0:T(8,128)(2,1)}, bf16[256,2048]{1,0:T(8,128)(2,1)}, f32[128,2048]{1,0:T(8,128)}) custom-call(f32[1024,128]{1,0:T(8,128)} %get-tuple-element.206.refs_1_.side, f32[1024,128]{1,0:T(8,128)} %get-tuple-element.239.totals, ...), custom_call_target="tpu_custom_call" | custom-call | flops 1 | bytes 1 | tf_op jit(solution)/shard_map/back/pallas_call | solution.py:68
  386.1 11.4 %weight_product.17 = (bf16[1024,1408]{1,0:T(8,128)(2,1)}, bf16[1024,1408]{1,0:T(8,128)(2,1)}) custom-call(s32[8]{0:T(128)} %fusion.5.blocks, bf16[576,2048]{1,0:T(8,128)(2,1)} %get-tuple-element.253.refs_0_, bf16[576,1408]{1,0:T(8,128)(2,1)} %get-tuple-element.255.refs_2_.refs_1_), custom_call_target="tpu_custom_call" | custom-call | flops 1 | bytes 1 | tf_op jit(solution)/shard_map/weight_product/pallas_call | solution.py:68
  398.1 10.8 %weight_product.18 = bf16[2048,1408]{1,0:T(8,128)(2,1)} custom-call(s32[8]{0:T(128)} %iota.11.blocks, bf16[576,2048]{1,0:T(8,128)(2,1)} %get-tuple-element.253.refs_0_, bf16[576,1408]{1,0:T(8,128)(2,1)} %get-tuple-element.258.refs_3_.refs_1_), custom_call_target="tpu_custom_call" | custom-call | flops 1 | bytes 1 | tf_op jit(solution)/shard_map/weight_product/pallas_call | solution.py:68
  410.3 3.2 add_convert_fusion.5
  416.6 2.8 add_convert_fusion.12
  427.1 18.1 %collective-permute-done.26 = bf16[256,2048]{1,0:T(8,128)(2,1)} collective-permute-done((bf16[256,2048]{1,0:T(8,128)(2,1)}, bf16[256,2048]{1,0:T(8,128)(2,1)}, u32[]{:S(2)}, u32[]{:S(2)}) %collective-permute-start.26) | collective-permute-done | bytes 1048608 | tf_op jit(solution)/shard_map/ppermute | solution.py:115
  448.8 4.0 fusion.6
  452.8 40.7 %collective-permute-done.21 = bf16[512,1408]{1,0:T(8,128)(2,1)S(1)} collective-permute-done((bf16[512,1408]{1,0:T(8,128)(2,1)S(1)}, bf16[512,1408]{1,0:T(8,128)(2,1)S(1)}, u32[]{:S(2)}, u32[]{:S(2)}) %collective-permute-start.21) | collective-permute-done | bytes 1441824 | tf_op jit(solution)/shard_map/ppermute | solution.py:115
  500.0 11.8 %weight_product.19 = (bf16[1408,1024]{1,0:T(8,128)(2,1)}, bf16[1408,1024]{1,0:T(8,128)(2,1)}) custom-call(s32[8]{0:T(128)} %fusion.5.blocks, bf16[576,2048]{1,0:T(8,128)(2,1)} %get-tuple-element.271.refs_0_, bf16[576,1408]{1,0:T(8,128)(2,1)} %get-tuple-element.272.refs_1_), custom_call_target="tpu_custom_call" | custom-call | flops 1 | bytes 1 | tf_op jit(solution)/shard_map/weight_product/pallas_call | solution.py:68
  514.0 11.3 %collective-permute-done.28 = bf16[512,1408]{1,0:T(8,128)(2,1)S(1)} collective-permute-done((bf16[512,1408]{1,0:T(8,128)(2,1)}, bf16[512,1408]{1,0:T(8,128)(2,1)S(1)}, u32[]{:S(2)}, u32[]{:S(2)}) %collective-permute-start.28) | collective-permute-done | bytes 1441824 | tf_op jit(solution)/shard_map/ppermute | solution.py:115
  525.3 3.0 add_convert_fusion.18
  529.1 15.8 %collective-permute-start.38 = (bf16[512,1408]{1,0:T(8,128)(2,1)S(1)}, bf16[512,1408]{1,0:T(8,128)(2,1)}, u32[]{:S(2)}, u32[]{:S(2)}) collective-permute-start(bf16[512,1408]{1,0:T(8,128)(2,1)S(1)} %add_convert_fusion.4), channel_id=1, source_target_pairs={{0,8},{4,12},{8,0},{12,4},{16,24},{20,28},{24,16},{28,20},{1,9},{5... | collective-permute-start | bytes 4325384 | tf_op jit(solution)/shard_map/ppermute | solution.py:115
  544.9 3.6 convert_add_fusion.2
  554.0 6.1 attended_gradient.1.out_grad
  560.2 21.9 %attend_back.1 = (bf16[1024,512]{1,0:T(8,128)(2,1)}, bf16[1024,512]{1,0:T(8,128)(2,1)}, bf16[1024,512]{1,0:T(8,128)(2,1)}, f32[3,8,512]{2,1,0:T(8,128)}) custom-call(s32[4]{0:T(128)} %iota_xor_fusion.places, bf16[3,1024,512]{2,1,0:T(8,128)(2,1)} %get-tuple-element.191.query.key.value, bf16[3,1024,512]{2,1,0:T(8,128)(2,1)} %get-tuple-element.191.query.key.value, ...), custom_call_target="tpu_custom_call" | custom-call | flops 1 | bytes 1 | tf_op jit(solution)/shard_map/attend_back/pallas_call | solution.py:68
  582.0 3.3 pad_maximum_fusion.1.refs_1_
  585.4 13.5 %weight_product.20 = (bf16[1024,1536]{1,0:T(8,128)(2,1)}, bf16[1024,1536]{1,0:T(8,128)(2,1)}) custom-call(s32[8]{0:T(128)} %fusion.5.blocks, bf16[1024,2048]{1,0:T(8,128)(2,1)} %get-tuple-element.294.refs_0_, bf16[1024,1536]{1,0:T(8,128)(2,1)} %pad_maximum_fusion.1.refs_1_), custom_call_target="tpu_custom_call" | custom-call | flops 1 | bytes 1 | tf_op jit(solution)/shard_map/weight_product/pallas_call | solution.py:68
  599.0 2.8 add_convert_fusion.17
  601.9 3.1 add_convert_fusion.3
  605.0 10.5 %collective-permute-start.41 = (bf16[1408,512]{1,0:T(8,128)(2,1)}, bf16[1408,512]{1,0:T(8,128)(2,1)}, u32[]{:S(2)}, u32[]{:S(2)}) collective-permute-start(bf16[1408,512]{1,0:T(8,128)(2,1)} %add_convert_fusion.3), channel_id=1, source_target_pairs={{0,8},{4,12},{8,0},{12,4},{16,24},{20,28},{24,16},{28,20},{1,9},{5... | collective-permute-start | bytes 4325384 | tf_op jit(solution)/shard_map/ppermute | solution.py:115
  619.1 5.5 collective-permute-start.42
  624.6 9.3 %weight_product.21 = (bf16[512,1024]{1,0:T(8,128)(2,1)}, bf16[512,1024]{1,0:T(8,128)(2,1)}) custom-call(s32[8]{0:T(128)} %fusion.5.blocks, bf16[256,2048]{1,0:T(8,128)(2,1)} %copy-done.14, bf16[256,2048]{1,0:T(8,128)(2,1)} %copy-done.19, bf16[256,2048]{1,0:T(8,128)(2,1)} %copy-done.18, bf16[256,2048]{1,0:T(8,128)(2,1)} %copy-done.20, ...), custom_call_target="tpu_custom_call" | custom-call | flops 1 | bytes 1 | tf_op jit(solution)/shard_map/weight_product/pallas_call | solution.py:68
  633.9 12.5 %first_back.1 = (bf16[256,2048]{1,0:T(8,128)(2,1)}, bf16[256,2048]{1,0:T(8,128)(2,1)}, bf16[256,2048]{1,0:T(8,128)(2,1)}, bf16[256,2048]{1,0:T(8,128)(2,1)}, f32[8,2048]{1,0:T(8,128)}) custom-call(bf16[1024,512]{1,0:T(8,128)(2,1)} %get-tuple-element.304.query, bf16[1024,512]{1,0:T(8,128)(2,1)} %get-tuple-element.295.key, ...), custom_call_target="tpu_custom_call" | custom-call | flops 1 | bytes 1 | tf_op jit(solution)/shard_map/first_back/pallas_call | solution.py:68
  647.5 3.1 add_convert_fusion.10
  650.7 2.8 add_convert_fusion.16
  653.5 2.9 add_convert_fusion.2
  656.5 18.5 %collective-permute-start.46 = (bf16[512,1408]{1,0:T(8,128)(2,1)}, bf16[512,1408]{1,0:T(8,128)(2,1)}, u32[]{:S(2)}, u32[]{:S(2)}) collective-permute-start(bf16[512,1408]{1,0:T(8,128)(2,1)} %add_convert_fusion.2), channel_id=1, source_target_pairs={{0,8},{4,12},{8,0},{12,4},{16,24},{20,28},{24,16},{28,20},{1,9},{5... | collective-permute-start | bytes 4325384 | tf_op jit(solution)/shard_map/ppermute | solution.py:115
  675.0 3.1 add_bitcast_fusion.3
  681.0 17.0 %collective-permute-done.47 = bf16[1408,256]{1,0:T(8,128)(2,1)S(1)} collective-permute-done((bf16[1408,256]{1,0:T(8,128)(2,1)}, bf16[1408,256]{1,0:T(8,128)(2,1)S(1)}, u32[]{:S(2)}, u32[]{:S(2)}) %collective-permute-start.47) | collective-permute-done | bytes 720928 | tf_op jit(solution)/shard_map/ppermute | solution.py:115
  701.8 21.1 %collective-permute-done.46 = bf16[512,1408]{1,0:T(8,128)(2,1)} collective-permute-done((bf16[512,1408]{1,0:T(8,128)(2,1)}, bf16[512,1408]{1,0:T(8,128)(2,1)}, u32[]{:S(2)}, u32[]{:S(2)}) %collective-permute-start.46) | collective-permute-done | bytes 1441824 | tf_op jit(solution)/shard_map/ppermute | solution.py:115
  728.3 19.6 %collective-permute-done.43 = bf16[256,2048]{1,0:T(8,128)(2,1)S(1)} collective-permute-done((bf16[256,2048]{1,0:T(8,128)(2,1)S(1)}, bf16[256,2048]{1,0:T(8,128)(2,1)S(1)}, u32[]{:S(2)}, u32[]{:S(2)}) %collective-permute-start.43) | collective-permute-done | bytes 1048608 | tf_op jit(solution)/shard_map/ppermute | solution.py:115
  747.8 3.6 collective-permute-start.48
  755.2 4.4 collective-permute-done.49
  761.3 23.1 %collective-permute-done.48 = bf16[512,1536]{1,0:T(8,128)(2,1)S(1)} collective-permute-done((bf16[512,1536]{1,0:T(8,128)(2,1)S(1)}, bf16[512,1536]{1,0:T(8,128)(2,1)S(1)}, u32[]{:S(2)}, u32[]{:S(2)}) %collective-permute-start.48) | collective-permute-done | bytes 1572896 | tf_op jit(solution)/shard_map/ppermute | solution.py:115
  785.9 4.1 collective-permute-start.50
  791.9 3.0 collective-permute-start.54
  795.1 2.9 pad_maximum_fusion
  798.0 25.0 %collective-permute-done.50 = bf16[256,1536]{1,0:T(8,128)(2,1)} collective-permute-done((bf16[256,1536]{1,0:T(8,128)(2,1)S(1)}, bf16[256,1536]{1,0:T(8,128)(2,1)}, u32[]{:S(2)}, u32[]{:S(2)}) %collective-permute-start.50) | collective-permute-done | bytes 786464 | tf_op jit(solution)/shard_map/ppermute | solution.py:115
  823.0 16.9 %all-reduce.3.cloned.1.call-done = f32[14,2048]{1,0:T(8,128)} async-done(((f32[14,2048]{1,0:T(8,128)}), f32[14,2048]{1,0:T(8,128)}) %all-reduce.3.cloned.1.call-update) | async-done | bytes 114704 | tf_op jit(solution)/shard_map/psum | solution.py:1365
  852.8 4.3 collective-permute-done.53
  859.0 28.8 %collective-permute-done.56 = bf16[1408,256]{1,0:T(8,128)(2,1)} collective-permute-done((bf16[1408,256]{1,0:T(8,128)(2,1)}, bf16[1408,256]{1,0:T(8,128)(2,1)}, u32[]{:S(2)}, u32[]{:S(2)}) %collective-permute-start.56) | collective-permute-done | bytes 720928 | tf_op jit(solution)/shard_map/ppermute | solution.py:115
  887.9 3.3 add_bitcast_fusion
  (304 shorter events, 116.3 us)
Async XLA Ops:
  7.2 78.4 %all-gather.3.cloned.1.call-start = ((), (), s32[]{:S(2)}) async-start(), calls=%async_computation.5 | async-start | bytes 2359296 | tf_op jit(solution)/shard_map/all_gather | solution.py:1204
  8.2 9.4 %collective-permute-start.11 = (bf16[64,2048]{1,0:T(8,128)(2,1)S(1)}, bf16[64,2048]{1,0:T(8,128)(2,1)S(1)}, u32[]{:S(2)}, u32[]{:S(2)}) collective-permute-start(bf16[64,2048]{1,0:T(8,128)(2,1)S(1)} %constant_dynamic-slice_fusion.1), channel_id=1, source_target_pairs={{0,2},{1,3},{2,0},{3,1},{4,6},{5,7},{6,4},{7,5},{8,10},{9,11},{10,... | collective-permute-start | bytes 786440 | tf_op jit(solution)/shard_map/ppermute | solution.py:115
  11.9 4.5 collective-permute-start.2
  16.4 1.2 collective-permute-start.3
  18.3 306.2 %reduce-scatter.3.cloned.1.call-start = ((), (), s32[]{:S(2)}) async-start(), calls=%async_computation.2 | async-start | bytes 6488064 | tf_op jit(solution)/shard_map/reduce_scatter | solution.py:1165
  18.4 25.5 %collective-permute-start = (bf16[256,2048]{1,0:T(8,128)(2,1)}, bf16[256,2048]{1,0:T(8,128)(2,1)S(1)}, u32[]{:S(2)}, u32[]{:S(2)}) collective-permute-start(bf16[256,2048]{1,0:T(8,128)(2,1)} %refs_1_), channel_id=1, source_target_pairs={{0,2},{1,3},{2,0},{3,1},{4,6},{5,7},{6,4},{7,5},{8,10},{9,11},{10,... | collective-permute-start | bytes 3145736 | tf_op jit(solution)/shard_map/ppermute | solution.py:115
  19.9 58.8 %collective-permute-start.7 = (bf16[512,2048]{1,0:T(8,128)(2,1)}, bf16[512,2048]{1,0:T(8,128)(2,1)}, u32[]{:S(2)}, u32[]{:S(2)}) collective-permute-start(bf16[512,2048]{1,0:T(8,128)(2,1)} %weight), channel_id=1, source_target_pairs={{0,1},{1,0},{2,3},{3,2},{4,5},{5,4},{6,7},{7,6},{8,9},{9,8},{10,11... | collective-permute-start | bytes 6291464 | tf_op jit(solution)/shard_map/ppermute | solution.py:115
  19.9 3.8 collective-permute-start.1
  20.5 27.5 %collective-permute-start.4 = (bf16[256,2048]{1,0:T(8,128)(2,1)}, bf16[256,2048]{1,0:T(8,128)(2,1)S(1)}, u32[]{:S(2)}, u32[]{:S(2)}) collective-permute-start(bf16[256,2048]{1,0:T(8,128)(2,1)} %refs_1_), channel_id=1, source_target_pairs={{0,1},{1,0},{2,3},{3,2},{4,5},{5,4},{6,7},{7,6},{8,9},{9,8},{10,11... | collective-permute-start | bytes 3145736 | tf_op jit(solution)/shard_map/ppermute | solution.py:115
  43.9 14.9 %collective-permute-start.5 = (bf16[256,2048]{1,0:T(8,128)(2,1)S(1)}, bf16[256,2048]{1,0:T(8,128)(2,1)S(1)}, u32[]{:S(2)}, u32[]{:S(2)}) collective-permute-start(bf16[256,2048]{1,0:T(8,128)(2,1)S(1)} %collective-permute-done.refs_0_.refs_3_), channel_id=1, source_target_pairs={{0,1},{1,0},{2,3},{3,2},{4,5},{5,4},{6,7},{7,6},{8,9},{9,8},{10,11... | collective-permute-start | bytes 3145736 | tf_op jit(solution)/shard_map/ppermute | solution.py:115
  43.9 34.9 %collective-permute-start.6 = (bf16[256,2048]{1,0:T(8,128)(2,1)}, bf16[256,2048]{1,0:T(8,128)(2,1)S(1)}, u32[]{:S(2)}, u32[]{:S(2)}) collective-permute-start(bf16[256,2048]{1,0:T(8,128)(2,1)} %refs_4_.1), channel_id=1, source_target_pairs={{0,2},{1,3},{2,0},{3,1},{4,6},{5,7},{6,4},{7,5},{8,10},{9,11},{10,... | collective-permute-start | bytes 3145736 | tf_op jit(solution)/shard_map/ppermute | solution.py:115
  78.7 51.2 %copy-start.5 = (bf16[256,2048]{1,0:T(8,128)(2,1)}, bf16[256,2048]{1,0:T(8,128)(2,1)S(1)}, u32[]{:S(2)}) copy-start(bf16[256,2048]{1,0:T(8,128)(2,1)S(1)} %collective-permute-done.6.refs_4_.refs_5_.refs_6_) | copy-start | bytes 3145732
  85.5 17.6 %collective-permute-start.12 = (bf16[512,2048]{1,0:T(8,128)(2,1)}, bf16[512,2048]{1,0:T(8,128)(2,1)}, u32[]{:S(2)}, u32[]{:S(2)}) collective-permute-start(bf16[512,2048]{1,0:T(8,128)(2,1)} %all-gather.3.cloned.1.call-done), channel_id=1, source_target_pairs={{0,1},{1,0},{2,3},{3,2},{4,5},{5,4},{6,7},{7,6},{8,9},{9,8},{10,11... | collective-permute-start | bytes 6291464 | tf_op jit(solution)/shard_map/ppermute | solution.py:115
  85.9 14.0 %collective-permute-start.9 = (bf16[512,512]{1,0:T(8,128)(2,1)S(1)}, bf16[512,512]{1,0:T(8,128)(2,1)S(1)}, u32[]{:S(2)}, u32[]{:S(2)}) collective-permute-start(bf16[512,512]{1,0:T(8,128)(2,1)S(1)} %copy-done.30), channel_id=1, source_target_pairs={{0,2},{1,3},{2,0},{3,1},{4,6},{5,7},{6,4},{7,5},{8,10},{9,11},{10,... | collective-permute-start | bytes 1572872 | tf_op jit(solution)/shard_map/ppermute | solution.py:115
  86.4 16.7 %collective-permute-start.8 = (bf16[512,512]{1,0:T(8,128)(2,1)}, bf16[512,512]{1,0:T(8,128)(2,1)}, u32[]{:S(2)}, u32[]{:S(2)}) collective-permute-start(bf16[512,512]{1,0:T(8,128)(2,1)} %get-tuple-element.302.refs_2_.refs_4_), channel_id=1, source_target_pairs={{0,1},{1,0},{2,3},{3,2},{4,5},{5,4},{6,7},{7,6},{8,9},{9,8},{10,11... | collective-permute-start | bytes 1572872 | tf_op jit(solution)/shard_map/ppermute | solution.py:115
  99.9 3.2 collective-permute-start.10
  99.9 15.3 %collective-permute-start.14 = (bf16[512,512]{1,0:T(8,128)(2,1)}, bf16[512,512]{1,0:T(8,128)(2,1)S(1)}, u32[]{:S(2)}, u32[]{:S(2)}) collective-permute-start(bf16[512,512]{1,0:T(8,128)(2,1)} %get-tuple-element.302.refs_2_.refs_4_), channel_id=1, source_target_pairs={{0,2},{1,3},{2,0},{3,1},{4,6},{5,7},{6,4},{7,5},{8,10},{9,11},{10,... | collective-permute-start | bytes 1572872 | tf_op jit(solution)/shard_map/ppermute | solution.py:115
  102.9 13.0 %collective-permute-start.13 = (bf16[512,512]{1,0:T(8,128)(2,1)S(1)}, bf16[512,512]{1,0:T(8,128)(2,1)S(1)}, u32[]{:S(2)}, u32[]{:S(2)}) collective-permute-start(bf16[512,512]{1,0:T(8,128)(2,1)S(1)} %copy-done.30), channel_id=1, source_target_pairs={{0,1},{1,0},{2,3},{3,2},{4,5},{5,4},{6,7},{7,6},{8,9},{9,8},{10,11... | collective-permute-start | bytes 1572872 | tf_op jit(solution)/shard_map/ppermute | solution.py:115
  115.2 2.0 collective-permute-start.15
  115.6 14.7 %collective-permute-start.16 = (bf16[256,2048]{1,0:T(8,128)(2,1)S(1)}, bf16[256,2048]{1,0:T(8,128)(2,1)S(1)}, u32[]{:S(2)}, u32[]{:S(2)}) collective-permute-start(bf16[256,2048]{1,0:T(8,128)(2,1)S(1)} %copy-done.3), channel_id=1, source_target_pairs={{0,1},{1,0},{2,3},{3,2},{4,5},{5,4},{6,7},{7,6},{8,9},{9,8},{10,11... | collective-permute-start | bytes 3145736 | tf_op jit(solution)/shard_map/ppermute | solution.py:115
  129.9 2.7 collective-permute-start.17
  175.8 474.8 %reduce-scatter.5.cloned.1.call-start = ((), (), s32[]{:S(2)}) async-start(), calls=%async_computation.3 | async-start | bytes 6488064 | tf_op jit(solution)/shard_map/reduce_scatter | solution.py:1165
  190.6 92.9 %collective-permute-start.18 = (bf16[1408,1024]{1,0:T(8,128)(2,1)}, bf16[1408,1024]{1,0:T(8,128)(2,1)}, u32[]{:S(2)}, u32[]{:S(2)}) collective-permute-start(bf16[1408,1024]{1,0:T(8,128)(2,1)} %get-tuple-element.215), channel_id=1, source_target_pairs={{0,4},{4,0},{8,12},{12,8},{16,20},{20,16},{24,28},{28,24},{1,5},{5... | collective-permute-start | bytes 8650760 | tf_op jit(solution)/shard_map/ppermute | solution.py:115
  205.6 178.5 %collective-permute-start.19 = (bf16[1024,1408]{1,0:T(8,128)(2,1)}, bf16[1024,1408]{1,0:T(8,128)(2,1)S(1)}, u32[]{:S(2)}, u32[]{:S(2)}) collective-permute-start(bf16[1024,1408]{1,0:T(8,128)(2,1)} %get-tuple-element.238), channel_id=1, source_target_pairs={{0,4},{4,0},{8,12},{12,8},{16,20},{20,16},{24,28},{28,24},{1,5},{5... | collective-permute-start | bytes 8650760 | tf_op jit(solution)/shard_map/ppermute | solution.py:115
  286.5 47.1 %collective-permute-start.20 = (bf16[1408,512]{1,0:T(8,128)(2,1)}, bf16[1408,512]{1,0:T(8,128)(2,1)}, u32[]{:S(2)}, u32[]{:S(2)}) collective-permute-start(bf16[1408,512]{1,0:T(8,128)(2,1)} %add_convert_fusion.7), channel_id=1, source_target_pairs={{0,8},{4,12},{8,0},{12,4},{16,24},{20,28},{24,16},{28,20},{1,9},{5... | collective-permute-start | bytes 4325384 | tf_op jit(solution)/shard_map/ppermute | solution.py:115
  286.8 123.4 %collective-permute-start.22 = (bf16[1024,1408]{1,0:T(8,128)(2,1)}, bf16[1024,1408]{1,0:T(8,128)(2,1)}, u32[]{:S(2)}, u32[]{:S(2)}) collective-permute-start(bf16[1024,1408]{1,0:T(8,128)(2,1)} %get-tuple-element.252), channel_id=1, source_target_pairs={{0,4},{4,0},{8,12},{12,8},{16,20},{20,16},{24,28},{28,24},{1,5},{5... | collective-permute-start | bytes 8650760 | tf_op jit(solution)/shard_map/ppermute | solution.py:115
  335.4 62.1 %collective-permute-start.23 = (bf16[1408,256]{1,0:T(8,128)(2,1)S(1)}, bf16[1408,256]{1,0:T(8,128)(2,1)}, u32[]{:S(2)}, u32[]{:S(2)}) collective-permute-start(bf16[1408,256]{1,0:T(8,128)(2,1)S(1)} %add_convert_fusion.20), channel_id=1, source_target_pairs={{0,24},{4,28},{8,16},{12,20},{16,8},{20,12},{24,0},{28,4},{1,25},{... | collective-permute-start | bytes 2162696 | tf_op jit(solution)/shard_map/ppermute | solution.py:115
  337.1 47.0 %copy-start.26 = (bf16[1024,1408]{1,0:T(8,128)(2,1)S(1)}, bf16[1024,1408]{1,0:T(8,128)(2,1)}, u32[]{:S(2)}) copy-start(bf16[1024,1408]{1,0:T(8,128)(2,1)} %get-tuple-element.218) | copy-start | bytes 8650756
  408.9 431.0 %all-reduce.3.cloned.1.call-start = ((), (), s32[]{:S(2)}) async-start(), calls=%async_computation.4 | async-start | bytes 262144 | tf_op jit(solution)/shard_map/psum | solution.py:1365
  413.5 3.0 collective-permute-start.25
  415.0 96.8 %collective-permute-start.29 = (bf16[1024,1408]{1,0:T(8,128)(2,1)}, bf16[1024,1408]{1,0:T(8,128)(2,1)}, u32[]{:S(2)}, u32[]{:S(2)}) collective-permute-start(bf16[1024,1408]{1,0:T(8,128)(2,1)} %get-tuple-element.270), channel_id=1, source_target_pairs={{0,4},{4,0},{8,12},{12,8},{16,20},{20,16},{24,28},{28,24},{1,5},{5... | collective-permute-start | bytes 8650760 | tf_op jit(solution)/shard_map/ppermute | solution.py:115
  416.5 29.7 %collective-permute-start.24 = (bf16[256,2048]{1,0:T(8,128)(2,1)}, bf16[256,2048]{1,0:T(8,128)(2,1)}, u32[]{:S(2)}, u32[]{:S(2)}) collective-permute-start(bf16[256,2048]{1,0:T(8,128)(2,1)} %get-tuple-element.260), channel_id=1, source_target_pairs={{0,1},{1,0},{2,3},{3,2},{4,5},{5,4},{6,7},{7,6},{8,9},{9,8},{10,11... | collective-permute-start | bytes 3145736 | tf_op jit(solution)/shard_map/ppermute | solution.py:115
  419.4 25.9 %collective-permute-start.26 = (bf16[256,2048]{1,0:T(8,128)(2,1)}, bf16[256,2048]{1,0:T(8,128)(2,1)}, u32[]{:S(2)}, u32[]{:S(2)}) collective-permute-start(bf16[256,2048]{1,0:T(8,128)(2,1)} %add_convert_fusion.12), channel_id=1, source_target_pairs={{0,2},{1,3},{2,0},{3,1},{4,6},{5,7},{6,4},{7,5},{8,10},{9,11},{10,... | collective-permute-start | bytes 3145736 | tf_op jit(solution)/shard_map/ppermute | solution.py:115
  423.5 70.0 %collective-permute-start.21 = (bf16[512,1408]{1,0:T(8,128)(2,1)S(1)}, bf16[512,1408]{1,0:T(8,128)(2,1)S(1)}, u32[]{:S(2)}, u32[]{:S(2)}) collective-permute-start(bf16[512,1408]{1,0:T(8,128)(2,1)S(1)} %copy-done.31), channel_id=1, source_target_pairs={{0,8},{4,12},{8,0},{12,4},{16,24},{20,28},{24,16},{28,20},{1,9},{5... | collective-permute-start | bytes 4325384 | tf_op jit(solution)/shard_map/ppermute | solution.py:115
  426.3 99.0 %collective-permute-start.28 = (bf16[512,1408]{1,0:T(8,128)(2,1)}, bf16[512,1408]{1,0:T(8,128)(2,1)S(1)}, u32[]{:S(2)}, u32[]{:S(2)}) collective-permute-start(bf16[512,1408]{1,0:T(8,128)(2,1)} %add_convert_fusion.5), channel_id=1, source_target_pairs={{0,8},{4,12},{8,0},{12,4},{16,24},{20,28},{24,16},{28,20},{1,9},{5... | collective-permute-start | bytes 4325384 | tf_op jit(solution)/shard_map/ppermute | solution.py:115
  445.2 156.7 %collective-permute-start.37 = (bf16[1408,1024]{1,0:T(8,128)(2,1)}, bf16[1408,1024]{1,0:T(8,128)(2,1)}, u32[]{:S(2)}, u32[]{:S(2)}) collective-permute-start(bf16[1408,1024]{1,0:T(8,128)(2,1)} %get-tuple-element.292), channel_id=1, source_target_pairs={{0,4},{4,0},{8,12},{12,8},{16,20},{20,16},{24,28},{28,24},{1,5},{5... | collective-permute-start | bytes 8650760 | tf_op jit(solution)/shard_map/ppermute | solution.py:115
  452.8 75.7 %copy-start.14 = (bf16[256,2048]{1,0:T(8,128)(2,1)}, bf16[256,2048]{1,0:T(8,128)(2,1)S(1)}, u32[]{:S(2)}) copy-start(bf16[256,2048]{1,0:T(8,128)(2,1)S(1)} %get-tuple-element.380.refs_0_) | copy-start | bytes 3145732
  497.1 47.7 %collective-permute-start.33 = (bf16[256,2048]{1,0:T(8,128)(2,1)S(1)}, bf16[256,2048]{1,0:T(8,128)(2,1)S(1)}, u32[]{:S(2)}, u32[]{:S(2)}) collective-permute-start(bf16[256,2048]{1,0:T(8,128)(2,1)S(1)} %get-tuple-element.380.refs_0_), channel_id=1, source_target_pairs={{0,2},{1,3},{2,0},{3,1},{4,6},{5,7},{6,4},{7,5},{8,10},{9,11},{10,... | collective-permute-start | bytes 3145736 | tf_op jit(solution)/shard_map/ppermute | solution.py:115
  498.7 29.6 %collective-permute-start.27 = (bf16[256,1408]{1,0:T(8,128)(2,1)}, bf16[256,1408]{1,0:T(8,128)(2,1)}, u32[]{:S(2)}, u32[]{:S(2)}) collective-permute-start(bf16[256,1408]{1,0:T(8,128)(2,1)} %add_convert_fusion.19), channel_id=1, source_target_pairs={{0,24},{4,28},{8,16},{12,20},{16,8},{20,12},{24,0},{28,4},{1,25},{... | collective-permute-start | bytes 2162696 | tf_op jit(solution)/shard_map/ppermute | solution.py:115
  528.3 20.1 %collective-permute-start.31 = (bf16[256,2048]{1,0:T(8,128)(2,1)S(1)}, bf16[256,2048]{1,0:T(8,128)(2,1)S(1)}, u32[]{:S(2)}, u32[]{:S(2)}) collective-permute-start(bf16[256,2048]{1,0:T(8,128)(2,1)S(1)} %copy-done.64), channel_id=1, source_target_pairs={{0,1},{1,0},{2,3},{3,2},{4,5},{5,4},{6,7},{7,6},{8,9},{9,8},{10,11... | collective-permute-start | bytes 3145736 | tf_op jit(solution)/shard_map/ppermute | solution.py:115
  528.5 24.1 %collective-permute-start.32 = (bf16[256,2048]{1,0:T(8,128)(2,1)S(1)}, bf16[256,2048]{1,0:T(8,128)(2,1)S(1)}, u32[]{:S(2)}, u32[]{:S(2)}) collective-permute-start(bf16[256,2048]{1,0:T(8,128)(2,1)S(1)} %get-tuple-element.380.refs_0_), channel_id=1, source_target_pairs={{0,1},{1,0},{2,3},{3,2},{4,5},{5,4},{6,7},{7,6},{8,9},{9,8},{10,11... | collective-permute-start | bytes 3145736 | tf_op jit(solution)/shard_map/ppermute | solution.py:115
  529.1 69.8 %collective-permute-start.38 = (bf16[512,1408]{1,0:T(8,128)(2,1)S(1)}, bf16[512,1408]{1,0:T(8,128)(2,1)}, u32[]{:S(2)}, u32[]{:S(2)}) collective-permute-start(bf16[512,1408]{1,0:T(8,128)(2,1)S(1)} %add_convert_fusion.4), channel_id=1, source_target_pairs={{0,8},{4,12},{8,0},{12,4},{16,24},{20,28},{24,16},{28,20},{1,9},{5... | collective-permute-start | bytes 4325384 | tf_op jit(solution)/shard_map/ppermute | solution.py:115
  544.9 7.8 collective-permute-start.34
  548.5 56.6 %collective-permute-start.36 = (bf16[256,1408]{1,0:T(8,128)(2,1)}, bf16[256,1408]{1,0:T(8,128)(2,1)}, u32[]{:S(2)}, u32[]{:S(2)}) collective-permute-start(bf16[256,1408]{1,0:T(8,128)(2,1)} %add_convert_fusion.18), channel_id=1, source_target_pairs={{0,24},{4,28},{8,16},{12,20},{16,8},{20,12},{24,0},{28,4},{1,25},{... | collective-permute-start | bytes 2162696 | tf_op jit(solution)/shard_map/ppermute | solution.py:115
  552.6 94.8 %collective-permute-start.30 = (bf16[256,2048]{1,0:T(8,128)(2,1)}, bf16[256,2048]{1,0:T(8,128)(2,1)}, u32[]{:S(2)}, u32[]{:S(2)}) collective-permute-start(bf16[256,2048]{1,0:T(8,128)(2,1)} %get-tuple-element.277), channel_id=1, source_target_pairs={{0,1},{1,0},{2,3},{3,2},{4,5},{5,4},{6,7},{7,6},{8,9},{9,8},{10,11... | collective-permute-start | bytes 3145736 | tf_op jit(solution)/shard_map/ppermute | solution.py:115
  553.7 99.8 %collective-permute-start.44 = (bf16[1024,1408]{1,0:T(8,128)(2,1)}, bf16[1024,1408]{1,0:T(8,128)(2,1)}, u32[]{:S(2)}, u32[]{:S(2)}) collective-permute-start(bf16[1024,1408]{1,0:T(8,128)(2,1)} %get-tuple-element.320), channel_id=1, source_target_pairs={{0,4},{4,0},{8,12},{12,8},{16,20},{20,16},{24,28},{28,24},{1,5},{5... | collective-permute-start | bytes 8650760 | tf_op jit(solution)/shard_map/ppermute | solution.py:115
  598.9 48.5 %collective-permute-start.35 = (bf16[256,2048]{1,0:T(8,128)(2,1)}, bf16[256,2048]{1,0:T(8,128)(2,1)}, u32[]{:S(2)}, u32[]{:S(2)}) collective-permute-start(bf16[256,2048]{1,0:T(8,128)(2,1)} %add_convert_fusion.11), channel_id=1, source_target_pairs={{0,2},{1,3},{2,0},{3,1},{4,6},{5,7},{6,4},{7,5},{8,10},{9,11},{10,... | collective-permute-start | bytes 3145736 | tf_op jit(solution)/shard_map/ppermute | solution.py:115
  605.0 45.7 %collective-permute-start.41 = (bf16[1408,512]{1,0:T(8,128)(2,1)}, bf16[1408,512]{1,0:T(8,128)(2,1)}, u32[]{:S(2)}, u32[]{:S(2)}) collective-permute-start(bf16[1408,512]{1,0:T(8,128)(2,1)} %add_convert_fusion.3), channel_id=1, source_target_pairs={{0,8},{4,12},{8,0},{12,4},{16,24},{20,28},{24,16},{28,20},{1,9},{5... | collective-permute-start | bytes 4325384 | tf_op jit(solution)/shard_map/ppermute | solution.py:115
  619.1 31.5 %collective-permute-start.42 = (bf16[256,1408]{1,0:T(8,128)(2,1)}, bf16[256,1408]{1,0:T(8,128)(2,1)}, u32[]{:S(2)}, u32[]{:S(2)}) collective-permute-start(bf16[256,1408]{1,0:T(8,128)(2,1)} %add_convert_fusion.17), channel_id=1, source_target_pairs={{0,24},{4,28},{8,16},{12,20},{16,8},{20,12},{24,0},{28,4},{1,25},{... | collective-permute-start | bytes 2162696 | tf_op jit(solution)/shard_map/ppermute | solution.py:115
  647.4 78.8 %collective-permute-start.45 = (bf16[1024,1536]{1,0:T(8,128)(2,1)}, bf16[1024,1536]{1,0:T(8,128)(2,1)}, u32[]{:S(2)}, u32[]{:S(2)}) collective-permute-start(bf16[1024,1536]{1,0:T(8,128)(2,1)} %get-tuple-element.325), channel_id=1, source_target_pairs={{0,4},{4,0},{8,12},{12,8},{16,20},{20,16},{24,28},{28,24},{1,5},{5... | collective-permute-start | bytes 9437192 | tf_op jit(solution)/shard_map/ppermute | solution.py:115
  650.6 47.4 %collective-permute-start.40 = (bf16[256,2048]{1,0:T(8,128)(2,1)}, bf16[256,2048]{1,0:T(8,128)(2,1)}, u32[]{:S(2)}, u32[]{:S(2)}) collective-permute-start(bf16[256,2048]{1,0:T(8,128)(2,1)} %get-tuple-element.313), channel_id=1, source_target_pairs={{0,1},{1,0},{2,3},{3,2},{4,5},{5,4},{6,7},{7,6},{8,9},{9,8},{10,11... | collective-permute-start | bytes 3145736 | tf_op jit(solution)/shard_map/ppermute | solution.py:115
  656.5 66.4 %collective-permute-start.46 = (bf16[512,1408]{1,0:T(8,128)(2,1)}, bf16[512,1408]{1,0:T(8,128)(2,1)}, u32[]{:S(2)}, u32[]{:S(2)}) collective-permute-start(bf16[512,1408]{1,0:T(8,128)(2,1)} %add_convert_fusion.2), channel_id=1, source_target_pairs={{0,8},{4,12},{8,0},{12,4},{16,24},{20,28},{24,16},{28,20},{1,9},{5... | collective-permute-start | bytes 4325384 | tf_op jit(solution)/shard_map/ppermute | solution.py:115
  678.7 72.7 %collective-permute-start.39 = (bf16[256,2048]{1,0:T(8,128)(2,1)}, bf16[256,2048]{1,0:T(8,128)(2,1)S(1)}, u32[]{:S(2)}, u32[]{:S(2)}) collective-permute-start(bf16[256,2048]{1,0:T(8,128)(2,1)} %get-tuple-element.310), channel_id=1, source_target_pairs={{0,1},{1,0},{2,3},{3,2},{4,5},{5,4},{6,7},{7,6},{8,9},{9,8},{10,11... | collective-permute-start | bytes 3145736 | tf_op jit(solution)/shard_map/ppermute | solution.py:115
  679.0 18.9 %collective-permute-start.47 = (bf16[1408,256]{1,0:T(8,128)(2,1)}, bf16[1408,256]{1,0:T(8,128)(2,1)S(1)}, u32[]{:S(2)}, u32[]{:S(2)}) collective-permute-start(bf16[1408,256]{1,0:T(8,128)(2,1)} %add_convert_fusion.16), channel_id=1, source_target_pairs={{0,24},{4,28},{8,16},{12,20},{16,8},{20,12},{24,0},{28,4},{1,25},{... | collective-permute-start | bytes 2162696 | tf_op jit(solution)/shard_map/ppermute | solution.py:115
  698.0 87.9 %collective-permute-start.51 = (bf16[1408,1024]{1,0:T(8,128)(2,1)S(1)}, bf16[1408,1024]{1,0:T(8,128)(2,1)S(1)}, u32[]{:S(2)}, u32[]{:S(2)}) collective-permute-start(bf16[1408,1024]{1,0:T(8,128)(2,1)S(1)} %copy-done.63), channel_id=1, source_target_pairs={{0,4},{4,0},{8,12},{12,8},{16,20},{20,16},{24,28},{28,24},{1,5},{5... | collective-permute-start | bytes 8650760 | tf_op jit(solution)/shard_map/ppermute | solution.py:115
  698.0 142.0 %collective-permute-start.52 = (bf16[512,1024]{1,0:T(8,128)(2,1)}, bf16[512,1024]{1,0:T(8,128)(2,1)}, u32[]{:S(2)}, u32[]{:S(2)}) collective-permute-start(bf16[512,1024]{1,0:T(8,128)(2,1)} %get-tuple-element.342), channel_id=1, source_target_pairs={{0,4},{4,0},{8,12},{12,8},{16,20},{20,16},{24,28},{28,24},{1,5},{5... | collective-permute-start | bytes 3145736 | tf_op jit(solution)/shard_map/ppermute | solution.py:115
  722.8 25.0 %collective-permute-start.43 = (bf16[256,2048]{1,0:T(8,128)(2,1)S(1)}, bf16[256,2048]{1,0:T(8,128)(2,1)S(1)}, u32[]{:S(2)}, u32[]{:S(2)}) collective-permute-start(bf16[256,2048]{1,0:T(8,128)(2,1)S(1)} %add_convert_fusion.9), channel_id=1, source_target_pairs={{0,2},{1,3},{2,0},{3,1},{4,6},{5,7},{6,4},{7,5},{8,10},{9,11},{10,... | collective-permute-start | bytes 3145736 | tf_op jit(solution)/shard_map/ppermute | solution.py:115
  726.2 33.4 %collective-permute-start.49 = (bf16[256,1408]{1,0:T(8,128)(2,1)S(1)}, bf16[256,1408]{1,0:T(8,128)(2,1)S(1)}, u32[]{:S(2)}, u32[]{:S(2)}) collective-permute-start(bf16[256,1408]{1,0:T(8,128)(2,1)S(1)} %add_convert_fusion.15), channel_id=1, source_target_pairs={{0,24},{4,28},{8,16},{12,20},{16,8},{20,12},{24,0},{28,4},{1,25},{... | collective-permute-start | bytes 2162696 | tf_op jit(solution)/shard_map/ppermute | solution.py:115
  747.8 36.6 %collective-permute-start.48 = (bf16[512,1536]{1,0:T(8,128)(2,1)S(1)}, bf16[512,1536]{1,0:T(8,128)(2,1)S(1)}, u32[]{:S(2)}, u32[]{:S(2)}) collective-permute-start(bf16[512,1536]{1,0:T(8,128)(2,1)S(1)} %add_convert_fusion), channel_id=1, source_target_pairs={{0,8},{4,12},{8,0},{12,4},{16,24},{20,28},{24,16},{28,20},{1,9},{5... | collective-permute-start | bytes 4718600 | tf_op jit(solution)/shard_map/ppermute | solution.py:115
  785.9 37.2 %collective-permute-start.50 = (bf16[256,1536]{1,0:T(8,128)(2,1)S(1)}, bf16[256,1536]{1,0:T(8,128)(2,1)}, u32[]{:S(2)}, u32[]{:S(2)}) collective-permute-start(bf16[256,1536]{1,0:T(8,128)(2,1)S(1)} %add_convert_fusion.13), channel_id=1, source_target_pairs={{0,24},{4,28},{8,16},{12,20},{16,8},{20,12},{24,0},{28,4},{1,25},{... | collective-permute-start | bytes 2359304 | tf_op jit(solution)/shard_map/ppermute | solution.py:115
  791.9 52.8 %collective-permute-start.54 = (bf16[1408,512]{1,0:T(8,128)(2,1)}, bf16[1408,512]{1,0:T(8,128)(2,1)}, u32[]{:S(2)}, u32[]{:S(2)}) collective-permute-start(bf16[1408,512]{1,0:T(8,128)(2,1)} %add_convert_fusion.1), channel_id=1, source_target_pairs={{0,8},{4,12},{8,0},{12,4},{16,24},{20,28},{24,16},{28,20},{1,9},{5... | collective-permute-start | bytes 4325384 | tf_op jit(solution)/shard_map/ppermute | solution.py:115
  842.0 15.2 %collective-permute-start.53 = (bf16[512,512]{1,0:T(8,128)(2,1)}, bf16[512,512]{1,0:T(8,128)(2,1)}, u32[]{:S(2)}, u32[]{:S(2)}) collective-permute-start(bf16[512,512]{1,0:T(8,128)(2,1)} %add_convert_fusion.21), channel_id=1, source_target_pairs={{0,8},{4,12},{8,0},{12,4},{16,24},{20,28},{24,16},{28,20},{1,9},{5... | collective-permute-start | bytes 1572872 | tf_op jit(solution)/shard_map/ppermute | solution.py:115
  847.4 40.5 %collective-permute-start.56 = (bf16[1408,256]{1,0:T(8,128)(2,1)}, bf16[1408,256]{1,0:T(8,128)(2,1)}, u32[]{:S(2)}, u32[]{:S(2)}) collective-permute-start(bf16[1408,256]{1,0:T(8,128)(2,1)} %add_convert_fusion.14), channel_id=1, source_target_pairs={{0,24},{4,28},{8,16},{12,20},{16,8},{20,12},{24,0},{28,4},{1,25},{... | collective-permute-start | bytes 2162696 | tf_op jit(solution)/shard_map/ppermute | solution.py:115
  858.3 32.9 %collective-permute-start.55 = (bf16[512,256]{1,0:T(8,128)(2,1)S(1)}, bf16[512,256]{1,0:T(8,128)(2,1)S(1)}, u32[]{:S(2)}, u32[]{:S(2)}) collective-permute-start(bf16[512,256]{1,0:T(8,128)(2,1)S(1)} %add_convert_fusion.22), channel_id=1, source_target_pairs={{0,24},{4,28},{8,16},{12,20},{16,8},{20,12},{24,0},{28,4},{1,25},{... | collective-permute-start | bytes 786440 | tf_op jit(solution)/shard_map/ppermute | solution.py:115
  (62 other events, 685.7 us)
Sparse Core Ops, SparseCore 0:
  18.4 50.5 all-gather.2
  175.9 142.1 reduce-scatter.2
  409.0 177.5 reduce-scatter.4
  678.9 161.0 all-reduce.2

commit v7 on v5

--- a/solution.py
+++ b/solution.py
@@ -32,13 +32,13 @@
     "Su": "Su+",
     "0g": "0g+",
     "E1": "Sd- Sd+",
-    "mix": " ".join(["Sg- Su- Su+ Sd-", "Sd+ 0u+"]),
+    "mix": "Sg- Sd- Sd+ 0u+",
     "back": "Su- Su+",
     "1g": "0g- Sd- 0g+",
     "n1": "0d+",
     "1u": "1u+",
-    "norm": "Su-",
-    "h": " ".join(["0u- 0u+ 0g- 0g+", "1g+"]),
+    "norm": "Su- Su+",
+    "h": " ".join(["0u- 0u+ 0g- 0g+", "Su- 1g+"]),
     "q": " ".join(["0u- 0u+ 0d- q+", "0g- 0d+"]),
     "fb": "1u-",
     "r1": "0u- 1d+ 0d-",

time: 908 us -> 930 us (1.024)
  starting transfers between devices: 50.7 us -> 95.8 us
  waiting for transfers between devices: 323 us -> 298 us
    ppermute x57, starting transfers between devices: 50.5 us -> 95.7 us  [swap(): return lax.ppermute(values, axis, pairs)]
    ppermute x57, waiting for transfers between devices: 323 us -> 296 us  [swap(): return lax.ppermute(values, axis, pairs)]
  transfers between devices with their start and end apart: 61 -> 61, of which waited for: 24 -> 25; matrix products, arithmetic and copies ran while one was open for 11% -> 11% of each run, Pallas kernels for 38% -> 37%
where the time goes in v7:
time: 930 us; the launch traced here: 921 us
  Pallas kernels  394 us (42%)
  waiting for transfers between devices  298 us (32%)
  starting transfers between devices  95.8 us (10%)
  other arithmetic  93.8 us (10%)
  local copies, waits for them, and re-layouts  25.3 us (3%)
  between operations  14.7 us (2%)
    pallas_call x26, Pallas kernels, kernel_call(): pl.pallas_call(body, name=name, grid_spec=pltpu.PrefetchScalarGridSpec(nu...  394 us
    ppermute x57, waiting for transfers between devices, swap(): return lax.ppermute(values, axis, pairs)  296 us
    ppermute x57, starting transfers between devices, swap(): return lax.ppermute(values, axis, pairs)  95.7 us
    convert_element_type x18, other arithmetic, collect(): self.sent = self.part(self.size, 2 * self.size).astype(BF16)  40.8 us
  transfers between devices with their start and end apart: 61, of which 25 were waited for; matrix products, arithmetic and copies ran while one was open for 11% of the time, Pallas kernels for 37%

profile of v7, /device:TPU:8, one launch (start us, length us, event | category | flops | bytes accessed | tf_op | source)
XLA Modules:
  0.0 921.5 jit_solution(16920495436217517550)
XLA Ops:
  12.4 4.0 collective-permute-done.2.refs_2_
  21.0 2.8 collective-permute-done.1.refs_1_
  24.3 7.0 prepare.1
  31.3 12.5 %collective-permute-done.refs_0_.refs_3_ = bf16[256,2048]{1,0:T(8,128)(2,1)S(1)} collective-permute-done((bf16[256,2048]{1,0:T(8,128)(2,1)}, bf16[256,2048]{1,0:T(8,128)(2,1)S(1)}, u32[]{:S(2)}, u32[]{:S(2)}) %collective-permute-start) | collective-permute-done | bytes 1048608 | tf_op jit(solution)/shard_map/ppermute | solution.py:115
  48.9 9.8 %project.2 = (bf16[3,1024,512]{2,1,0:T(8,128)(2,1)}, bf16[1024,2048]{1,0:T(8,128)(2,1)}) custom-call(bf16[256,2048]{1,0:T(8,128)(2,1)} %refs_1_, bf16[256,2048]{1,0:T(8,128)(2,1)} %copy-done.12, bf16[1,2048]{1,0:T(2,128)(2,1)} %broadcast_in_dim.45.refs_2_, bf16[3,2048,512]{2,1,0:T(8,128)(2,1)} %refs_0_.3, bf16[3,1,512]{2,1,0:T(2,128)(2,1)} %copy.47.refs_4_, ...), custom_call_target="tpu_custom_call" | custom-call | flops 1 | bytes 1 | tf_op jit(solution)/shard_map/project/pallas_call | solution.py:68
  59.7 9.4 %project.3 = (bf16[3,1024,512]{2,1,0:T(8,128)(2,1)}, bf16[1024,2048]{1,0:T(8,128)(2,1)}) custom-call(bf16[256,2048]{1,0:T(8,128)(2,1)} %copy-done.8, bf16[256,2048]{1,0:T(8,128)(2,1)} %copy-done.10, bf16[1,2048]{1,0:T(2,128)(2,1)} %broadcast_in_dim.45.refs_2_, bf16[3,2048,512]{2,1,0:T(8,128)(2,1)} %refs_0_.3, ...), custom_call_target="tpu_custom_call", output_to_operand_aliasing={{0}: (7, {}), {1}: (8, {})} | custom-call | flops 1 | bytes 1 | tf_op jit(solution)/shard_map/project/pallas_call | solution.py:68
  69.1 9.5 %attend.2 = (bf16[512,512]{1,0:T(8,128)(2,1)}, f32[4,512,1]{2,1,0:T(8,128)}) custom-call(s32[4]{0:T(128)} %iota_xor_fusion.places, bf16[3,1024,512]{2,1,0:T(8,128)(2,1)} %get-tuple-element.191.query.key.value, bf16[3,1024,512]{2,1,0:T(8,128)(2,1)} %get-tuple-element.191.query.key.value, bf16[3,1024,512]{2,1,0:T(8,128)(2,1)} %get-tuple-element.191.query.key.value, ...), custom_call_target="tpu_custom_call" | custom-call | flops 1 | bytes 1 | tf_op jit(solution)/shard_map/attend/pallas_call | solution.py:68
  78.7 6.7 attend.3
  86.3 13.5 %collective-permute-done.9.refs_4_ = bf16[512,512]{1,0:T(8,128)(2,1)S(1)} collective-permute-done((bf16[512,512]{1,0:T(8,128)(2,1)S(1)}, bf16[512,512]{1,0:T(8,128)(2,1)S(1)}, u32[]{:S(2)}, u32[]{:S(2)}) %collective-permute-start.9) | collective-permute-done | bytes 524320 | tf_op jit(solution)/shard_map/ppermute | solution.py:115
  102.9 12.3 %out_project.2 = (bf16[1024,2048]{1,0:T(8,128)(2,1)}, f32[1024,128]{1,0:T(8,128)}, f32[256,2048]{1,0:T(8,128)}) custom-call(bf16[256,2048]{1,0:T(8,128)(2,1)} %refs_1_, bf16[256,2048]{1,0:T(8,128)(2,1)} %copy-done.12, bf16[512,512]{1,0:T(8,128)(2,1)} %get-tuple-element.302.refs_2_.refs_4_, bf16[512,512]{1,0:T(8,128)(2,1)} %collective-permute-done.8.refs_3_, ...), custom_call_target="tpu_custom_call" | custom-call | flops 1 | bytes 1 | tf_op jit(solution)/shard_map/out_project/pallas_call | solution.py:68
  118.0 12.0 %out_project.3 = (bf16[1024,2048]{1,0:T(8,128)(2,1)}, f32[1024,128]{1,0:T(8,128)}, f32[256,2048]{1,0:T(8,128)}) custom-call(bf16[256,2048]{1,0:T(8,128)(2,1)} %copy-done.8, bf16[256,2048]{1,0:T(8,128)(2,1)} %copy-done.10, bf16[512,512]{1,0:T(8,128)(2,1)} %get-tuple-element.198.refs_2_.refs_5_, ...), custom_call_target="tpu_custom_call", output_to_operand_aliasing={{0}: (12, {}), {1}: (13, {})} | custom-call | flops 1 | bytes 1 | tf_op jit(solution)/shard_map/out_project/pallas_call | solution.py:68
  133.7 29.0 %shared_inner.1 = (bf16[1024,1408]{1,0:T(8,128)(2,1)}, bf16[1024,1408]{1,0:T(8,128)(2,1)}, bf16[1024,1408]{1,0:T(8,128)(2,1)}, bf16[1024,2048]{1,0:T(8,128)(2,1)}) custom-call(bf16[1024,2048]{1,0:T(8,128)(2,1)} %get-tuple-element.232.refs_0_.refs_6_, f32[1024,128]{1,0:T(8,128)} %get-tuple-element.206.refs_1_.side, bf16[256,2048]{1,0:T(8,128)(2,1)} %refs_4_.1, ...), custom_call_target="tpu_custom_call" | custom-call | flops 1 | bytes 1 | tf_op jit(solution)/shard_map/shared_inner/pallas_call | solution.py:68
  163.2 12.7 %weight_product.11 = bf16[2048,1408]{1,0:T(8,128)(2,1)} custom-call(s32[8]{0:T(128)} %iota.10.blocks, bf16[1024,2048]{1,0:T(8,128)(2,1)} %get-tuple-element.232.refs_0_.refs_6_, bf16[1024,1408]{1,0:T(8,128)(2,1)} %get-tuple-element.244.refs_1_.gate_grad), custom_call_target="tpu_custom_call" | custom-call | flops 1 | bytes 1 | tf_op jit(solution)/shard_map/weight_product/pallas_call | solution.py:68
  177.2 13.6 %weight_product.12 = (bf16[1408,1024]{1,0:T(8,128)(2,1)}, bf16[1408,1024]{1,0:T(8,128)(2,1)}) custom-call(s32[8]{0:T(128)} %fusion.5.blocks, bf16[1024,2048]{1,0:T(8,128)(2,1)} %get-tuple-element.210.refs_0_, bf16[1024,1408]{1,0:T(8,128)(2,1)} %get-tuple-element.235.refs_1_.act), custom_call_target="tpu_custom_call" | custom-call | flops 1 | bytes 1 | tf_op jit(solution)/shard_map/weight_product/pallas_call | solution.py:68
  192.4 13.4 %weight_product.13 = (bf16[1024,1408]{1,0:T(8,128)(2,1)}, bf16[1024,1408]{1,0:T(8,128)(2,1)}) custom-call(s32[8]{0:T(128)} %fusion.5.blocks, bf16[1024,2048]{1,0:T(8,128)(2,1)} %get-tuple-element.232.refs_0_.refs_6_, bf16[1024,1408]{1,0:T(8,128)(2,1)} %get-tuple-element.217.refs_1_.up_grad), custom_call_target="tpu_custom_call" | custom-call | flops 1 | bytes 1 | tf_op jit(solution)/shard_map/weight_product/pallas_call | solution.py:68
  206.1 21.6 %expert_inner.2 = (bf16[576,1408]{1,0:T(8,128)(2,1)}, bf16[576,1408]{1,0:T(8,128)(2,1)}, bf16[576,1408]{1,0:T(8,128)(2,1)}, bf16[576,2048]{1,0:T(8,128)(2,1)}, bf16[576,2048]{1,0:T(8,128)(2,1)}) custom-call(s32[1]{0:T(128)} %bitcast.1.first, bf16[1024,2048]{1,0:T(8,128)(2,1)} %get-tuple-element.232.refs_0_.refs_6_, ...), custom_call_target="tpu_custom_call" | custom-call | flops 1 | bytes 1 | tf_op jit(solution)/shard_map/expert_inner/pallas_call | solution.py:68
  227.6 11.5 %weight_product.14 = (bf16[1024,1408]{1,0:T(8,128)(2,1)}, bf16[1024,1408]{1,0:T(8,128)(2,1)}) custom-call(s32[8]{0:T(128)} %fusion.5.blocks, bf16[576,2048]{1,0:T(8,128)(2,1)} %get-tuple-element.223.refs_0_, bf16[576,1408]{1,0:T(8,128)(2,1)} %get-tuple-element.226.refs_1_.refs_0_), custom_call_target="tpu_custom_call" | custom-call | flops 1 | bytes 1 | tf_op jit(solution)/shard_map/weight_product/pallas_call | solution.py:68
  240.8 11.5 %weight_product.15 = (bf16[1024,1408]{1,0:T(8,128)(2,1)}, bf16[1024,1408]{1,0:T(8,128)(2,1)}) custom-call(s32[8]{0:T(128)} %fusion.5.blocks, bf16[576,2048]{1,0:T(8,128)(2,1)} %get-tuple-element.223.refs_0_, bf16[576,1408]{1,0:T(8,128)(2,1)} %get-tuple-element.228.refs_1_), custom_call_target="tpu_custom_call" | custom-call | flops 1 | bytes 1 | tf_op jit(solution)/shard_map/weight_product/pallas_call | solution.py:68
  252.3 11.4 %weight_product.16 = (bf16[1408,1024]{1,0:T(8,128)(2,1)}, bf16[1408,1024]{1,0:T(8,128)(2,1)}) custom-call(s32[8]{0:T(128)} %fusion.5.blocks, bf16[576,2048]{1,0:T(8,128)(2,1)} %get-tuple-element.221.refs_0_, bf16[576,1408]{1,0:T(8,128)(2,1)} %get-tuple-element.230.refs_1_.refs_0_), custom_call_target="tpu_custom_call" | custom-call | flops 1 | bytes 1 | tf_op jit(solution)/shard_map/weight_product/pallas_call | solution.py:68
  263.7 22.0 %expert_inner.3 = (bf16[576,1408]{1,0:T(8,128)(2,1)}, bf16[576,1408]{1,0:T(8,128)(2,1)}, bf16[576,1408]{1,0:T(8,128)(2,1)}, bf16[576,2048]{1,0:T(8,128)(2,1)}, bf16[576,2048]{1,0:T(8,128)(2,1)}) custom-call(s32[1]{0:T(128)} %bitcast.1.first, bf16[1024,2048]{1,0:T(8,128)(2,1)} %get-tuple-element.232.refs_0_.refs_6_, ...), custom_call_target="tpu_custom_call" | custom-call | flops 1 | bytes 1 | tf_op jit(solution)/shard_map/expert_inner/pallas_call | solution.py:68
  285.8 3.0 add_convert_fusion.7
  289.2 36.0 %mix.1 = (bf16[256,2048]{1,0:T(8,128)(2,1)}, bf16[256,2048]{1,0:T(8,128)(2,1)}, bf16[256,2048]{1,0:T(8,128)(2,1)}, bf16[256,2048]{1,0:T(8,128)(2,1)}, f32[1024,128]{1,0:T(8,128)}) custom-call(s32[1]{0:T(128)} %bitcast.1.first, f32[1024,128]{1,0:T(8,128)} %get-tuple-element.206.refs_1_.side, bf16[1024,1408]{1,0:T(8,128)(2,1)} %get-tuple-element.235.refs_1_.act, ...), custom_call_target="tpu_custom_call" | custom-call | flops 1 | bytes 1 | tf_op jit(solution)/shard_map/mix/pallas_call | solution.py:68
  325.2 8.6 collective-permute-done.20
  335.7 47.0 %back.1 = (bf16[256,2048]{1,0:T(8,128)(2,1)}, bf16[256,2048]{1,0:T(8,128)(2,1)}, bf16[256,2048]{1,0:T(8,128)(2,1)}, bf16[256,2048]{1,0:T(8,128)(2,1)}, f32[128,2048]{1,0:T(8,128)}) custom-call(f32[1024,128]{1,0:T(8,128)} %get-tuple-element.206.refs_1_.side, f32[1024,128]{1,0:T(8,128)} %get-tuple-element.239.totals, ...), custom_call_target="tpu_custom_call" | custom-call | flops 1 | bytes 1 | tf_op jit(solution)/shard_map/back/pallas_call | solution.py:68
  385.2 2.8 add_convert_fusion.6
  388.0 11.6 %weight_product.17 = (bf16[1024,1408]{1,0:T(8,128)(2,1)}, bf16[1024,1408]{1,0:T(8,128)(2,1)}) custom-call(s32[8]{0:T(128)} %fusion.5.blocks, bf16[576,2048]{1,0:T(8,128)(2,1)} %get-tuple-element.258.refs_0_, bf16[576,1408]{1,0:T(8,128)(2,1)} %get-tuple-element.259.refs_2_.refs_1_), custom_call_target="tpu_custom_call" | custom-call | flops 1 | bytes 1 | tf_op jit(solution)/shard_map/weight_product/pallas_call | solution.py:68
  399.6 10.7 %collective-permute-done.25 = bf16[1024,1408]{1,0:T(8,128)(2,1)S(1)} collective-permute-done((bf16[1024,1408]{1,0:T(8,128)(2,1)}, bf16[1024,1408]{1,0:T(8,128)(2,1)S(1)}, u32[]{:S(2)}, u32[]{:S(2)}) %collective-permute-start.25) | collective-permute-done | bytes 2883616 | tf_op jit(solution)/shard_map/ppermute | solution.py:115
  412.3 3.9 collective-permute-done.24
  417.6 10.8 %weight_product.18 = bf16[2048,1408]{1,0:T(8,128)(2,1)} custom-call(s32[8]{0:T(128)} %iota.11.blocks, bf16[576,2048]{1,0:T(8,128)(2,1)} %get-tuple-element.258.refs_0_, bf16[576,1408]{1,0:T(8,128)(2,1)} %get-tuple-element.264.refs_3_.refs_1_), custom_call_target="tpu_custom_call" | custom-call | flops 1 | bytes 1 | tf_op jit(solution)/shard_map/weight_product/pallas_call | solution.py:68
  431.6 2.7 add_convert_fusion.12
  441.1 18.8 %collective-permute-done.26 = bf16[256,2048]{1,0:T(8,128)(2,1)} collective-permute-done((bf16[256,2048]{1,0:T(8,128)(2,1)}, bf16[256,2048]{1,0:T(8,128)(2,1)}, u32[]{:S(2)}, u32[]{:S(2)}) %collective-permute-start.26) | collective-permute-done | bytes 1048608 | tf_op jit(solution)/shard_map/ppermute | solution.py:115
  463.6 3.9 fusion.6
  467.6 42.9 %collective-permute-done.21 = bf16[512,1408]{1,0:T(8,128)(2,1)S(1)} collective-permute-done((bf16[512,1408]{1,0:T(8,128)(2,1)}, bf16[512,1408]{1,0:T(8,128)(2,1)S(1)}, u32[]{:S(2)}, u32[]{:S(2)}) %collective-permute-start.21) | collective-permute-done | bytes 1441824 | tf_op jit(solution)/shard_map/ppermute | solution.py:115
  515.9 11.8 %weight_product.19 = (bf16[1408,1024]{1,0:T(8,128)(2,1)}, bf16[1408,1024]{1,0:T(8,128)(2,1)}) custom-call(s32[8]{0:T(128)} %fusion.5.blocks, bf16[576,2048]{1,0:T(8,128)(2,1)} %get-tuple-element.271.refs_0_, bf16[576,1408]{1,0:T(8,128)(2,1)} %get-tuple-element.272.refs_1_), custom_call_target="tpu_custom_call" | custom-call | flops 1 | bytes 1 | tf_op jit(solution)/shard_map/weight_product/pallas_call | solution.py:68
  527.7 3.2 add_convert_fusion.4
  530.9 13.8 %collective-permute-done.28 = bf16[512,1408]{1,0:T(8,128)(2,1)} collective-permute-done((bf16[512,1408]{1,0:T(8,128)(2,1)S(1)}, bf16[512,1408]{1,0:T(8,128)(2,1)}, u32[]{:S(2)}, u32[]{:S(2)}) %collective-permute-start.28) | collective-permute-done | bytes 1441824 | tf_op jit(solution)/shard_map/ppermute | solution.py:115
  548.2 15.8 %collective-permute-start.38 = (bf16[512,1408]{1,0:T(8,128)(2,1)}, bf16[512,1408]{1,0:T(8,128)(2,1)}, u32[]{:S(2)}, u32[]{:S(2)}) collective-permute-start(bf16[512,1408]{1,0:T(8,128)(2,1)} %add_convert_fusion.4), channel_id=1, source_target_pairs={{0,8},{4,12},{8,0},{12,4},{16,24},{20,28},{24,16},{28,20},{1,9},{5... | collective-permute-start | bytes 4325384 | tf_op jit(solution)/shard_map/ppermute | solution.py:115
  564.1 3.3 convert_add_fusion.2
  567.5 2.9 collective-permute-start.36
  573.1 6.2 attended_gradient.1.out_grad
  579.2 22.0 %attend_back.1 = (bf16[1024,512]{1,0:T(8,128)(2,1)}, bf16[1024,512]{1,0:T(8,128)(2,1)}, bf16[1024,512]{1,0:T(8,128)(2,1)}, f32[3,8,512]{2,1,0:T(8,128)}) custom-call(s32[4]{0:T(128)} %iota_xor_fusion.places, bf16[3,1024,512]{2,1,0:T(8,128)(2,1)} %get-tuple-element.191.query.key.value, bf16[3,1024,512]{2,1,0:T(8,128)(2,1)} %get-tuple-element.191.query.key.value, ...), custom_call_target="tpu_custom_call" | custom-call | flops 1 | bytes 1 | tf_op jit(solution)/shard_map/attend_back/pallas_call | solution.py:68
  601.2 3.3 pad_maximum_fusion.1.refs_1_
  604.5 13.6 %weight_product.20 = (bf16[1024,1536]{1,0:T(8,128)(2,1)}, bf16[1024,1536]{1,0:T(8,128)(2,1)}) custom-call(s32[8]{0:T(128)} %fusion.5.blocks, bf16[1024,2048]{1,0:T(8,128)(2,1)} %get-tuple-element.294.refs_0_, bf16[1024,1536]{1,0:T(8,128)(2,1)} %pad_maximum_fusion.1.refs_1_), custom_call_target="tpu_custom_call" | custom-call | flops 1 | bytes 1 | tf_op jit(solution)/shard_map/weight_product/pallas_call | solution.py:68
  619.9 15.6 %collective-permute-start.35 = (bf16[256,2048]{1,0:T(8,128)(2,1)S(1)}, bf16[256,2048]{1,0:T(8,128)(2,1)}, u32[]{:S(2)}, u32[]{:S(2)}) collective-permute-start(bf16[256,2048]{1,0:T(8,128)(2,1)S(1)} %copy-done.37), channel_id=1, source_target_pairs={{0,2},{1,3},{2,0},{3,1},{4,6},{5,7},{6,4},{7,5},{8,10},{9,11},{10,... | collective-permute-start | bytes 3145736 | tf_op jit(solution)/shard_map/ppermute | solution.py:115
  638.2 3.2 add_convert_fusion.3
  648.5 9.3 %weight_product.21 = (bf16[512,1024]{1,0:T(8,128)(2,1)}, bf16[512,1024]{1,0:T(8,128)(2,1)}) custom-call(s32[8]{0:T(128)} %fusion.5.blocks, bf16[256,2048]{1,0:T(8,128)(2,1)} %copy-done.14, bf16[256,2048]{1,0:T(8,128)(2,1)} %copy-done.19, bf16[256,2048]{1,0:T(8,128)(2,1)} %copy-done.18, bf16[256,2048]{1,0:T(8,128)(2,1)} %copy-done.20, ...), custom_call_target="tpu_custom_call" | custom-call | flops 1 | bytes 1 | tf_op jit(solution)/shard_map/weight_product/pallas_call | solution.py:68
  657.8 12.4 %first_back.1 = (bf16[256,2048]{1,0:T(8,128)(2,1)}, bf16[256,2048]{1,0:T(8,128)(2,1)}, bf16[256,2048]{1,0:T(8,128)(2,1)}, bf16[256,2048]{1,0:T(8,128)(2,1)}, f32[8,2048]{1,0:T(8,128)}) custom-call(bf16[1024,512]{1,0:T(8,128)(2,1)} %get-tuple-element.304.query, bf16[1024,512]{1,0:T(8,128)(2,1)} %get-tuple-element.295.key, ...), custom_call_target="tpu_custom_call" | custom-call | flops 1 | bytes 1 | tf_op jit(solution)/shard_map/first_back/pallas_call | solution.py:68
  671.6 3.5 add_convert_fusion.10
  679.4 2.8 add_convert_fusion.2
  682.2 16.3 %collective-permute-start.46 = (bf16[512,1408]{1,0:T(8,128)(2,1)}, bf16[512,1408]{1,0:T(8,128)(2,1)}, u32[]{:S(2)}, u32[]{:S(2)}) collective-permute-start(bf16[512,1408]{1,0:T(8,128)(2,1)} %add_convert_fusion.2), channel_id=1, source_target_pairs={{0,8},{4,12},{8,0},{12,4},{16,24},{20,28},{24,16},{28,20},{1,9},{5... | collective-permute-start | bytes 4325384 | tf_op jit(solution)/shard_map/ppermute | solution.py:115
  698.5 3.4 add_bitcast_fusion.3
  704.8 17.0 %collective-permute-done.47 = bf16[1408,256]{1,0:T(8,128)(2,1)S(1)} collective-permute-done((bf16[1408,256]{1,0:T(8,128)(2,1)}, bf16[1408,256]{1,0:T(8,128)(2,1)S(1)}, u32[]{:S(2)}, u32[]{:S(2)}) %collective-permute-start.47) | collective-permute-done | bytes 720928 | tf_op jit(solution)/shard_map/ppermute | solution.py:115
  725.6 21.2 %collective-permute-done.46 = bf16[512,1408]{1,0:T(8,128)(2,1)} collective-permute-done((bf16[512,1408]{1,0:T(8,128)(2,1)}, bf16[512,1408]{1,0:T(8,128)(2,1)}, u32[]{:S(2)}, u32[]{:S(2)}) %collective-permute-start.46) | collective-permute-done | bytes 1441824 | tf_op jit(solution)/shard_map/ppermute | solution.py:115
  752.2 19.6 %collective-permute-done.43 = bf16[256,2048]{1,0:T(8,128)(2,1)S(1)} collective-permute-done((bf16[256,2048]{1,0:T(8,128)(2,1)S(1)}, bf16[256,2048]{1,0:T(8,128)(2,1)S(1)}, u32[]{:S(2)}, u32[]{:S(2)}) %collective-permute-start.43) | collective-permute-done | bytes 1048608 | tf_op jit(solution)/shard_map/ppermute | solution.py:115
  771.8 5.0 collective-permute-start.48
  780.5 3.1 collective-permute-done.49
  785.3 24.8 %collective-permute-done.48 = bf16[512,1536]{1,0:T(8,128)(2,1)S(1)} collective-permute-done((bf16[512,1536]{1,0:T(8,128)(2,1)S(1)}, bf16[512,1536]{1,0:T(8,128)(2,1)S(1)}, u32[]{:S(2)}, u32[]{:S(2)}) %collective-permute-start.48) | collective-permute-done | bytes 1572896 | tf_op jit(solution)/shard_map/ppermute | solution.py:115
  816.0 2.8 collective-permute-start.54
  818.9 2.9 pad_maximum_fusion
  821.8 25.6 %collective-permute-done.50 = bf16[256,1536]{1,0:T(8,128)(2,1)} collective-permute-done((bf16[256,1536]{1,0:T(8,128)(2,1)S(1)}, bf16[256,1536]{1,0:T(8,128)(2,1)}, u32[]{:S(2)}, u32[]{:S(2)}) %collective-permute-start.50) | collective-permute-done | bytes 786464 | tf_op jit(solution)/shard_map/ppermute | solution.py:115
  853.9 13.1 %collective-permute-done.54 = bf16[1408,512]{1,0:T(8,128)(2,1)} collective-permute-done((bf16[1408,512]{1,0:T(8,128)(2,1)}, bf16[1408,512]{1,0:T(8,128)(2,1)}, u32[]{:S(2)}, u32[]{:S(2)}) %collective-permute-start.54) | collective-permute-done | bytes 1441824 | tf_op jit(solution)/shard_map/ppermute | solution.py:115
  874.2 4.1 collective-permute-done.53
  879.8 28.0 %collective-permute-done.56 = bf16[1408,256]{1,0:T(8,128)(2,1)} collective-permute-done((bf16[1408,256]{1,0:T(8,128)(2,1)}, bf16[1408,256]{1,0:T(8,128)(2,1)}, u32[]{:S(2)}, u32[]{:S(2)}) %collective-permute-start.56) | collective-permute-done | bytes 720928 | tf_op jit(solution)/shard_map/ppermute | solution.py:115
  907.7 3.3 add_bitcast_fusion
  (310 shorter events, 125.3 us)
Async XLA Ops:
  7.2 78.2 %all-gather.3.cloned.1.call-start = ((), (), s32[]{:S(2)}) async-start(), calls=%async_computation.5 | async-start | bytes 2359296 | tf_op jit(solution)/shard_map/all_gather | solution.py:1204
  8.2 9.4 %collective-permute-start.11 = (bf16[64,2048]{1,0:T(8,128)(2,1)S(1)}, bf16[64,2048]{1,0:T(8,128)(2,1)S(1)}, u32[]{:S(2)}, u32[]{:S(2)}) collective-permute-start(bf16[64,2048]{1,0:T(8,128)(2,1)S(1)} %constant_dynamic-slice_fusion.1), channel_id=1, source_target_pairs={{0,2},{1,3},{2,0},{3,1},{4,6},{5,7},{6,4},{7,5},{8,10},{9,11},{10,... | collective-permute-start | bytes 786440 | tf_op jit(solution)/shard_map/ppermute | solution.py:115
  11.9 4.5 collective-permute-start.2
  16.4 1.2 collective-permute-start.3
  18.3 306.9 %reduce-scatter.3.cloned.1.call-start = ((), (), s32[]{:S(2)}) async-start(), calls=%async_computation.2 | async-start | bytes 6488064 | tf_op jit(solution)/shard_map/reduce_scatter | solution.py:1165
  18.4 25.5 %collective-permute-start = (bf16[256,2048]{1,0:T(8,128)(2,1)}, bf16[256,2048]{1,0:T(8,128)(2,1)S(1)}, u32[]{:S(2)}, u32[]{:S(2)}) collective-permute-start(bf16[256,2048]{1,0:T(8,128)(2,1)} %refs_1_), channel_id=1, source_target_pairs={{0,2},{1,3},{2,0},{3,1},{4,6},{5,7},{6,4},{7,5},{8,10},{9,11},{10,... | collective-permute-start | bytes 3145736 | tf_op jit(solution)/shard_map/ppermute | solution.py:115
  19.9 58.7 %collective-permute-start.7 = (bf16[512,2048]{1,0:T(8,128)(2,1)}, bf16[512,2048]{1,0:T(8,128)(2,1)}, u32[]{:S(2)}, u32[]{:S(2)}) collective-permute-start(bf16[512,2048]{1,0:T(8,128)(2,1)} %weight), channel_id=1, source_target_pairs={{0,1},{1,0},{2,3},{3,2},{4,5},{5,4},{6,7},{7,6},{8,9},{9,8},{10,11... | collective-permute-start | bytes 6291464 | tf_op jit(solution)/shard_map/ppermute | solution.py:115
  19.9 3.8 collective-permute-start.1
  20.5 27.5 %collective-permute-start.4 = (bf16[256,2048]{1,0:T(8,128)(2,1)}, bf16[256,2048]{1,0:T(8,128)(2,1)S(1)}, u32[]{:S(2)}, u32[]{:S(2)}) collective-permute-start(bf16[256,2048]{1,0:T(8,128)(2,1)} %refs_1_), channel_id=1, source_target_pairs={{0,1},{1,0},{2,3},{3,2},{4,5},{5,4},{6,7},{7,6},{8,9},{9,8},{10,11... | collective-permute-start | bytes 3145736 | tf_op jit(solution)/shard_map/ppermute | solution.py:115
  43.9 14.9 %collective-permute-start.5 = (bf16[256,2048]{1,0:T(8,128)(2,1)S(1)}, bf16[256,2048]{1,0:T(8,128)(2,1)S(1)}, u32[]{:S(2)}, u32[]{:S(2)}) collective-permute-start(bf16[256,2048]{1,0:T(8,128)(2,1)S(1)} %collective-permute-done.refs_0_.refs_3_), channel_id=1, source_target_pairs={{0,1},{1,0},{2,3},{3,2},{4,5},{5,4},{6,7},{7,6},{8,9},{9,8},{10,11... | collective-permute-start | bytes 3145736 | tf_op jit(solution)/shard_map/ppermute | solution.py:115
  43.9 34.8 %collective-permute-start.6 = (bf16[256,2048]{1,0:T(8,128)(2,1)}, bf16[256,2048]{1,0:T(8,128)(2,1)S(1)}, u32[]{:S(2)}, u32[]{:S(2)}) collective-permute-start(bf16[256,2048]{1,0:T(8,128)(2,1)} %refs_4_.1), channel_id=1, source_target_pairs={{0,2},{1,3},{2,0},{3,1},{4,6},{5,7},{6,4},{7,5},{8,10},{9,11},{10,... | collective-permute-start | bytes 3145736 | tf_op jit(solution)/shard_map/ppermute | solution.py:115
  78.7 51.3 %copy-start.5 = (bf16[256,2048]{1,0:T(8,128)(2,1)}, bf16[256,2048]{1,0:T(8,128)(2,1)S(1)}, u32[]{:S(2)}) copy-start(bf16[256,2048]{1,0:T(8,128)(2,1)S(1)} %collective-permute-done.6.refs_4_.refs_5_.refs_6_) | copy-start | bytes 3145732
  85.4 17.5 %collective-permute-start.12 = (bf16[512,2048]{1,0:T(8,128)(2,1)}, bf16[512,2048]{1,0:T(8,128)(2,1)}, u32[]{:S(2)}, u32[]{:S(2)}) collective-permute-start(bf16[512,2048]{1,0:T(8,128)(2,1)} %all-gather.3.cloned.1.call-done), channel_id=1, source_target_pairs={{0,1},{1,0},{2,3},{3,2},{4,5},{5,4},{6,7},{7,6},{8,9},{9,8},{10,11... | collective-permute-start | bytes 6291464 | tf_op jit(solution)/shard_map/ppermute | solution.py:115
  85.7 14.0 %collective-permute-start.9 = (bf16[512,512]{1,0:T(8,128)(2,1)S(1)}, bf16[512,512]{1,0:T(8,128)(2,1)S(1)}, u32[]{:S(2)}, u32[]{:S(2)}) collective-permute-start(bf16[512,512]{1,0:T(8,128)(2,1)S(1)} %copy-done.31), channel_id=1, source_target_pairs={{0,2},{1,3},{2,0},{3,1},{4,6},{5,7},{6,4},{7,5},{8,10},{9,11},{10,... | collective-permute-start | bytes 1572872 | tf_op jit(solution)/shard_map/ppermute | solution.py:115
  86.3 16.6 %collective-permute-start.8 = (bf16[512,512]{1,0:T(8,128)(2,1)}, bf16[512,512]{1,0:T(8,128)(2,1)}, u32[]{:S(2)}, u32[]{:S(2)}) collective-permute-start(bf16[512,512]{1,0:T(8,128)(2,1)} %get-tuple-element.302.refs_2_.refs_4_), channel_id=1, source_target_pairs={{0,1},{1,0},{2,3},{3,2},{4,5},{5,4},{6,7},{7,6},{8,9},{9,8},{10,11... | collective-permute-start | bytes 1572872 | tf_op jit(solution)/shard_map/ppermute | solution.py:115
  99.7 3.2 collective-permute-start.10
  99.8 15.4 %collective-permute-start.14 = (bf16[512,512]{1,0:T(8,128)(2,1)}, bf16[512,512]{1,0:T(8,128)(2,1)S(1)}, u32[]{:S(2)}, u32[]{:S(2)}) collective-permute-start(bf16[512,512]{1,0:T(8,128)(2,1)} %get-tuple-element.302.refs_2_.refs_4_), channel_id=1, source_target_pairs={{0,2},{1,3},{2,0},{3,1},{4,6},{5,7},{6,4},{7,5},{8,10},{9,11},{10,... | collective-permute-start | bytes 1572872 | tf_op jit(solution)/shard_map/ppermute | solution.py:115
  102.7 13.1 %collective-permute-start.13 = (bf16[512,512]{1,0:T(8,128)(2,1)S(1)}, bf16[512,512]{1,0:T(8,128)(2,1)S(1)}, u32[]{:S(2)}, u32[]{:S(2)}) collective-permute-start(bf16[512,512]{1,0:T(8,128)(2,1)S(1)} %copy-done.31), channel_id=1, source_target_pairs={{0,1},{1,0},{2,3},{3,2},{4,5},{5,4},{6,7},{7,6},{8,9},{9,8},{10,11... | collective-permute-start | bytes 1572872 | tf_op jit(solution)/shard_map/ppermute | solution.py:115
  115.2 2.0 collective-permute-start.15
  115.6 14.7 %collective-permute-start.16 = (bf16[256,2048]{1,0:T(8,128)(2,1)S(1)}, bf16[256,2048]{1,0:T(8,128)(2,1)S(1)}, u32[]{:S(2)}, u32[]{:S(2)}) collective-permute-start(bf16[256,2048]{1,0:T(8,128)(2,1)S(1)} %copy-done.3), channel_id=1, source_target_pairs={{0,1},{1,0},{2,3},{3,2},{4,5},{5,4},{6,7},{7,6},{8,9},{9,8},{10,11... | collective-permute-start | bytes 3145736 | tf_op jit(solution)/shard_map/ppermute | solution.py:115
  129.9 2.7 collective-permute-start.17
  175.9 499.2 %reduce-scatter.5.cloned.1.call-start = ((), (), s32[]{:S(2)}) async-start(), calls=%async_computation.3 | async-start | bytes 6488064 | tf_op jit(solution)/shard_map/reduce_scatter | solution.py:1165
  190.8 95.0 %collective-permute-start.18 = (bf16[1408,1024]{1,0:T(8,128)(2,1)}, bf16[1408,1024]{1,0:T(8,128)(2,1)}, u32[]{:S(2)}, u32[]{:S(2)}) collective-permute-start(bf16[1408,1024]{1,0:T(8,128)(2,1)} %get-tuple-element.215), channel_id=1, source_target_pairs={{0,4},{4,0},{8,12},{12,8},{16,20},{20,16},{24,28},{28,24},{1,5},{5... | collective-permute-start | bytes 8650760 | tf_op jit(solution)/shard_map/ppermute | solution.py:115
  205.7 176.9 %collective-permute-start.19 = (bf16[1024,1408]{1,0:T(8,128)(2,1)}, bf16[1024,1408]{1,0:T(8,128)(2,1)}, u32[]{:S(2)}, u32[]{:S(2)}) collective-permute-start(bf16[1024,1408]{1,0:T(8,128)(2,1)} %get-tuple-element.238), channel_id=1, source_target_pairs={{0,4},{4,0},{8,12},{12,8},{16,20},{20,16},{24,28},{28,24},{1,5},{5... | collective-permute-start | bytes 8650760 | tf_op jit(solution)/shard_map/ppermute | solution.py:115
  239.1 171.2 %collective-permute-start.25 = (bf16[1024,1408]{1,0:T(8,128)(2,1)}, bf16[1024,1408]{1,0:T(8,128)(2,1)S(1)}, u32[]{:S(2)}, u32[]{:S(2)}) collective-permute-start(bf16[1024,1408]{1,0:T(8,128)(2,1)} %get-tuple-element.257), channel_id=1, source_target_pairs={{0,4},{4,0},{8,12},{12,8},{16,20},{20,16},{24,28},{28,24},{1,5},{5... | collective-permute-start | bytes 8650760 | tf_op jit(solution)/shard_map/ppermute | solution.py:115
  288.8 45.0 %collective-permute-start.20 = (bf16[1408,512]{1,0:T(8,128)(2,1)}, bf16[1408,512]{1,0:T(8,128)(2,1)}, u32[]{:S(2)}, u32[]{:S(2)}) collective-permute-start(bf16[1408,512]{1,0:T(8,128)(2,1)} %add_convert_fusion.7), channel_id=1, source_target_pairs={{0,8},{4,12},{8,0},{12,4},{16,24},{20,28},{24,16},{28,20},{1,9},{5... | collective-permute-start | bytes 4325384 | tf_op jit(solution)/shard_map/ppermute | solution.py:115
  335.7 49.5 %copy-start.28 = (bf16[1024,1408]{1,0:T(8,128)(2,1)S(1)}, bf16[1024,1408]{1,0:T(8,128)(2,1)}, u32[]{:S(2)}) copy-start(bf16[1024,1408]{1,0:T(8,128)(2,1)} %get-tuple-element.218) | copy-start | bytes 8650756
  382.7 33.5 %collective-permute-start.24 = (bf16[1408,256]{1,0:T(8,128)(2,1)S(1)}, bf16[1408,256]{1,0:T(8,128)(2,1)S(1)}, u32[]{:S(2)}, u32[]{:S(2)}) collective-permute-start(bf16[1408,256]{1,0:T(8,128)(2,1)S(1)} %add_convert_fusion.20), channel_id=1, source_target_pairs={{0,24},{4,28},{8,16},{12,20},{16,8},{20,12},{24,0},{28,4},{1,25},{... | collective-permute-start | bytes 2162696 | tf_op jit(solution)/shard_map/ppermute | solution.py:115
  428.4 420.7 %all-reduce.3.cloned.1.call-start = ((), (), s32[]{:S(2)}) async-start(), calls=%async_computation.4 | async-start | bytes 262144 | tf_op jit(solution)/shard_map/psum | solution.py:1365
  428.5 3.1 collective-permute-start.23
  430.6 30.5 %collective-permute-start.22 = (bf16[256,2048]{1,0:T(8,128)(2,1)}, bf16[256,2048]{1,0:T(8,128)(2,1)}, u32[]{:S(2)}, u32[]{:S(2)}) collective-permute-start(bf16[256,2048]{1,0:T(8,128)(2,1)} %get-tuple-element.252), channel_id=1, source_target_pairs={{0,1},{1,0},{2,3},{3,2},{4,5},{5,4},{6,7},{7,6},{8,9},{9,8},{10,11... | collective-permute-start | bytes 3145736 | tf_op jit(solution)/shard_map/ppermute | solution.py:115
  430.7 97.0 %collective-permute-start.29 = (bf16[1024,1408]{1,0:T(8,128)(2,1)}, bf16[1024,1408]{1,0:T(8,128)(2,1)}, u32[]{:S(2)}, u32[]{:S(2)}) collective-permute-start(bf16[1024,1408]{1,0:T(8,128)(2,1)} %get-tuple-element.270), channel_id=1, source_target_pairs={{0,4},{4,0},{8,12},{12,8},{16,20},{20,16},{24,28},{28,24},{1,5},{5... | collective-permute-start | bytes 8650760 | tf_op jit(solution)/shard_map/ppermute | solution.py:115
  434.3 25.5 %collective-permute-start.26 = (bf16[256,2048]{1,0:T(8,128)(2,1)}, bf16[256,2048]{1,0:T(8,128)(2,1)}, u32[]{:S(2)}, u32[]{:S(2)}) collective-permute-start(bf16[256,2048]{1,0:T(8,128)(2,1)} %add_convert_fusion.12), channel_id=1, source_target_pairs={{0,2},{1,3},{2,0},{3,1},{4,6},{5,7},{6,4},{7,5},{8,10},{9,11},{10,... | collective-permute-start | bytes 3145736 | tf_op jit(solution)/shard_map/ppermute | solution.py:115
  437.4 73.0 %collective-permute-start.21 = (bf16[512,1408]{1,0:T(8,128)(2,1)}, bf16[512,1408]{1,0:T(8,128)(2,1)S(1)}, u32[]{:S(2)}, u32[]{:S(2)}) collective-permute-start(bf16[512,1408]{1,0:T(8,128)(2,1)} %add_convert_fusion.6), channel_id=1, source_target_pairs={{0,8},{4,12},{8,0},{12,4},{16,24},{20,28},{24,16},{28,20},{1,9},{5... | collective-permute-start | bytes 4325384 | tf_op jit(solution)/shard_map/ppermute | solution.py:115
  439.2 105.6 %collective-permute-start.28 = (bf16[512,1408]{1,0:T(8,128)(2,1)S(1)}, bf16[512,1408]{1,0:T(8,128)(2,1)}, u32[]{:S(2)}, u32[]{:S(2)}) collective-permute-start(bf16[512,1408]{1,0:T(8,128)(2,1)S(1)} %copy-done.32), channel_id=1, source_target_pairs={{0,8},{4,12},{8,0},{12,4},{16,24},{20,28},{24,16},{28,20},{1,9},{5... | collective-permute-start | bytes 4325384 | tf_op jit(solution)/shard_map/ppermute | solution.py:115
  459.9 178.3 %collective-permute-start.37 = (bf16[1408,1024]{1,0:T(8,128)(2,1)}, bf16[1408,1024]{1,0:T(8,128)(2,1)}, u32[]{:S(2)}, u32[]{:S(2)}) collective-permute-start(bf16[1408,1024]{1,0:T(8,128)(2,1)} %get-tuple-element.292), channel_id=1, source_target_pairs={{0,4},{4,0},{8,12},{12,8},{16,20},{20,16},{24,28},{28,24},{1,5},{5... | collective-permute-start | bytes 8650760 | tf_op jit(solution)/shard_map/ppermute | solution.py:115
  467.6 80.1 %copy-start.14 = (bf16[256,2048]{1,0:T(8,128)(2,1)}, bf16[256,2048]{1,0:T(8,128)(2,1)S(1)}, u32[]{:S(2)}) copy-start(bf16[256,2048]{1,0:T(8,128)(2,1)S(1)} %get-tuple-element.380.refs_0_) | copy-start | bytes 3145732
  513.2 50.9 %collective-permute-start.33 = (bf16[256,2048]{1,0:T(8,128)(2,1)S(1)}, bf16[256,2048]{1,0:T(8,128)(2,1)S(1)}, u32[]{:S(2)}, u32[]{:S(2)}) collective-permute-start(bf16[256,2048]{1,0:T(8,128)(2,1)S(1)} %get-tuple-element.380.refs_0_), channel_id=1, source_target_pairs={{0,2},{1,3},{2,0},{3,1},{4,6},{5,7},{6,4},{7,5},{8,10},{9,11},{10,... | collective-permute-start | bytes 3145736 | tf_op jit(solution)/shard_map/ppermute | solution.py:115
  513.9 33.6 %collective-permute-start.27 = (bf16[256,1408]{1,0:T(8,128)(2,1)S(1)}, bf16[256,1408]{1,0:T(8,128)(2,1)S(1)}, u32[]{:S(2)}, u32[]{:S(2)}) collective-permute-start(bf16[256,1408]{1,0:T(8,128)(2,1)S(1)} %add_convert_fusion.19), channel_id=1, source_target_pairs={{0,24},{4,28},{8,16},{12,20},{16,8},{20,12},{24,0},{28,4},{1,25},{... | collective-permute-start | bytes 2162696 | tf_op jit(solution)/shard_map/ppermute | solution.py:115
  547.5 20.0 %collective-permute-start.31 = (bf16[256,2048]{1,0:T(8,128)(2,1)S(1)}, bf16[256,2048]{1,0:T(8,128)(2,1)S(1)}, u32[]{:S(2)}, u32[]{:S(2)}) collective-permute-start(bf16[256,2048]{1,0:T(8,128)(2,1)S(1)} %copy-done.67), channel_id=1, source_target_pairs={{0,1},{1,0},{2,3},{3,2},{4,5},{5,4},{6,7},{7,6},{8,9},{9,8},{10,11... | collective-permute-start | bytes 3145736 | tf_op jit(solution)/shard_map/ppermute | solution.py:115
  547.7 24.1 %collective-permute-start.32 = (bf16[256,2048]{1,0:T(8,128)(2,1)S(1)}, bf16[256,2048]{1,0:T(8,128)(2,1)S(1)}, u32[]{:S(2)}, u32[]{:S(2)}) collective-permute-start(bf16[256,2048]{1,0:T(8,128)(2,1)S(1)} %get-tuple-element.380.refs_0_), channel_id=1, source_target_pairs={{0,1},{1,0},{2,3},{3,2},{4,5},{5,4},{6,7},{7,6},{8,9},{9,8},{10,11... | collective-permute-start | bytes 3145736 | tf_op jit(solution)/shard_map/ppermute | solution.py:115
  548.2 71.7 %collective-permute-start.38 = (bf16[512,1408]{1,0:T(8,128)(2,1)}, bf16[512,1408]{1,0:T(8,128)(2,1)}, u32[]{:S(2)}, u32[]{:S(2)}) collective-permute-start(bf16[512,1408]{1,0:T(8,128)(2,1)} %add_convert_fusion.4), channel_id=1, source_target_pairs={{0,8},{4,12},{8,0},{12,4},{16,24},{20,28},{24,16},{28,20},{1,9},{5... | collective-permute-start | bytes 4325384 | tf_op jit(solution)/shard_map/ppermute | solution.py:115
  564.0 7.7 collective-permute-start.34
  567.5 73.9 %collective-permute-start.36 = (bf16[256,1408]{1,0:T(8,128)(2,1)}, bf16[256,1408]{1,0:T(8,128)(2,1)}, u32[]{:S(2)}, u32[]{:S(2)}) collective-permute-start(bf16[256,1408]{1,0:T(8,128)(2,1)} %add_convert_fusion.18), channel_id=1, source_target_pairs={{0,24},{4,28},{8,16},{12,20},{16,8},{20,12},{24,0},{28,4},{1,25},{... | collective-permute-start | bytes 2162696 | tf_op jit(solution)/shard_map/ppermute | solution.py:115
  571.8 99.9 %collective-permute-start.30 = (bf16[256,2048]{1,0:T(8,128)(2,1)}, bf16[256,2048]{1,0:T(8,128)(2,1)}, u32[]{:S(2)}, u32[]{:S(2)}) collective-permute-start(bf16[256,2048]{1,0:T(8,128)(2,1)} %get-tuple-element.277), channel_id=1, source_target_pairs={{0,1},{1,0},{2,3},{3,2},{4,5},{5,4},{6,7},{7,6},{8,9},{9,8},{10,11... | collective-permute-start | bytes 3145736 | tf_op jit(solution)/shard_map/ppermute | solution.py:115
  571.8 107.6 %collective-permute-start.44 = (bf16[1024,1408]{1,0:T(8,128)(2,1)}, bf16[1024,1408]{1,0:T(8,128)(2,1)}, u32[]{:S(2)}, u32[]{:S(2)}) collective-permute-start(bf16[1024,1408]{1,0:T(8,128)(2,1)} %get-tuple-element.320), channel_id=1, source_target_pairs={{0,4},{4,0},{8,12},{12,8},{16,20},{20,16},{24,28},{28,24},{1,5},{5... | collective-permute-start | bytes 8650760 | tf_op jit(solution)/shard_map/ppermute | solution.py:115
  619.9 51.2 %collective-permute-start.35 = (bf16[256,2048]{1,0:T(8,128)(2,1)S(1)}, bf16[256,2048]{1,0:T(8,128)(2,1)}, u32[]{:S(2)}, u32[]{:S(2)}) collective-permute-start(bf16[256,2048]{1,0:T(8,128)(2,1)S(1)} %copy-done.37), channel_id=1, source_target_pairs={{0,2},{1,3},{2,0},{3,1},{4,6},{5,7},{6,4},{7,5},{8,10},{9,11},{10,... | collective-permute-start | bytes 3145736 | tf_op jit(solution)/shard_map/ppermute | solution.py:115
  641.4 35.3 %collective-permute-start.41 = (bf16[1408,512]{1,0:T(8,128)(2,1)}, bf16[1408,512]{1,0:T(8,128)(2,1)}, u32[]{:S(2)}, u32[]{:S(2)}) collective-permute-start(bf16[1408,512]{1,0:T(8,128)(2,1)} %add_convert_fusion.3), channel_id=1, source_target_pairs={{0,8},{4,12},{8,0},{12,4},{16,24},{20,28},{24,16},{28,20},{1,9},{5... | collective-permute-start | bytes 4325384 | tf_op jit(solution)/shard_map/ppermute | solution.py:115
  647.3 27.8 %collective-permute-start.42 = (bf16[256,1408]{1,0:T(8,128)(2,1)}, bf16[256,1408]{1,0:T(8,128)(2,1)}, u32[]{:S(2)}, u32[]{:S(2)}) collective-permute-start(bf16[256,1408]{1,0:T(8,128)(2,1)} %add_convert_fusion.17), channel_id=1, source_target_pairs={{0,24},{4,28},{8,16},{12,20},{16,8},{20,12},{24,0},{28,4},{1,25},{... | collective-permute-start | bytes 2162696 | tf_op jit(solution)/shard_map/ppermute | solution.py:115
  671.1 79.0 %collective-permute-start.45 = (bf16[1024,1536]{1,0:T(8,128)(2,1)}, bf16[1024,1536]{1,0:T(8,128)(2,1)}, u32[]{:S(2)}, u32[]{:S(2)}) collective-permute-start(bf16[1024,1536]{1,0:T(8,128)(2,1)} %get-tuple-element.325), channel_id=1, source_target_pairs={{0,4},{4,0},{8,12},{12,8},{16,20},{20,16},{24,28},{28,24},{1,5},{5... | collective-permute-start | bytes 9437192 | tf_op jit(solution)/shard_map/ppermute | solution.py:115
  675.1 47.3 %collective-permute-start.40 = (bf16[256,2048]{1,0:T(8,128)(2,1)}, bf16[256,2048]{1,0:T(8,128)(2,1)}, u32[]{:S(2)}, u32[]{:S(2)}) collective-permute-start(bf16[256,2048]{1,0:T(8,128)(2,1)} %get-tuple-element.313), channel_id=1, source_target_pairs={{0,1},{1,0},{2,3},{3,2},{4,5},{5,4},{6,7},{7,6},{8,9},{9,8},{10,11... | collective-permute-start | bytes 3145736 | tf_op jit(solution)/shard_map/ppermute | solution.py:115
  682.2 64.6 %collective-permute-start.46 = (bf16[512,1408]{1,0:T(8,128)(2,1)}, bf16[512,1408]{1,0:T(8,128)(2,1)}, u32[]{:S(2)}, u32[]{:S(2)}) collective-permute-start(bf16[512,1408]{1,0:T(8,128)(2,1)} %add_convert_fusion.2), channel_id=1, source_target_pairs={{0,8},{4,12},{8,0},{12,4},{16,24},{20,28},{24,16},{28,20},{1,9},{5... | collective-permute-start | bytes 4325384 | tf_op jit(solution)/shard_map/ppermute | solution.py:115
  702.6 74.2 %collective-permute-start.39 = (bf16[256,2048]{1,0:T(8,128)(2,1)}, bf16[256,2048]{1,0:T(8,128)(2,1)S(1)}, u32[]{:S(2)}, u32[]{:S(2)}) collective-permute-start(bf16[256,2048]{1,0:T(8,128)(2,1)} %get-tuple-element.310), channel_id=1, source_target_pairs={{0,1},{1,0},{2,3},{3,2},{4,5},{5,4},{6,7},{7,6},{8,9},{9,8},{10,11... | collective-permute-start | bytes 3145736 | tf_op jit(solution)/shard_map/ppermute | solution.py:115
  702.9 18.9 %collective-permute-start.47 = (bf16[1408,256]{1,0:T(8,128)(2,1)}, bf16[1408,256]{1,0:T(8,128)(2,1)S(1)}, u32[]{:S(2)}, u32[]{:S(2)}) collective-permute-start(bf16[1408,256]{1,0:T(8,128)(2,1)} %add_convert_fusion.16), channel_id=1, source_target_pairs={{0,24},{4,28},{8,16},{12,20},{16,8},{20,12},{24,0},{28,4},{1,25},{... | collective-permute-start | bytes 2162696 | tf_op jit(solution)/shard_map/ppermute | solution.py:115
  721.8 89.7 %collective-permute-start.51 = (bf16[1408,1024]{1,0:T(8,128)(2,1)S(1)}, bf16[1408,1024]{1,0:T(8,128)(2,1)S(1)}, u32[]{:S(2)}, u32[]{:S(2)}) collective-permute-start(bf16[1408,1024]{1,0:T(8,128)(2,1)S(1)} %copy-done.66), channel_id=1, source_target_pairs={{0,4},{4,0},{8,12},{12,8},{16,20},{20,16},{24,28},{28,24},{1,5},{5... | collective-permute-start | bytes 8650760 | tf_op jit(solution)/shard_map/ppermute | solution.py:115
  722.4 126.7 %collective-permute-start.52 = (bf16[512,1024]{1,0:T(8,128)(2,1)}, bf16[512,1024]{1,0:T(8,128)(2,1)}, u32[]{:S(2)}, u32[]{:S(2)}) collective-permute-start(bf16[512,1024]{1,0:T(8,128)(2,1)} %get-tuple-element.342), channel_id=1, source_target_pairs={{0,4},{4,0},{8,12},{12,8},{16,20},{20,16},{24,28},{28,24},{1,5},{5... | collective-permute-start | bytes 3145736 | tf_op jit(solution)/shard_map/ppermute | solution.py:115
  746.8 25.0 %collective-permute-start.43 = (bf16[256,2048]{1,0:T(8,128)(2,1)S(1)}, bf16[256,2048]{1,0:T(8,128)(2,1)S(1)}, u32[]{:S(2)}, u32[]{:S(2)}) collective-permute-start(bf16[256,2048]{1,0:T(8,128)(2,1)S(1)} %add_convert_fusion.9), channel_id=1, source_target_pairs={{0,2},{1,3},{2,0},{3,1},{4,6},{5,7},{6,4},{7,5},{8,10},{9,11},{10,... | collective-permute-start | bytes 3145736 | tf_op jit(solution)/shard_map/ppermute | solution.py:115
  750.2 33.5 %collective-permute-start.49 = (bf16[256,1408]{1,0:T(8,128)(2,1)S(1)}, bf16[256,1408]{1,0:T(8,128)(2,1)S(1)}, u32[]{:S(2)}, u32[]{:S(2)}) collective-permute-start(bf16[256,1408]{1,0:T(8,128)(2,1)S(1)} %add_convert_fusion.15), channel_id=1, source_target_pairs={{0,24},{4,28},{8,16},{12,20},{16,8},{20,12},{24,0},{28,4},{1,25},{... | collective-permute-start | bytes 2162696 | tf_op jit(solution)/shard_map/ppermute | solution.py:115
  771.8 38.3 %collective-permute-start.48 = (bf16[512,1536]{1,0:T(8,128)(2,1)S(1)}, bf16[512,1536]{1,0:T(8,128)(2,1)S(1)}, u32[]{:S(2)}, u32[]{:S(2)}) collective-permute-start(bf16[512,1536]{1,0:T(8,128)(2,1)S(1)} %add_convert_fusion), channel_id=1, source_target_pairs={{0,8},{4,12},{8,0},{12,4},{16,24},{20,28},{24,16},{28,20},{1,9},{5... | collective-permute-start | bytes 4718600 | tf_op jit(solution)/shard_map/ppermute | solution.py:115
  811.5 36.0 %collective-permute-start.50 = (bf16[256,1536]{1,0:T(8,128)(2,1)S(1)}, bf16[256,1536]{1,0:T(8,128)(2,1)}, u32[]{:S(2)}, u32[]{:S(2)}) collective-permute-start(bf16[256,1536]{1,0:T(8,128)(2,1)S(1)} %add_convert_fusion.13), channel_id=1, source_target_pairs={{0,24},{4,28},{8,16},{12,20},{16,8},{20,12},{24,0},{28,4},{1,25},{... | collective-permute-start | bytes 2359304 | tf_op jit(solution)/shard_map/ppermute | solution.py:115
  816.0 51.0 %collective-permute-start.54 = (bf16[1408,512]{1,0:T(8,128)(2,1)}, bf16[1408,512]{1,0:T(8,128)(2,1)}, u32[]{:S(2)}, u32[]{:S(2)}) collective-permute-start(bf16[1408,512]{1,0:T(8,128)(2,1)} %add_convert_fusion.1), channel_id=1, source_target_pairs={{0,8},{4,12},{8,0},{12,4},{16,24},{20,28},{24,16},{28,20},{1,9},{5... | collective-permute-start | bytes 4325384 | tf_op jit(solution)/shard_map/ppermute | solution.py:115
  851.1 27.1 %collective-permute-start.53 = (bf16[512,512]{1,0:T(8,128)(2,1)}, bf16[512,512]{1,0:T(8,128)(2,1)}, u32[]{:S(2)}, u32[]{:S(2)}) collective-permute-start(bf16[512,512]{1,0:T(8,128)(2,1)} %add_convert_fusion.21), channel_id=1, source_target_pairs={{0,8},{4,12},{8,0},{12,4},{16,24},{20,28},{24,16},{28,20},{1,9},{5... | collective-permute-start | bytes 1572872 | tf_op jit(solution)/shard_map/ppermute | solution.py:115
  869.7 38.0 %collective-permute-start.56 = (bf16[1408,256]{1,0:T(8,128)(2,1)}, bf16[1408,256]{1,0:T(8,128)(2,1)}, u32[]{:S(2)}, u32[]{:S(2)}) collective-permute-start(bf16[1408,256]{1,0:T(8,128)(2,1)} %add_convert_fusion.14), channel_id=1, source_target_pairs={{0,24},{4,28},{8,16},{12,20},{16,8},{20,12},{24,0},{28,4},{1,25},{... | collective-permute-start | bytes 2162696 | tf_op jit(solution)/shard_map/ppermute | solution.py:115
  879.4 31.7 %collective-permute-start.55 = (bf16[512,256]{1,0:T(8,128)(2,1)S(1)}, bf16[512,256]{1,0:T(8,128)(2,1)S(1)}, u32[]{:S(2)}, u32[]{:S(2)}) collective-permute-start(bf16[512,256]{1,0:T(8,128)(2,1)S(1)} %add_convert_fusion.22), channel_id=1, source_target_pairs={{0,24},{4,28},{8,16},{12,20},{16,8},{20,12},{24,0},{28,4},{1,25},{... | collective-permute-start | bytes 786440 | tf_op jit(solution)/shard_map/ppermute | solution.py:115
  (65 other events, 732.5 us)
Sparse Core Ops, SparseCore 0:
  18.4 50.5 all-gather.2
  176.0 141.9 reduce-scatter.2
  428.6 185.9 reduce-scatter.4
  702.7 146.3 all-reduce.2
